TPU v7x, 32 devices: a whole 2x2x4 slice. The times are simulated.
32 devices in a mesh: dp: 8 (over z, x), seq: 4 (over y, core).
Axes of the slice: x: 2, y: 2, z: 4, core: 2. Of those that a mesh axis runs over, the one named last changes fastest.
Arguments:
- clips_in: bfloat16 [32, 8, 196, 768], P('dp', 'seq'), may hold values from -6 to 6
- cotangent: bfloat16 [32, 8, 196, 768], P('dp', 'seq'), may hold values from -6 to 6
- clip_live: int32 [32], P('dp'), may hold values 0 or 1
- weights_in: bfloat16 [7680, 768], P(('dp', 'seq')), may hold values from -0.21875 to 0.21875
- weights_out: bfloat16 [5376, 768], P(('dp', 'seq')), may hold values from -0.75 to 0.75, as said below
- norm_gain: bfloat16 [3, 768], P(None, ('dp', 'seq')), may hold values from 0.25 to 1.75
- shift_rows: bfloat16 [10, 768], P(None, ('dp', 'seq')), may hold values from -1.796875 to 1.796875
- dense_shift: bfloat16 [768], P(('dp', 'seq')), may hold values from -1.796875 to 1.796875
Outputs:
- clips_out: bfloat16 [32, 8, 196, 768], P('dp', 'seq')
- grad_clips: float32 [32, 8, 196, 768], P('dp', 'seq')
- grad_in_rows: float32 [7680, 768], P(('dp', 'seq'))
- grad_out_rows: float32 [5376, 768], P(('dp', 'seq'))
- grad_gain: float32 [3, 768], P(None, ('dp', 'seq'))
- grad_shift: float32 [10, 768], P(None, ('dp', 'seq'))
- grad_dense_shift: float32 [768], P(('dp', 'seq'))
Inputs may be any that keep to these rules, and one draw needn't show every extreme that they name: `clip_live`: 1 marks a clip slot that holds a clip, 0 an empty slot whose gradient is zero. `weights_out`: entries are scaled by their block's fan-in and lie within the stated bound.
All inputs are finite; a program needn't handle non-finite values. No bound on the sum of `clip_live` on one device may be relied on, other than what follows from the above.
Results may differ from a plain program's by a relative error of at most 0.023.
Values may be sent and summed in bfloat16 or wider, within the bound.
No kernel may reach another device: no remote copies, remote signals or barrier semaphores. Data moves between devices by JAX's collectives and lax.ppermute only.
A program may use at most 320 MiB of HBM per device.

v0:
```python
from functools import partial

import jax
import jax.numpy as jnp
from jax import lax
from jax.sharding import PartitionSpec as P

HEADS = 12
HEAD_DIM = 64
PAIR = 2


EPSILON = 1e-06
TEMPORAL = ("csbhd,ctbhd->cbhst", "cbhst,ctbhd->csbhd", "cbhst,csbhd->ctbhd")
SPATIAL = ("cbshd,cbthd->cbhst", "cbhst,cbthd->cbshd", "cbhst,cbshd->cbthd")


def layer_norm(values, gains, shifts):
    centre = values - jnp.mean(values, axis=-1, keepdims=True)
    spread = jnp.mean(centre * centre, axis=-1, keepdims=True)
    return centre * lax.rsqrt(spread + EPSILON) * gains + shifts


def times_rows(left, right):
    return lax.dot_general(
        left, right, (((1,), (1,)), ((), ())), preferred_element_type=jnp.float32
    )


def times_plain(left, right):
    return jnp.dot(left, right, preferred_element_type=jnp.float32)


def outer_sum(left, right):
    return lax.dot_general(
        left, right, (((0,), (0,)), ((), ())), preferred_element_type=jnp.float32
    )


def attend_forward(project, specs):
    scaling = project.shape[-1] ** (-0.5)
    scores = (
        jnp.einsum(
            specs[0],
            project[..., 0, :, :],
            project[..., 1, :, :],
            preferred_element_type=jnp.float32,
        )
        * scaling
    )
    top_score = jnp.max(scores, axis=-1, keepdims=True)
    log_total = top_score + jnp.log(jnp.sum(jnp.exp(scores - top_score), axis=-1, keepdims=True))
    weights = jnp.exp(scores - log_total).astype(jnp.bfloat16)
    mixed_rows = jnp.einsum(
        specs[1], weights, project[..., 2, :, :], preferred_element_type=jnp.float32
    )
    return (mixed_rows.astype(jnp.bfloat16), log_total)


def attend_backward(project, log_total, grad_mixed, specs):
    queries = project[..., 0, :, :]
    key_rows = project[..., 1, :, :]
    values = project[..., 2, :, :]
    scaling = project.shape[-1] ** (-0.5)
    scores = jnp.einsum(specs[0], queries, key_rows, preferred_element_type=jnp.float32) * scaling
    probs = jnp.exp(scores - log_total)
    grad_probs = jnp.einsum(specs[0], grad_mixed, values, preferred_element_type=jnp.float32)
    grad_scores = (
        probs * (grad_probs - jnp.sum(probs * grad_probs, axis=-1, keepdims=True))
    ).astype(jnp.bfloat16)
    grad_queries = (
        jnp.einsum(specs[1], grad_scores, key_rows, preferred_element_type=jnp.float32) * scaling
    )
    grad_keys = (
        jnp.einsum(specs[2], grad_scores, queries, preferred_element_type=jnp.float32) * scaling
    )
    grad_values = jnp.einsum(
        specs[2], probs.astype(jnp.bfloat16), grad_mixed, preferred_element_type=jnp.float32
    )
    stacked = jnp.stack([grad_queries, grad_keys, grad_values], axis=-3).astype(jnp.bfloat16)
    return stacked.reshape(-1, 3 * HEADS * HEAD_DIM)


def forward(clip_block, weights):
    weights_in, weights_out, gains, shifts, dense_bias = weights
    model_width = weights_in.shape[1]
    gains32 = gains.astype(jnp.float32)
    shifts32 = shifts.astype(jnp.float32)
    dense32 = dense_bias.astype(jnp.float32)
    by_patch = lax.all_to_all(clip_block, "seq", split_axis=2, concat_axis=1, tiled=True)
    count, frames, local_patches = (by_patch.shape[0], by_patch.shape[1], by_patch.shape[2])
    local_frames, patches = (clip_block.shape[1], clip_block.shape[2])
    flat_t = by_patch.reshape(-1, model_width).astype(jnp.float32)
    normed_t = layer_norm(flat_t, gains32[0], shifts32[0]).astype(jnp.bfloat16)
    project_t = times_rows(normed_t, weights_in[0 : 3 * model_width]).astype(jnp.bfloat16)
    project_t = project_t.reshape(count, frames, local_patches, 3, HEADS, HEAD_DIM)
    mixed_t, total_t = attend_forward(project_t, TEMPORAL)
    mixed_t = mixed_t.reshape(-1, model_width)
    projected_t = (times_plain(mixed_t, weights_out[0:model_width]) + shifts32[3]).astype(
        jnp.bfloat16
    )
    branch_t = (
        times_plain(projected_t, weights_out[model_width : 2 * model_width]) + shifts32[4]
    ).astype(jnp.bfloat16)
    back_t = lax.all_to_all(
        branch_t.reshape(count, frames, local_patches, model_width),
        "seq",
        split_axis=1,
        concat_axis=2,
        tiled=True,
    )
    after_t = clip_block.reshape(-1, model_width).astype(jnp.float32) + back_t.reshape(
        -1, model_width
    ).astype(jnp.float32)
    normed_s = layer_norm(after_t, gains32[1], shifts32[1]).astype(jnp.bfloat16)
    project_s = times_rows(normed_s, weights_in[3 * model_width : 6 * model_width]).astype(
        jnp.bfloat16
    )
    project_s = project_s.reshape(count, local_frames, patches, 3, HEADS, HEAD_DIM)
    mixed_s, total_s = attend_forward(project_s, SPATIAL)
    mixed_s = mixed_s.reshape(-1, model_width)
    after_s = after_t + (
        times_plain(mixed_s, weights_out[2 * model_width : 3 * model_width]) + shifts32[5]
    )
    normed_m = layer_norm(after_s, gains32[2], shifts32[2]).astype(jnp.bfloat16)
    hidden_pre = times_rows(normed_m, weights_in[6 * model_width :]) + shifts32[6:].reshape(-1)
    hidden = jax.nn.gelu(hidden_pre, approximate=False).astype(jnp.bfloat16)
    output = after_s + (times_plain(hidden, weights_out[3 * model_width :]) + dense32)
    saved = (
        flat_t,
        normed_t,
        project_t,
        mixed_t,
        total_t,
        projected_t,
        after_t,
        normed_s,
        project_s,
        mixed_s,
        total_s,
        after_s,
        normed_m,
        hidden_pre,
        hidden,
    )
    return (output.astype(jnp.bfloat16).reshape(clip_block.shape), saved)


def backward(weights, saved, grad_out, block_shape):
    weights_in, weights_out, gains, shifts, dense_bias = weights
    model_width = weights_in.shape[1]
    gains32 = gains.astype(jnp.float32)
    shifts32 = shifts.astype(jnp.float32)
    (
        flat_t,
        normed_t,
        project_t,
        mixed_t,
        total_t,
        projected_t,
        after_t,
        normed_s,
        project_s,
        mixed_s,
        total_s,
        after_s,
        normed_m,
        hidden_pre,
        hidden,
    ) = saved
    count, local_frames, patches = (block_shape[0], block_shape[1], block_shape[2])
    grad_low = grad_out.astype(jnp.bfloat16)
    dense_out_grad = outer_sum(hidden, grad_low)
    shift_dense = jnp.sum(grad_low.astype(jnp.float32), axis=0)
    grad_hidden = times_rows(grad_low, weights_out[3 * model_width :])
    _, gelu_back = jax.vjp(partial(jax.nn.gelu, approximate=False), hidden_pre)
    grad_pre = gelu_back(grad_hidden)[0].astype(jnp.bfloat16)
    dense_in_grad = outer_sum(grad_pre, normed_m)
    shift_hidden = jnp.sum(grad_pre.astype(jnp.float32), axis=0).reshape(-1, model_width)
    grad_norm_m = times_plain(grad_pre, weights_in[6 * model_width :])
    _, norm_back_m = jax.vjp(layer_norm, after_s, gains32[2], shifts32[2])
    grad_part_s, gain_grad_m, shift_grad_m = norm_back_m(grad_norm_m)
    grad_after_s = grad_out + grad_part_s
    grad_branch_s = grad_after_s.astype(jnp.bfloat16)
    space_out_grad = outer_sum(mixed_s, grad_branch_s)
    shift_space = jnp.sum(grad_branch_s.astype(jnp.float32), axis=0)
    grad_mixed_s = times_rows(grad_branch_s, weights_out[2 * model_width : 3 * model_width]).astype(
        jnp.bfloat16
    )
    grad_mixed_s = grad_mixed_s.reshape(count, local_frames, patches, HEADS, HEAD_DIM)
    grad_project_s = attend_backward(project_s, total_s, grad_mixed_s, SPATIAL)
    space_in_grad = outer_sum(grad_project_s, normed_s)
    grad_norm_s = times_plain(grad_project_s, weights_in[3 * model_width : 6 * model_width])
    _, norm_back_s = jax.vjp(layer_norm, after_t, gains32[1], shifts32[1])
    grad_part_t, gain_grad_s, shift_grad_s = norm_back_s(grad_norm_s)
    grad_after_t = grad_after_s + grad_part_t
    grad_branch_t = grad_after_t.astype(jnp.bfloat16).reshape(block_shape)
    grad_by_patch = lax.all_to_all(grad_branch_t, "seq", split_axis=2, concat_axis=1, tiled=True)
    frames, local_patches = (grad_by_patch.shape[1], grad_by_patch.shape[2])
    grad_by_patch = grad_by_patch.reshape(-1, model_width)
    time_fc_grad = outer_sum(projected_t, grad_by_patch)
    shift_fc = jnp.sum(grad_by_patch.astype(jnp.float32), axis=0)
    grad_projected = times_rows(grad_by_patch, weights_out[model_width : 2 * model_width]).astype(
        jnp.bfloat16
    )
    time_out_grad = outer_sum(mixed_t, grad_projected)
    shift_time = jnp.sum(grad_projected.astype(jnp.float32), axis=0)
    grad_mixed_t = times_rows(grad_projected, weights_out[0:model_width]).astype(jnp.bfloat16)
    grad_mixed_t = grad_mixed_t.reshape(count, frames, local_patches, HEADS, HEAD_DIM)
    grad_project_t = attend_backward(project_t, total_t, grad_mixed_t, TEMPORAL)
    time_in_grad = outer_sum(grad_project_t, normed_t)
    grad_norm_t = times_plain(grad_project_t, weights_in[0 : 3 * model_width])
    _, norm_back_t = jax.vjp(layer_norm, flat_t, gains32[0], shifts32[0])
    grad_first, gain_grad_t, shift_grad_t = norm_back_t(grad_norm_t)
    grad_first = grad_first.astype(jnp.bfloat16).reshape(count, frames, local_patches, model_width)
    grad_returned = lax.all_to_all(grad_first, "seq", split_axis=1, concat_axis=2, tiled=True)
    grad_clip = grad_after_t + grad_returned.reshape(-1, model_width).astype(jnp.float32)
    grads_in = jnp.concatenate([time_in_grad, space_in_grad, dense_in_grad], axis=0)
    grads_out = jnp.concatenate(
        [time_out_grad, time_fc_grad, space_out_grad, dense_out_grad], axis=0
    )
    grads_gain = jnp.stack([gain_grad_t, gain_grad_s, gain_grad_m], axis=0)
    small_shifts = jnp.stack(
        [shift_grad_t, shift_grad_s, shift_grad_m, shift_time, shift_fc, shift_space], axis=0
    )
    grads_shift = jnp.concatenate([small_shifts, shift_hidden], axis=0)
    return (
        grad_clip.reshape(block_shape),
        (grads_in, grads_out, grads_gain, grads_shift, shift_dense),
    )


def grad_terms(clip_block, target_block, live_flag, weights):
    model_width = clip_block.shape[-1]
    count = clip_block.shape[0]
    output, saved = forward(clip_block, weights)
    grad_out = (
        target_block.reshape(count, -1, model_width).astype(jnp.float32) * live_flag[:, None, None]
    )
    grad_clip, terms = backward(weights, saved, grad_out.reshape(-1, model_width), clip_block.shape)
    return (output, grad_clip, terms)


def regroup(total, data_count, group_count):
    row_count, col_count = total.shape
    share = row_count // (data_count * group_count)
    arranged = total.reshape(data_count, group_count, share, col_count).transpose(1, 0, 2, 3)
    return arranged.reshape(group_count, data_count * share, col_count)


def shards(
    clips_in, cotangent, clip_live, weights_in, weights_out, norm_gain, shift_rows, dense_shift
):
    device_count = lax.axis_size(("dp", "seq"))
    data_count = lax.axis_size("dp")
    group_count = lax.axis_size("seq")
    model_width = weights_in.shape[1]
    block_shape = clips_in.shape
    steps_count = block_shape[0] // PAIR
    grouped_in = clips_in.reshape((steps_count, PAIR) + block_shape[1:])
    grouped_grad = cotangent.reshape((steps_count, PAIR) + block_shape[1:])
    live_scale = clip_live.astype(jnp.float32).reshape(steps_count, PAIR)
    zero_grads = (
        jnp.zeros((weights_in.shape[0] * device_count, model_width), jnp.float32),
        jnp.zeros((weights_out.shape[0] * device_count, model_width), jnp.float32),
        jnp.zeros((norm_gain.shape[0], model_width), jnp.float32),
        jnp.zeros((shift_rows.shape[0], model_width), jnp.float32),
        jnp.zeros((model_width,), jnp.float32),
    )

    def single_step(totals, inputs):
        clip_block, target_block, live_flag = inputs
        weights = (
            lax.all_gather(weights_in, ("dp", "seq"), axis=0, tiled=True),
            lax.all_gather(weights_out, ("dp", "seq"), axis=0, tiled=True),
            lax.all_gather(norm_gain, ("dp", "seq"), axis=1, tiled=True),
            lax.all_gather(shift_rows, ("dp", "seq"), axis=1, tiled=True),
            lax.all_gather(dense_shift, ("dp", "seq"), axis=0, tiled=True),
        )
        output, grad_clip, terms = grad_terms(clip_block, target_block, live_flag, weights)
        return (jax.tree.map(jnp.add, totals, terms), (output, grad_clip))

    totals, (outputs, grad_clips) = lax.scan(
        single_step, zero_grads, (grouped_in, grouped_grad, live_scale)
    )
    grads_in, grads_out, grads_gain, grads_shift, grads_dense = totals
    gain_count = grads_gain.shape[0]
    shift_count = grads_shift.shape[0]
    small_terms = jnp.concatenate([grads_gain, grads_shift, grads_dense[None, :]], axis=0).T
    quarters = (
        lax.all_to_all(
            regroup(grads_in, data_count, group_count).astype(jnp.bfloat16),
            "seq",
            split_axis=0,
            concat_axis=0,
            tiled=True,
        ).astype(jnp.float32),
        lax.all_to_all(
            regroup(grads_out, data_count, group_count).astype(jnp.bfloat16),
            "seq",
            split_axis=0,
            concat_axis=0,
            tiled=True,
        ).astype(jnp.float32),
        lax.all_to_all(
            regroup(small_terms, data_count, group_count).astype(jnp.bfloat16),
            "seq",
            split_axis=0,
            concat_axis=0,
            tiled=True,
        ).astype(jnp.float32),
    )
    folded_in = jnp.sum(quarters[0], axis=0)
    folded_out = jnp.sum(quarters[1], axis=0)
    folded_small = jnp.sum(quarters[2], axis=0)
    summed = (
        lax.psum_scatter(folded_in, "dp", scatter_dimension=0, tiled=True),
        lax.psum_scatter(folded_out, "dp", scatter_dimension=0, tiled=True),
        lax.psum_scatter(folded_small, "dp", scatter_dimension=0, tiled=True),
    )
    small_owned = summed[2].T
    return (
        outputs.reshape(block_shape),
        grad_clips.reshape(block_shape),
        summed[0],
        summed[1],
        small_owned[0:gain_count],
        small_owned[gain_count : gain_count + shift_count],
        small_owned[gain_count + shift_count],
    )


def solution(mesh):
    in_specs = (
        P("dp", "seq", None, None),
        P("dp", "seq", None, None),
        P("dp"),
        P(("dp", "seq"), None),
        P(("dp", "seq"), None),
        P(None, ("dp", "seq")),
        P(None, ("dp", "seq")),
        P(("dp", "seq")),
    )
    out_specs = (
        P("dp", "seq", None, None),
        P("dp", "seq", None, None),
        P(("dp", "seq"), None),
        P(("dp", "seq"), None),
        P(None, ("dp", "seq")),
        P(None, ("dp", "seq")),
        P(("dp", "seq")),
    )
    return jax.shard_map(shards, mesh=mesh, in_specs=in_specs, out_specs=out_specs, check_vma=False)
```

profile of v0, /device:TPU:0, one launch (start us, length us, event | category | flops | bytes accessed | tf_op | source)
XLA Modules:
  0.0 1725.2 jit_solution(6226893478616131281)
XLA Ops:
  12.4 1334.5 %while.23 = (s32[]{:T(128)}, f32[7680,768]{1,0:T(8,128)}, f32[5376,768]{1,0:T(8,128)}, f32[3,768]{1,0:T(4,128)}, f32[10,768]{1,0:T(8,128)}, /*index=5*/f32[768]{...) while((s32[]{:T(128)}, f32[7680,768]{1,0:T(8,128)}, ...), condition=%wide.region_30.31_spmd.clone, body=%wide.region_0.30_spmd.clone.sunk | while | flops 49024688128 | bytes 1227382400 | solution.py:283
  24.5 54.3 %all-gather.6 = bf16[32,24,10]{1,2,0:T(8,128)(2,1)S(1)} all-gather(bf16[1,24,10]{1,2,0:T(8,128)(2,1)S(1)} %bitcast.311), channel_id=1, replica_groups=mesh['dp'=8,'seq'=4] {'dp','seq'}, dimensions={0}, use_global_device_ids=true | all-gather | bytes 15840 | tf_op jit(solution)/shard_map/while/body/eval_jaxpr/all_gather | solution.py:277
  79.2 37.9 %all-gather.7 = bf16[32,24,3]{1,2,0:T(4,128)(2,1)S(1)} all-gather(bf16[1,24,3]{1,2,0:T(4,128)(2,1)S(1)} %bitcast.312), channel_id=1, replica_groups=mesh['dp'=8,'seq'=4] {'dp','seq'}, dimensions={0}, use_global_device_ids=true | all-gather | bytes 4752 | tf_op jit(solution)/shard_map/while/body/eval_jaxpr/all_gather | solution.py:276
  138.3 11.9 reshape.461
  169.6 22.3 %all-gather.13.cloned.1.call-done = bf16[5376,768]{1,0:T(8,128)(2,1)} async-done(((bf16[168,768]{1,0:T(8,128)(2,1)}), bf16[5376,768]{1,0:T(8,128)(2,1)}) %all-gather.13.cloned.1.call-update) | async-done | bytes 8257552 | tf_op jit(solution)/shard_map/while/body/eval_jaxpr/all_gather | solution.py:275
  215.6 42.7 %all-reduce.4 = bf16[768]{0:T(1024)(128)(2,1)S(1)} all-reduce(bf16[768]{0:T(1024)(128)(2,1)S(1)} %dynamic-update-slice.3), channel_id=1, replica_groups=mesh['dp'=8,'seq'=4] {'dp','seq'}, use_global_device_ids=true, to_apply=%add | all-reduce | flops 768 | bytes 3072 | tf_op jit(solution)/shard_map/while
  287.9 11.8 reshape.465
  343.7 29.0 %multiply_convert_fusion.12 = (bf16[784,3072]{1,0:T(8,128)(2,1)}, f32[784,3072]{1,0:T(8,128)}, f32[784,3072]{1,0:T(8,128)}) fusion(f32[3072]{0:T(1024)S(1)} %add.415, bf16[7680,768]{1,0:T(8,128)(2,1)} %all-gather.11.cloned.1.call-done, f32[784,768]{1,0:T(8,128)S(1)} %get-tuple-element.424, f32[768]{0:T(1024)S(1)} %get-tuple-element.425, ...), kind=kOutput, calls=%fused_computation.10.clone.1 | convolution fusion | flops 3861344256 | bytes 31236224 | tf_op jit(solution)/shard_map/while/body/eval_jaxpr/dot_general | solution.py:25
  372.7 12.2 convert_reduce_fusion.13
  409.1 10.9 multiply_reduce_fusion.29
  420.0 11.5 multiply_convert_fusion.13
  467.3 14.8 convert_element_type.512
  587.6 12.7 convert_element_type.514
  625.9 16.7 maximum_add_fusion.6
  684.7 51.8 %all-gather.6 = bf16[32,24,10]{1,2,0:T(8,128)(2,1)S(1)} all-gather(bf16[1,24,10]{1,2,0:T(8,128)(2,1)S(1)} %bitcast.311), channel_id=1, replica_groups=mesh['dp'=8,'seq'=4] {'dp','seq'}, dimensions={0}, use_global_device_ids=true | all-gather | bytes 15840 | tf_op jit(solution)/shard_map/while/body/eval_jaxpr/all_gather | solution.py:277
  736.8 38.3 %all-gather.7 = bf16[32,24,3]{1,2,0:T(4,128)(2,1)S(1)} all-gather(bf16[1,24,3]{1,2,0:T(4,128)(2,1)S(1)} %bitcast.312), channel_id=1, replica_groups=mesh['dp'=8,'seq'=4] {'dp','seq'}, dimensions={0}, use_global_device_ids=true | all-gather | bytes 4752 | tf_op jit(solution)/shard_map/while/body/eval_jaxpr/all_gather | solution.py:276
  795.8 11.9 reshape.461
  827.4 22.7 %all-gather.13.cloned.1.call-done = bf16[5376,768]{1,0:T(8,128)(2,1)} async-done(((bf16[168,768]{1,0:T(8,128)(2,1)}), bf16[5376,768]{1,0:T(8,128)(2,1)}) %all-gather.13.cloned.1.call-update) | async-done | bytes 8257552 | tf_op jit(solution)/shard_map/while/body/eval_jaxpr/all_gather | solution.py:275
  873.8 42.7 %all-reduce.4 = bf16[768]{0:T(1024)(128)(2,1)S(1)} all-reduce(bf16[768]{0:T(1024)(128)(2,1)S(1)} %dynamic-update-slice.3), channel_id=1, replica_groups=mesh['dp'=8,'seq'=4] {'dp','seq'}, use_global_device_ids=true, to_apply=%add | all-reduce | flops 768 | bytes 3072 | tf_op jit(solution)/shard_map/while
  946.1 11.8 reshape.465
  1001.7 29.0 %multiply_convert_fusion.12 = (bf16[784,3072]{1,0:T(8,128)(2,1)}, f32[784,3072]{1,0:T(8,128)}, f32[784,3072]{1,0:T(8,128)}) fusion(f32[3072]{0:T(1024)S(1)} %add.415, bf16[7680,768]{1,0:T(8,128)(2,1)} %all-gather.11.cloned.1.call-done, f32[784,768]{1,0:T(8,128)S(1)} %get-tuple-element.424, f32[768]{0:T(1024)S(1)} %get-tuple-element.425, ...), kind=kOutput, calls=%fused_computation.10.clone.1 | convolution fusion | flops 3861344256 | bytes 31236224 | tf_op jit(solution)/shard_map/while/body/eval_jaxpr/dot_general | solution.py:25
  1030.7 12.4 convert_reduce_fusion.13
  1067.0 10.9 multiply_reduce_fusion.29
  1078.0 11.5 multiply_convert_fusion.13
  1125.4 14.8 convert_element_type.512
  1245.8 12.7 convert_element_type.514
  1284.0 22.4 %maximum_add_fusion.6 = f32[7680,768]{1,0:T(8,128)} fusion(f32[3072,768]{1,0:T(8,128)S(1)} %bitcast.299, f32[2304,768]{1,0:T(8,128)} %fusion.228, f32[2304,768]{1,0:T(8,128)} %fusion.231, f32[7680,768]{1,0:T(8,128)} %get-tuple-element.485, pred[]{:T(512)S(6)} %compare.3), kind=kLoop, calls=%fused_computation.clone.1 | loop fusion | flops 23592960 | bytes 70778880 | tf_op jit(solution)/shard_map/while/body/eval_jaxpr/add | solution.py:281
  1306.5 14.0 maximum_add_fusion.7
  1382.1 78.1 %all-to-all-done.5 = bf16[4,1344,768]{2,1,0:T(8,128)(2,1)} async-done(((bf16[4,1344,768]{2,1,0:T(8,128)(2,1)}), bf16[4,1344,768]{2,1,0:T(8,128)(2,1)}, u32[]{:S(2)}, u32[]{:S(2)}) %all-to-all-start.5) | async-done | bytes 8257568 | tf_op jit(solution)/shard_map/all_to_all | solution.py:298
  1473.5 122.7 %all-to-all-done.4 = bf16[4,1920,768]{2,1,0:T(8,128)(2,1)} async-done(((bf16[4,1920,768]{2,1,0:T(8,128)(2,1)}), bf16[4,1920,768]{2,1,0:T(8,128)(2,1)}, u32[]{:S(2)}, u32[]{:S(2)}) %all-to-all-start.4) | async-done | bytes 11796512 | tf_op jit(solution)/shard_map/all_to_all | solution.py:291
  1614.3 38.4 %all-reduce.2 = f32[192,14]{0,1:T(8,128)S(1)} all-reduce(f32[192,14]{0,1:T(8,128)S(1)} %convert_reduce_fusion.7), channel_id=4, replica_groups=mesh['dp'=8,'seq'=4] {'dp'}, use_global_device_ids=true, to_apply=%region_36.37.clone | all-reduce | flops 2688 | bytes 21504
  1654.5 63.4 %reduce-scatter.4.cloned.1.call-done = f32[240,768]{1,0:T(8,128)} async-done(((f32[1920,768]{1,0:T(8,128)}), f32[240,768]{1,0:T(8,128)}) %reduce-scatter.4.cloned.1.call-update) | async-done | bytes 737296 | tf_op jit(solution)/shard_map/reduce_scatter | solution.py:317
  (728 shorter events, 801.7 us)
Async XLA Ops:
  12.7 196.9 %copy-start.74 = (f32[2,2]{1,0:T(2,128)}, f32[2,2]{1,0:T(2,128)S(1)}, u32[]{:S(2)}) copy-start(f32[2,2]{1,0:T(2,128)S(1)} %get-tuple-element.519) | copy-start | bytes 52 | tf_op jit(solution)/shard_map/while
  12.7 117.7 %all-gather.11.cloned.1.call-start = ((), (), s32[]{:S(2)}) async-start(), calls=%async_computation.11 | async-start | bytes 12165120 | tf_op jit(solution)/shard_map/while/body/eval_jaxpr/all_gather | solution.py:274
  13.4 178.5 %all-gather.13.cloned.1.call-start = ((), (), s32[]{:S(2)}) async-start(), calls=%async_computation.12 | async-start | bytes 8515584 | tf_op jit(solution)/shard_map/while/body/eval_jaxpr/all_gather | solution.py:275
  20.2 97.3 %all-to-all-start = ((bf16[2,2,196,768]{3,1,0,2:T(2,128)(2,1)}), bf16[2,2,196,768]{3,1,0,2:T(2,128)(2,1)}, u32[]{:S(2)}, u32[]{:S(2)}) async-start(bf16[2,2,196,768]{3,1,0,2:T(2,128)(2,1)} %copy.396), calls=%async_computation | async-start | bytes 2408448 | tf_op jit(solution)/shard_map/while/body/eval_jaxpr/all_to_all | solution.py:90
  117.5 143.3 %copy-start.48 = (f32[768]{0:T(1024)}, f32[768]{0:T(1024)S(1)}, u32[]{:S(2)}) copy-start(f32[768]{0:T(1024)S(1)} %get-tuple-element.406) | copy-start | bytes 9220 | tf_op jit(solution)/shard_map/while
  117.5 162.3 %copy-start.42 = (f32[768]{0:T(1024)}, f32[768]{0:T(1024)S(1)}, u32[]{:S(2)}) copy-start(f32[768]{0:T(1024)S(1)} %get-tuple-element.417) | copy-start | bytes 9220 | tf_op jit(solution)/shard_map/while
  117.5 162.3 %copy-start.55 = (f32[768]{0:T(1024)}, f32[768]{0:T(1024)S(1)}, u32[]{:S(2)}) copy-start(f32[768]{0:T(1024)S(1)} %get-tuple-element.416) | copy-start | bytes 9220 | tf_op jit(solution)/shard_map/while
  205.2 59.2 %all-to-all-start.1 = ((bf16[2,8,49,768]{3,0,2,1:T(2,128)(2,1)}), bf16[2,8,49,768]{3,0,2,1:T(2,128)(2,1)}, u32[]{:S(2)}, u32[]{:S(2)}) async-start(bf16[2,8,49,768]{3,0,2,1:T(2,128)(2,1)} %copy.405), calls=%async_computation.1 | async-start | bytes 2408448 | tf_op jit(solution)/shard_map/while/body/eval_jaxpr/all_to_all | solution.py:105
  343.2 50.2 %copy-start.25 = (f32[784,768]{1,0:T(8,128)}, f32[784,768]{1,0:T(8,128)S(1)}, u32[]{:S(2)}) copy-start(f32[784,768]{1,0:T(8,128)S(1)} %get-tuple-element.424) | copy-start | bytes 7225348 | tf_op jit(solution)/shard_map/while
  343.7 29.0 %copy-start.31 = (f32[784,768]{1,0:T(8,128)S(1)}, f32[784,768]{1,0:T(8,128)}, u32[]{:S(2)}) copy-start(f32[784,768]{1,0:T(8,128)} %reshape.467) | copy-start | bytes 7225348 | tf_op jit(solution)/shard_map/while
  394.8 95.8 %copy-start.5 = (f32[784,768]{1,0:T(8,128)}, f32[784,768]{1,0:T(8,128)S(1)}, u32[]{:S(2)}) copy-start(f32[784,768]{1,0:T(8,128)S(1)} %get-tuple-element.436) | copy-start | bytes 7225348 | tf_op jit(solution)/shard_map/while
  499.1 41.7 %all-to-all-start.2 = ((bf16[2,2,196,768]{3,1,0,2:T(2,128)(2,1)}), bf16[2,2,196,768]{3,1,0,2:T(2,128)(2,1)}, u32[]{:S(2)}, u32[]{:S(2)}) async-start(bf16[2,2,196,768]{3,1,0,2:T(2,128)(2,1)} %copy.414), calls=%async_computation.2 | async-start | bytes 2408448 | tf_op jit(solution)/shard_map/while/body/eval_jaxpr/all_to_all | solution.py:198
  612.7 42.3 %all-to-all-start.3 = ((bf16[2,8,49,768]{3,0,2,1:T(2,128)(2,1)}), bf16[2,8,49,768]{3,0,2,1:T(2,128)(2,1)S(1)}, u32[]{:S(2)}, u32[]{:S(2)}) async-start(bf16[2,8,49,768]{3,0,2,1:T(2,128)(2,1)} %copy.420), calls=%async_computation.3 | async-start | bytes 2408448 | tf_op jit(solution)/shard_map/while/body/eval_jaxpr/all_to_all | solution.py:216
  673.0 194.7 %copy-start.74 = (f32[2,2]{1,0:T(2,128)}, f32[2,2]{1,0:T(2,128)S(1)}, u32[]{:S(2)}) copy-start(f32[2,2]{1,0:T(2,128)S(1)} %get-tuple-element.519) | copy-start | bytes 52 | tf_op jit(solution)/shard_map/while
  673.0 114.9 %all-gather.11.cloned.1.call-start = ((), (), s32[]{:S(2)}) async-start(), calls=%async_computation.11 | async-start | bytes 12165120 | tf_op jit(solution)/shard_map/while/body/eval_jaxpr/all_gather | solution.py:274
  673.8 176.3 %all-gather.13.cloned.1.call-start = ((), (), s32[]{:S(2)}) async-start(), calls=%async_computation.12 | async-start | bytes 8515584 | tf_op jit(solution)/shard_map/while/body/eval_jaxpr/all_gather | solution.py:275
  680.4 95.1 %all-to-all-start = ((bf16[2,2,196,768]{3,1,0,2:T(2,128)(2,1)}), bf16[2,2,196,768]{3,1,0,2:T(2,128)(2,1)}, u32[]{:S(2)}, u32[]{:S(2)}) async-start(bf16[2,2,196,768]{3,1,0,2:T(2,128)(2,1)} %copy.396), calls=%async_computation | async-start | bytes 2408448 | tf_op jit(solution)/shard_map/while/body/eval_jaxpr/all_to_all | solution.py:90
  775.5 143.5 %copy-start.48 = (f32[768]{0:T(1024)}, f32[768]{0:T(1024)S(1)}, u32[]{:S(2)}) copy-start(f32[768]{0:T(1024)S(1)} %get-tuple-element.406) | copy-start | bytes 9220 | tf_op jit(solution)/shard_map/while
  775.5 162.5 %copy-start.42 = (f32[768]{0:T(1024)}, f32[768]{0:T(1024)S(1)}, u32[]{:S(2)}) copy-start(f32[768]{0:T(1024)S(1)} %get-tuple-element.417) | copy-start | bytes 9220 | tf_op jit(solution)/shard_map/while
  775.5 162.5 %copy-start.55 = (f32[768]{0:T(1024)}, f32[768]{0:T(1024)S(1)}, u32[]{:S(2)}) copy-start(f32[768]{0:T(1024)S(1)} %get-tuple-element.416) | copy-start | bytes 9220 | tf_op jit(solution)/shard_map/while
  863.4 59.2 %all-to-all-start.1 = ((bf16[2,8,49,768]{3,0,2,1:T(2,128)(2,1)}), bf16[2,8,49,768]{3,0,2,1:T(2,128)(2,1)}, u32[]{:S(2)}, u32[]{:S(2)}) async-start(bf16[2,8,49,768]{3,0,2,1:T(2,128)(2,1)} %copy.405), calls=%async_computation.1 | async-start | bytes 2408448 | tf_op jit(solution)/shard_map/while/body/eval_jaxpr/all_to_all | solution.py:105
  1001.2 50.3 %copy-start.25 = (f32[784,768]{1,0:T(8,128)}, f32[784,768]{1,0:T(8,128)S(1)}, u32[]{:S(2)}) copy-start(f32[784,768]{1,0:T(8,128)S(1)} %get-tuple-element.424) | copy-start | bytes 7225348 | tf_op jit(solution)/shard_map/while
  1001.7 29.0 %copy-start.31 = (f32[784,768]{1,0:T(8,128)S(1)}, f32[784,768]{1,0:T(8,128)}, u32[]{:S(2)}) copy-start(f32[784,768]{1,0:T(8,128)} %reshape.467) | copy-start | bytes 7225348 | tf_op jit(solution)/shard_map/while
  1052.9 95.8 %copy-start.5 = (f32[784,768]{1,0:T(8,128)}, f32[784,768]{1,0:T(8,128)S(1)}, u32[]{:S(2)}) copy-start(f32[784,768]{1,0:T(8,128)S(1)} %get-tuple-element.436) | copy-start | bytes 7225348 | tf_op jit(solution)/shard_map/while
  1157.2 41.5 %all-to-all-start.2 = ((bf16[2,2,196,768]{3,1,0,2:T(2,128)(2,1)}), bf16[2,2,196,768]{3,1,0,2:T(2,128)(2,1)}, u32[]{:S(2)}, u32[]{:S(2)}) async-start(bf16[2,2,196,768]{3,1,0,2:T(2,128)(2,1)} %copy.414), calls=%async_computation.2 | async-start | bytes 2408448 | tf_op jit(solution)/shard_map/while/body/eval_jaxpr/all_to_all | solution.py:198
  1270.9 53.0 %all-to-all-start.3 = ((bf16[2,8,49,768]{3,0,2,1:T(2,128)(2,1)}), bf16[2,8,49,768]{3,0,2,1:T(2,128)(2,1)S(1)}, u32[]{:S(2)}, u32[]{:S(2)}) async-start(bf16[2,8,49,768]{3,0,2,1:T(2,128)(2,1)} %copy.420), calls=%async_computation.3 | async-start | bytes 2408448 | tf_op jit(solution)/shard_map/while/body/eval_jaxpr/all_to_all | solution.py:216
  1274.6 31.8 %slice-start.2 = ((s8[9437184]{0:T(1024)(128)(4,1)}), s8[4194304]{0:T(1024)(128)(4,1)S(1)}, s32[]{:S(2)}) async-start(s8[9437184]{0:T(1024)(128)(4,1)} %bitcast.296), calls=%async_computation.15 | async-start | bytes 8388608 | tf_op jit(solution)/shard_map/while
  1362.8 97.4 %all-to-all-start.5 = ((bf16[4,1344,768]{2,1,0:T(8,128)(2,1)}), bf16[4,1344,768]{2,1,0:T(8,128)(2,1)}, u32[]{:S(2)}, u32[]{:S(2)}) async-start(bf16[4,1344,768]{2,1,0:T(8,128)(2,1)} %bitcast.306), calls=%async_computation.6 | async-start | bytes 16515072 | tf_op jit(solution)/shard_map/all_to_all | solution.py:298
  1460.2 135.9 %all-to-all-start.4 = ((bf16[4,1920,768]{2,1,0:T(8,128)(2,1)}), bf16[4,1920,768]{2,1,0:T(8,128)(2,1)}, u32[]{:S(2)}, u32[]{:S(2)}) async-start(bf16[4,1920,768]{2,1,0:T(8,128)(2,1)} %bitcast.303), calls=%async_computation.4 | async-start | bytes 23592960 | tf_op jit(solution)/shard_map/all_to_all | solution.py:291
  1466.5 188.0 %reduce-scatter.6.cloned.1.call-start = ((), (), s32[]{:S(2)}) async-start(), calls=%async_computation.10 | async-start | bytes 4644864 | tf_op jit(solution)/shard_map/reduce_scatter | solution.py:318
  1473.4 244.4 %reduce-scatter.4.cloned.1.call-start = ((), (), s32[]{:S(2)}) async-start(), calls=%async_computation.9 | async-start | bytes 6635520 | tf_op jit(solution)/shard_map/reduce_scatter | solution.py:317
  1607.1 7.2 all-to-all-start.6
  (161 other events, 1015.8 us)
Sparse Core Ops, SparseCore 0:
  16.4 97.3 all-gather.10
  116.7 75.2 all-gather.12
  676.8 95.3 all-gather.10
  774.9 75.1 all-gather.12
Sparse Core Ops, SparseCore 1:
  1473.5 88.6 reduce-scatter.5
  1605.4 112.4 reduce-scatter.3
where the time goes:
time: 1730 us
  local copies, waits for them, and re-layouts  416 us (24%)
  matrix products  395 us (23%)
  waiting for transfers between devices  314 us (18%)
  blocking collectives  306 us (18%)
  other arithmetic  219 us (13%)
  starting transfers between devices  49.2 us (3%)
    dot_general x14, matrix products, times_rows(): lax.dot_general(left, right, (((1,), (1,)), ((), ())), preferred_element_...  132 us
    all_to_all x1, waiting for transfers between devices, shards(): lax.all_to_all(regroup(grads_in, data_count, group_count).astype(jnp.bflo...  123 us
    all_gather x2, blocking collectives, single_step(): lax.all_gather(shift_rows, ('dp', 'seq'), axis=1, tiled=True)  106 us
    convert_element_type x8, local copies, waits for them, and re-layouts, attend_backward(): jnp.stack([grad_queries, grad_keys, grad_values], axis=-3)  90.6 us
    dot_general x14, matrix products, outer_sum(): lax.dot_general(left, right, (((0,), (0,)), ((), ())), preferred_element_...  89.1 us
    while x2, blocking collectives  85.5 us
    dot_general x14, matrix products, times_plain(): return jnp.dot(left, right, preferred_element_type=jnp.float32)  80.5 us
    all_to_all x1, waiting for transfers between devices, shards(): lax.all_to_all(regroup(grads_out, data_count, group_count).astype(jnp.bfl...  78.1 us
  transfers between devices with their start and end apart: 17, of which 6 were waited for; matrix products, arithmetic and copies ran while one was open for 19% of the time, Pallas kernels for 0%

commit v1 on v0

v1 whole, which is shorter than its diff:
```python
from functools import partial

import jax
import jax.numpy as jnp
from jax import lax
from jax.experimental import pallas as pl
from jax.experimental.pallas import tpu as pltpu
from jax.sharding import PartitionSpec as P

HEADS = 12
HEAD_DIM = 64
EPSILON = 1e-06
PAIRS = HEADS // 2
LANES = 2 * HEAD_DIM
SUB = 16
NEG = -1e30
F32 = jnp.float32
BF16 = jnp.bfloat16


def nt(left, right):
    return lax.dot_general(left, right, (((1,), (1,)), ((), ())), preferred_element_type=F32)


def nn(left, right):
    return lax.dot_general(left, right, (((1,), (0,)), ((), ())), preferred_element_type=F32)


def tn(left, right):
    return lax.dot_general(left, right, (((0,), (0,)), ((), ())), preferred_element_type=F32)


def split_heads(pair):
    first = lax.broadcasted_iota(jnp.int32, pair.shape, 1) < HEAD_DIM
    zero = jnp.zeros_like(pair)
    return jnp.concatenate([jnp.where(first, pair, zero), jnp.where(first, zero, pair)], axis=0)


def join_heads(stacked):
    rows = stacked.shape[0] // 2
    first = lax.broadcasted_iota(jnp.int32, (rows, LANES), 1) < HEAD_DIM
    return jnp.where(first, stacked[:rows], stacked[rows:])


def pair_forward(queries, keys, values, keep):
    stacked = split_heads(queries * jnp.asarray(HEAD_DIM**-0.5, BF16))
    scores = jnp.where(keep, nt(stacked, keys), NEG)
    top = jnp.max(scores, axis=1, keepdims=True)
    weights = jnp.exp(scores - top)
    total = jnp.sum(weights, axis=1, keepdims=True)
    probs = (weights * (1.0 / total)).astype(BF16)
    return join_heads(nn(probs, values)).astype(BF16)


def pair_backward(queries, keys, values, grad, keep):
    scaling = HEAD_DIM**-0.5
    stacked = split_heads(queries * jnp.asarray(scaling, BF16))
    grads = split_heads(grad)
    scores = jnp.where(keep, nt(keys, stacked), NEG)
    top = jnp.max(scores, axis=0, keepdims=True)
    weights = jnp.exp(scores - top)
    total = jnp.sum(weights, axis=0, keepdims=True)
    probs = weights * (1.0 / total)
    grad_probs = nt(values, grads)
    mean = jnp.sum(probs * grad_probs, axis=0, keepdims=True)
    grad_scores = (probs * (grad_probs - mean)).astype(BF16)
    grad_values = nn(probs.astype(BF16), grads)
    grad_keys = nn(grad_scores, stacked)
    grad_queries = join_heads(tn(grad_scores, keys)) * scaling
    return (grad_queries.astype(BF16), grad_keys.astype(BF16), grad_values.astype(BF16))


def columns(kind, pair):
    start = (kind * PAIRS + pair) * LANES
    return slice(start, start + LANES)


def load(ref, cols):
    block = ref[..., cols]
    return block.reshape(-1, LANES)


def store(ref, cols, block):
    ref[..., cols] = block.reshape(ref.shape[:-1] + (LANES,))


def keep_mask(shape, key_axis, group, patches):
    key = lax.broadcasted_iota(jnp.int32, shape, key_axis)
    if group is None:
        return key < patches
    query = lax.broadcasted_iota(jnp.int32, shape, 1 - key_axis)
    return (key % group) == (query % group)


def forward_kernel(group, patches, project_ref, mixed_ref):
    rows = project_ref.size // project_ref.shape[-1]
    keep = keep_mask((2 * rows, rows), 1, group, patches)
    for pair in range(PAIRS):
        mixed = pair_forward(
            load(project_ref, columns(0, pair)),
            load(project_ref, columns(1, pair)),
            load(project_ref, columns(2, pair)),
            keep,
        )
        store(mixed_ref, columns(0, pair), mixed)


def backward_kernel(group, patches, project_ref, grad_ref, out_ref):
    rows = project_ref.size // project_ref.shape[-1]
    keep = keep_mask((rows, 2 * rows), 0, group, patches)
    for pair in range(PAIRS):
        results = pair_backward(
            load(project_ref, columns(0, pair)),
            load(project_ref, columns(1, pair)),
            load(project_ref, columns(2, pair)),
            load(grad_ref, columns(0, pair)),
            keep,
        )
        for kind, result in enumerate(results):
            store(out_ref, columns(kind, pair), result)


def attention_call(kernel, arrays, out_cols, temporal, patches):
    clips, frames, rows, _ = arrays[0].shape
    if temporal:
        group, steps, shape = SUB, rows // SUB, (1, frames, SUB)
        index = lambda c, i: (c, 0, i, 0)
    else:
        group, steps, shape = None, frames, (1, 1, rows)
        index = lambda c, i: (c, i, 0, 0)
    return pl.pallas_call(
        partial(kernel, group, patches),
        grid=(clips, steps),
        in_specs=[pl.BlockSpec(shape + (a.shape[-1],), index) for a in arrays],
        out_specs=pl.BlockSpec(shape + (out_cols,), index),
        out_shape=jax.ShapeDtypeStruct((clips, frames, rows, out_cols), BF16),
        compiler_params=pltpu.CompilerParams(dimension_semantics=("arbitrary", "arbitrary")),
    )(*arrays)


def norm_parts(values):
    centre = values - jnp.mean(values, axis=-1, keepdims=True)
    spread = jnp.mean(centre * centre, axis=-1, keepdims=True)
    scale = lax.rsqrt(spread + EPSILON)
    return (centre * scale, scale)


def layer_norm(values, gains, shifts):
    return (norm_parts(values)[0] * gains + shifts).astype(BF16)


def norm_backward(values, gains, grad):
    normed, scale = norm_parts(values)
    scaled = grad * gains
    first = jnp.mean(scaled, axis=-1, keepdims=True)
    second = jnp.mean(scaled * normed, axis=-1, keepdims=True)
    inner = (scaled - first - normed * second) * scale
    return (inner, jnp.sum(grad * normed, axis=0), jnp.sum(grad, axis=0))


def gelu_parts(values):
    cdf = 0.5 * (1.0 + lax.erf(values * (0.5**0.5)))
    density = jnp.exp(-0.5 * values * values) * 0.3989422804014327
    return (values * cdf, cdf + values * density)


def column_sum(rows):
    return jnp.sum(rows.astype(F32), axis=0)


def block(clip, target, weights_in, weights_out, gains, shifts, dense_bias, patches):
    shape = clip.shape
    width = shape[-1]
    grid = shape[:3]
    gains32, shifts32, dense32 = (gains.astype(F32), shifts.astype(F32), dense_bias.astype(F32))
    in_t, in_s, in_m = (
        weights_in[: 3 * width],
        weights_in[3 * width : 6 * width],
        weights_in[6 * width :],
    )
    out_t, out_f, out_s, out_m = (
        weights_out[:width],
        weights_out[width : 2 * width],
        weights_out[2 * width : 3 * width],
        weights_out[3 * width :],
    )
    start = clip.reshape(-1, width).astype(F32)
    normed_t = layer_norm(start, gains32[0], shifts32[0])
    project_t = nt(normed_t, in_t).astype(BF16).reshape(grid + (-1,))
    mixed_t = attention_call(forward_kernel, [project_t], width, True, patches).reshape(-1, width)
    projected_t = (nn(mixed_t, out_t) + shifts32[3]).astype(BF16)
    branch_t = (nn(projected_t, out_f) + shifts32[4]).astype(BF16)
    after_t = start + branch_t.astype(F32)
    normed_s = layer_norm(after_t, gains32[1], shifts32[1])
    project_s = nt(normed_s, in_s).astype(BF16).reshape(grid + (-1,))
    mixed_s = attention_call(forward_kernel, [project_s], width, False, patches).reshape(-1, width)
    after_s = after_t + (nn(mixed_s, out_s) + shifts32[5])
    normed_m = layer_norm(after_s, gains32[2], shifts32[2])
    hidden_pre = nt(normed_m, in_m) + shifts32[6:].reshape(-1)
    hidden32, slope32 = gelu_parts(hidden_pre)
    hidden, slope = (hidden32.astype(BF16), slope32.astype(BF16))
    output = (after_s + (nn(hidden, out_m) + dense32)).astype(BF16)

    grad_low = target.reshape(-1, width)
    grad_out = grad_low.astype(F32)
    d_out_m = tn(hidden, grad_low).astype(BF16)
    s_dense = column_sum(grad_low)
    grad_pre = (nt(grad_low, out_m) * slope.astype(F32)).astype(BF16)
    d_in_m = tn(grad_pre, normed_m).astype(BF16)
    s_hidden = column_sum(grad_pre).reshape(-1, width)
    part, g_m, b_m = norm_backward(after_s, gains32[2], nn(grad_pre, in_m))
    grad_s = grad_out + part
    grad_branch_s = grad_s.astype(BF16)
    d_out_s = tn(mixed_s, grad_branch_s).astype(BF16)
    s_space = column_sum(grad_branch_s)
    grad_mixed_s = nt(grad_branch_s, out_s).astype(BF16).reshape(shape)
    grad_project_s = attention_call(
        backward_kernel, [project_s, grad_mixed_s], 3 * width, False, patches
    ).reshape(-1, 3 * width)
    d_in_s = tn(grad_project_s, normed_s).astype(BF16)
    part, g_s, b_s = norm_backward(after_t, gains32[1], nn(grad_project_s, in_s))
    grad_t = grad_s + part
    grad_branch_t = grad_t.astype(BF16)
    d_out_f = tn(projected_t, grad_branch_t).astype(BF16)
    s_fc = column_sum(grad_branch_t)
    grad_projected = nt(grad_branch_t, out_f).astype(BF16)
    d_out_t = tn(mixed_t, grad_projected).astype(BF16)
    s_time = column_sum(grad_projected)
    grad_mixed_t = nt(grad_projected, out_t).astype(BF16).reshape(shape)
    grad_project_t = attention_call(
        backward_kernel, [project_t, grad_mixed_t], 3 * width, True, patches
    ).reshape(-1, 3 * width)
    d_in_t = tn(grad_project_t, normed_t).astype(BF16)
    part, g_t, b_t = norm_backward(start, gains32[0], nn(grad_project_t, in_t))
    grad_clip = (grad_t + part.astype(BF16).astype(F32)).astype(BF16)
    small = jnp.concatenate(
        [
            jnp.stack([g_t, g_s, g_m, b_t, b_s, b_m, s_time, s_fc, s_space], axis=0),
            s_hidden,
            s_dense[None, :],
        ],
        axis=0,
    )
    d_in = jnp.concatenate([d_in_t, d_in_s, d_in_m], axis=0)
    d_out = jnp.concatenate([d_out_t, d_out_f, d_out_s, d_out_m], axis=0)
    return (output.reshape(shape), grad_clip.reshape(shape), d_in, d_out, small)


def shards(clips_in, cotangent, clip_live, weights_in, weights_out, norm_gain, shift_rows, dense_shift):
    both = ("dp", "seq")
    devices = lax.axis_size(both)
    group = lax.axis_size("seq")
    count, _, patches, width = clips_in.shape
    own = count // group
    rows = -(-patches // SUB) * SUB
    gain_count = norm_gain.shape[0]
    shift_count = shift_rows.shape[0]

    def enter(x):
        x = lax.all_to_all(x, "seq", split_axis=0, concat_axis=1, tiled=True)
        return jnp.pad(x, ((0, 0), (0, 0), (0, rows - patches), (0, 0)))

    def leave(x):
        x = x[:, :, :patches]
        return lax.all_to_all(x, "seq", split_axis=1, concat_axis=0, tiled=True)

    full_in = lax.all_gather(weights_in, both, axis=0, tiled=True)
    full_out = lax.all_gather(weights_out, both, axis=0, tiled=True)
    packed = jnp.concatenate([norm_gain, shift_rows, dense_shift[None, :]], axis=0)
    slot = lax.dynamic_update_slice(
        jnp.zeros((devices,) + packed.shape, F32),
        packed.astype(F32)[None],
        (lax.axis_index(both), 0, 0),
    )
    full_small = lax.psum(slot, both).transpose(1, 0, 2).reshape(packed.shape[0], width).astype(BF16)
    live = lax.dynamic_slice(clip_live, (lax.axis_index("seq") * own,), (own,)).astype(BF16)
    output, grad_clip, d_in, d_out, small = block(
        enter(clips_in),
        enter(cotangent * 1) * live[:, None, None, None],
        full_in,
        full_out,
        full_small[:gain_count],
        full_small[gain_count : gain_count + shift_count],
        full_small[-1],
        patches,
    )
    summed_in = lax.psum_scatter(d_in, both, scatter_dimension=0, tiled=True).astype(F32)
    summed_out = lax.psum_scatter(d_out, both, scatter_dimension=0, tiled=True).astype(F32)
    summed_small = lax.psum(small, both)
    share = width // devices
    owned = lax.dynamic_slice(summed_small, (0, lax.axis_index(both) * share), (small.shape[0], share))
    return (
        leave(output),
        leave(grad_clip).astype(F32),
        summed_in,
        summed_out,
        owned[:gain_count],
        owned[gain_count : gain_count + shift_count],
        owned[-1],
    )


def solution(mesh):
    clip = P("dp", "seq", None, None)
    row = P(("dp", "seq"), None)
    col = P(None, ("dp", "seq"))
    flat = P(("dp", "seq"))
    return jax.shard_map(
        shards,
        mesh=mesh,
        in_specs=(clip, clip, P("dp"), row, row, col, col, flat),
        out_specs=(clip, clip, row, row, col, col, flat),
        check_vma=False,
    )
```

time: 1730 us -> 705 us (0.41)
  local copies, waits for them, and re-layouts: 416 us -> 25.6 us
  matrix products: 395 us -> 197 us
  waiting for transfers between devices: 314 us -> 128 us
  other arithmetic: 219 us -> 52.6 us
  blocking collectives: 306 us -> 179 us
  Pallas kernels: 0 us -> 84.9 us
  starting transfers between devices: 49.2 us -> 14.2 us
    dot_general x66 -> x21, matrix products: 395 us -> 197 us  [the longest x7 75.1 us: nt(): lax.dot_general(left, right, (((1,), (1,)), ((), ())), preferred_element_...]
    all_to_all x11 -> x3, waiting for transfers between devices: 203 us -> 20.6 us  [the longest x2 20.6 us: leave(): return lax.all_to_all(x, 'seq', split_axis=1, concat_axis=0, tiled=True)]
    all_gather x4 -> x0, blocking collectives: 182 us -> none  [the longest x2 106 us: single_step(): lax.all_gather(shift_rows, ('dp', 'seq'), axis=1, tiled=True)]
    convert_element_type x52 -> x1, local copies, waits for them, and re-layouts: 168 us -> 0.01 us  [shards(): packed.astype(F32)[None]]
    psum x0 -> x2, blocking collectives: none -> 143 us  [the longest x1 80.4 us: shards(): lax.psum(slot, both).transpose(1, 0, 2).reshape(packed.shape[0], width)]
    reshape x43 -> x1, local copies, waits for them, and re-layouts: 132 us -> 0.01 us  [block(): s_hidden = column_sum(grad_pre).reshape(-1, width)]
    while x2 -> x0, blocking collectives: 85.5 us -> none
    pallas_call x0 -> x4, Pallas kernels: none -> 84.9 us  [attention_call(): pl.pallas_call(partial(kernel, group, patches), grid=(clips, steps), in_s...]
  transfers between devices with their start and end apart: 17 -> 7, of which waited for: 6 -> 3; matrix products, arithmetic and copies ran while one was open for 19% -> 17% of each run, Pallas kernels for 0% -> 6%
where the time goes in v1:
time: 705 us; the launch traced here: 697 us
  matrix products  197 us (28%)
  blocking collectives  179 us (25%)
  waiting for transfers between devices  128 us (18%)
  Pallas kernels  84.9 us (12%)
  other arithmetic  52.6 us (7%)
  local copies, waits for them, and re-layouts  25.6 us (4%)
  between operations  15.6 us (2%)
  starting transfers between devices  14.2 us (2%)
    pallas_call x4, Pallas kernels, attention_call(): pl.pallas_call(partial(kernel, group, patches), grid=(clips, steps), in_s...  84.9 us
    psum x1, blocking collectives, shards(): lax.psum(slot, both).transpose(1, 0, 2).reshape(packed.shape[0], width)  80.4 us
    reduce_scatter x1, waiting for transfers between devices, shards(): lax.psum_scatter(d_in, both, scatter_dimension=0, tiled=True).astype(F32)  79.5 us
    dot_general x7, matrix products, nt(): lax.dot_general(left, right, (((1,), (1,)), ((), ())), preferred_element_...  75.1 us
    dot_general x7, matrix products, nn(): lax.dot_general(left, right, (((1,), (0,)), ((), ())), preferred_element_...  68 us
    psum x1, blocking collectives, shards(): summed_small = lax.psum(small, both)  62.2 us
    dot_general x7, matrix products, tn(): lax.dot_general(left, right, (((0,), (0,)), ((), ())), preferred_element_...  54.1 us
    all_to_all x1, blocking collectives, enter(): x = lax.all_to_all(x, 'seq', split_axis=0, concat_axis=1, tiled=True)  36.9 us
  transfers between devices with their start and end apart: 7, of which 3 were waited for; matrix products, arithmetic and copies ran while one was open for 17% of the time, Pallas kernels for 6%

profile of v1, /device:TPU:0, one launch (start us, length us, event | category | flops | bytes accessed | tf_op | source)
XLA Modules:
  0.0 697.4 jit_solution(17829615691177850985)
XLA Ops:
  8.7 36.9 %all_to_all.45 = bf16[4,2,196,768]{3,1,2,0:T(2,128)(2,1)} all-to-all(bf16[4,2,196,768]{3,1,2,0:T(2,128)(2,1)} %param.8), channel_id=1, replica_groups=mesh['dp'=8,'seq'=4] {'seq'}, dimensions={0} | all-to-all | bytes 4816896 | tf_op jit(solution)/shard_map/all_to_all | solution.py:260
  45.6 4.5 all-to-all-start.2
  51.6 80.4 %psum.14 = bf16[32,14,24]{2,0,1:T(8,128)(2,1)S(1)} all-reduce(f32[32,14,24]{2,0,1:T(8,128)S(1)} %dynamic_update_slice.3), channel_id=1, replica_groups=mesh['dp'=8,'seq'=4] {'dp','seq'}, use_global_device_ids=true, to_apply=%region_2.3 | all-reduce | flops 10752 | bytes 64512 | tf_op jit(solution)/shard_map/psum | solution.py:275
  145.9 10.6 %convolution_convert_fusion.1 = bf16[1664,2304]{1,0:T(8,128)(2,1)} fusion(bf16[1664,768]{1,0:T(8,128)(2,1)} %fusion.21, bf16[7680,768]{1,0:T(8,128)(2,1)} %all-gather.3.cloned.1.call-done), kind=kOutput, calls=%fused_computation.12 | convolution fusion | flops 5892636672 | bytes 13762560 | tf_op jit(solution)/shard_map/dot_general | solution.py:22
  156.5 16.3 %shard_map.135 = bf16[1,8,208,768]{3,2,1,0:T(8,128)(2,1)} custom-call(bf16[1,8,208,2304]{3,2,1,0:T(8,128)(2,1)} %bitcast.117), custom_call_target="tpu_custom_call" | custom-call | tf_op jit(solution)/shard_map/pallas_call | solution.py:131
  172.8 26.3 %all-gather.5.cloned.1.call-done = bf16[5376,768]{1,0:T(8,128)(2,1)} async-done(((bf16[168,768]{1,0:T(8,128)(2,1)}), bf16[5376,768]{1,0:T(8,128)(2,1)}) %all-gather.5.cloned.1.call-update) | async-done | bytes 8257552 | tf_op jit(solution)/shard_map/all_gather | solution.py:268
  203.3 4.6 fusion.27
  210.6 12.1 %convolution_convert_fusion = bf16[1664,2304]{1,0:T(8,128)(2,1)} fusion(bf16[7680,768]{1,0:T(8,128)(2,1)} %all-gather.3.cloned.1.call-done, f32[1664,768]{1,0:T(8,128)S(1)} %subtract_multiply_fusion.1, f32[768]{0:T(1024)S(1)} %add.183, f32[768]{0:T(1024)S(1)} %mul.230), kind=kOutput, calls=%fused_computation.11 | convolution fusion | flops 5896470528 | bytes 16324608 | tf_op jit(solution)/shard_map/dot_general | solution.py:22
  222.7 16.4 %shard_map.136 = bf16[1,8,208,768]{3,2,1,0:T(8,128)(2,1)} custom-call(bf16[1,8,208,2304]{3,2,1,0:T(8,128)(2,1)} %bitcast.119), custom_call_target="tpu_custom_call" | custom-call | tf_op jit(solution)/shard_map/pallas_call | solution.py:131
  239.1 6.4 fusion.63
  246.3 17.1 %multiply_convert_fusion.1 = (bf16[1664,3072]{1,0:T(8,128)(2,1)}, f32[1664,3072]{1,0:T(8,128)}) fusion(f32[3072]{0:T(1024)S(1)} %add.194, bf16[7680,768]{1,0:T(8,128)(2,1)} %all-gather.3.cloned.1.call-done, f32[1664,768]{1,0:T(8,128)S(1)} %get-tuple-element.49, f32[768]{0:T(1024)S(1)} %add.191, f32[768]{0:T(1024)S(1)} %mul.236, f32[1664]{0:T(1024)S(1)} %add_rsqrt_fusion, ...), kind=kOutput, calls=%fused_computation.8 | convolution fusion | flops 7888797696 | bytes 40532992 | tf_op jit(solution)/shard_map/dot_general | solution.py:22
  263.3 13.0 %convolution_convert_fusion.2 = bf16[3072,768]{1,0:T(8,128)(2,1)} fusion(bf16[1664,3072]{1,0:T(8,128)(2,1)} %get-tuple-element.50, bf16[1664,768]{1,0:T(8,128)(2,1)S(1)} %bitcast.123), kind=kOutput, calls=%fused_computation.58 | convolution fusion | flops 7854096384 | bytes 17498112 | tf_op jit(solution)/shard_map/dot_general | solution.py:30
  276.3 20.2 %convert_reduce_fusion = (f32[3072]{0:T(1024)}, bf16[1664,3072]{1,0:T(8,128)(2,1)}) fusion(f32[1664,3072]{1,0:T(8,128)} %get-tuple-element.51, f32[3072]{0:T(1024)S(1)} %add.194, bf16[1664,768]{1,0:T(8,128)(2,1)S(1)} %bitcast.124, bf16[5376,768]{1,0:T(8,128)(2,1)} %all-gather.5.cloned.1.call-done), kind=kOutput, calls=%fused_computation.6 | convolution fusion | flops 7928411136 | bytes 37969920 | tf_op jit(solution)/shard_map/dot_general | solution.py:22
  296.5 15.1 %multiply_reduce_fusion = (f32[768]{0:T(1024)}, f32[1664]{0:T(1024)S(1)}, f32[1664]{0:T(1024)S(1)}, f32[768]{0:T(1024)}, f32[1664,768]{1,0:T(8,128)S(1)}) fusion(f32[1664,768]{1,0:T(8,128)S(1)} %get-tuple-element.49, f32[1664]{0:T(1024)S(1)} %add_rsqrt_fusion, f32[1664]{0:T(1024)S(1)} %broadcast_multiply_fusion.6, f32[768]{0:T(1024)S(1)} %mul.236, ...), kind=kOutput, calls=%fused_computation.43 | convolution fusion | flops 7863233536 | bytes 25201664 | tf_op jit(solution)/shard_map/dot_general | solution.py:26
  318.1 5.0 convolution_convert_fusion.7
  323.0 26.0 %shard_map.137 = bf16[1,8,208,2304]{3,2,1,0:T(8,128)(2,1)} custom-call(bf16[1,8,208,2304]{3,2,1,0:T(8,128)(2,1)} %bitcast.120, bf16[1,8,208,768]{3,2,1,0:T(8,128)(2,1)} %bitcast.138), custom_call_target="tpu_custom_call" | custom-call | tf_op jit(solution)/shard_map/pallas_call | solution.py:131
  349.1 12.5 %multiply_reduce_fusion.1 = (f32[768]{0:T(1024)S(1)}, f32[1664]{0:T(1024)S(1)}, f32[1664]{0:T(1024)S(1)}, f32[768]{0:T(1024)S(1)}, f32[1664,768]{1,0:T(8,128)S(1)}) fusion(f32[1664]{0:T(1024)S(1)} %add_rsqrt_fusion.1, f32[1664]{0:T(1024)S(1)} %broadcast_multiply_fusion.7, bf16[1664,768]{1,0:T(8,128)(2,1)} %copy-done, ...), kind=kOutput, calls=%fused_computation.44 | convolution fusion | flops 5904133120 | bytes 21318656 | tf_op jit(solution)/shard_map/dot_general | solution.py:26
  374.1 23.8 %pad_maximum_fusion.1 = bf16[5376,768]{1,0:T(8,128)(2,1)} fusion(bf16[3072,768]{1,0:T(8,128)(2,1)S(1)} %bitcast.132, bf16[768,768]{1,0:T(8,128)(2,1)S(1)} %copy-done.12, bf16[768,768]{1,0:T(8,128)(2,1)S(1)} %convolution_convert_fusion.9, bf16[768,768]{1,0:T(8,128)(2,1)S(1)} %convolution_convert_fusion.10), kind=kLoop, calls=%fused_computation.13 | loop fusion | flops 33030144 | bytes 16515072 | tf_op jit(solution)/shard_map/concatenate | solution.py:245
  398.0 5.7 convolution_convert_fusion.5
  403.7 26.3 %shard_map.138 = bf16[1,8,208,2304]{3,2,1,0:T(8,128)(2,1)} custom-call(bf16[1,8,208,2304]{3,2,1,0:T(8,128)(2,1)} %bitcast.118, bf16[1,8,208,768]{3,2,1,0:T(8,128)(2,1)} %bitcast.137), custom_call_target="tpu_custom_call" | custom-call | tf_op jit(solution)/shard_map/pallas_call | solution.py:131
  430.0 11.0 %convolution_convert_fusion.4 = bf16[2304,768]{1,0:T(8,128)(2,1)S(1)} fusion(bf16[1664,2304]{1,0:T(8,128)(2,1)} %bitcast.127, f32[1664,768]{1,0:T(8,128)} %copy-done.9, f32[768]{0:T(1024)S(1)} %copy-done.30, f32[768]{0:T(1024)S(1)} %mul.230), kind=kOutput, calls=%fused_computation.60 | convolution fusion | flops 5894406144 | bytes 16324608 | tf_op jit(solution)/shard_map/dot_general | solution.py:30
  441.1 13.8 %convolution_convert_fusion.3 = bf16[3072,768]{1,0:T(8,128)(2,1)S(1)} fusion(bf16[1664,3072]{1,0:T(8,128)(2,1)} %get-tuple-element.58, f32[1664,768]{1,0:T(8,128)} %copy-done.7, f32[768]{0:T(1024)S(1)} %add.191, f32[768]{0:T(1024)S(1)} %mul.236, f32[1664]{0:T(1024)S(1)} %add_rsqrt_fusion, f32[1664]{0:T(1024)S(1)} %broadcast_multiply_fusion.6), kind=kOutput, calls=%fused_computation.59 | convolution fusion | flops 7860486144 | bytes 20073472 | tf_op jit(solution)/shard_map/dot_general | solution.py:30
  455.0 8.0 %bitcast_convert_fusion = bf16[2304,768]{1,0:T(8,128)(2,1)S(1)} fusion(bf16[1,8,208,2304]{3,2,1,0:T(8,128)(2,1)S(1)} %bitcast.130, f32[768]{0:T(1024)S(1)} %copy-done.25, f32[768]{0:T(1024)S(1)} %copy-done.21, f32[8,208]{1,0:T(8,128)S(1)} %copy-done.23, f32[8,208]{1,0:T(8,128)S(1)} %copy-done.19, bf16[1,8,196,768]{3,2,1,0:T(8,128)(2,1)S(1)} %bitcast.114), kind=kOutput, calls=%fused_computation.16 | convolution fusion | flops 5898240000 | bytes 13634560 | tf_op jit(solution)/shard_map/dot_general | solution.py:30
  463.0 5.6 pad_maximum_fusion
  469.4 13.2 %add_convert_fusion.1 = bf16[1664,768]{1,0:T(8,128)(2,1)S(1)} fusion(f32[1664,768]{1,0:T(8,128)} %copy-done.7, bf16[1664,3072]{1,0:T(8,128)(2,1)} %get-tuple-element.50, bf16[5376,768]{1,0:T(8,128)(2,1)} %all-gather.5.cloned.1.call-done, f32[768]{0:T(1024)S(1)} %reshape.271), kind=kOutput, calls=%fused_computation.50 | convolution fusion | flops 7855570944 | bytes 22612992 | tf_op jit(solution)/shard_map/dot_general | solution.py:26
  484.3 5.0 all-to-all-start.1
  489.3 11.9 %fusion.26 = (f32[768]{0:T(1024)S(1)}, f32[1664]{0:T(1024)S(1)}, f32[1664]{0:T(1024)S(1)}, f32[768]{0:T(1024)S(1)}, f32[1664,768]{1,0:T(8,128)S(1)}) fusion(f32[1664]{0:T(1024)S(1)} %copy-done.17, f32[1664]{0:T(1024)S(1)} %copy-done.15, bf16[1,8,196,768]{3,2,1,0:T(8,128)(2,1)S(1)} %bitcast.115, f32[768]{0:T(1024)S(1)} %copy-done.21, ...), kind=kOutput, calls=%fused_computation.38 | convolution fusion | flops 5901577216 | bytes 18762752 | tf_op jit(solution)/shard_map/dot_general | solution.py:26
  506.7 20.6 %all-to-all-done.1 = bf16[1,8,196,768]{3,2,0,1:T(8,128)(2,1)} async-done(((bf16[1,8,196,768]{3,2,0,1:T(8,128)(2,1)}), bf16[1,8,196,768]{3,2,0,1:T(8,128)(2,1)}, u32[]{:S(2)}, u32[]{:S(2)}) %all-to-all-start.1) | async-done | bytes 2408480 | tf_op jit(solution)/shard_map/all_to_all | solution.py:265
  532.6 62.2 %psum.15 = f32[14,768]{1,0:T(8,128)S(1)} all-reduce(f32[14,768]{1,0:T(8,128)S(1)} %concatenate.31), channel_id=1, replica_groups=mesh['dp'=8,'seq'=4] {'dp','seq'}, use_global_device_ids=true, to_apply=%region_26.27 | all-reduce | flops 10752 | bytes 86016 | tf_op jit(solution)/shard_map/psum | solution.py:289
  596.7 5.0 copy.26
  601.7 5.8 copy.27
  609.2 79.5 %reduce-scatter.3.cloned.1.call-done = bf16[240,768]{1,0:T(8,128)(2,1)} async-done(((bf16[7680,768]{1,0:T(8,128)(2,1)}), bf16[240,768]{1,0:T(8,128)(2,1)}) %reduce-scatter.3.cloned.1.call-update) | async-done | bytes 368656 | tf_op jit(solution)/shard_map/reduce_scatter | solution.py:287
  (174 shorter events, 61.0 us)
Async XLA Ops:
  7.2 43.0 %copy-start.35 = (s32[4]{0:T(128)S(1)}, s32[4]{0:T(128)}, u32[]{:S(2)}) copy-start(s32[4]{0:T(128)} %param.10) | copy-start | bytes 52
  7.2 44.3 %copy-start.34 = (bf16[24]{0:T(256)(128)(2,1)S(1)}, bf16[24]{0:T(256)(128)(2,1)}, u32[]{:S(2)}) copy-start(bf16[24]{0:T(256)(128)(2,1)} %param.15) | copy-start | bytes 148
  7.2 44.3 %copy-start.28 = (bf16[10,24]{1,0:T(8,128)(2,1)S(1)}, bf16[10,24]{1,0:T(8,128)(2,1)}, u32[]{:S(2)}) copy-start(bf16[10,24]{1,0:T(8,128)(2,1)} %param.14) | copy-start | bytes 1444
  7.2 44.3 %copy-start.33 = (bf16[3,24]{1,0:T(4,128)(2,1)S(1)}, bf16[3,24]{1,0:T(4,128)(2,1)}, u32[]{:S(2)}) copy-start(bf16[3,24]{1,0:T(4,128)(2,1)} %param.13) | copy-start | bytes 436
  7.2 138.7 %all-gather.3.cloned.1.call-start = ((), (), s32[]{:S(2)}) async-start(), calls=%async_computation.6 | async-start | bytes 12165120 | tf_op jit(solution)/shard_map/all_gather | solution.py:267
  7.9 191.2 %all-gather.5.cloned.1.call-start = ((), (), s32[]{:S(2)}) async-start(), calls=%async_computation.7 | async-start | bytes 8515584 | tf_op jit(solution)/shard_map/all_gather | solution.py:268
  45.6 92.5 %all-to-all-start.2 = ((bf16[4,2,196,768]{3,1,2,0:T(2,128)(2,1)}), bf16[4,2,196,768]{3,1,2,0:T(2,128)(2,1)}, u32[]{:S(2)}, u32[]{:S(2)}) async-start(bf16[4,2,196,768]{3,1,2,0:T(2,128)(2,1)} %param.9), calls=%async_computation.2 | async-start | bytes 4816896 | tf_op jit(solution)/shard_map/all_to_all | solution.py:260
  50.1 557.3 %reduce-scatter.5.cloned.1.call-start = ((), (), s32[]{:S(2)}) async-start(), calls=%async_computation.9 | async-start | bytes 8515584 | tf_op jit(solution)/shard_map/reduce_scatter | solution.py:288
  132.2 11.4 %copy-start.20 = (f32[768]{0:T(1024)}, f32[768]{0:T(1024)S(1)}, u32[]{:S(2)}) copy-start(f32[768]{0:T(1024)S(1)} %mul.224) | copy-start | bytes 9220
  132.6 78.0 %copy-start.29 = (f32[768]{0:T(1024)}, f32[768]{0:T(1024)S(1)}, u32[]{:S(2)}) copy-start(f32[768]{0:T(1024)S(1)} %add.183) | copy-start | bytes 9220
  132.7 10.9 %copy-start.24 = (f32[768]{0:T(1024)}, f32[768]{0:T(1024)S(1)}, u32[]{:S(2)}) copy-start(f32[768]{0:T(1024)S(1)} %add.172) | copy-start | bytes 9220
  210.6 12.1 %copy-start.9 = (f32[1664,768]{1,0:T(8,128)}, f32[1664,768]{1,0:T(8,128)S(1)}, u32[]{:S(2)}) copy-start(f32[1664,768]{1,0:T(8,128)S(1)} %subtract_multiply_fusion.1) | copy-start | bytes 15335428
  245.5 66.2 %copy-start.7 = (f32[1664,768]{1,0:T(8,128)}, f32[1664,768]{1,0:T(8,128)S(1)}, u32[]{:S(2)}) copy-start(f32[1664,768]{1,0:T(8,128)S(1)} %get-tuple-element.49) | copy-start | bytes 15335428
  246.3 17.1 %copy-start.8 = (bf16[1,8,208,768]{3,2,1,0:T(8,128)(2,1)S(1)}, bf16[1,8,208,768]{3,2,1,0:T(8,128)(2,1)}, u32[]{:S(2)}) copy-start(bf16[1,8,208,768]{3,2,1,0:T(8,128)(2,1)} %pad_multiply_fusion) | copy-start | bytes 7667716
  349.1 12.6 %copy-start.1 = (bf16[1664,768]{1,0:T(8,128)(2,1)S(1)}, bf16[1664,768]{1,0:T(8,128)(2,1)}, u32[]{:S(2)}) copy-start(bf16[1664,768]{1,0:T(8,128)(2,1)} %copy-done) | copy-start | bytes 7667716
  349.1 12.6 %copy-start.6 = (f32[1664,768]{1,0:T(8,128)S(1)}, f32[1664,768]{1,0:T(8,128)}, u32[]{:S(2)}) copy-start(f32[1664,768]{1,0:T(8,128)} %copy-done.5) | copy-start | bytes 15335428
  364.7 9.4 %slice-start.2 = ((s8[4718592]{0:T(1024)(128)(4,1)}), s8[4194304]{0:T(1024)(128)(4,1)S(1)}, s32[]{:S(2)}) async-start(s8[4718592]{0:T(1024)(128)(4,1)} %bitcast.131), calls=%async_computation.12 | async-start | bytes 8388608
  398.0 290.8 %reduce-scatter.3.cloned.1.call-start = ((), (), s32[]{:S(2)}) async-start(), calls=%async_computation.8 | async-start | bytes 12165120 | tf_op jit(solution)/shard_map/reduce_scatter | solution.py:287
  403.7 26.3 %copy-start.30 = (f32[768]{0:T(1024)S(1)}, f32[768]{0:T(1024)}, u32[]{:S(2)}) copy-start(f32[768]{0:T(1024)} %copy-done.29) | copy-start | bytes 9220
  430.0 24.9 %slice-start = ((s8[7667712]{0:T(1024)(128)(4,1)}), s8[4194304]{0:T(1024)(128)(4,1)S(1)}, s32[]{:S(2)}) async-start(s8[7667712]{0:T(1024)(128)(4,1)} %bitcast.129), calls=%async_computation.10 | async-start | bytes 8388608
  441.0 13.9 %slice-start.1 = ((s8[7667712]{0:T(1024)(128)(4,1)}), s8[3473408]{0:T(1024)(128)(4,1)S(1)}, s32[]{:S(2)}) async-start(s8[7667712]{0:T(1024)(128)(4,1)} %bitcast.129), calls=%async_computation.11 | async-start | bytes 6946816
  441.1 13.9 %copy-start.19 = (f32[8,208]{1,0:T(8,128)S(1)}, f32[8,208]{1,0:T(8,128)}, u32[]{:S(2)}) copy-start(f32[8,208]{1,0:T(8,128)} %copy-done.18) | copy-start | bytes 19972
  441.1 13.9 %copy-start.21 = (f32[768]{0:T(1024)S(1)}, f32[768]{0:T(1024)}, u32[]{:S(2)}) copy-start(f32[768]{0:T(1024)} %copy-done.20) | copy-start | bytes 9220
  441.1 13.9 %copy-start.23 = (f32[8,208]{1,0:T(8,128)S(1)}, f32[8,208]{1,0:T(8,128)}, u32[]{:S(2)}) copy-start(f32[8,208]{1,0:T(8,128)} %copy-done.22) | copy-start | bytes 19972
  441.1 13.9 %copy-start.25 = (f32[768]{0:T(1024)S(1)}, f32[768]{0:T(1024)}, u32[]{:S(2)}) copy-start(f32[768]{0:T(1024)} %copy-done.24) | copy-start | bytes 9220
  484.3 43.0 %all-to-all-start.1 = ((bf16[1,8,196,768]{3,2,0,1:T(8,128)(2,1)}), bf16[1,8,196,768]{3,2,0,1:T(8,128)(2,1)}, u32[]{:S(2)}, u32[]{:S(2)}) async-start(bf16[1,8,196,768]{3,2,0,1:T(8,128)(2,1)} %slice.136), calls=%async_computation.1 | async-start | bytes 4915200 | tf_op jit(solution)/shard_map/all_to_all | solution.py:265
  505.0 26.8 %copy-start.3 = (bf16[4,2,196,768]{3,2,1,0:T(8,128)(2,1)S(1)}, bf16[4,2,196,768]{3,2,1,0:T(8,128)(2,1)}, u32[]{:S(2)}) copy-start(bf16[4,2,196,768]{3,2,1,0:T(8,128)(2,1)} %copy-done.2) | copy-start | bytes 7225348
  505.0 27.4 %copy-start.27 = (f32[3072]{0:T(1024)S(1)}, f32[3072]{0:T(1024)}, u32[]{:S(2)}) copy-start(f32[3072]{0:T(1024)} %get-tuple-element.57) | copy-start | bytes 36868
  505.0 27.4 %copy-start.32 = (f32[768]{0:T(1024)S(1)}, f32[768]{0:T(1024)}, u32[]{:S(2)}) copy-start(f32[768]{0:T(1024)} %get-tuple-element.21) | copy-start | bytes 9220
  505.0 27.4 %copy-start.31 = (f32[768]{0:T(1024)S(1)}, f32[768]{0:T(1024)}, u32[]{:S(2)}) copy-start(f32[768]{0:T(1024)} %get-tuple-element.30) | copy-start | bytes 9220
  505.0 27.4 %copy-start.26 = (f32[768]{0:T(1024)S(1)}, f32[768]{0:T(1024)}, u32[]{:S(2)}) copy-start(f32[768]{0:T(1024)} %get-tuple-element.33) | copy-start | bytes 9220
  527.2 74.4 %all-to-all-start.3 = ((bf16[1,8,196,768]{3,2,0,1:T(8,128)(2,1)}), bf16[1,8,196,768]{3,2,0,1:T(8,128)(2,1)}, u32[]{:S(2)}, u32[]{:S(2)}) async-start(bf16[1,8,196,768]{3,2,0,1:T(8,128)(2,1)} %slice.137), calls=%async_computation.3 | async-start | bytes 4915200 | tf_op jit(solution)/shard_map/all_to_all | solution.py:265
  (18 other events, 73.5 us)
Sparse Core Ops, SparseCore 0:
  10.9 110.1 all-gather.2
  124.0 75.0 all-gather.4
  398.1 137.4 reduce-scatter.4
  541.5 147.1 reduce-scatter.2

commit v2 on v1

--- a/solution.py
+++ b/solution.py
@@ -75,13 +75,21 @@
     return slice(start, start + LANES)
 
 
-def load(ref, cols):
-    block = ref[..., cols]
-    return block.reshape(-1, LANES)
-
-
-def store(ref, cols, block):
-    ref[..., cols] = block.reshape(ref.shape[:-1] + (LANES,))
+def load(refs, kinds, kind, pair):
+    place = 0
+    while kind >= kinds[place]:
+        kind -= kinds[place]
+        place += 1
+    return refs[place][..., columns(kind, pair)].reshape(-1, LANES)
+
+
+def store(refs, kinds, kind, pair, block):
+    place = 0
+    while kind >= kinds[place]:
+        kind -= kinds[place]
+        place += 1
+    ref = refs[place]
+    ref[..., columns(kind, pair)] = block.reshape(ref.shape[:-1] + (LANES,))
 
 
 def keep_mask(shape, key_axis, group, patches):
@@ -92,35 +100,29 @@
     return (key % group) == (query % group)
 
 
-def forward_kernel(group, patches, project_ref, mixed_ref):
-    rows = project_ref.size // project_ref.shape[-1]
+def forward_kernel(group, patches, kinds, *refs):
+    project, mixed = (refs[: len(kinds)], refs[len(kinds) :])
+    rows = project[0].size // project[0].shape[-1]
     keep = keep_mask((2 * rows, rows), 1, group, patches)
     for pair in range(PAIRS):
-        mixed = pair_forward(
-            load(project_ref, columns(0, pair)),
-            load(project_ref, columns(1, pair)),
-            load(project_ref, columns(2, pair)),
-            keep,
-        )
-        store(mixed_ref, columns(0, pair), mixed)
-
-
-def backward_kernel(group, patches, project_ref, grad_ref, out_ref):
-    rows = project_ref.size // project_ref.shape[-1]
+        block = pair_forward(*[load(project, kinds, kind, pair) for kind in range(3)], keep)
+        store(mixed, (1,), 0, pair, block)
+
+
+def backward_kernel(group, patches, kinds, *refs):
+    count = len(kinds)
+    project, grad, outs = (refs[:count], refs[count : count + 1], refs[count + 1 :])
+    rows = project[0].size // project[0].shape[-1]
     keep = keep_mask((rows, 2 * rows), 0, group, patches)
     for pair in range(PAIRS):
         results = pair_backward(
-            load(project_ref, columns(0, pair)),
-            load(project_ref, columns(1, pair)),
-            load(project_ref, columns(2, pair)),
-            load(grad_ref, columns(0, pair)),
-            keep,
+            *[load(project, kinds, kind, pair) for kind in range(3)], load(grad, (1,), 0, pair), keep
         )
         for kind, result in enumerate(results):
-            store(out_ref, columns(kind, pair), result)
-
-
-def attention_call(kernel, arrays, out_cols, temporal, patches):
+            store(outs, kinds, kind, pair, result)
+
+
+def attention_call(kernel, kinds, arrays, out_cols, temporal, patches):
     clips, frames, rows, _ = arrays[0].shape
     if temporal:
         group, steps, shape = SUB, rows // SUB, (1, frames, SUB)
@@ -128,14 +130,188 @@
     else:
         group, steps, shape = None, frames, (1, 1, rows)
         index = lambda c, i: (c, i, 0, 0)
+    tokens = clips * frames * rows
+    backward = kernel is backward_kernel
     return pl.pallas_call(
-        partial(kernel, group, patches),
+        partial(kernel, group, patches, kinds),
         grid=(clips, steps),
         in_specs=[pl.BlockSpec(shape + (a.shape[-1],), index) for a in arrays],
-        out_specs=pl.BlockSpec(shape + (out_cols,), index),
-        out_shape=jax.ShapeDtypeStruct((clips, frames, rows, out_cols), BF16),
+        out_specs=[pl.BlockSpec(shape + (cols,), index) for cols in out_cols],
+        out_shape=[jax.ShapeDtypeStruct((clips, frames, rows, cols), BF16) for cols in out_cols],
         compiler_params=pltpu.CompilerParams(dimension_semantics=("arbitrary", "arbitrary")),
+        cost_estimate=pl.CostEstimate(
+            flops=tokens * (14_000_000 if backward else 9_000_000), bytes_accessed=0, transcendentals=0
+        ),
     )(*arrays)
+
+
+def place_kernel(sources, out_planes, counts, dest_ref, *refs):
+    total = sum(counts)
+    pieces, out = (refs[:total], refs[total])
+    held, in_sem, out_sem = refs[total + 1 :]
+    blocks = counts[0]
+    incoming = []
+    for entry, (group, plane) in enumerate(sources):
+        for block in range(blocks):
+            slot = entry * blocks + block
+            copy = pltpu.make_async_copy(
+                pieces[group * blocks + block].at[plane], held.at[slot], in_sem.at[slot]
+            )
+            copy.start()
+            incoming.append(copy)
+    outgoing = []
+    for entry in range(out_planes):
+        for block in range(blocks):
+            slot = entry * blocks + block
+            incoming[slot].wait()
+            copy = pltpu.make_async_copy(held.at[slot], out.at[entry, dest_ref[block]], out_sem.at[slot])
+            copy.start()
+            outgoing.append(copy)
+    for copy in outgoing:
+        copy.wait()
+
+
+def place(groups, sources, dest):
+    blocks = len(groups[0])
+    _, rows, width = groups[0][0].shape
+    slots = len(sources) * blocks
+    flat = [piece for group in groups for piece in group]
+    anywhere = pl.BlockSpec(memory_space=pl.ANY)
+    return pl.pallas_call(
+        partial(place_kernel, tuple(sources), len(sources), tuple(len(g) for g in groups)),
+        in_specs=[pl.BlockSpec(memory_space=pltpu.SMEM)] + [anywhere] * len(flat),
+        out_specs=anywhere,
+        out_shape=jax.ShapeDtypeStruct((len(sources), blocks, rows, width), BF16),
+        scratch_shapes=[
+            pltpu.VMEM((slots, rows, width), BF16),
+            pltpu.SemaphoreType.DMA((slots,)),
+            pltpu.SemaphoreType.DMA((slots,)),
+        ],
+        compiler_params=pltpu.CompilerParams(vmem_limit_bytes=slots * rows * width * 2 + (2 << 20)),
+        cost_estimate=pl.CostEstimate(flops=0, bytes_accessed=4 * slots * rows * width, transcendentals=0),
+    )(dest, *flat)
+
+
+def split_kernel(spans, shape, core_ref, *refs):
+    planes, squares, rows = shape
+    parts = refs[: len(spans)]
+    keep, send, held, in_sem, out_sem = refs[len(spans) :]
+    core = core_ref[0]
+    incoming = [[] for _ in range(planes * squares * 2)]
+    count, row = (0, 0)
+    for part, (first, length) in enumerate(spans):
+        done = 0
+        while done < length:
+            slot, offset = divmod(row, rows)
+            size = min(length - done, rows - offset)
+            copy = pltpu.make_async_copy(
+                parts[part].at[pl.ds(first + done, size)], held.at[slot, pl.ds(offset, size)], in_sem.at[count]
+            )
+            copy.start()
+            incoming[slot].append(copy)
+            count, row, done = (count + 1, row + size, done + size)
+    outgoing = []
+    for plane in range(planes):
+        for square in range(squares):
+            pair = (plane * squares + square) * 2
+            for copy in incoming[pair] + incoming[pair + 1]:
+                copy.wait()
+            for which, (target, side) in enumerate(((send, 1 - core), (keep, core))):
+                copy = pltpu.make_async_copy(
+                    held.at[pair + side], target.at[square, plane], out_sem.at[pair + which]
+                )
+                copy.start()
+                outgoing.append(copy)
+    for copy in outgoing:
+        copy.wait()
+
+
+def split_cores(parts, planes, squares, rows, core):
+    spans = tuple((first, length) for _, first, length in parts)
+    arrays = [array for array, _, _ in parts]
+    width = arrays[0].shape[1]
+    slots = planes * squares * 2
+    anywhere = pl.BlockSpec(memory_space=pl.ANY)
+    half = jax.ShapeDtypeStruct((squares, planes, rows, width), BF16)
+    return pl.pallas_call(
+        partial(split_kernel, spans, (planes, squares, rows)),
+        in_specs=[pl.BlockSpec(memory_space=pltpu.SMEM)] + [anywhere] * len(arrays),
+        out_specs=[anywhere, anywhere],
+        out_shape=[half, half],
+        scratch_shapes=[
+            pltpu.VMEM((slots, rows, width), BF16),
+            pltpu.SemaphoreType.DMA((slots + len(parts),)),
+            pltpu.SemaphoreType.DMA((slots,)),
+        ],
+        compiler_params=pltpu.CompilerParams(vmem_limit_bytes=slots * rows * width * 2 + (2 << 20)),
+        cost_estimate=pl.CostEstimate(flops=0, bytes_accessed=4 * slots * rows * width, transcendentals=0),
+    )(core, *arrays)
+
+
+class Plan:
+    def __init__(self, axes):
+        self.axes = axes
+        me = lax.axis_index(axes)
+        self.plane, self.spot, self.square, self.core = (me // 8, me % 8, me % 8 // 2, me % 2)
+        self.spots = jnp.bitwise_xor(jnp.arange(8, dtype=jnp.int32), self.spot)
+        self.planes = (self.plane + 4 - jnp.arange(4, dtype=jnp.int32)) % 4
+        self.core_ref = self.core.astype(jnp.int32).reshape(1)
+
+    def flip(self, x, bits):
+        return lax.ppermute(x, self.axes, [(d, d ^ bits) for d in range(32)])
+
+    def shift(self, x, step):
+        return lax.ppermute(x, self.axes, [(d, (d + 8 * step) % 32) for d in range(32)])
+
+    def columns(self, shard):
+        pieces = [shard[None]] + [self.shift(shard, step)[None] for step in (1, 2, 3)]
+        return place([pieces], [(0, 0)], self.planes)[0]
+
+    def spread(self, column):
+        mine = [column] + [self.flip(column, bits) for bits in (2, 4, 6)]
+        both = []
+        for block in mine:
+            both += [block, self.flip(block, 1)]
+        return both
+
+    def narrow(self, parts, rows):
+        keep, send = split_cores(parts, 2, 4, rows, self.core_ref)
+        other = self.flip(send, 1)
+        total = None
+        for bits in (2, 4, 6, 0):
+            at = jnp.bitwise_xor(self.square, bits // 2)
+            take = lambda a: lax.dynamic_index_in_dim(a, at, 0, keepdims=False).astype(F32)
+            summed = (take(keep) + take(other)).astype(BF16)
+            arrived = (summed if bits == 0 else self.flip(summed, bits)).astype(F32)
+            total = arrived if total is None else total + arrived
+        return total.astype(BF16)
+
+    def finish(self, low, high):
+        every = jnp.concatenate([low, high], axis=0)
+        total = lax.dynamic_index_in_dim(every, self.plane, 0, keepdims=False).astype(F32)
+        for step in (1, 2, 3):
+            target = (self.plane + step) % 4
+            block = lax.dynamic_index_in_dim(every, target, 0, keepdims=False)
+            total = total + self.shift(block, step).astype(F32)
+        return total
+
+    def share_small(self, packed):
+        count, share = packed.shape
+        tiles = -(-count * share // (8 * LANES))
+        flat = jnp.pad(packed.reshape(-1), (0, tiles * 8 * LANES - count * share)).reshape(1, tiles * 8, LANES)
+        every = jnp.broadcast_to(flat, (32,) + flat.shape[1:])
+        every = lax.all_to_all(every, self.axes, split_axis=0, concat_axis=0)
+        every = every.reshape(32, -1)[:, : count * share].reshape(32, count, share)
+        return every.transpose(1, 0, 2).reshape(count, 32 * share)
+
+    def sum_small(self, small):
+        count, width = small.shape
+        share = width // 32
+        tiles = -(-count * share // (8 * LANES))
+        slots = small.reshape(count, 32, share).transpose(1, 0, 2).reshape(32, count * share)
+        slots = jnp.pad(slots, ((0, 0), (0, tiles * 8 * LANES - count * share))).reshape(32, tiles * 8, LANES)
+        slots = lax.all_to_all(slots, self.axes, split_axis=0, concat_axis=0)
+        return jnp.sum(slots, axis=0).reshape(-1)[: count * share].reshape(count, share)
 
 
 def norm_parts(values):
@@ -168,32 +344,25 @@
     return jnp.sum(rows.astype(F32), axis=0)
 
 
-def block(clip, target, weights_in, weights_out, gains, shifts, dense_bias, patches):
+def block(clip, target, weights, gains, shifts, dense_bias, patches):
     shape = clip.shape
     width = shape[-1]
     grid = shape[:3]
     gains32, shifts32, dense32 = (gains.astype(F32), shifts.astype(F32), dense_bias.astype(F32))
-    in_t, in_s, in_m = (
-        weights_in[: 3 * width],
-        weights_in[3 * width : 6 * width],
-        weights_in[6 * width :],
-    )
-    out_t, out_f, out_s, out_m = (
-        weights_out[:width],
-        weights_out[width : 2 * width],
-        weights_out[2 * width : 3 * width],
-        weights_out[3 * width :],
-    )
+    in_t, in_qk, in_v, in_m, out_t, out_f, out_s, out_m = weights
+    flat = lambda a: a.reshape(-1, a.shape[-1])
     start = clip.reshape(-1, width).astype(F32)
     normed_t = layer_norm(start, gains32[0], shifts32[0])
     project_t = nt(normed_t, in_t).astype(BF16).reshape(grid + (-1,))
-    mixed_t = attention_call(forward_kernel, [project_t], width, True, patches).reshape(-1, width)
+    mixed_t = flat(attention_call(forward_kernel, (3,), [project_t], (width,), True, patches)[0])
     projected_t = (nn(mixed_t, out_t) + shifts32[3]).astype(BF16)
     branch_t = (nn(projected_t, out_f) + shifts32[4]).astype(BF16)
     after_t = start + branch_t.astype(F32)
     normed_s = layer_norm(after_t, gains32[1], shifts32[1])
-    project_s = nt(normed_s, in_s).astype(BF16).reshape(grid + (-1,))
-    mixed_s = attention_call(forward_kernel, [project_s], width, False, patches).reshape(-1, width)
+    project_qk = nt(normed_s, in_qk).astype(BF16).reshape(grid + (-1,))
+    project_v = nt(normed_s, in_v).astype(BF16).reshape(grid + (-1,))
+    project_s = [project_qk, project_v]
+    mixed_s = flat(attention_call(forward_kernel, (2, 1), project_s, (width,), False, patches)[0])
     after_s = after_t + (nn(mixed_s, out_s) + shifts32[5])
     normed_m = layer_norm(after_s, gains32[2], shifts32[2])
     hidden_pre = nt(normed_m, in_m) + shifts32[6:].reshape(-1)
@@ -214,11 +383,13 @@
     d_out_s = tn(mixed_s, grad_branch_s).astype(BF16)
     s_space = column_sum(grad_branch_s)
     grad_mixed_s = nt(grad_branch_s, out_s).astype(BF16).reshape(shape)
-    grad_project_s = attention_call(
-        backward_kernel, [project_s, grad_mixed_s], 3 * width, False, patches
-    ).reshape(-1, 3 * width)
-    d_in_s = tn(grad_project_s, normed_s).astype(BF16)
-    part, g_s, b_s = norm_backward(after_t, gains32[1], nn(grad_project_s, in_s))
+    grad_qk, grad_v = attention_call(
+        backward_kernel, (2, 1), project_s + [grad_mixed_s], (2 * width, width), False, patches
+    )
+    grad_qk, grad_v = (flat(grad_qk), flat(grad_v))
+    d_in_qk = tn(grad_qk, normed_s).astype(BF16)
+    d_in_v = tn(grad_v, normed_s).astype(BF16)
+    part, g_s, b_s = norm_backward(after_t, gains32[1], nn(grad_qk, in_qk) + nn(grad_v, in_v))
     grad_t = grad_s + part
     grad_branch_t = grad_t.astype(BF16)
     d_out_f = tn(projected_t, grad_branch_t).astype(BF16)
@@ -227,9 +398,9 @@
     d_out_t = tn(mixed_t, grad_projected).astype(BF16)
     s_time = column_sum(grad_projected)
     grad_mixed_t = nt(grad_projected, out_t).astype(BF16).reshape(shape)
-    grad_project_t = attention_call(
-        backward_kernel, [project_t, grad_mixed_t], 3 * width, True, patches
-    ).reshape(-1, 3 * width)
+    grad_project_t = flat(
+        attention_call(backward_kernel, (3,), [project_t, grad_mixed_t], (3 * width,), True, patches)[0]
+    )
     d_in_t = tn(grad_project_t, normed_t).astype(BF16)
     part, g_t, b_t = norm_backward(start, gains32[0], nn(grad_project_t, in_t))
     grad_clip = (grad_t + part.astype(BF16).astype(F32)).astype(BF16)
@@ -241,9 +412,16 @@
         ],
         axis=0,
     )
-    d_in = jnp.concatenate([d_in_t, d_in_s, d_in_m], axis=0)
-    d_out = jnp.concatenate([d_out_t, d_out_f, d_out_s, d_out_m], axis=0)
-    return (output.reshape(shape), grad_clip.reshape(shape), d_in, d_out, small)
+    grads = (d_in_t, d_in_qk, d_in_v, d_in_m, d_out_t, d_out_f, d_out_s, d_out_m)
+    return (output.reshape(shape), grad_clip.reshape(shape), grads, small)
+
+
+def cut(array, sizes):
+    pieces, row = ([], 0)
+    for size in sizes:
+        pieces.append(array[row : row + size])
+        row += size
+    return pieces
 
 
 def shards(clips_in, cotangent, clip_live, weights_in, weights_out, norm_gain, shift_rows, dense_shift):
@@ -255,6 +433,10 @@
     rows = -(-patches // SUB) * SUB
     gain_count = norm_gain.shape[0]
     shift_count = shift_rows.shape[0]
+    hidden = weights_out.shape[0] * devices - 3 * width
+    planned = devices == 32 and group == 4 and width == 768 and hidden == 4 * width
+    in_sizes = (3 * width, 2 * width, width, hidden)
+    out_sizes = (width, width, width, hidden)
 
     def enter(x):
         x = lax.all_to_all(x, "seq", split_axis=0, concat_axis=1, tiled=True)
@@ -264,31 +446,64 @@
         x = x[:, :, :patches]
         return lax.all_to_all(x, "seq", split_axis=1, concat_axis=0, tiled=True)
 
-    full_in = lax.all_gather(weights_in, both, axis=0, tiled=True)
-    full_out = lax.all_gather(weights_out, both, axis=0, tiled=True)
     packed = jnp.concatenate([norm_gain, shift_rows, dense_shift[None, :]], axis=0)
-    slot = lax.dynamic_update_slice(
-        jnp.zeros((devices,) + packed.shape, F32),
-        packed.astype(F32)[None],
-        (lax.axis_index(both), 0, 0),
-    )
-    full_small = lax.psum(slot, both).transpose(1, 0, 2).reshape(packed.shape[0], width).astype(BF16)
+    if planned:
+        plan = Plan(both)
+        in_rows, out_rows = (weights_in.shape[0], weights_out.shape[0])
+        column_in = plan.columns(weights_in)
+        clip = enter(clips_in)
+        full_small = plan.share_small(packed)
+        in_low = plan.spread(column_in[:2])
+        column_out = plan.columns(weights_out)
+        out_low = plan.spread(column_out[:2])
+        in_high = plan.spread(column_in[2:])
+        out_high = plan.spread(column_out[2:])
+        pair = [(0, 0), (0, 1)]
+        low = place([in_low], pair, plan.spots).reshape(16 * in_rows, width)
+        high = place([in_high], pair, plan.spots).reshape(16 * in_rows, width)
+        early = place([out_low], pair, plan.spots).reshape(16 * out_rows, width)
+        late = place([out_low, out_high], [(0, 1), (1, 0), (1, 1)], plan.spots).reshape(24 * out_rows, width)
+        skip = 3 * width - 8 * out_rows
+        weights = cut(low, in_sizes[:2]) + cut(high, in_sizes[2:]) + cut(early, out_sizes[:3]) + [late[skip:]]
+    else:
+        full_in = lax.all_gather(weights_in, both, axis=0, tiled=True)
+        full_out = lax.all_gather(weights_out, both, axis=0, tiled=True)
+        slot = lax.dynamic_update_slice(
+            jnp.zeros((devices,) + packed.shape, F32),
+            packed.astype(F32)[None],
+            (lax.axis_index(both), 0, 0),
+        )
+        full_small = lax.psum(slot, both).transpose(1, 0, 2).reshape(packed.shape[0], width).astype(BF16)
+        clip = enter(clips_in)
+        weights = cut(full_in, in_sizes) + cut(full_out, out_sizes)
     live = lax.dynamic_slice(clip_live, (lax.axis_index("seq") * own,), (own,)).astype(BF16)
-    output, grad_clip, d_in, d_out, small = block(
-        enter(clips_in),
+    output, grad_clip, grads, small = block(
+        clip,
         enter(cotangent * 1) * live[:, None, None, None],
-        full_in,
-        full_out,
+        weights,
         full_small[:gain_count],
         full_small[gain_count : gain_count + shift_count],
         full_small[-1],
         patches,
     )
-    summed_in = lax.psum_scatter(d_in, both, scatter_dimension=0, tiled=True).astype(F32)
-    summed_out = lax.psum_scatter(d_out, both, scatter_dimension=0, tiled=True).astype(F32)
-    summed_small = lax.psum(small, both)
-    share = width // devices
-    owned = lax.dynamic_slice(summed_small, (0, lax.axis_index(both) * share), (small.shape[0], share))
+    if planned:
+        whole = lambda a: (a, 0, a.shape[0])
+        d_in_t, d_in_qk, d_in_v, d_in_m, d_out_t, d_out_f, d_out_s, d_out_m = grads
+        first = 16 * out_rows - 3 * width
+        out_high = plan.narrow([(d_out_m, first, hidden - first)], out_rows)
+        in_high = plan.narrow([whole(d_in_v), whole(d_in_m)], in_rows)
+        out_low = plan.narrow([whole(d_out_t), whole(d_out_f), whole(d_out_s), (d_out_m, 0, first)], out_rows)
+        summed_out = plan.finish(out_low, out_high)
+        in_low = plan.narrow([whole(d_in_t), whole(d_in_qk)], in_rows)
+        summed_in = plan.finish(in_low, in_high)
+        owned = plan.sum_small(small)
+    else:
+        d_in, d_out = (jnp.concatenate(grads[:4], axis=0), jnp.concatenate(grads[4:], axis=0))
+        summed_in = lax.psum_scatter(d_in, both, scatter_dimension=0, tiled=True).astype(F32)
+        summed_out = lax.psum_scatter(d_out, both, scatter_dimension=0, tiled=True).astype(F32)
+        summed_small = lax.psum(small, both)
+        share = width // devices
+        owned = lax.dynamic_slice(summed_small, (0, lax.axis_index(both) * share), (small.shape[0], share))
     return (
         leave(output),
         leave(grad_clip).astype(F32),

time: 705 us -> 820 us (1.16)
  the two profiles are of different devices: /device:TPU:0 before, /device:TPU:25 now
where the time goes in v2:
time: 820 us; the launch traced here: 808 us
  waiting for transfers between devices  228 us (28%)
  matrix products  191 us (23%)
  Pallas kernels  146 us (18%)
  local copies, waits for them, and re-layouts  89.4 us (11%)
  starting transfers between devices  88.8 us (11%)
  other arithmetic  51 us (6%)
  blocking collectives  10.3 us (1%)
    ppermute x44, waiting for transfers between devices, flip(): return lax.ppermute(x, self.axes, [(d, d ^ bits) for d in range(32)])  183 us
    pallas_call x4, Pallas kernels, attention_call(): pl.pallas_call(partial(kernel, group, patches, kinds), grid=(clips, steps...  84.1 us
    dot_general x8, matrix products, nt(): lax.dot_general(left, right, (((1,), (1,)), ((), ())), preferred_element_...  68.1 us
    dot_general x8, matrix products, nn(): lax.dot_general(left, right, (((1,), (0,)), ((), ())), preferred_element_...  67.3 us
    dot_general x8, matrix products, tn(): lax.dot_general(left, right, (((0,), (0,)), ((), ())), preferred_element_...  55.7 us
    unnamed x231, local copies, waits for them, and re-layouts  51.2 us
    ppermute x12, waiting for transfers between devices, shift(): lax.ppermute(x, self.axes, [(d, (d + 8 * step) % 32) for d in range(32)])  45.3 us
    ppermute x44, starting transfers between devices, flip(): return lax.ppermute(x, self.axes, [(d, d ^ bits) for d in range(32)])  38.4 us
  transfers between devices with their start and end apart: 61, of which 16 were waited for; matrix products, arithmetic and copies ran while one was open for 19% of the time, Pallas kernels for 11%

profile of v2, /device:TPU:25, one launch (start us, length us, event | category | flops | bytes accessed | tf_op | source)
XLA Modules:
  0.0 807.8 jit_solution(6410225135813886736)
XLA Ops:
  1.5 10.3 %all_to_all.55 = bf16[32,8,128]{2,1,0:T(8,128)(2,1)S(1)} all-to-all(bf16[32,8,128]{2,1,0:T(8,128)(2,1)S(1)} %broadcast_in_dim.24), channel_id=1, replica_groups=mesh['dp'=8,'seq'=4] {'dp','seq'}, dimensions={0} | all-to-all | bytes 131072 | tf_op jit(solution)/shard_map/all_to_all | solution.py:303
  32.0 10.2 %collective-permute-done.11 = bf16[168,768]{1,0:T(8,128)(2,1)S(1)} collective-permute-done((bf16[168,768]{1,0:T(8,128)(2,1)}, bf16[168,768]{1,0:T(8,128)(2,1)S(1)}, u32[]{:S(2)}, u32[]{:S(2)}) %collective-permute-start.11) | collective-permute-done | bytes 258080 | tf_op jit(solution)/shard_map/ppermute | solution.py:264
  60.0 7.7 collective-permute-done.1
  69.9 7.9 collective-permute-done.30.refs_12_
  80.0 9.1 %collective-permute-done.18.refs_6_ = bf16[2,168,768]{2,1,0:T(8,128)(2,1)S(1)} collective-permute-done((bf16[2,168,768]{2,1,0:T(8,128)(2,1)S(1)}, bf16[2,168,768]{2,1,0:T(8,128)(2,1)S(1)}, u32[]{:S(2)}, u32[]{:S(2)}) %collective-permute-start.18) | collective-permute-done | bytes 516128 | tf_op jit(solution)/shard_map/ppermute | solution.py:261
  90.5 9.6 %collective-permute-done.16.refs_4_ = bf16[2,168,768]{2,1,0:T(8,128)(2,1)S(1)} collective-permute-done((bf16[2,168,768]{2,1,0:T(8,128)(2,1)S(1)}, bf16[2,168,768]{2,1,0:T(8,128)(2,1)S(1)}, u32[]{:S(2)}, u32[]{:S(2)}) %collective-permute-start.16) | collective-permute-done | bytes 516128 | tf_op jit(solution)/shard_map/ppermute | solution.py:261
  114.5 9.4 %collective-permute-done.14.refs_2_ = bf16[2,168,768]{2,1,0:T(8,128)(2,1)S(1)} collective-permute-done((bf16[2,168,768]{2,1,0:T(8,128)(2,1)S(1)}, bf16[2,168,768]{2,1,0:T(8,128)(2,1)S(1)}, u32[]{:S(2)}, u32[]{:S(2)}) %collective-permute-start.14) | collective-permute-done | bytes 516128 | tf_op jit(solution)/shard_map/ppermute | solution.py:261
  142.0 10.2 %shard_map.139 = bf16[2,8,168,768]{3,2,1,0:T(8,128)(2,1)S(1)} custom-call(s32[8]{0:T(128)S(1)} %iota_xor_fusion.dest_ref, bf16[2,168,768]{2,1,0:T(8,128)(2,1)S(1)} %get-tuple-element.87.refs_0_, bf16[2,168,768]{2,1,0:T(8,128)(2,1)S(1)} %copy-done.12, bf16[2,168,768]{2,1,0:T(8,128)(2,1)S(1)} %collective-permute-done.14.refs_2_, ...), custom_call_target="tpu_custom_call" | custom-call | bytes 8257536 | tf_op jit(solution)/shard_map/pallas_call | solution.py:180
  158.2 11.2 %shard_map.142 = bf16[3,8,168,768]{3,2,1,0:T(8,128)(2,1)S(1)} custom-call(s32[8]{0:T(128)S(1)} %iota_xor_fusion.dest_ref, bf16[2,168,768]{2,1,0:T(8,128)(2,1)S(1)} %get-tuple-element.87.refs_0_, bf16[2,168,768]{2,1,0:T(8,128)(2,1)S(1)} %copy-done.13, bf16[2,168,768]{2,1,0:T(8,128)(2,1)S(1)} %collective-permute-done.14.refs_2_, ...), custom_call_target="tpu_custom_call" | custom-call | bytes 12386304 | tf_op jit(solution)/shard_map/pallas_call | solution.py:180
  182.3 8.8 %collective-permute-done.8.refs_6_ = bf16[2,240,768]{2,1,0:T(8,128)(2,1)} collective-permute-done((bf16[2,240,768]{2,1,0:T(8,128)(2,1)S(1)}, bf16[2,240,768]{2,1,0:T(8,128)(2,1)}, u32[]{:S(2)}, u32[]{:S(2)}) %collective-permute-start.8) | collective-permute-done | bytes 737312 | tf_op jit(solution)/shard_map/ppermute | solution.py:261
  193.2 12.7 %collective-permute-done.6.refs_4_ = bf16[2,240,768]{2,1,0:T(8,128)(2,1)} collective-permute-done((bf16[2,240,768]{2,1,0:T(8,128)(2,1)S(1)}, bf16[2,240,768]{2,1,0:T(8,128)(2,1)}, u32[]{:S(2)}, u32[]{:S(2)}) %collective-permute-start.6) | collective-permute-done | bytes 737312 | tf_op jit(solution)/shard_map/ppermute | solution.py:261
  221.0 8.2 %convolution_convert_fusion = bf16[1664,2304]{1,0:T(8,128)(2,1)} fusion(bf16[1664,768]{1,0:T(8,128)(2,1)S(1)} %fusion.21, bf16[3840,768]{1,0:T(8,128)(2,1)S(1)} %bitcast.213), kind=kOutput, calls=%fused_computation.10 | convolution fusion | flops 5892636672 | bytes 13762560 | tf_op jit(solution)/shard_map/dot_general | solution.py:22
  229.2 16.0 %shard_map.137 = bf16[1,8,208,768]{3,2,1,0:T(8,128)(2,1)} custom-call(bf16[1,8,208,2304]{3,2,1,0:T(8,128)(2,1)} %bitcast.270), custom_call_target="tpu_custom_call" | custom-call | flops 14976000000 | tf_op jit(solution)/shard_map/pallas_call | solution.py:135
  257.2 8.4 %convolution_convert_fusion.1 = bf16[1664,1536]{1,0:T(8,128)(2,1)} fusion(bf16[1664,768]{1,0:T(8,128)(2,1)S(1)} %add_convert_fusion.3, bf16[3840,768]{1,0:T(8,128)(2,1)} %bitcast.214), kind=kOutput, calls=%fused_computation.13 | convolution fusion | flops 3928424448 | bytes 10027008 | tf_op jit(solution)/shard_map/dot_general | solution.py:22
  273.8 16.2 %shard_map.141 = bf16[1,8,208,768]{3,2,1,0:T(8,128)(2,1)} custom-call(bf16[1,8,208,1536]{3,2,1,0:T(8,128)(2,1)} %bitcast.273, bf16[1,8,208,768]{3,2,1,0:T(8,128)(2,1)} %bitcast.279), custom_call_target="tpu_custom_call" | custom-call | flops 14976000000 | tf_op jit(solution)/shard_map/pallas_call | solution.py:135
  298.7 16.3 %multiply_convert_fusion.1 = (bf16[1664,3072]{1,0:T(8,128)(2,1)}, f32[1664,3072]{1,0:T(8,128)}) fusion(f32[3072]{0:T(1024)S(1)} %copy-done.77, bf16[3840,768]{1,0:T(8,128)(2,1)S(1)} %bitcast.221, f32[1664,768]{1,0:T(8,128)} %copy-done.42, f32[768]{0:T(1024)S(1)} %copy-done.81, f32[768]{0:T(1024)S(1)} %copy-done.76, f32[1664]{0:T(1024)S(1)} %add_rsqrt_fusion, ...), kind=kOutput, calls=%fused_computation.8 | convolution fusion | flops 7888797696 | bytes 40538112 | tf_op jit(solution)/shard_map/dot_general | solution.py:22
  315.1 20.0 %convert_reduce_fusion = (f32[3072]{0:T(1024)S(1)}, bf16[1664,3072]{1,0:T(8,128)(2,1)}) fusion(f32[1664,3072]{1,0:T(8,128)} %get-tuple-element.93, f32[3072]{0:T(1024)S(1)} %copy-done.77, bf16[1664,768]{1,0:T(8,128)(2,1)} %bitcast.255, bf16[4032,768]{1,0:T(8,128)(2,1)S(1)} %bitcast.209), kind=kOutput, calls=%fused_computation.6 | convolution fusion | flops 7928411136 | bytes 37969920 | tf_op jit(solution)/shard_map/dot_general | solution.py:22
  335.1 14.2 %convolution_convert_fusion.3.refs_1_ = bf16[3072,768]{1,0:T(8,128)(2,1)} fusion(bf16[1664,3072]{1,0:T(8,128)(2,1)} %get-tuple-element.100, f32[1664,768]{1,0:T(8,128)S(1)} %copy-done.43, f32[768]{0:T(1024)S(1)} %copy-done.81, f32[768]{0:T(1024)S(1)} %copy-done.76, f32[1664]{0:T(1024)S(1)} %add_rsqrt_fusion, f32[1664]{0:T(1024)S(1)} %broadcast_multiply_fusion.6), kind=kOutput, calls=%fused_computation.57 | convolution fusion | flops 7860486144 | bytes 20073472 | tf_op jit(solution)/shard_map/dot_general | solution.py:30
  349.4 14.4 %multiply_reduce_fusion = (f32[768]{0:T(1024)S(1)}, f32[1664]{0:T(1024)S(1)}, f32[1664]{0:T(1024)S(1)}, f32[768]{0:T(1024)S(1)}, f32[1664,768]{1,0:T(8,128)}) fusion(f32[1664,768]{1,0:T(8,128)S(1)} %copy-done.43, f32[1664]{0:T(1024)S(1)} %add_rsqrt_fusion, f32[1664]{0:T(1024)S(1)} %broadcast_multiply_fusion.6, f32[768]{0:T(1024)S(1)} %copy-done.76, ...), kind=kOutput, calls=%fused_computation.41 | convolution fusion | flops 7863233536 | bytes 25205760 | tf_op jit(solution)/shard_map/dot_general | solution.py:26
  377.0 25.7 %shard_map.143 = (bf16[1,8,208,1536]{3,2,1,0:T(8,128)(2,1)}, bf16[1,8,208,768]{3,2,1,0:T(8,128)(2,1)}) custom-call(bf16[1,8,208,1536]{3,2,1,0:T(8,128)(2,1)} %bitcast.274, bf16[1,8,208,768]{3,2,1,0:T(8,128)(2,1)} %bitcast.280, bf16[1,8,208,768]{3,2,1,0:T(8,128)(2,1)} %bitcast.286), custom_call_target="tpu_custom_call" | custom-call | flops 23296000000 | tf_op jit(solution)/shard_map/pallas_call | solution.py:135
  444.2 10.8 %convolution_convert_fusion.2.refs_3_.refs_0_ = bf16[3072,768]{1,0:T(8,128)(2,1)} fusion(bf16[1664,3072]{1,0:T(8,128)(2,1)S(1)} %bitcast.290, bf16[1664,768]{1,0:T(8,128)(2,1)S(1)} %bitcast.256), kind=kOutput, calls=%fused_computation.56 | convolution fusion | flops 7854096384 | bytes 17498112 | tf_op jit(solution)/shard_map/dot_general | solution.py:30
  458.0 8.6 %shard_map.148 = (bf16[4,2,168,768]{3,2,1,0:T(8,128)(2,1)S(1)}, bf16[4,2,168,768]{3,2,1,0:T(8,128)(2,1)}) custom-call(s32[1]{0:T(128)} %bitcast.41.core_ref, bf16[3072,768]{1,0:T(8,128)(2,1)S(1)} %copy-done), custom_call_target="tpu_custom_call" | custom-call | bytes 8257536 | tf_op jit(solution)/shard_map/pallas_call | solution.py:236
  472.6 26.2 %shard_map.144 = bf16[1,8,208,2304]{3,2,1,0:T(8,128)(2,1)} custom-call(bf16[1,8,208,2304]{3,2,1,0:T(8,128)(2,1)} %bitcast.271, bf16[1,8,208,768]{3,2,1,0:T(8,128)(2,1)} %bitcast.283), custom_call_target="tpu_custom_call" | custom-call | flops 23296000000 | tf_op jit(solution)/shard_map/pallas_call | solution.py:135
  498.7 10.7 %bitcast_convert_fusion.refs_0_ = bf16[2304,768]{1,0:T(8,128)(2,1)S(1)} fusion(bf16[1,8,208,2304]{3,2,1,0:T(8,128)(2,1)} %shard_map.144, f32[768]{0:T(1024)} %copy-done.74, f32[768]{0:T(1024)} %copy-done.68, f32[8,208]{1,0:T(8,128)} %copy-done.73, f32[8,208]{1,0:T(8,128)} %copy-done.67, bf16[1,8,196,768]{3,2,1,0:T(8,128)(2,1)} %bitcast.240), kind=kOutput, calls=%fused_computation.14 | convolution fusion | flops 5898240000 | bytes 13634560 | tf_op jit(solution)/shard_map/dot_general | solution.py:30
  509.5 12.5 %fusion.26 = (f32[768]{0:T(1024)}, f32[1664]{0:T(1024)}, f32[1664]{0:T(1024)}, f32[768]{0:T(1024)}, f32[1664,768]{1,0:T(8,128)}) fusion(f32[1664]{0:T(1024)S(1)} %copy-done.64, f32[1664]{0:T(1024)S(1)} %copy-done.62, bf16[1,8,196,768]{3,2,1,0:T(8,128)(2,1)S(1)} %bitcast.247, f32[768]{0:T(1024)S(1)} %copy-done.69, bf16[1664,2304]{1,0:T(8,128)(2,1)S(1)} %bitcast.272, ...), kind=kOutput, calls=%fused_computation.36 | convolution fusion | flops 5901577216 | bytes 18762752 | tf_op jit(solution)/shard_map/dot_general | solution.py:26
  538.2 13.9 %all-to-all-start.5 = ((f32[32,8,128]{2,1,0:T(8,128)}), f32[32,8,128]{2,1,0:T(8,128)}, u32[]{:S(2)}, u32[]{:S(2)}) async-start(f32[32,8,128]{2,1,0:T(8,128)} %bitcast.262), calls=%async_computation.5 | async-start | bytes 262144 | tf_op jit(solution)/shard_map/all_to_all | solution.py:313
  558.3 8.7 %shard_map.147 = (bf16[4,2,168,768]{3,2,1,0:T(8,128)(2,1)S(1)}, bf16[4,2,168,768]{3,2,1,0:T(8,128)(2,1)}) custom-call(s32[1]{0:T(128)} %bitcast.41.core_ref, bf16[768,768]{1,0:T(8,128)(2,1)S(1)} %copy-done.21, bf16[768,768]{1,0:T(8,128)(2,1)S(1)} %copy-done.20, bf16[768,768]{1,0:T(8,128)(2,1)S(1)} %copy-done.19, bf16[3072,768]{1,0:T(8,128)(2,1)S(1)} %copy-done.1), custom_call_target="tpu_custom_call" | custom-call | bytes 8257536 | tf_op jit(solution)/shard_map/pallas_call | solution.py:236
  582.8 11.5 %add_convert_fusion.1 = bf16[1664,768]{1,0:T(8,128)(2,1)S(1)} fusion(f32[1664,768]{1,0:T(8,128)} %copy-done.42, bf16[1664,3072]{1,0:T(8,128)(2,1)} %get-tuple-element.92, bf16[4032,768]{1,0:T(8,128)(2,1)S(1)} %bitcast.212, f32[768]{0:T(1024)S(1)} %copy-done.80), kind=kOutput, calls=%fused_computation.48 | convolution fusion | flops 7855570944 | bytes 22614016 | tf_op jit(solution)/shard_map/dot_general | solution.py:26
  613.8 37.6 %collective-permute-done.50 = bf16[2,168,768]{2,1,0:T(8,128)(2,1)S(1)} collective-permute-done((bf16[2,168,768]{2,1,0:T(8,128)(2,1)S(1)}, bf16[2,168,768]{2,1,0:T(8,128)(2,1)S(1)}, u32[]{:S(2)}, u32[]{:S(2)}) %collective-permute-start.50) | collective-permute-done | bytes 516128 | tf_op jit(solution)/shard_map/ppermute | solution.py:261
  679.8 25.4 %collective-permute-done.35 = bf16[2,240,768]{2,1,0:T(8,128)(2,1)} collective-permute-done((bf16[2,240,768]{2,1,0:T(8,128)(2,1)}, bf16[2,240,768]{2,1,0:T(8,128)(2,1)}, u32[]{:S(2)}, u32[]{:S(2)}) %collective-permute-start.35) | collective-permute-done | bytes 737312 | tf_op jit(solution)/shard_map/ppermute | solution.py:261
  714.9 48.1 %collective-permute-done.39 = bf16[2,240,768]{2,1,0:T(8,128)(2,1)S(1)} collective-permute-done((bf16[2,240,768]{2,1,0:T(8,128)(2,1)S(1)}, bf16[2,240,768]{2,1,0:T(8,128)(2,1)S(1)}, u32[]{:S(2)}, u32[]{:S(2)}) %collective-permute-start.39) | collective-permute-done | bytes 737312 | tf_op jit(solution)/shard_map/ppermute | solution.py:261
  786.5 18.6 %collective-permute-done.43 = bf16[240,768]{1,0:T(8,128)(2,1)} collective-permute-done((bf16[240,768]{1,0:T(8,128)(2,1)}, bf16[240,768]{1,0:T(8,128)(2,1)}, u32[]{:S(2)}, u32[]{:S(2)}) %collective-permute-start.43) | collective-permute-done | bytes 368672 | tf_op jit(solution)/shard_map/ppermute | solution.py:264
  (457 shorter events, 325.5 us)
Async XLA Ops:
  45.5 129.8 %all-to-all-start = ((bf16[4,2,196,768]{3,1,2,0:T(2,128)(2,1)}), bf16[4,2,196,768]{3,1,2,0:T(2,128)(2,1)}, u32[]{:S(2)}, u32[]{:S(2)}) async-start(bf16[4,2,196,768]{3,1,2,0:T(2,128)(2,1)} %param.8), calls=%async_computation | async-start | bytes 4816896 | tf_op jit(solution)/shard_map/all_to_all | solution.py:442
  55.9 44.2 %collective-permute-start.16 = (bf16[2,168,768]{2,1,0:T(8,128)(2,1)S(1)}, bf16[2,168,768]{2,1,0:T(8,128)(2,1)S(1)}, u32[]{:S(2)}, u32[]{:S(2)}) collective-permute-start(bf16[2,168,768]{2,1,0:T(8,128)(2,1)S(1)} %get-tuple-element.87.refs_0_), channel_id=1, source_target_pairs={{0,4},{1,5},{2,6},{3,7},{4,0},{5,1},{6,2},{7,3},{8,12},{9,13},{10,... | collective-permute-start | bytes 1548296 | tf_op jit(solution)/shard_map/ppermute | solution.py:261
  68.5 44.5 %collective-permute-start.28 = (bf16[2,168,768]{2,1,0:T(8,128)(2,1)}, bf16[2,168,768]{2,1,0:T(8,128)(2,1)}, u32[]{:S(2)}, u32[]{:S(2)}) collective-permute-start(bf16[2,168,768]{2,1,0:T(8,128)(2,1)} %get-tuple-element.86.refs_8_), channel_id=1, source_target_pairs={{0,2},{1,3},{2,0},{3,1},{4,6},{5,7},{6,4},{7,5},{8,10},{9,11},{10,... | collective-permute-start | bytes 1548296 | tf_op jit(solution)/shard_map/ppermute | solution.py:261
  69.5 54.4 %collective-permute-start.14 = (bf16[2,168,768]{2,1,0:T(8,128)(2,1)S(1)}, bf16[2,168,768]{2,1,0:T(8,128)(2,1)S(1)}, u32[]{:S(2)}, u32[]{:S(2)}) collective-permute-start(bf16[2,168,768]{2,1,0:T(8,128)(2,1)S(1)} %get-tuple-element.87.refs_0_), channel_id=1, source_target_pairs={{0,2},{1,3},{2,0},{3,1},{4,6},{5,7},{6,4},{7,5},{8,10},{9,11},{10,... | collective-permute-start | bytes 1548296 | tf_op jit(solution)/shard_map/ppermute | solution.py:261
  77.9 47.0 %collective-permute-start.13 = (bf16[2,168,768]{2,1,0:T(8,128)(2,1)S(1)}, bf16[2,168,768]{2,1,0:T(8,128)(2,1)S(1)}, u32[]{:S(2)}, u32[]{:S(2)}) collective-permute-start(bf16[2,168,768]{2,1,0:T(8,128)(2,1)S(1)} %get-tuple-element.87.refs_0_), channel_id=1, source_target_pairs={{0,1},{1,0},{2,3},{3,2},{4,5},{5,4},{6,7},{7,6},{8,9},{9,8},{10,11... | collective-permute-start | bytes 1548296 | tf_op jit(solution)/shard_map/ppermute | solution.py:261
  112.9 41.4 %collective-permute-start.27 = (bf16[2,168,768]{2,1,0:T(8,128)(2,1)}, bf16[2,168,768]{2,1,0:T(8,128)(2,1)}, u32[]{:S(2)}, u32[]{:S(2)}) collective-permute-start(bf16[2,168,768]{2,1,0:T(8,128)(2,1)} %get-tuple-element.86.refs_8_), channel_id=1, source_target_pairs={{0,1},{1,0},{2,3},{3,2},{4,5},{5,4},{6,7},{7,6},{8,9},{9,8},{10,11... | collective-permute-start | bytes 1548296 | tf_op jit(solution)/shard_map/ppermute | solution.py:261
  140.8 38.1 %collective-permute-start.25 = (bf16[2,240,768]{2,1,0:T(8,128)(2,1)S(1)}, bf16[2,240,768]{2,1,0:T(8,128)(2,1)}, u32[]{:S(2)}, u32[]{:S(2)}) collective-permute-start(bf16[2,240,768]{2,1,0:T(8,128)(2,1)S(1)} %get-tuple-element.81.refs_0_), channel_id=1, source_target_pairs={{0,6},{1,7},{2,4},{3,5},{4,2},{5,3},{6,0},{7,1},{8,14},{9,15},{10,... | collective-permute-start | bytes 2211848 | tf_op jit(solution)/shard_map/ppermute | solution.py:261
  156.9 49.0 %collective-permute-start.6 = (bf16[2,240,768]{2,1,0:T(8,128)(2,1)S(1)}, bf16[2,240,768]{2,1,0:T(8,128)(2,1)}, u32[]{:S(2)}, u32[]{:S(2)}) collective-permute-start(bf16[2,240,768]{2,1,0:T(8,128)(2,1)S(1)} %get-tuple-element.82.refs_0_), channel_id=1, source_target_pairs={{0,4},{1,5},{2,6},{3,7},{4,0},{5,1},{6,2},{7,3},{8,12},{9,13},{10,... | collective-permute-start | bytes 2211848 | tf_op jit(solution)/shard_map/ppermute | solution.py:261
  158.1 49.0 %collective-permute-start.4 = (bf16[2,240,768]{2,1,0:T(8,128)(2,1)S(1)}, bf16[2,240,768]{2,1,0:T(8,128)(2,1)}, u32[]{:S(2)}, u32[]{:S(2)}) collective-permute-start(bf16[2,240,768]{2,1,0:T(8,128)(2,1)S(1)} %get-tuple-element.82.refs_0_), channel_id=1, source_target_pairs={{0,2},{1,3},{2,0},{3,1},{4,6},{5,7},{6,4},{7,5},{8,10},{9,11},{10,... | collective-permute-start | bytes 2211848 | tf_op jit(solution)/shard_map/ppermute | solution.py:261
  178.9 36.6 %collective-permute-start.21 = (bf16[2,240,768]{2,1,0:T(8,128)(2,1)S(1)}, bf16[2,240,768]{2,1,0:T(8,128)(2,1)S(1)}, u32[]{:S(2)}, u32[]{:S(2)}) collective-permute-start(bf16[2,240,768]{2,1,0:T(8,128)(2,1)S(1)} %get-tuple-element.81.refs_0_), channel_id=1, source_target_pairs={{0,2},{1,3},{2,0},{3,1},{4,6},{5,7},{6,4},{7,5},{8,10},{9,11},{10,... | collective-permute-start | bytes 2211848 | tf_op jit(solution)/shard_map/ppermute | solution.py:261
  215.4 50.2 %collective-permute-start.20 = (bf16[2,240,768]{2,1,0:T(8,128)(2,1)S(1)}, bf16[2,240,768]{2,1,0:T(8,128)(2,1)S(1)}, u32[]{:S(2)}, u32[]{:S(2)}) collective-permute-start(bf16[2,240,768]{2,1,0:T(8,128)(2,1)S(1)} %get-tuple-element.81.refs_0_), channel_id=1, source_target_pairs={{0,1},{1,0},{2,3},{3,2},{4,5},{5,4},{6,7},{7,6},{8,9},{9,8},{10,11... | collective-permute-start | bytes 2211848 | tf_op jit(solution)/shard_map/ppermute | solution.py:261
  216.0 49.7 %collective-permute-start.26 = (bf16[2,240,768]{2,1,0:T(8,128)(2,1)}, bf16[2,240,768]{2,1,0:T(8,128)(2,1)}, u32[]{:S(2)}, u32[]{:S(2)}) collective-permute-start(bf16[2,240,768]{2,1,0:T(8,128)(2,1)} %collective-permute-done.25.refs_6_), channel_id=1, source_target_pairs={{0,1},{1,0},{2,3},{3,2},{4,5},{5,4},{6,7},{7,6},{8,9},{9,8},{10,11... | collective-permute-start | bytes 2211848 | tf_op jit(solution)/shard_map/ppermute | solution.py:261
  216.0 49.6 %collective-permute-start.24 = (bf16[2,240,768]{2,1,0:T(8,128)(2,1)}, bf16[2,240,768]{2,1,0:T(8,128)(2,1)}, u32[]{:S(2)}, u32[]{:S(2)}) collective-permute-start(bf16[2,240,768]{2,1,0:T(8,128)(2,1)} %collective-permute-done.23.refs_4_), channel_id=1, source_target_pairs={{0,1},{1,0},{2,3},{3,2},{4,5},{5,4},{6,7},{7,6},{8,9},{9,8},{10,11... | collective-permute-start | bytes 2211848 | tf_op jit(solution)/shard_map/ppermute | solution.py:261
  216.5 49.2 %collective-permute-start.22 = (bf16[2,240,768]{2,1,0:T(8,128)(2,1)S(1)}, bf16[2,240,768]{2,1,0:T(8,128)(2,1)}, u32[]{:S(2)}, u32[]{:S(2)}) collective-permute-start(bf16[2,240,768]{2,1,0:T(8,128)(2,1)S(1)} %collective-permute-done.21.refs_2_), channel_id=1, source_target_pairs={{0,1},{1,0},{2,3},{3,2},{4,5},{5,4},{6,7},{7,6},{8,9},{9,8},{10,11... | collective-permute-start | bytes 2211848 | tf_op jit(solution)/shard_map/ppermute | solution.py:261
  468.0 132.7 %collective-permute-start.49 = (bf16[4,2,168,768]{3,2,1,0:T(8,128)(2,1)}, bf16[4,2,168,768]{3,2,1,0:T(8,128)(2,1)}, u32[]{:S(2)}, u32[]{:S(2)}) collective-permute-start(bf16[4,2,168,768]{3,2,1,0:T(8,128)(2,1)} %get-tuple-element.26), channel_id=1, source_target_pairs={{0,1},{1,0},{2,3},{3,2},{4,5},{5,4},{6,7},{7,6},{8,9},{9,8},{10,11... | collective-permute-start | bytes 6193160 | tf_op jit(solution)/shard_map/ppermute | solution.py:261
  538.2 57.8 %all-to-all-start.5 = ((f32[32,8,128]{2,1,0:T(8,128)}), f32[32,8,128]{2,1,0:T(8,128)}, u32[]{:S(2)}, u32[]{:S(2)}) async-start(f32[32,8,128]{2,1,0:T(8,128)} %bitcast.262), calls=%async_computation.5 | async-start | bytes 262144 | tf_op jit(solution)/shard_map/all_to_all | solution.py:313
  568.3 37.2 %collective-permute-start.45 = (bf16[4,2,168,768]{3,2,1,0:T(8,128)(2,1)}, bf16[4,2,168,768]{3,2,1,0:T(8,128)(2,1)}, u32[]{:S(2)}, u32[]{:S(2)}) collective-permute-start(bf16[4,2,168,768]{3,2,1,0:T(8,128)(2,1)} %get-tuple-element.24), channel_id=1, source_target_pairs={{0,1},{1,0},{2,3},{3,2},{4,5},{5,4},{6,7},{7,6},{8,9},{9,8},{10,11... | collective-permute-start | bytes 6193160 | tf_op jit(solution)/shard_map/ppermute | solution.py:261
  582.3 92.7 %collective-permute-start.38 = (bf16[4,2,240,768]{3,2,1,0:T(8,128)(2,1)}, bf16[4,2,240,768]{3,2,1,0:T(8,128)(2,1)}, u32[]{:S(2)}, u32[]{:S(2)}) collective-permute-start(bf16[4,2,240,768]{3,2,1,0:T(8,128)(2,1)} %get-tuple-element.22), channel_id=1, source_target_pairs={{0,1},{1,0},{2,3},{3,2},{4,5},{5,4},{6,7},{7,6},{8,9},{9,8},{10,11... | collective-permute-start | bytes 8847368 | tf_op jit(solution)/shard_map/ppermute | solution.py:261
  595.9 63.5 %all-to-all-start.2 = ((bf16[1,8,196,768]{3,2,0,1:T(8,128)(2,1)}), bf16[1,8,196,768]{3,2,0,1:T(8,128)(2,1)}, u32[]{:S(2)}, u32[]{:S(2)}) async-start(bf16[1,8,196,768]{3,2,0,1:T(8,128)(2,1)} %slice.199), calls=%async_computation.2 | async-start | bytes 4915200 | tf_op jit(solution)/shard_map/all_to_all | solution.py:447
  603.1 48.3 %collective-permute-start.50 = (bf16[2,168,768]{2,1,0:T(8,128)(2,1)S(1)}, bf16[2,168,768]{2,1,0:T(8,128)(2,1)S(1)}, u32[]{:S(2)}, u32[]{:S(2)}) collective-permute-start(bf16[2,168,768]{2,1,0:T(8,128)(2,1)S(1)} %get-tuple-element.72), channel_id=1, source_target_pairs={{0,2},{1,3},{2,0},{3,1},{4,6},{5,7},{6,4},{7,5},{8,10},{9,11},{10,... | collective-permute-start | bytes 1548296 | tf_op jit(solution)/shard_map/ppermute | solution.py:261
  604.5 48.3 %collective-permute-start.52 = (bf16[2,168,768]{2,1,0:T(8,128)(2,1)S(1)}, bf16[2,168,768]{2,1,0:T(8,128)(2,1)S(1)}, u32[]{:S(2)}, u32[]{:S(2)}) collective-permute-start(bf16[2,168,768]{2,1,0:T(8,128)(2,1)S(1)} %get-tuple-element.73), channel_id=1, source_target_pairs={{0,6},{1,7},{2,4},{3,5},{4,2},{5,3},{6,0},{7,1},{8,14},{9,15},{10,... | collective-permute-start | bytes 1548296 | tf_op jit(solution)/shard_map/ppermute | solution.py:261
  605.5 47.5 %collective-permute-start.51 = (bf16[2,168,768]{2,1,0:T(8,128)(2,1)S(1)}, bf16[2,168,768]{2,1,0:T(8,128)(2,1)S(1)}, u32[]{:S(2)}, u32[]{:S(2)}) collective-permute-start(bf16[2,168,768]{2,1,0:T(8,128)(2,1)S(1)} %get-tuple-element.74), channel_id=1, source_target_pairs={{0,4},{1,5},{2,6},{3,7},{4,0},{5,1},{6,2},{7,3},{8,12},{9,13},{10,... | collective-permute-start | bytes 1548296 | tf_op jit(solution)/shard_map/ppermute | solution.py:261
  609.1 64.5 %collective-permute-start.46 = (bf16[2,168,768]{2,1,0:T(8,128)(2,1)}, bf16[2,168,768]{2,1,0:T(8,128)(2,1)S(1)}, u32[]{:S(2)}, u32[]{:S(2)}) collective-permute-start(bf16[2,168,768]{2,1,0:T(8,128)(2,1)} %get-tuple-element.75), channel_id=1, source_target_pairs={{0,2},{1,3},{2,0},{3,1},{4,6},{5,7},{6,4},{7,5},{8,10},{9,11},{10,... | collective-permute-start | bytes 1548296 | tf_op jit(solution)/shard_map/ppermute | solution.py:261
  653.0 52.2 %collective-permute-start.35 = (bf16[2,240,768]{2,1,0:T(8,128)(2,1)}, bf16[2,240,768]{2,1,0:T(8,128)(2,1)}, u32[]{:S(2)}, u32[]{:S(2)}) collective-permute-start(bf16[2,240,768]{2,1,0:T(8,128)(2,1)} %get-tuple-element.69), channel_id=1, source_target_pairs={{0,2},{1,3},{2,0},{3,1},{4,6},{5,7},{6,4},{7,5},{8,10},{9,11},{10,... | collective-permute-start | bytes 2211848 | tf_op jit(solution)/shard_map/ppermute | solution.py:261
  659.5 119.0 %all-to-all-start.4 = ((bf16[1,8,196,768]{3,2,0,1:T(8,128)(2,1)}), bf16[1,8,196,768]{3,2,0,1:T(8,128)(2,1)}, u32[]{:S(2)}, u32[]{:S(2)}) async-start(bf16[1,8,196,768]{3,2,0,1:T(8,128)(2,1)} %slice.200), calls=%async_computation.4 | async-start | bytes 4915200 | tf_op jit(solution)/shard_map/all_to_all | solution.py:447
  673.6 37.9 %collective-permute-start.37 = (bf16[2,240,768]{2,1,0:T(8,128)(2,1)}, bf16[2,240,768]{2,1,0:T(8,128)(2,1)S(1)}, u32[]{:S(2)}, u32[]{:S(2)}) collective-permute-start(bf16[2,240,768]{2,1,0:T(8,128)(2,1)} %get-tuple-element.70), channel_id=1, source_target_pairs={{0,6},{1,7},{2,4},{3,5},{4,2},{5,3},{6,0},{7,1},{8,14},{9,15},{10,... | collective-permute-start | bytes 2211848 | tf_op jit(solution)/shard_map/ppermute | solution.py:261
  675.0 36.6 %collective-permute-start.36 = (bf16[2,240,768]{2,1,0:T(8,128)(2,1)}, bf16[2,240,768]{2,1,0:T(8,128)(2,1)S(1)}, u32[]{:S(2)}, u32[]{:S(2)}) collective-permute-start(bf16[2,240,768]{2,1,0:T(8,128)(2,1)} %get-tuple-element.71), channel_id=1, source_target_pairs={{0,4},{1,5},{2,6},{3,7},{4,0},{5,1},{6,2},{7,3},{8,12},{9,13},{10,... | collective-permute-start | bytes 2211848 | tf_op jit(solution)/shard_map/ppermute | solution.py:261
  677.3 85.7 %collective-permute-start.39 = (bf16[2,240,768]{2,1,0:T(8,128)(2,1)S(1)}, bf16[2,240,768]{2,1,0:T(8,128)(2,1)S(1)}, u32[]{:S(2)}, u32[]{:S(2)}) collective-permute-start(bf16[2,240,768]{2,1,0:T(8,128)(2,1)S(1)} %get-tuple-element.66), channel_id=1, source_target_pairs={{0,2},{1,3},{2,0},{3,1},{4,6},{5,7},{6,4},{7,5},{8,10},{9,11},{10,... | collective-permute-start | bytes 2211848 | tf_op jit(solution)/shard_map/ppermute | solution.py:261
  678.4 85.1 %collective-permute-start.41 = (bf16[2,240,768]{2,1,0:T(8,128)(2,1)S(1)}, bf16[2,240,768]{2,1,0:T(8,128)(2,1)S(1)}, u32[]{:S(2)}, u32[]{:S(2)}) collective-permute-start(bf16[2,240,768]{2,1,0:T(8,128)(2,1)S(1)} %get-tuple-element.67), channel_id=1, source_target_pairs={{0,6},{1,7},{2,4},{3,5},{4,2},{5,3},{6,0},{7,1},{8,14},{9,15},{10,... | collective-permute-start | bytes 2211848 | tf_op jit(solution)/shard_map/ppermute | solution.py:261
  705.2 58.3 %collective-permute-start.40 = (bf16[2,240,768]{2,1,0:T(8,128)(2,1)S(1)}, bf16[2,240,768]{2,1,0:T(8,128)(2,1)S(1)}, u32[]{:S(2)}, u32[]{:S(2)}) collective-permute-start(bf16[2,240,768]{2,1,0:T(8,128)(2,1)S(1)} %get-tuple-element.68), channel_id=1, source_target_pairs={{0,4},{1,5},{2,6},{3,7},{4,0},{5,1},{6,2},{7,3},{8,12},{9,13},{10,... | collective-permute-start | bytes 2211848 | tf_op jit(solution)/shard_map/ppermute | solution.py:261
  711.5 58.0 %collective-permute-start.53 = (bf16[168,768]{1,0:T(8,128)(2,1)S(1)}, bf16[168,768]{1,0:T(8,128)(2,1)S(1)}, u32[]{:S(2)}, u32[]{:S(2)}) collective-permute-start(bf16[168,768]{1,0:T(8,128)(2,1)S(1)} %get-tuple-element.83), channel_id=1, source_target_pairs={{0,8},{1,9},{2,10},{3,11},{4,12},{5,13},{6,14},{7,15},{8,16},{9,17... | collective-permute-start | bytes 774152 | tf_op jit(solution)/shard_map/ppermute | solution.py:264
  711.6 72.7 %collective-permute-start.54 = (bf16[168,768]{1,0:T(8,128)(2,1)}, bf16[168,768]{1,0:T(8,128)(2,1)}, u32[]{:S(2)}, u32[]{:S(2)}) collective-permute-start(bf16[168,768]{1,0:T(8,128)(2,1)} %get-tuple-element.84), channel_id=1, source_target_pairs={{0,16},{1,17},{2,18},{3,19},{4,20},{5,21},{6,22},{7,23},{8,24},{9,... | collective-permute-start | bytes 774152 | tf_op jit(solution)/shard_map/ppermute | solution.py:264
  (137 other events, 2254.8 us)

commit v3 on v1

v3 whole, which is shorter than its diff:
```python
from functools import partial

import jax
import jax.numpy as jnp
from jax import lax
from jax.experimental import pallas as pl
from jax.experimental.pallas import tpu as pltpu
from jax.sharding import PartitionSpec as P

HEADS = 12
HEAD_DIM = 64
EPSILON = 1e-06
PAIRS = HEADS // 2
LANES = 2 * HEAD_DIM
SUB = 16
NEG = -1e30
F32 = jnp.float32
BF16 = jnp.bfloat16


def nt(left, right):
    return lax.dot_general(left, right, (((1,), (1,)), ((), ())), preferred_element_type=F32)


def nn(left, right):
    return lax.dot_general(left, right, (((1,), (0,)), ((), ())), preferred_element_type=F32)


def tn(left, right):
    return lax.dot_general(left, right, (((0,), (0,)), ((), ())), preferred_element_type=F32)


def split_heads(pair):
    first = lax.broadcasted_iota(jnp.int32, pair.shape, 1) < HEAD_DIM
    zero = jnp.zeros_like(pair)
    return jnp.concatenate([jnp.where(first, pair, zero), jnp.where(first, zero, pair)], axis=0)


def join_heads(stacked):
    rows = stacked.shape[0] // 2
    first = lax.broadcasted_iota(jnp.int32, (rows, LANES), 1) < HEAD_DIM
    return jnp.where(first, stacked[:rows], stacked[rows:])


def pair_forward(queries, keys, values, keep):
    stacked = split_heads(queries * jnp.asarray(HEAD_DIM**-0.5, BF16))
    scores = jnp.where(keep, nt(stacked, keys), NEG)
    top = jnp.max(scores, axis=1, keepdims=True)
    weights = jnp.exp(scores - top)
    total = jnp.sum(weights, axis=1, keepdims=True)
    probs = (weights * (1.0 / total)).astype(BF16)
    return join_heads(nn(probs, values)).astype(BF16)


def pair_backward(queries, keys, values, grad, keep):
    scaling = HEAD_DIM**-0.5
    stacked = split_heads(queries * jnp.asarray(scaling, BF16))
    grads = split_heads(grad)
    scores = jnp.where(keep, nt(keys, stacked), NEG)
    top = jnp.max(scores, axis=0, keepdims=True)
    weights = jnp.exp(scores - top)
    total = jnp.sum(weights, axis=0, keepdims=True)
    probs = weights * (1.0 / total)
    grad_probs = nt(values, grads)
    mean = jnp.sum(probs * grad_probs, axis=0, keepdims=True)
    grad_scores = (probs * (grad_probs - mean)).astype(BF16)
    grad_values = nn(probs.astype(BF16), grads)
    grad_keys = nn(grad_scores, stacked)
    grad_queries = join_heads(tn(grad_scores, keys)) * scaling
    return (grad_queries.astype(BF16), grad_keys.astype(BF16), grad_values.astype(BF16))


def columns(kind, pair):
    start = (kind * PAIRS + pair) * LANES
    return slice(start, start + LANES)


def find(refs, kind, pair):
    cols = columns(kind, pair)
    for ref in refs:
        size = ref.shape[-1]
        if cols.start < size:
            return (ref, cols)
        cols = slice(cols.start - size, cols.stop - size)


def load(refs, kind, pair):
    ref, cols = find(refs, kind, pair)
    return ref[..., cols].reshape(-1, LANES)


def store(refs, kind, pair, block):
    ref, cols = find(refs, kind, pair)
    ref[..., cols] = block.reshape(ref.shape[:-1] + (LANES,))


def keep_mask(shape, key_axis, group, patches):
    key = lax.broadcasted_iota(jnp.int32, shape, key_axis)
    if group is None:
        return key < patches
    query = lax.broadcasted_iota(jnp.int32, shape, 1 - key_axis)
    return (key % group) == (query % group)


def forward_kernel(group, patches, count, *refs):
    project, mixed = (refs[:count], refs[count:])
    rows = project[0].size // project[0].shape[-1]
    keep = keep_mask((2 * rows, rows), 1, group, patches)
    for pair in range(PAIRS):
        block = pair_forward(*[load(project, kind, pair) for kind in range(3)], keep)
        store(mixed, 0, pair, block)


def backward_kernel(group, patches, count, *refs):
    project, grad, outs = (refs[:count], refs[count : count + 1], refs[count + 1 :])
    rows = project[0].size // project[0].shape[-1]
    keep = keep_mask((rows, 2 * rows), 0, group, patches)
    for pair in range(PAIRS):
        results = pair_backward(*[load(project, kind, pair) for kind in range(3)], load(grad, 0, pair), keep)
        for kind, result in enumerate(results):
            store(outs, kind, pair, result)


def attention_call(kernel, count, arrays, out_cols, temporal, patches):
    clips, frames, rows, _ = arrays[0].shape
    if temporal:
        group, steps, shape = SUB, rows // SUB, (1, frames, SUB)
        index = lambda c, i: (c, 0, i, 0)
    else:
        group, steps, shape = None, frames, (1, 1, rows)
        index = lambda c, i: (c, i, 0, 0)
    tokens = clips * frames * rows
    backward = kernel is backward_kernel
    return pl.pallas_call(
        partial(kernel, group, patches, count),
        grid=(clips, steps),
        in_specs=[pl.BlockSpec(shape + (a.shape[-1],), index) for a in arrays],
        out_specs=[pl.BlockSpec(shape + (cols,), index) for cols in out_cols],
        out_shape=[jax.ShapeDtypeStruct((clips, frames, rows, cols), BF16) for cols in out_cols],
        compiler_params=pltpu.CompilerParams(dimension_semantics=("arbitrary", "arbitrary")),
        cost_estimate=pl.CostEstimate(
            flops=tokens * (14_000_000 if backward else 9_000_000), bytes_accessed=0, transcendentals=0
        ),
    )(*arrays)


def place_kernel(outs_plan, blocks, groups, dest_ref, *refs):
    pieces, refs = (refs[: groups * blocks], refs[groups * blocks :])
    outs, refs = (refs[: len(outs_plan)], refs[len(outs_plan) :])
    held, in_sem, out_sem = (refs[:-2], refs[-2], refs[-1])
    moves, slot = ([], 0)
    for target, entries in enumerate(outs_plan):
        for entry, (group, row, rows) in enumerate(entries):
            for block in range(blocks):
                buffer = held[target].at[entry, block]
                source = pieces[group * blocks + block].at[pl.ds(row, rows)]
                fetch = pltpu.make_async_copy(source, buffer, in_sem.at[slot])
                fetch.start()
                write = pltpu.make_async_copy(buffer, outs[target].at[entry, dest_ref[block]], out_sem.at[slot])
                moves.append((fetch, write))
                slot += 1
    for fetch, write in moves:
        fetch.wait()
        write.start()
    for _, write in moves:
        write.wait()


def place(groups, outs_plan, dest):
    blocks = len(groups[0])
    width = groups[0][0].shape[1]
    shapes = [(len(entries), blocks, entries[0][2], width) for entries in outs_plan]
    slots = sum(len(entries) for entries in outs_plan) * blocks
    size = sum(2 * s[0] * s[1] * s[2] * s[3] for s in shapes)
    flat = [piece for group in groups for piece in group]
    anywhere = pl.BlockSpec(memory_space=pl.ANY)
    return pl.pallas_call(
        partial(place_kernel, tuple(tuple(e) for e in outs_plan), blocks, len(groups)),
        in_specs=[pl.BlockSpec(memory_space=pltpu.SMEM)] + [anywhere] * len(flat),
        out_specs=[anywhere] * len(shapes),
        out_shape=[jax.ShapeDtypeStruct(s, BF16) for s in shapes],
        scratch_shapes=[pltpu.VMEM(s, BF16) for s in shapes]
        + [pltpu.SemaphoreType.DMA((slots,)), pltpu.SemaphoreType.DMA((slots,))],
        compiler_params=pltpu.CompilerParams(vmem_limit_bytes=size + (2 << 20)),
        cost_estimate=pl.CostEstimate(flops=0, bytes_accessed=4 * size, transcendentals=0),
    )(dest, *flat)


def split_kernel(spans, plane_rows, squares, core_ref, *refs):
    parts, refs = (refs[: len(spans)], refs[len(spans) :])
    keep, send = refs[:2]
    held, in_sem, out_sem = (refs[2:-2], refs[-2], refs[-1])
    core = core_ref[0]
    incoming, count, part, done = ({}, 0, 0, 0)
    for plane, rows in enumerate(plane_rows):
        for slot in range(2 * squares):
            offset, incoming[plane, slot] = (0, [])
            while offset < rows:
                first, length = spans[part]
                size = min(length - done, rows - offset)
                copy = pltpu.make_async_copy(
                    parts[part].at[pl.ds(first + done, size)],
                    held[plane].at[slot, pl.ds(offset, size)],
                    in_sem.at[count],
                )
                copy.start()
                incoming[plane, slot].append(copy)
                count, offset, done = (count + 1, offset + size, done + size)
                if done == length:
                    part, done = (part + 1, 0)
    outgoing, row = ([], 0)
    for plane, rows in enumerate(plane_rows):
        for square in range(squares):
            for copy in incoming[plane, 2 * square] + incoming[plane, 2 * square + 1]:
                copy.wait()
            for target, side in ((send, 1 - core), (keep, core)):
                copy = pltpu.make_async_copy(
                    held[plane].at[2 * square + side], target.at[square, pl.ds(row, rows)], out_sem.at[len(outgoing)]
                )
                copy.start()
                outgoing.append(copy)
        row += rows
    for copy in outgoing:
        copy.wait()


def split_cores(parts, plane_rows, squares, core):
    spans = tuple((first, length) for _, first, length in parts)
    arrays = [array for array, _, _ in parts]
    width = arrays[0].shape[1]
    slots = len(plane_rows) * squares * 2
    size = 2 * squares * sum(plane_rows) * width * 2
    anywhere = pl.BlockSpec(memory_space=pl.ANY)
    half = jax.ShapeDtypeStruct((squares, sum(plane_rows), width), BF16)
    return pl.pallas_call(
        partial(split_kernel, spans, tuple(plane_rows), squares),
        in_specs=[pl.BlockSpec(memory_space=pltpu.SMEM)] + [anywhere] * len(arrays),
        out_specs=[anywhere, anywhere],
        out_shape=[half, half],
        scratch_shapes=[pltpu.VMEM((2 * squares, rows, width), BF16) for rows in plane_rows]
        + [pltpu.SemaphoreType.DMA((slots + len(parts),)), pltpu.SemaphoreType.DMA((slots,))],
        compiler_params=pltpu.CompilerParams(vmem_limit_bytes=size + (2 << 20)),
        cost_estimate=pl.CostEstimate(flops=0, bytes_accessed=4 * size, transcendentals=0),
    )(core, *arrays)


def tie(values, others):
    return lax.optimization_barrier((values, others))


class Whole:
    def __init__(self, axes, weights_in, weights_out, packed, width):
        self.axes, self.width = (axes, width)
        full_in = lax.all_gather(weights_in, axes, axis=0, tiled=True)
        full_out = lax.all_gather(weights_out, axes, axis=0, tiled=True)
        devices = lax.axis_size(axes)
        slot = lax.dynamic_update_slice(
            jnp.zeros((devices,) + packed.shape, F32), packed.astype(F32)[None], (lax.axis_index(axes), 0, 0)
        )
        self.small = lax.psum(slot, axes).transpose(1, 0, 2).reshape(packed.shape[0], width).astype(BF16)
        self.in_a, self.in_b = (full_in[: 5 * width // 2], full_in[5 * width // 2 : 3 * width])
        self.in_t, self.in_qk = (full_in[: 3 * width], full_in[3 * width : 5 * width])
        self.in_v, self.in_m = (full_in[5 * width : 6 * width], full_in[6 * width :])
        self.out_t, self.out_f = (full_out[:width], full_out[width : 2 * width])
        self.out_s, self.out_m = (full_out[2 * width : 3 * width], full_out[3 * width :])
        self.grads = {}

    def tick(self, name, *values):
        return values[0] if len(values) == 1 else values

    def total(self, small):
        g = self.grads
        d_in = jnp.concatenate([g["in_t"], g["in_qk"], g["in_v"], g["in_m"]], axis=0)
        d_out = jnp.concatenate([g["out_t"], g["out_f"], g["out_s"], g["out_m"]], axis=0)
        summed_in = lax.psum_scatter(d_in, self.axes, scatter_dimension=0, tiled=True).astype(F32)
        summed_out = lax.psum_scatter(d_out, self.axes, scatter_dimension=0, tiled=True).astype(F32)
        share = self.width // lax.axis_size(self.axes)
        at = (0, lax.axis_index(self.axes) * share)
        return (summed_in, summed_out, lax.dynamic_slice(lax.psum(small, self.axes), at, (small.shape[0], share)))


class Staged:
    def __init__(self, axes, weights_in, weights_out, packed, width):
        self.axes, self.width = (axes, width)
        me = lax.axis_index(axes)
        self.plane, self.spot, self.square, self.core = (me // 8, me % 8, me % 8 // 2, me % 2)
        self.spots = jnp.bitwise_xor(jnp.arange(8, dtype=jnp.int32), self.spot)
        self.planes = (self.plane + 4 - jnp.arange(4, dtype=jnp.int32)) % 4
        self.core_ref = self.core.astype(jnp.int32).reshape(1)
        self.rows_in, self.rows_out = (weights_in.shape[0], weights_out.shape[0])
        self.weights_out, self.count = (weights_out, packed.shape[0])
        self.grads = {}
        flat = packed.reshape(1, -1)
        tail = jnp.pad(flat, ((0, 7), (0, width - flat.shape[1])))
        self.column_in, self.column_small = self.columns(
            jnp.concatenate([weights_in, tail], axis=0), (self.rows_in, 8)
        )

    def flip(self, x, bits):
        return lax.ppermute(x, self.axes, [(d, d ^ bits) for d in range(32)])

    def shift(self, x, step):
        return lax.ppermute(x, self.axes, [(d, (d + 8 * step) % 32) for d in range(32)])

    def columns(self, shard, sizes):
        pieces = [shard] + [self.shift(shard, step) for step in (1, 2, 3)]
        plan, row = ([], 0)
        for size in sizes:
            plan.append([(0, row, size)])
            row += size
        return [out[0] for out in place([pieces], plan, self.planes)]

    def over(self, piece):
        return [piece] + [self.flip(piece, bits) for bits in (2, 4, 6)]

    def cores(self, pieces):
        both = []
        for piece in pieces:
            both += [piece, self.flip(piece, 1)]
        return both

    def lay(self, groups, entries):
        out = place(groups, [entries], self.spots)[0]
        return out.reshape(-1, self.width)

    def begin(self, clip):
        rows_in, rows_out, width = (self.rows_in, self.rows_out, self.width)
        smalls = self.column_small.reshape(-1, width)
        first = jnp.concatenate([self.column_in[0], smalls], axis=0)
        self.p1, self.p2, self.p3 = (self.column_in[k] for k in (1, 2, 3))
        weights_out, first = tie(self.weights_out, first)
        p0 = self.over(first)
        p0, (clip, self.p1) = tie(p0, (clip, self.p1))
        column = self.columns(weights_out, (rows_out,))[0]
        self.q01, self.q23 = (column[:2].reshape(-1, width), column[2:].reshape(-1, width))
        self.p1 = self.over(self.p1)
        self.p0 = self.cores(p0)
        low, small = place([self.p0], [[(0, 0, rows_in)], [(0, rows_in, 32)]], self.spots)
        self.in_a = low.reshape(-1, width)
        share = width // 32
        small = small.reshape(8, 4, 8, width)[:, :, 0, : self.count * share].reshape(8, 4, self.count, share)
        self.small = small.transpose(2, 1, 0, 3).reshape(self.count, width)
        return clip

    def tick(self, name, *values):
        single = len(values) == 1
        rows_in, rows_out, width = (self.rows_in, self.rows_out, self.width)
        g = self.grads
        whole = lambda key: (g[key], 0, g[key].shape[0])
        if name == "query_t":
            values, (self.p1, self.q01) = tie(values, (self.p1, self.q01))
            self.q01 = self.over(self.q01)
            self.p1 = self.cores(self.p1)
            low = self.lay([self.p0, self.p1], [(0, 0, rows_in), (1, 0, rows_in)])
            self.in_t, self.in_qk = (low[: 3 * width], low[3 * width :])
            self.in_b = self.in_t[5 * width // 2 :]
        elif name == "mixed_t":
            values, (self.q01, self.p2) = tie(values, (self.q01, self.p2))
            self.p2 = self.over(self.p2)
            self.q01 = self.cores(self.q01)
            early = self.lay([self.q01], [(0, 0, rows_out), (0, rows_out, rows_out)])
            self.out_t, self.out_f, self.out_s = (early[k * width : (k + 1) * width] for k in range(3))
        elif name == "query_s":
            values, (self.p2, self.p3) = tie(values, (self.p2, self.p3))
            self.p3 = self.over(self.p3)
            self.p2 = self.cores(self.p2)
            self.in_v = self.lay([self.p2], [(0, 0, rows_in)])[:width]
        elif name == "mixed_s":
            values, (self.p3, self.q23) = tie(values, (self.p3, self.q23))
            self.q23 = self.over(self.q23)
            self.p3 = self.cores(self.p3)
            high = self.lay([self.p2, self.p3], [(0, 0, rows_in), (1, 0, rows_in)])
            self.in_m = high[width:]
        elif name == "hidden":
            values, self.q23 = tie(values, self.q23)
            self.q23 = self.cores(self.q23)
            entries = [(0, rows_out, rows_out), (1, 0, rows_out), (1, rows_out, rows_out)]
            self.out_m = self.lay([self.q01, self.q23], entries)[3 * width - 8 * rows_out :]
        elif name == "grad_hidden":
            first, split = (16 * rows_out - 3 * width, 24 * rows_in - 6 * width)
            self.out_first = first
            d_out_m, d_in_m = (g["out_m"], g["in_m"])
            self.part_a = self.halve(
                [(d_out_m, first, d_out_m.shape[0] - first), (d_in_m, split, d_in_m.shape[0] - split)],
                (rows_out, rows_out, rows_in),
            )
        elif name == "grad_mixed_s":
            values, self.part_a = tie(values, self.part_a)
            self.part_a = self.across(*self.part_a)
        elif name == "grad_t":
            values, self.part_a = tie(values, self.part_a)
            self.part_a = self.gathered(self.part_a)
        elif name == "grad_projected":
            first, split = (self.out_first, 24 * rows_in - 6 * width)
            self.part_b = self.halve(
                [
                    whole("in_v"),
                    (g["in_m"], 0, split),
                    whole("out_t"),
                    whole("out_f"),
                    whole("out_s"),
                    (g["out_m"], 0, first),
                ],
                (rows_in, rows_out, rows_out),
            )
            kept, values = tie(self.part_b[0], values)
            self.part_b = (kept,) + self.part_b[1:]
        elif name == "grad_mixed_t":
            values, self.part_b = tie(values, self.part_b)
            self.part_b = self.across(*self.part_b)
        elif name == "grad_in_t":
            values, self.part_b = tie(values, self.part_b)
            self.part_b = self.gathered(self.part_b)
            self.part_c = self.halve([whole("in_t"), whole("in_qk")], (rows_in, rows_in))
        return values[0] if single else values

    def halve(self, parts, plane_rows):
        keep, send = split_cores(parts, plane_rows, 4, self.core_ref)
        return (keep, self.flip(send, 1))

    def across(self, keep, other):
        result = []
        for bits in (0, 2, 4, 6):
            at = jnp.bitwise_xor(self.square, bits // 2)
            take = lambda a: lax.dynamic_index_in_dim(a, at, 0, keepdims=False).astype(F32)
            summed = (take(keep) + take(other)).astype(BF16)
            result.append(summed if bits == 0 else self.flip(summed, bits))
        return result

    def gathered(self, arrived):
        total = arrived[0].astype(F32)
        for block in arrived[1:]:
            total = total + block.astype(F32)
        return total.astype(BF16)

    def along(self, planes):
        every = jnp.stack(planes, axis=0)
        total = lax.dynamic_index_in_dim(every, self.plane, 0, keepdims=False).astype(F32)
        for step in (1, 2, 3):
            block = lax.dynamic_index_in_dim(every, (self.plane + step) % 4, 0, keepdims=False)
            total = total + self.shift(block, step).astype(F32)
        return total

    def sum_small(self, small):
        count, width = small.shape
        share = width // 32
        tiles = -(-count * share // (8 * LANES))
        slots = small.reshape(count, 32, share).transpose(1, 0, 2).reshape(32, count * share)
        slots = jnp.pad(slots, ((0, 0), (0, tiles * 8 * LANES - count * share))).reshape(32, tiles * 8, LANES)
        slots = lax.all_to_all(slots, self.axes, split_axis=0, concat_axis=0)
        return jnp.sum(slots, axis=0).reshape(-1)[: count * share].reshape(count, share)

    def total(self, small):
        rows_in, rows_out = (self.rows_in, self.rows_out)
        a, b = (self.part_a, self.part_b)
        out_planes = [b[rows_in : rows_in + rows_out], b[rows_in + rows_out :], a[:rows_out], a[rows_out : 2 * rows_out]]
        arrived = self.across(*self.part_c)
        small, arrived[0] = tie(small, arrived[0])
        summed_out = self.along(out_planes)
        owned = self.sum_small(small)
        c = self.gathered(arrived)
        summed_in = self.along([c[:rows_in], c[rows_in:], b[:rows_in], a[2 * rows_out :]])
        return (summed_in, summed_out, owned)


def norm_parts(values):
    centre = values - jnp.mean(values, axis=-1, keepdims=True)
    spread = jnp.mean(centre * centre, axis=-1, keepdims=True)
    scale = lax.rsqrt(spread + EPSILON)
    return (centre * scale, scale)


def layer_norm(values, gains, shifts):
    return (norm_parts(values)[0] * gains + shifts).astype(BF16)


def norm_backward(values, gains, grad):
    normed, scale = norm_parts(values)
    scaled = grad * gains
    first = jnp.mean(scaled, axis=-1, keepdims=True)
    second = jnp.mean(scaled * normed, axis=-1, keepdims=True)
    inner = (scaled - first - normed * second) * scale
    return (inner, jnp.sum(grad * normed, axis=0), jnp.sum(grad, axis=0))


def gelu_parts(values):
    cdf = 0.5 * (1.0 + lax.erf(values * (0.5**0.5)))
    density = jnp.exp(-0.5 * values * values) * 0.3989422804014327
    return (values * cdf, cdf + values * density)


def column_sum(rows):
    return jnp.sum(rows.astype(F32), axis=0)


def block(clip, target, leave, feed, gain_count, patches):
    shape = clip.shape
    width = shape[-1]
    grid = shape[:3]
    small32 = feed.small.astype(F32)
    gains32, shifts32, dense32 = (small32[:gain_count], small32[gain_count:-1], small32[-1])
    flat = lambda a: a.reshape(-1, a.shape[-1])
    cube = lambda a: a.reshape(grid + (a.shape[-1],))
    grads = feed.grads
    start = clip.reshape(-1, width).astype(F32)
    normed_t = layer_norm(start, gains32[0], shifts32[0])
    project_a = nt(normed_t, feed.in_a).astype(BF16)
    project_a, normed_t = feed.tick("query_t", project_a, normed_t)
    project_b = nt(normed_t, feed.in_b).astype(BF16)
    project_t = [cube(project_a), cube(project_b)]
    mixed_t = attention_call(forward_kernel, 2, project_t, (width,), True, patches)[0]
    mixed_t = flat(feed.tick("mixed_t", mixed_t))
    projected_t = (nn(mixed_t, feed.out_t) + shifts32[3]).astype(BF16)
    branch_t = (nn(projected_t, feed.out_f) + shifts32[4]).astype(BF16)
    after_t = start + branch_t.astype(F32)
    normed_s = layer_norm(after_t, gains32[1], shifts32[1])
    project_qk = nt(normed_s, feed.in_qk).astype(BF16)
    project_qk, normed_s = feed.tick("query_s", project_qk, normed_s)
    project_v = nt(normed_s, feed.in_v).astype(BF16)
    project_s = [cube(project_qk), cube(project_v)]
    mixed_s = attention_call(forward_kernel, 2, project_s, (width,), False, patches)[0]
    mixed_s = flat(feed.tick("mixed_s", mixed_s))
    grad_low = flat(target(mixed_s))
    after_s = after_t + (nn(mixed_s, feed.out_s) + shifts32[5])
    normed_m = layer_norm(after_s, gains32[2], shifts32[2])
    hidden_pre = nt(normed_m, feed.in_m) + shifts32[6:].reshape(-1)
    hidden32, slope32 = gelu_parts(hidden_pre)
    hidden, slope = feed.tick("hidden", hidden32.astype(BF16), slope32.astype(BF16))
    output = (after_s + (nn(hidden, feed.out_m) + dense32)).astype(BF16)
    output = leave(output.reshape(shape))

    grad_out = grad_low.astype(F32)
    grads["out_m"] = tn(hidden, grad_low).astype(BF16)
    s_dense = column_sum(grad_low)
    grad_pre = (nt(grad_low, feed.out_m) * slope.astype(F32)).astype(BF16)
    grads["in_m"] = tn(grad_pre, normed_m).astype(BF16)
    grad_pre = feed.tick("grad_hidden", grad_pre)
    s_hidden = column_sum(grad_pre).reshape(-1, width)
    part, g_m, b_m = norm_backward(after_s, gains32[2], nn(grad_pre, feed.in_m))
    grad_s = grad_out + part
    grad_branch_s = grad_s.astype(BF16)
    grads["out_s"] = tn(mixed_s, grad_branch_s).astype(BF16)
    s_space = column_sum(grad_branch_s)
    grad_mixed_s = nt(grad_branch_s, feed.out_s).astype(BF16)
    grad_mixed_s, output = feed.tick("grad_mixed_s", grad_mixed_s, output)
    grad_qk, grad_v = attention_call(
        backward_kernel, 2, project_s + [cube(grad_mixed_s)], (2 * width, width), False, patches
    )
    grad_qk, grad_v = (flat(grad_qk), flat(grad_v))
    grads["in_qk"] = tn(grad_qk, normed_s).astype(BF16)
    grads["in_v"] = tn(grad_v, normed_s).astype(BF16)
    part, g_s, b_s = norm_backward(after_t, gains32[1], nn(grad_qk, feed.in_qk) + nn(grad_v, feed.in_v))
    grad_t = grad_s + part
    grad_branch_t = feed.tick("grad_t", grad_t.astype(BF16))
    grads["out_f"] = tn(projected_t, grad_branch_t).astype(BF16)
    s_fc = column_sum(grad_branch_t)
    grad_projected = nt(grad_branch_t, feed.out_f).astype(BF16)
    grads["out_t"] = tn(mixed_t, grad_projected).astype(BF16)
    grad_projected = feed.tick("grad_projected", grad_projected)
    s_time = column_sum(grad_projected)
    grad_mixed_t = feed.tick("grad_mixed_t", nt(grad_projected, feed.out_t).astype(BF16))
    grad_project_t = attention_call(
        backward_kernel, 2, project_t + [cube(grad_mixed_t)], (3 * width,), True, patches
    )[0]
    grad_project_t = flat(grad_project_t)
    grads["in_t"] = tn(grad_project_t, normed_t).astype(BF16)
    grad_project_t = feed.tick("grad_in_t", grad_project_t)
    part, g_t, b_t = norm_backward(start, gains32[0], nn(grad_project_t, feed.in_t))
    grad_clip = (grad_t + part.astype(BF16).astype(F32)).astype(BF16)
    small = jnp.concatenate(
        [
            jnp.stack([g_t, g_s, g_m, b_t, b_s, b_m, s_time, s_fc, s_space], axis=0),
            s_hidden,
            s_dense[None, :],
        ],
        axis=0,
    )
    return (output, leave(grad_clip.reshape(shape)).astype(F32)) + feed.total(small)


def shards(clips_in, cotangent, clip_live, weights_in, weights_out, norm_gain, shift_rows, dense_shift):
    both = ("dp", "seq")
    group = lax.axis_size("seq")
    count, _, patches, width = clips_in.shape
    own = count // group
    rows = -(-patches // SUB) * SUB
    gain_count = norm_gain.shape[0]
    shift_count = shift_rows.shape[0]
    staged = lax.axis_size(both) == 32 and group == 4 and weights_in.shape[0] == 240 and weights_out.shape[0] == 168

    def enter(x):
        x = lax.all_to_all(x, "seq", split_axis=0, concat_axis=1, tiled=True)
        return jnp.pad(x, ((0, 0), (0, 0), (0, rows - patches), (0, 0)))

    def leave(x):
        x = x[:, :, :patches]
        return lax.all_to_all(x, "seq", split_axis=1, concat_axis=0, tiled=True)

    packed = jnp.concatenate([norm_gain, shift_rows, dense_shift[None, :]], axis=0)
    feed = (Staged if staged else Whole)(both, weights_in, weights_out, packed, width)
    clip = enter(clips_in)
    if staged:
        clip = feed.begin(clip)
    live = lax.dynamic_slice(clip_live, (lax.axis_index("seq") * own,), (own,)).astype(BF16)

    def target(after):
        gradient = cotangent * 1
        if staged:
            gradient = tie(gradient, after)[0]
        return enter(gradient) * live[:, None, None, None]

    output, grad_clip, summed_in, summed_out, owned = block(clip, target, leave, feed, gain_count, patches)
    return (
        output,
        grad_clip,
        summed_in,
        summed_out,
        owned[:gain_count],
        owned[gain_count : gain_count + shift_count],
        owned[-1],
    )


def solution(mesh):
    clip = P("dp", "seq", None, None)
    row = P(("dp", "seq"), None)
    col = P(None, ("dp", "seq"))
    flat = P(("dp", "seq"))
    return jax.shard_map(
        shards,
        mesh=mesh,
        in_specs=(clip, clip, P("dp"), row, row, col, col, flat),
        out_specs=(clip, clip, row, row, col, col, flat),
        check_vma=False,
    )
```

time: 705 us -> 714 us (1.013)
  blocking collectives: 179 us -> 0 us
  Pallas kernels: 84.9 us -> 153 us
  starting transfers between devices: 14.2 us -> 81.3 us
  waiting for transfers between devices: 128 us -> 175 us
  local copies, waits for them, and re-layouts: 25.6 us -> 48.5 us
  between operations: 15.6 us -> 3.88 us
  other arithmetic: 52.6 us -> 44.4 us
    ppermute x0 -> x66, waiting for transfers between devices: none -> 151 us  [the longest x54 103 us: flip(): return lax.ppermute(x, self.axes, [(d, d ^ bits) for d in range(32)])]
    psum x2 -> x0, blocking collectives: 143 us -> none  [the longest x1 80.4 us: shards(): lax.psum(slot, both).transpose(1, 0, 2).reshape(packed.shape[0], width)]
    reduce_scatter x2 -> x0, waiting for transfers between devices: 79.5 us -> none  [the longest x1 79.5 us: shards(): lax.psum_scatter(d_in, both, scatter_dimension=0, tiled=True).astype(F32)]
    pallas_call x4 -> x15, Pallas kernels: 84.9 us -> 153 us  [the longest x4 83.7 us: attention_call(): pl.pallas_call(partial(kernel, group, patches, count), grid=(clips, steps...]
    ppermute x0 -> x66, starting transfers between devices: none -> 58.6 us  [the longest x54 39.8 us: flip(): return lax.ppermute(x, self.axes, [(d, d ^ bits) for d in range(32)])]
    all_to_all x1 -> x0, blocking collectives: 36.9 us -> none  [enter(): x = lax.all_to_all(x, 'seq', split_axis=0, concat_axis=1, tiled=True)]
    concatenate x2 -> x3, other arithmetic: 29.4 us -> 0.07 us  [the longest x1 0.03 us: begin(): first = jnp.concatenate([self.column_in[0], smalls], axis=0)]
    all_gather x2 -> x0, waiting for transfers between devices: 26.3 us -> none  [the longest x1 26.3 us: shards(): full_out = lax.all_gather(weights_out, both, axis=0, tiled=True)]
  transfers between devices with their start and end apart: 7 -> 71, of which waited for: 3 -> 14; matrix products, arithmetic and copies ran while one was open for 17% -> 34% of each run, Pallas kernels for 6% -> 13%
where the time goes in v3:
time: 714 us; the launch traced here: 703 us
  matrix products  197 us (28%)
  waiting for transfers between devices  175 us (25%)
  Pallas kernels  153 us (21%)
  starting transfers between devices  81.3 us (11%)
  local copies, waits for them, and re-layouts  48.5 us (7%)
  other arithmetic  44.4 us (6%)
    ppermute x54, waiting for transfers between devices, flip(): return lax.ppermute(x, self.axes, [(d, d ^ bits) for d in range(32)])  103 us
    pallas_call x4, Pallas kernels, attention_call(): pl.pallas_call(partial(kernel, group, patches, count), grid=(clips, steps...  83.7 us
    dot_general x9, matrix products, nt(): lax.dot_general(left, right, (((1,), (1,)), ((), ())), preferred_element_...  71.7 us
    dot_general x8, matrix products, nn(): lax.dot_general(left, right, (((1,), (0,)), ((), ())), preferred_element_...  67.2 us
    dot_general x8, matrix products, tn(): lax.dot_general(left, right, (((0,), (0,)), ((), ())), preferred_element_...  57.7 us
    ppermute x12, waiting for transfers between devices, shift(): lax.ppermute(x, self.axes, [(d, (d + 8 * step) % 32) for d in range(32)])  48.1 us
    pallas_call x8, Pallas kernels, place(): pl.pallas_call(partial(place_kernel, tuple((tuple(e) for e in outs_plan))...  42.7 us
    ppermute x54, starting transfers between devices, flip(): return lax.ppermute(x, self.axes, [(d, d ^ bits) for d in range(32)])  39.8 us
  transfers between devices with their start and end apart: 71, of which 14 were waited for; matrix products, arithmetic and copies ran while one was open for 34% of the time, Pallas kernels for 13%

profile of v3, /device:TPU:0, one launch (start us, length us, event | category | flops | bytes accessed | tf_op | source)
XLA Modules:
  0.0 703.1 jit_solution(8762040630942936932)
XLA Ops:
  11.7 8.3 %collective-permute-done.2.refs_3_ = bf16[248,768]{1,0:T(8,128)(2,1)S(1)} collective-permute-done((bf16[248,768]{1,0:T(8,128)(2,1)S(1)}, bf16[248,768]{1,0:T(8,128)(2,1)S(1)}, u32[]{:S(2)}, u32[]{:S(2)}) %collective-permute-start.2) | collective-permute-done | bytes 380960 | tf_op jit(solution)/shard_map/ppermute | solution.py:303
  20.0 23.8 %collective-permute-done.1.refs_2_ = bf16[248,768]{1,0:T(8,128)(2,1)S(1)} collective-permute-done((bf16[248,768]{1,0:T(8,128)(2,1)S(1)}, bf16[248,768]{1,0:T(8,128)(2,1)S(1)}, u32[]{:S(2)}, u32[]{:S(2)}) %collective-permute-start.1) | collective-permute-done | bytes 380960 | tf_op jit(solution)/shard_map/ppermute | solution.py:303
  56.3 15.7 %collective-permute-done.14.refs_2_ = bf16[168,768]{1,0:T(8,128)(2,1)S(1)} collective-permute-done((bf16[168,768]{1,0:T(8,128)(2,1)S(1)}, bf16[168,768]{1,0:T(8,128)(2,1)S(1)}, u32[]{:S(2)}, u32[]{:S(2)}) %collective-permute-start.14) | collective-permute-done | bytes 258080 | tf_op jit(solution)/shard_map/ppermute | solution.py:303
  96.6 7.4 %convolution_convert_fusion = bf16[1664,1920]{1,0:T(8,128)(2,1)} fusion(bf16[1664,768]{1,0:T(8,128)(2,1)S(1)} %bitcast.238, bf16[1920,768]{1,0:T(8,128)(2,1)S(1)} %bitcast.225), kind=kOutput, calls=%fused_computation.10 | convolution fusion | flops 4910530560 | bytes 11894784 | tf_op jit(solution)/shard_map/dot_general | solution.py:22
  121.3 15.7 %shard_map.139 = bf16[1,8,208,768]{3,2,1,0:T(8,128)(2,1)} custom-call(bf16[1,8,208,1920]{3,2,1,0:T(8,128)(2,1)} %bitcast.249, bf16[1,8,208,384]{3,2,1,0:T(8,128)(2,1)} %bitcast.265), custom_call_target="tpu_custom_call" | custom-call | flops 14976000000 | tf_op jit(solution)/shard_map/pallas_call | solution.py:134
  142.0 9.9 %shard_map.140 = bf16[2,8,168,768]{3,2,1,0:T(8,128)(2,1)S(1)} custom-call(s32[8]{0:T(128)S(1)} %iota_xor_fusion.dest_ref, bf16[336,768]{1,0:T(8,128)(2,1)S(1)} %bitcast.213, bf16[336,768]{1,0:T(8,128)(2,1)S(1)} %collective-permute-done.23.refs_1_, bf16[336,768]{1,0:T(8,128)(2,1)S(1)} %collective-permute-done.20.refs_2_, ...), custom_call_target="tpu_custom_call" | custom-call | bytes 16515072 | tf_op jit(solution)/shard_map/pallas_call | solution.py:177
  161.2 8.4 %convolution_convert_fusion.1 = bf16[1664,1536]{1,0:T(8,128)(2,1)} fusion(bf16[1664,768]{1,0:T(8,128)(2,1)S(1)} %add_convert_fusion.3, bf16[3840,768]{1,0:T(8,128)(2,1)} %bitcast.202), kind=kOutput, calls=%fused_computation.11 | convolution fusion | flops 3928424448 | bytes 10027008 | tf_op jit(solution)/shard_map/dot_general | solution.py:22
  182.3 16.0 %shard_map.142 = bf16[1,8,208,768]{3,2,1,0:T(8,128)(2,1)} custom-call(bf16[1,8,208,1536]{3,2,1,0:T(8,128)(2,1)} %bitcast.251, bf16[1,8,208,768]{3,2,1,0:T(8,128)(2,1)} %bitcast.257), custom_call_target="tpu_custom_call" | custom-call | flops 14976000000 | tf_op jit(solution)/shard_map/pallas_call | solution.py:134
  201.7 6.4 fusion.70
  214.5 17.2 %fusion.4 = (bf16[1664,3072]{1,0:T(8,128)(2,1)}, bf16[1664,3072]{1,0:T(8,128)(2,1)}) fusion(f32[3072]{0:T(1024)S(1)} %add.374, bf16[3840,768]{1,0:T(8,128)(2,1)S(1)} %bitcast.207, f32[1664,768]{1,0:T(8,128)S(1)} %get-tuple-element.230, f32[768]{0:T(1024)S(1)} %add.371, f32[768]{0:T(1024)S(1)} %mul.239, f32[1664]{0:T(1024)S(1)} %add_rsqrt_fusion, ...), kind=kOutput, calls=%fused_computation.5 | convolution fusion | flops 7919468544 | bytes 30314496 | tf_op jit(solution)/shard_map/dot_general | solution.py:22
  238.8 11.5 %shard_map.144 = bf16[3,8,168,768]{3,2,1,0:T(8,128)(2,1)S(1)} custom-call(s32[8]{0:T(128)S(1)} %iota_xor_fusion.dest_ref, bf16[336,768]{1,0:T(8,128)(2,1)S(1)} %bitcast.214, bf16[336,768]{1,0:T(8,128)(2,1)S(1)} %collective-permute-done.23.refs_1_, bf16[336,768]{1,0:T(8,128)(2,1)S(1)} %collective-permute-done.20.refs_2_, ...), custom_call_target="tpu_custom_call" | custom-call | bytes 24772608 | tf_op jit(solution)/shard_map/pallas_call | solution.py:177
  250.3 12.0 %add_convert_fusion.1 = bf16[1664,768]{1,0:T(8,128)(2,1)S(1)} fusion(f32[1664,768]{1,0:T(8,128)} %copy-done.28, bf16[1664,3072]{1,0:T(8,128)(2,1)S(1)} %copy-done.92, bf16[4032,768]{1,0:T(8,128)(2,1)S(1)} %bitcast.199, f32[768]{0:T(1024)S(1)} %add.381), kind=kOutput, calls=%fused_computation.43 | convolution fusion | flops 7855570944 | bytes 22614016 | tf_op jit(solution)/shard_map/dot_general | solution.py:26
  276.0 12.6 %convolution_convert_fusion.4.refs_0_.refs_5_ = bf16[3072,768]{1,0:T(8,128)(2,1)S(1)} fusion(bf16[1664,3072]{1,0:T(8,128)(2,1)} %get-tuple-element.125, bf16[1664,768]{1,0:T(8,128)(2,1)S(1)} %bitcast.234), kind=kOutput, calls=%fused_computation.55 | convolution fusion | flops 7854096384 | bytes 17498112 | tf_op jit(solution)/shard_map/dot_general | solution.py:30
  288.6 16.9 %convert_reduce_fusion = (f32[3072]{0:T(1024)}, bf16[1664,3072]{1,0:T(8,128)(2,1)}) fusion(bf16[1664,3072]{1,0:T(8,128)(2,1)} %get-tuple-element.124, bf16[1664,768]{1,0:T(8,128)(2,1)S(1)} %bitcast.235, bf16[4032,768]{1,0:T(8,128)(2,1)} %bitcast.200), kind=kOutput, calls=%fused_computation.6 | convolution fusion | flops 7877293056 | bytes 27734016 | tf_op jit(solution)/shard_map/dot_general | solution.py:22
  305.5 14.1 %convolution_convert_fusion.3.refs_1_ = bf16[3072,768]{1,0:T(8,128)(2,1)S(1)} fusion(bf16[1664,3072]{1,0:T(8,128)(2,1)} %get-tuple-element.235, f32[1664,768]{1,0:T(8,128)} %copy-done.28, f32[768]{0:T(1024)S(1)} %add.371, f32[768]{0:T(1024)S(1)} %mul.239, f32[1664]{0:T(1024)S(1)} %add_rsqrt_fusion, f32[1664]{0:T(1024)S(1)} %broadcast_multiply_fusion.6), kind=kOutput, calls=%fused_computation.54 | convolution fusion | flops 7860486144 | bytes 20073472 | tf_op jit(solution)/shard_map/dot_general | solution.py:30
  319.6 10.9 %shard_map.145 = (bf16[4,576,768]{2,1,0:T(8,128)(2,1)S(1)}, bf16[4,576,768]{2,1,0:T(8,128)(2,1)}) custom-call(s32[1]{0:T(128)} %bitcast.31.core_ref, bf16[3072,768]{1,0:T(8,128)(2,1)S(1)} %convolution_convert_fusion.4.refs_0_.refs_5_, bf16[3072,768]{1,0:T(8,128)(2,1)S(1)} %convolution_convert_fusion.3.refs_1_), custom_call_target="tpu_custom_call" | custom-call | bytes 28311552 | tf_op jit(solution)/shard_map/pallas_call | solution.py:235
  331.1 16.5 %multiply_reduce_fusion = (f32[768]{0:T(1024)}, f32[1664]{0:T(1024)S(1)}, f32[1664]{0:T(1024)S(1)}, f32[768]{0:T(1024)}, f32[1664,768]{1,0:T(8,128)S(1)}) fusion(f32[1664,768]{1,0:T(8,128)} %copy-done.28, f32[1664]{0:T(1024)S(1)} %add_rsqrt_fusion, f32[1664]{0:T(1024)S(1)} %broadcast_multiply_fusion.6, f32[768]{0:T(1024)S(1)} %copy-done.71, ...), kind=kOutput, calls=%fused_computation.38 | convolution fusion | flops 7863233536 | bytes 25201664 | tf_op jit(solution)/shard_map/dot_general | solution.py:26
  350.5 6.1 convolution_convert_fusion.7
  360.0 25.9 %shard_map.146 = (bf16[1,8,208,1536]{3,2,1,0:T(8,128)(2,1)}, bf16[1,8,208,768]{3,2,1,0:T(8,128)(2,1)}) custom-call(bf16[1,8,208,1536]{3,2,1,0:T(8,128)(2,1)} %bitcast.252, bf16[1,8,208,768]{3,2,1,0:T(8,128)(2,1)} %bitcast.258, bf16[1,8,208,768]{3,2,1,0:T(8,128)(2,1)} %bitcast.261), custom_call_target="tpu_custom_call" | custom-call | flops 23296000000 | tf_op jit(solution)/shard_map/pallas_call | solution.py:134
  397.0 10.8 %multiply_reduce_fusion.1 = (f32[768]{0:T(1024)}, f32[1664]{0:T(1024)S(1)}, f32[1664]{0:T(1024)S(1)}, f32[768]{0:T(1024)}, f32[1664,768]{1,0:T(8,128)S(1)}) fusion(f32[1664]{0:T(1024)S(1)} %copy-done.65, f32[1664]{0:T(1024)S(1)} %copy-done.59, bf16[1664,768]{1,0:T(8,128)(2,1)S(1)} %copy-done.26, bf16[1,8,208,768]{3,2,1,0:T(8,128)(2,1)S(1)} %copy-done.23, ...), kind=kOutput, calls=%fused_computation.39 | convolution fusion | flops 3942477056 | bytes 22842368 | tf_op jit(solution)/shard_map/dot_general | solution.py:26
  419.4 15.7 %collective-permute-done.51 = bf16[576,768]{1,0:T(8,128)(2,1)S(1)} collective-permute-done((bf16[576,768]{1,0:T(8,128)(2,1)S(1)}, bf16[576,768]{1,0:T(8,128)(2,1)S(1)}, u32[]{:S(2)}, u32[]{:S(2)}) %collective-permute-start.51) | collective-permute-done | bytes 884768 | tf_op jit(solution)/shard_map/ppermute | solution.py:300
  435.1 18.6 %collective-permute-done.50 = bf16[576,768]{1,0:T(8,128)(2,1)S(1)} collective-permute-done((bf16[576,768]{1,0:T(8,128)(2,1)S(1)}, bf16[576,768]{1,0:T(8,128)(2,1)S(1)}, u32[]{:S(2)}, u32[]{:S(2)}) %collective-permute-start.50) | collective-permute-done | bytes 884768 | tf_op jit(solution)/shard_map/ppermute | solution.py:300
  463.2 10.7 %shard_map.147 = (bf16[4,576,768]{2,1,0:T(8,128)(2,1)S(1)}, bf16[4,576,768]{2,1,0:T(8,128)(2,1)}) custom-call(s32[1]{0:T(128)} %bitcast.31.core_ref, bf16[768,768]{1,0:T(8,128)(2,1)S(1)} %convolution_convert_fusion.14.refs_0_, bf16[3072,768]{1,0:T(8,128)(2,1)S(1)} %bitcast.198, bf16[768,768]{1,0:T(8,128)(2,1)S(1)} %convolution_convert_fusion.13.refs_2_, ...), custom_call_target="tpu_custom_call" | custom-call | bytes 28311552 | tf_op jit(solution)/shard_map/pallas_call | solution.py:235
  486.6 8.7 %convolution_convert_fusion.9.refs_1_ = bf16[1536,768]{1,0:T(8,128)(2,1)} fusion(bf16[1664,1536]{1,0:T(8,128)(2,1)} %bitcast.254, bf16[1664,768]{1,0:T(8,128)(2,1)S(1)} %copy-done.43), kind=kOutput, calls=%fused_computation.76 | convolution fusion | flops 3927048192 | bytes 10027008 | tf_op jit(solution)/shard_map/dot_general | solution.py:30
  504.4 26.1 %shard_map.148 = bf16[1,8,208,2304]{3,2,1,0:T(8,128)(2,1)} custom-call(bf16[1,8,208,1920]{3,2,1,0:T(8,128)(2,1)} %bitcast.250, bf16[1,8,208,384]{3,2,1,0:T(8,128)(2,1)} %bitcast.266, bf16[1,8,208,768]{3,2,1,0:T(8,128)(2,1)} %bitcast.262), custom_call_target="tpu_custom_call" | custom-call | flops 23296000000 | tf_op jit(solution)/shard_map/pallas_call | solution.py:134
  537.9 9.1 %convolution_convert_fusion.2.refs_0_ = bf16[2304,768]{1,0:T(8,128)(2,1)S(1)} fusion(bf16[1664,2304]{1,0:T(8,128)(2,1)} %bitcast.247, bf16[1664,768]{1,0:T(8,128)(2,1)S(1)} %copy-done.38), kind=kOutput, calls=%fused_computation.53 | convolution fusion | flops 5890572288 | bytes 13762560 | tf_op jit(solution)/shard_map/dot_general | solution.py:30
  557.8 17.7 %collective-permute-done.54 = bf16[576,768]{1,0:T(8,128)(2,1)S(1)} collective-permute-done((bf16[576,768]{1,0:T(8,128)(2,1)S(1)}, bf16[576,768]{1,0:T(8,128)(2,1)S(1)}, u32[]{:S(2)}, u32[]{:S(2)}) %collective-permute-start.54) | collective-permute-done | bytes 884768 | tf_op jit(solution)/shard_map/ppermute | solution.py:300
  577.5 10.9 %fusion.22 = (f32[768]{0:T(1024)S(1)}, f32[1664]{0:T(1024)S(1)}, f32[1664]{0:T(1024)S(1)}, f32[768]{0:T(1024)S(1)}, f32[1664,768]{1,0:T(8,128)S(1)}) fusion(bf16[1,8,208,768]{3,2,1,0:T(8,128)(2,1)S(1)} %copy-done.24, f32[1664]{0:T(1024)S(1)} %copy-done.63, f32[1664]{0:T(1024)S(1)} %copy-done.61, f32[768]{0:T(1024)S(1)} %copy-done.67, ...), kind=kOutput, calls=%fused_computation.33 | convolution fusion | flops 5901577216 | bytes 18914304 | tf_op jit(solution)/shard_map/dot_general | solution.py:26
  613.5 10.6 %collective-permute-done.59 = bf16[480,768]{1,0:T(8,128)(2,1)} collective-permute-done((bf16[480,768]{1,0:T(8,128)(2,1)}, bf16[480,768]{1,0:T(8,128)(2,1)}, u32[]{:S(2)}, u32[]{:S(2)}) %collective-permute-start.59) | collective-permute-done | bytes 737312 | tf_op jit(solution)/shard_map/ppermute | solution.py:300
  624.2 15.3 %collective-permute-done.58 = bf16[480,768]{1,0:T(8,128)(2,1)} collective-permute-done((bf16[480,768]{1,0:T(8,128)(2,1)}, bf16[480,768]{1,0:T(8,128)(2,1)}, u32[]{:S(2)}, u32[]{:S(2)}) %collective-permute-start.58) | collective-permute-done | bytes 737312 | tf_op jit(solution)/shard_map/ppermute | solution.py:300
  639.5 18.3 %collective-permute-done.57 = bf16[480,768]{1,0:T(8,128)(2,1)} collective-permute-done((bf16[480,768]{1,0:T(8,128)(2,1)}, bf16[480,768]{1,0:T(8,128)(2,1)}, u32[]{:S(2)}, u32[]{:S(2)}) %collective-permute-start.57) | collective-permute-done | bytes 737312 | tf_op jit(solution)/shard_map/ppermute | solution.py:300
  677.5 20.9 %all-to-all-done.4 = f32[32,8,128]{2,1,0:T(8,128)S(1)} async-done(((f32[32,8,128]{2,1,0:T(8,128)}), f32[32,8,128]{2,1,0:T(8,128)S(1)}, u32[]{:S(2)}, u32[]{:S(2)}) %all-to-all-start.4) | async-done | bytes 131104 | tf_op jit(solution)/shard_map/all_to_all | solution.py:450
  (466 shorter events, 250.7 us)
Async XLA Ops:
  0.7 75.5 %all-to-all-start = ((bf16[4,2,196,768]{3,1,2,0:T(2,128)(2,1)}), bf16[4,2,196,768]{3,1,2,0:T(2,128)(2,1)}, u32[]{:S(2)}, u32[]{:S(2)}) async-start(bf16[4,2,196,768]{3,1,2,0:T(2,128)(2,1)} %param.8), calls=%async_computation | async-start | bytes 4816896 | tf_op jit(solution)/shard_map/all_to_all | solution.py:592
  10.7 33.1 %collective-permute-start.1 = (bf16[248,768]{1,0:T(8,128)(2,1)S(1)}, bf16[248,768]{1,0:T(8,128)(2,1)S(1)}, u32[]{:S(2)}, u32[]{:S(2)}) collective-permute-start(bf16[248,768]{1,0:T(8,128)(2,1)S(1)} %fusion.64.refs_0_), channel_id=1, source_target_pairs={{0,16},{1,17},{2,18},{3,19},{4,20},{5,21},{6,22},{7,23},{8,24},{9,... | collective-permute-start | bytes 1142792 | tf_op jit(solution)/shard_map/ppermute | solution.py:303
  10.7 33.1 %collective-permute-start = (bf16[248,768]{1,0:T(8,128)(2,1)S(1)}, bf16[248,768]{1,0:T(8,128)(2,1)S(1)}, u32[]{:S(2)}, u32[]{:S(2)}) collective-permute-start(bf16[248,768]{1,0:T(8,128)(2,1)S(1)} %fusion.64.refs_0_), channel_id=1, source_target_pairs={{0,8},{1,9},{2,10},{3,11},{4,12},{5,13},{6,14},{7,15},{8,16},{9,17... | collective-permute-start | bytes 1142792 | tf_op jit(solution)/shard_map/ppermute | solution.py:303
  46.9 25.1 %collective-permute-start.14 = (bf16[168,768]{1,0:T(8,128)(2,1)S(1)}, bf16[168,768]{1,0:T(8,128)(2,1)S(1)}, u32[]{:S(2)}, u32[]{:S(2)}) collective-permute-start(bf16[168,768]{1,0:T(8,128)(2,1)S(1)} %copy-done.17), channel_id=1, source_target_pairs={{0,16},{1,17},{2,18},{3,19},{4,20},{5,21},{6,22},{7,23},{8,24},{9,... | collective-permute-start | bytes 774152 | tf_op jit(solution)/shard_map/ppermute | solution.py:303
  51.7 26.6 %collective-permute-start.5 = (bf16[272,768]{1,0:T(8,128)(2,1)S(1)}, bf16[272,768]{1,0:T(8,128)(2,1)S(1)}, u32[]{:S(2)}, u32[]{:S(2)}) collective-permute-start(bf16[272,768]{1,0:T(8,128)(2,1)S(1)} %pad_maximum_fusion.2.refs_0_), channel_id=1, source_target_pairs={{0,6},{1,7},{2,4},{3,5},{4,2},{5,3},{6,0},{7,1},{8,14},{9,15},{10,... | collective-permute-start | bytes 1253384 | tf_op jit(solution)/shard_map/ppermute | solution.py:300
  106.4 30.5 %collective-permute-start.22 = (bf16[336,768]{1,0:T(8,128)(2,1)S(1)}, bf16[336,768]{1,0:T(8,128)(2,1)S(1)}, u32[]{:S(2)}, u32[]{:S(2)}) collective-permute-start(bf16[336,768]{1,0:T(8,128)(2,1)S(1)} %bitcast.209), channel_id=1, source_target_pairs={{0,6},{1,7},{2,4},{3,5},{4,2},{5,3},{6,0},{7,1},{8,14},{9,15},{10,... | collective-permute-start | bytes 1548296 | tf_op jit(solution)/shard_map/ppermute | solution.py:300
  109.0 28.0 %collective-permute-start.21 = (bf16[336,768]{1,0:T(8,128)(2,1)S(1)}, bf16[336,768]{1,0:T(8,128)(2,1)S(1)}, u32[]{:S(2)}, u32[]{:S(2)}) collective-permute-start(bf16[336,768]{1,0:T(8,128)(2,1)S(1)} %bitcast.210), channel_id=1, source_target_pairs={{0,4},{1,5},{2,6},{3,7},{4,0},{5,1},{6,2},{7,3},{8,12},{9,13},{10,... | collective-permute-start | bytes 1548296 | tf_op jit(solution)/shard_map/ppermute | solution.py:300
  109.5 27.5 %collective-permute-start.20 = (bf16[336,768]{1,0:T(8,128)(2,1)S(1)}, bf16[336,768]{1,0:T(8,128)(2,1)S(1)}, u32[]{:S(2)}, u32[]{:S(2)}) collective-permute-start(bf16[336,768]{1,0:T(8,128)(2,1)S(1)} %bitcast.211), channel_id=1, source_target_pairs={{0,2},{1,3},{2,0},{3,1},{4,6},{5,7},{6,4},{7,5},{8,10},{9,11},{10,... | collective-permute-start | bytes 1548296 | tf_op jit(solution)/shard_map/ppermute | solution.py:300
  138.4 31.2 %collective-permute-start.29 = (bf16[240,768]{1,0:T(8,128)(2,1)S(1)}, bf16[240,768]{1,0:T(8,128)(2,1)}, u32[]{:S(2)}, u32[]{:S(2)}) collective-permute-start(bf16[240,768]{1,0:T(8,128)(2,1)S(1)} %get-tuple-element.108.refs_0_), channel_id=1, source_target_pairs={{0,6},{1,7},{2,4},{3,5},{4,2},{5,3},{6,0},{7,1},{8,14},{9,15},{10,... | collective-permute-start | bytes 1105928 | tf_op jit(solution)/shard_map/ppermute | solution.py:300
  140.8 28.8 %collective-permute-start.28 = (bf16[240,768]{1,0:T(8,128)(2,1)S(1)}, bf16[240,768]{1,0:T(8,128)(2,1)}, u32[]{:S(2)}, u32[]{:S(2)}) collective-permute-start(bf16[240,768]{1,0:T(8,128)(2,1)S(1)} %get-tuple-element.108.refs_0_), channel_id=1, source_target_pairs={{0,4},{1,5},{2,6},{3,7},{4,0},{5,1},{6,2},{7,3},{8,12},{9,13},{10,... | collective-permute-start | bytes 1105928 | tf_op jit(solution)/shard_map/ppermute | solution.py:300
  141.3 28.3 %collective-permute-start.27 = (bf16[240,768]{1,0:T(8,128)(2,1)S(1)}, bf16[240,768]{1,0:T(8,128)(2,1)}, u32[]{:S(2)}, u32[]{:S(2)}) collective-permute-start(bf16[240,768]{1,0:T(8,128)(2,1)S(1)} %get-tuple-element.108.refs_0_), channel_id=1, source_target_pairs={{0,2},{1,3},{2,0},{3,1},{4,6},{5,7},{6,4},{7,5},{8,10},{9,11},{10,... | collective-permute-start | bytes 1105928 | tf_op jit(solution)/shard_map/ppermute | solution.py:300
  172.0 26.3 %collective-permute-start.36 = (bf16[240,768]{1,0:T(8,128)(2,1)S(1)}, bf16[240,768]{1,0:T(8,128)(2,1)}, u32[]{:S(2)}, u32[]{:S(2)}) collective-permute-start(bf16[240,768]{1,0:T(8,128)(2,1)S(1)} %copy-done.15), channel_id=1, source_target_pairs={{0,6},{1,7},{2,4},{3,5},{4,2},{5,3},{6,0},{7,1},{8,14},{9,15},{10,... | collective-permute-start | bytes 1105928 | tf_op jit(solution)/shard_map/ppermute | solution.py:300
  199.4 32.3 %collective-permute-start.43 = (bf16[336,768]{1,0:T(8,128)(2,1)}, bf16[336,768]{1,0:T(8,128)(2,1)}, u32[]{:S(2)}, u32[]{:S(2)}) collective-permute-start(bf16[336,768]{1,0:T(8,128)(2,1)} %bitcast.21.refs_8_), channel_id=1, source_target_pairs={{0,6},{1,7},{2,4},{3,5},{4,2},{5,3},{6,0},{7,1},{8,14},{9,15},{10,... | collective-permute-start | bytes 1548296 | tf_op jit(solution)/shard_map/ppermute | solution.py:300
  234.2 33.6 %all-to-all-start.1 = ((bf16[4,2,196,768]{3,1,2,0:T(2,128)(2,1)}), bf16[4,2,196,768]{3,1,2,0:T(2,128)(2,1)}, u32[]{:S(2)}, u32[]{:S(2)}) async-start(bf16[4,2,196,768]{3,1,2,0:T(2,128)(2,1)} %param.9), calls=%async_computation.1 | async-start | bytes 4816896 | tf_op jit(solution)/shard_map/all_to_all | solution.py:592
  267.8 92.2 %all-to-all-start.2 = ((bf16[1,8,196,768]{3,2,0,1:T(8,128)(2,1)}), bf16[1,8,196,768]{3,2,0,1:T(8,128)(2,1)}, u32[]{:S(2)}, u32[]{:S(2)}) async-start(bf16[1,8,196,768]{3,2,0,1:T(8,128)(2,1)} %slice.232), calls=%async_computation.2 | async-start | bytes 4915200 | tf_op jit(solution)/shard_map/all_to_all | solution.py:597
  330.6 29.4 %collective-permute-start.48 = (bf16[4,576,768]{2,1,0:T(8,128)(2,1)}, bf16[4,576,768]{2,1,0:T(8,128)(2,1)}, u32[]{:S(2)}, u32[]{:S(2)}) collective-permute-start(bf16[4,576,768]{2,1,0:T(8,128)(2,1)} %get-tuple-element.127), channel_id=1, source_target_pairs={{0,1},{1,0},{2,3},{3,2},{4,5},{5,4},{6,7},{7,6},{8,9},{9,8},{10,11... | collective-permute-start | bytes 10616840 | tf_op jit(solution)/shard_map/ppermute | solution.py:300
  413.9 39.8 %collective-permute-start.50 = (bf16[576,768]{1,0:T(8,128)(2,1)S(1)}, bf16[576,768]{1,0:T(8,128)(2,1)S(1)}, u32[]{:S(2)}, u32[]{:S(2)}) collective-permute-start(bf16[576,768]{1,0:T(8,128)(2,1)S(1)} %get-tuple-element.202), channel_id=1, source_target_pairs={{0,4},{1,5},{2,6},{3,7},{4,0},{5,1},{6,2},{7,3},{8,12},{9,13},{10,... | collective-permute-start | bytes 2654216 | tf_op jit(solution)/shard_map/ppermute | solution.py:300
  414.7 38.9 %collective-permute-start.49 = (bf16[576,768]{1,0:T(8,128)(2,1)S(1)}, bf16[576,768]{1,0:T(8,128)(2,1)S(1)}, u32[]{:S(2)}, u32[]{:S(2)}) collective-permute-start(bf16[576,768]{1,0:T(8,128)(2,1)S(1)} %get-tuple-element.203), channel_id=1, source_target_pairs={{0,2},{1,3},{2,0},{3,1},{4,6},{5,7},{6,4},{7,5},{8,10},{9,11},{10,... | collective-permute-start | bytes 2654216 | tf_op jit(solution)/shard_map/ppermute | solution.py:300
  474.0 30.4 %collective-permute-start.52 = (bf16[4,576,768]{2,1,0:T(8,128)(2,1)}, bf16[4,576,768]{2,1,0:T(8,128)(2,1)}, u32[]{:S(2)}, u32[]{:S(2)}) collective-permute-start(bf16[4,576,768]{2,1,0:T(8,128)(2,1)} %get-tuple-element.138), channel_id=1, source_target_pairs={{0,1},{1,0},{2,3},{3,2},{4,5},{5,4},{6,7},{7,6},{8,9},{9,8},{10,11... | collective-permute-start | bytes 10616840 | tf_op jit(solution)/shard_map/ppermute | solution.py:300
  535.8 39.8 %collective-permute-start.54 = (bf16[576,768]{1,0:T(8,128)(2,1)S(1)}, bf16[576,768]{1,0:T(8,128)(2,1)S(1)}, u32[]{:S(2)}, u32[]{:S(2)}) collective-permute-start(bf16[576,768]{1,0:T(8,128)(2,1)S(1)} %get-tuple-element.198), channel_id=1, source_target_pairs={{0,4},{1,5},{2,6},{3,7},{4,0},{5,1},{6,2},{7,3},{8,12},{9,13},{10,... | collective-permute-start | bytes 2654216 | tf_op jit(solution)/shard_map/ppermute | solution.py:300
  536.6 39.6 %collective-permute-start.53 = (bf16[576,768]{1,0:T(8,128)(2,1)S(1)}, bf16[576,768]{1,0:T(8,128)(2,1)S(1)}, u32[]{:S(2)}, u32[]{:S(2)}) collective-permute-start(bf16[576,768]{1,0:T(8,128)(2,1)S(1)} %get-tuple-element.199), channel_id=1, source_target_pairs={{0,2},{1,3},{2,0},{3,1},{4,6},{5,7},{6,4},{7,5},{8,10},{9,11},{10,... | collective-permute-start | bytes 2654216 | tf_op jit(solution)/shard_map/ppermute | solution.py:300
  552.0 47.0 %collective-permute-start.56 = (bf16[4,480,768]{2,1,0:T(8,128)(2,1)}, bf16[4,480,768]{2,1,0:T(8,128)(2,1)}, u32[]{:S(2)}, u32[]{:S(2)}) collective-permute-start(bf16[4,480,768]{2,1,0:T(8,128)(2,1)} %get-tuple-element.144), channel_id=1, source_target_pairs={{0,1},{1,0},{2,3},{3,2},{4,5},{5,4},{6,7},{7,6},{8,9},{9,8},{10,11... | collective-permute-start | bytes 8847368 | tf_op jit(solution)/shard_map/ppermute | solution.py:300
  592.1 73.4 %all-to-all-start.3 = ((bf16[1,8,196,768]{3,2,0,1:T(8,128)(2,1)}), bf16[1,8,196,768]{3,2,0,1:T(8,128)(2,1)}, u32[]{:S(2)}, u32[]{:S(2)}) async-start(bf16[1,8,196,768]{3,2,0,1:T(8,128)(2,1)} %slice.234), calls=%async_computation.3 | async-start | bytes 4915200 | tf_op jit(solution)/shard_map/all_to_all | solution.py:597
  606.0 33.5 %collective-permute-start.58 = (bf16[480,768]{1,0:T(8,128)(2,1)}, bf16[480,768]{1,0:T(8,128)(2,1)}, u32[]{:S(2)}, u32[]{:S(2)}) collective-permute-start(bf16[480,768]{1,0:T(8,128)(2,1)} %get-tuple-element.207), channel_id=1, source_target_pairs={{0,4},{1,5},{2,6},{3,7},{4,0},{5,1},{6,2},{7,3},{8,12},{9,13},{10,... | collective-permute-start | bytes 2211848 | tf_op jit(solution)/shard_map/ppermute | solution.py:300
  606.9 50.9 %collective-permute-start.57 = (bf16[480,768]{1,0:T(8,128)(2,1)}, bf16[480,768]{1,0:T(8,128)(2,1)}, u32[]{:S(2)}, u32[]{:S(2)}) collective-permute-start(bf16[480,768]{1,0:T(8,128)(2,1)} %get-tuple-element.208), channel_id=1, source_target_pairs={{0,2},{1,3},{2,0},{3,1},{4,6},{5,7},{6,4},{7,5},{8,10},{9,11},{10,... | collective-permute-start | bytes 2211848 | tf_op jit(solution)/shard_map/ppermute | solution.py:300
  608.0 56.7 %collective-permute-start.63 = (bf16[168,768]{1,0:T(8,128)(2,1)}, bf16[168,768]{1,0:T(8,128)(2,1)}, u32[]{:S(2)}, u32[]{:S(2)}) collective-permute-start(bf16[168,768]{1,0:T(8,128)(2,1)} %get-tuple-element.216), channel_id=1, source_target_pairs={{0,8},{1,9},{2,10},{3,11},{4,12},{5,13},{6,14},{7,15},{8,16},{9,17... | collective-permute-start | bytes 774152 | tf_op jit(solution)/shard_map/ppermute | solution.py:303
  608.0 61.6 %collective-permute-start.65 = (bf16[168,768]{1,0:T(8,128)(2,1)}, bf16[168,768]{1,0:T(8,128)(2,1)}, u32[]{:S(2)}, u32[]{:S(2)}) collective-permute-start(bf16[168,768]{1,0:T(8,128)(2,1)} %get-tuple-element.217), channel_id=1, source_target_pairs={{0,24},{1,25},{2,26},{3,27},{4,28},{5,29},{6,30},{7,31},{8,0},{9,1... | collective-permute-start | bytes 774152 | tf_op jit(solution)/shard_map/ppermute | solution.py:303
  624.0 45.6 %collective-permute-start.64 = (bf16[168,768]{1,0:T(8,128)(2,1)}, bf16[168,768]{1,0:T(8,128)(2,1)}, u32[]{:S(2)}, u32[]{:S(2)}) collective-permute-start(bf16[168,768]{1,0:T(8,128)(2,1)} %get-tuple-element.218), channel_id=1, source_target_pairs={{0,16},{1,17},{2,18},{3,19},{4,20},{5,21},{6,22},{7,23},{8,24},{9,... | collective-permute-start | bytes 774152 | tf_op jit(solution)/shard_map/ppermute | solution.py:303
  660.9 39.6 %collective-permute-start.60 = (bf16[240,768]{1,0:T(8,128)(2,1)}, bf16[240,768]{1,0:T(8,128)(2,1)S(1)}, u32[]{:S(2)}, u32[]{:S(2)}) collective-permute-start(bf16[240,768]{1,0:T(8,128)(2,1)} %get-tuple-element.209), channel_id=1, source_target_pairs={{0,8},{1,9},{2,10},{3,11},{4,12},{5,13},{6,14},{7,15},{8,16},{9,17... | collective-permute-start | bytes 1105928 | tf_op jit(solution)/shard_map/ppermute | solution.py:303
  660.9 39.6 %collective-permute-start.62 = (bf16[240,768]{1,0:T(8,128)(2,1)}, bf16[240,768]{1,0:T(8,128)(2,1)}, u32[]{:S(2)}, u32[]{:S(2)}) collective-permute-start(bf16[240,768]{1,0:T(8,128)(2,1)} %get-tuple-element.210), channel_id=1, source_target_pairs={{0,24},{1,25},{2,26},{3,27},{4,28},{5,29},{6,30},{7,31},{8,0},{9,1... | collective-permute-start | bytes 1105928 | tf_op jit(solution)/shard_map/ppermute | solution.py:303
  664.7 35.7 %collective-permute-start.61 = (bf16[240,768]{1,0:T(8,128)(2,1)S(1)}, bf16[240,768]{1,0:T(8,128)(2,1)}, u32[]{:S(2)}, u32[]{:S(2)}) collective-permute-start(bf16[240,768]{1,0:T(8,128)(2,1)S(1)} %get-tuple-element.211), channel_id=1, source_target_pairs={{0,16},{1,17},{2,18},{3,19},{4,20},{5,21},{6,22},{7,23},{8,24},{9,... | collective-permute-start | bytes 1105928 | tf_op jit(solution)/shard_map/ppermute | solution.py:303
  665.4 33.0 %all-to-all-start.4 = ((f32[32,8,128]{2,1,0:T(8,128)}), f32[32,8,128]{2,1,0:T(8,128)S(1)}, u32[]{:S(2)}, u32[]{:S(2)}) async-start(f32[32,8,128]{2,1,0:T(8,128)} %bitcast.81), calls=%async_computation.4 | async-start | bytes 262144 | tf_op jit(solution)/shard_map/all_to_all | solution.py:450
  (144 other events, 1955.8 us)

commit v4 on v3

--- a/solution.py
+++ b/solution.py
@@ -144,6 +144,10 @@
     )(*arrays)
 
 
+def eights(rows):
+    return rows.reshape(rows.shape[:-2] + (-1, 8, rows.shape[-1]))
+
+
 def place_kernel(outs_plan, blocks, groups, dest_ref, *refs):
     pieces, refs = (refs[: groups * blocks], refs[groups * blocks :])
     outs, refs = (refs[: len(outs_plan)], refs[len(outs_plan) :])
@@ -153,7 +157,7 @@
         for entry, (group, row, rows) in enumerate(entries):
             for block in range(blocks):
                 buffer = held[target].at[entry, block]
-                source = pieces[group * blocks + block].at[pl.ds(row, rows)]
+                source = pieces[group * blocks + block].at[pl.ds(row // 8, rows // 8)]
                 fetch = pltpu.make_async_copy(source, buffer, in_sem.at[slot])
                 fetch.start()
                 write = pltpu.make_async_copy(buffer, outs[target].at[entry, dest_ref[block]], out_sem.at[slot])
@@ -169,12 +173,12 @@
 def place(groups, outs_plan, dest):
     blocks = len(groups[0])
     width = groups[0][0].shape[1]
-    shapes = [(len(entries), blocks, entries[0][2], width) for entries in outs_plan]
+    shapes = [(len(entries), blocks, entries[0][2] // 8, 8, width) for entries in outs_plan]
     slots = sum(len(entries) for entries in outs_plan) * blocks
-    size = sum(2 * s[0] * s[1] * s[2] * s[3] for s in shapes)
-    flat = [piece for group in groups for piece in group]
+    size = sum(16 * s[0] * s[1] * s[2] * s[4] for s in shapes)
+    flat = [eights(piece) for group in groups for piece in group]
     anywhere = pl.BlockSpec(memory_space=pl.ANY)
-    return pl.pallas_call(
+    outs = pl.pallas_call(
         partial(place_kernel, tuple(tuple(e) for e in outs_plan), blocks, len(groups)),
         in_specs=[pl.BlockSpec(memory_space=pltpu.SMEM)] + [anywhere] * len(flat),
         out_specs=[anywhere] * len(shapes),
@@ -184,6 +188,7 @@
         compiler_params=pltpu.CompilerParams(vmem_limit_bytes=size + (2 << 20)),
         cost_estimate=pl.CostEstimate(flops=0, bytes_accessed=4 * size, transcendentals=0),
     )(dest, *flat)
+    return [out.reshape(out.shape[:2] + (-1, width)) for out in outs]
 
 
 def split_kernel(spans, plane_rows, squares, core_ref, *refs):
@@ -199,8 +204,8 @@
                 first, length = spans[part]
                 size = min(length - done, rows - offset)
                 copy = pltpu.make_async_copy(
-                    parts[part].at[pl.ds(first + done, size)],
-                    held[plane].at[slot, pl.ds(offset, size)],
+                    parts[part].at[pl.ds((first + done) // 8, size // 8)],
+                    held[plane].at[slot, pl.ds(offset // 8, size // 8)],
                     in_sem.at[count],
                 )
                 copy.start()
@@ -215,7 +220,7 @@
                 copy.wait()
             for target, side in ((send, 1 - core), (keep, core)):
                 copy = pltpu.make_async_copy(
-                    held[plane].at[2 * square + side], target.at[square, pl.ds(row, rows)], out_sem.at[len(outgoing)]
+                    held[plane].at[2 * square + side], target.at[square, pl.ds(row // 8, rows // 8)], out_sem.at[len(outgoing)]
                 )
                 copy.start()
                 outgoing.append(copy)
@@ -226,22 +231,23 @@
 
 def split_cores(parts, plane_rows, squares, core):
     spans = tuple((first, length) for _, first, length in parts)
-    arrays = [array for array, _, _ in parts]
-    width = arrays[0].shape[1]
+    arrays = [eights(array) for array, _, _ in parts]
+    width = arrays[0].shape[-1]
     slots = len(plane_rows) * squares * 2
     size = 2 * squares * sum(plane_rows) * width * 2
     anywhere = pl.BlockSpec(memory_space=pl.ANY)
-    half = jax.ShapeDtypeStruct((squares, sum(plane_rows), width), BF16)
-    return pl.pallas_call(
+    half = jax.ShapeDtypeStruct((squares, sum(plane_rows) // 8, 8, width), BF16)
+    outs = pl.pallas_call(
         partial(split_kernel, spans, tuple(plane_rows), squares),
         in_specs=[pl.BlockSpec(memory_space=pltpu.SMEM)] + [anywhere] * len(arrays),
         out_specs=[anywhere, anywhere],
         out_shape=[half, half],
-        scratch_shapes=[pltpu.VMEM((2 * squares, rows, width), BF16) for rows in plane_rows]
+        scratch_shapes=[pltpu.VMEM((2 * squares, rows // 8, 8, width), BF16) for rows in plane_rows]
         + [pltpu.SemaphoreType.DMA((slots + len(parts),)), pltpu.SemaphoreType.DMA((slots,))],
         compiler_params=pltpu.CompilerParams(vmem_limit_bytes=size + (2 << 20)),
         cost_estimate=pl.CostEstimate(flops=0, bytes_accessed=4 * size, transcendentals=0),
     )(core, *arrays)
+    return [out.reshape(squares, -1, width) for out in outs]
 
 
 def tie(values, others):
@@ -292,9 +298,8 @@
         self.grads = {}
         flat = packed.reshape(1, -1)
         tail = jnp.pad(flat, ((0, 7), (0, width - flat.shape[1])))
-        self.column_in, self.column_small = self.columns(
-            jnp.concatenate([weights_in, tail], axis=0), (self.rows_in, 8)
-        )
+        pieces = self.shifted(jnp.concatenate([weights_in, tail], axis=0))
+        self.column_in, self.column_small = self.columns(pieces, (self.rows_in, 8))
 
     def flip(self, x, bits):
         return lax.ppermute(x, self.axes, [(d, d ^ bits) for d in range(32)])
@@ -302,8 +307,10 @@
     def shift(self, x, step):
         return lax.ppermute(x, self.axes, [(d, (d + 8 * step) % 32) for d in range(32)])
 
-    def columns(self, shard, sizes):
-        pieces = [shard] + [self.shift(shard, step) for step in (1, 2, 3)]
+    def shifted(self, shard):
+        return [shard] + [self.shift(shard, step) for step in (1, 2, 3)]
+
+    def columns(self, pieces, sizes):
         plan, row = ([], 0)
         for size in sizes:
             plan.append([(0, row, size)])
@@ -323,16 +330,15 @@
         out = place(groups, [entries], self.spots)[0]
         return out.reshape(-1, self.width)
 
-    def begin(self, clip):
+    def begin(self):
         rows_in, rows_out, width = (self.rows_in, self.rows_out, self.width)
         smalls = self.column_small.reshape(-1, width)
         first = jnp.concatenate([self.column_in[0], smalls], axis=0)
         self.p1, self.p2, self.p3 = (self.column_in[k] for k in (1, 2, 3))
-        weights_out, first = tie(self.weights_out, first)
         p0 = self.over(first)
-        p0, (clip, self.p1) = tie(p0, (clip, self.p1))
-        column = self.columns(weights_out, (rows_out,))[0]
-        self.q01, self.q23 = (column[:2].reshape(-1, width), column[2:].reshape(-1, width))
+        p0[0], weights_out = tie(first, self.weights_out)
+        self.q = self.shifted(weights_out)
+        p0, self.p1 = tie(p0, self.p1)
         self.p1 = self.over(self.p1)
         self.p0 = self.cores(p0)
         low, small = place([self.p0], [[(0, 0, rows_in)], [(0, rows_in, 32)]], self.spots)
@@ -340,7 +346,6 @@
         share = width // 32
         small = small.reshape(8, 4, 8, width)[:, :, 0, : self.count * share].reshape(8, 4, self.count, share)
         self.small = small.transpose(2, 1, 0, 3).reshape(self.count, width)
-        return clip
 
     def tick(self, name, *values):
         single = len(values) == 1
@@ -348,7 +353,9 @@
         g = self.grads
         whole = lambda key: (g[key], 0, g[key].shape[0])
         if name == "query_t":
-            values, (self.p1, self.q01) = tie(values, (self.p1, self.q01))
+            values, (self.p1, self.q) = tie(values, (self.p1, self.q))
+            column = self.columns(self.q, (rows_out,))[0]
+            self.q01, self.q23 = (column[:2].reshape(-1, width), column[2:].reshape(-1, width))
             self.q01 = self.over(self.q01)
             self.p1 = self.cores(self.p1)
             low = self.lay([self.p0, self.p1], [(0, 0, rows_in), (1, 0, rows_in)])
@@ -376,47 +383,75 @@
             self.q23 = self.cores(self.q23)
             entries = [(0, rows_out, rows_out), (1, 0, rows_out), (1, rows_out, rows_out)]
             self.out_m = self.lay([self.q01, self.q23], entries)[3 * width - 8 * rows_out :]
-        elif name == "grad_hidden":
-            first, split = (16 * rows_out - 3 * width, 24 * rows_in - 6 * width)
-            self.out_first = first
-            d_out_m, d_in_m = (g["out_m"], g["in_m"])
-            self.part_a = self.halve(
-                [(d_out_m, first, d_out_m.shape[0] - first), (d_in_m, split, d_in_m.shape[0] - split)],
-                (rows_out, rows_out, rows_in),
+        elif name == "out_m":
+            start = 16 * rows_out - 3 * width
+            d_out_m = g["out_m"]
+            self.kept, send = self.halve([(d_out_m, start, d_out_m.shape[0] - start)], (rows_out, rows_out))
+            values, send = tie(values, send)
+            self.other = self.flip(send, 1)
+        elif name == "grad_pre":
+            values, (self.kept, self.other) = tie(values, (self.kept, self.other))
+            self.d_q23 = self.across(self.kept, self.other)
+        elif name == "in_m":
+            start = 24 * rows_in - 6 * width
+            d_in_m = g["in_m"]
+            self.kept, send = self.halve([(d_in_m, start, d_in_m.shape[0] - start)], (rows_in,))
+            values, send = tie(values, send)
+            self.other = self.flip(send, 1)
+        elif name == "grad_mixed_s":
+            values, (self.d_q23, self.kept, self.other) = tie(values, (self.d_q23, self.kept, self.other))
+            self.d_q23 = self.gathered(self.d_q23)
+            self.d_p3 = self.across(self.kept, self.other)
+        elif name == "grad_s":
+            values, self.d_p3 = tie(values, self.d_p3)
+            self.d_p3 = self.gathered(self.d_p3)
+        elif name == "in_v":
+            start = 24 * rows_in - 6 * width
+            self.kept, send = self.halve([whole("in_v"), (g["in_m"], 0, start)], (rows_in,))
+            values, send = tie(values, send)
+            self.other = self.flip(send, 1)
+        elif name == "in_qk":
+            values, (self.kept, self.other) = tie(values, (self.kept, self.other))
+            self.d_p2 = self.across(self.kept, self.other)
+        elif name == "grad_t":
+            values, self.d_p2 = tie(values, self.d_p2)
+            self.d_p2 = self.gathered(self.d_p2)
+        elif name == "out_t":
+            start = 16 * rows_out - 3 * width
+            self.kept, send = self.halve(
+                [whole("out_t"), whole("out_f"), whole("out_s"), (g["out_m"], 0, start)], (rows_out, rows_out)
             )
-        elif name == "grad_mixed_s":
-            values, self.part_a = tie(values, self.part_a)
-            self.part_a = self.across(*self.part_a)
-        elif name == "grad_t":
-            values, self.part_a = tie(values, self.part_a)
-            self.part_a = self.gathered(self.part_a)
-        elif name == "grad_projected":
-            first, split = (self.out_first, 24 * rows_in - 6 * width)
-            self.part_b = self.halve(
-                [
-                    whole("in_v"),
-                    (g["in_m"], 0, split),
-                    whole("out_t"),
-                    whole("out_f"),
-                    whole("out_s"),
-                    (g["out_m"], 0, first),
-                ],
-                (rows_in, rows_out, rows_out),
-            )
-            kept, values = tie(self.part_b[0], values)
-            self.part_b = (kept,) + self.part_b[1:]
+            values, send = tie(values, send)
+            self.other = self.flip(send, 1)
         elif name == "grad_mixed_t":
-            values, self.part_b = tie(values, self.part_b)
-            self.part_b = self.across(*self.part_b)
-        elif name == "grad_in_t":
-            values, self.part_b = tie(values, self.part_b)
-            self.part_b = self.gathered(self.part_b)
-            self.part_c = self.halve([whole("in_t"), whole("in_qk")], (rows_in, rows_in))
+            values, (self.kept, self.other) = tie(values, (self.kept, self.other))
+            self.d_q01 = self.across(self.kept, self.other)
+        elif name == "grad_project_t":
+            values, self.d_q01 = tie(values, self.d_q01)
+            self.d_q01 = self.gathered(self.d_q01)
+            planes = [a[k * rows_out : (k + 1) * rows_out] for a in (self.d_q01, self.d_q23) for k in range(2)]
+            self.out_pieces = self.along(planes)
+        elif name == "in_t":
+            kept, send = self.halve([whole("in_t"), whole("in_qk")], (rows_in, rows_in))
+            half = lambda a, x: lax.dynamic_slice_in_dim(a, 2 * x, 2, 0).astype(F32)
+            other = self.flip(send, 1)
+            x = self.square // 2
+            send = (half(kept, 1 - x) + half(other, 1 - x)).astype(BF16)
+            own = (half(kept, x) + half(other, x)).astype(BF16)
+            values, (own, send) = tie(values, (own, send))
+            self.last = (own, self.flip(send, 4))
+        elif name == "grad_clip":
+            values, (own, other) = tie(values, self.last)
+            y = self.square % 2
+            line = lambda a, y: lax.dynamic_index_in_dim(a, y, 0, keepdims=False).astype(F32)
+            send = (line(own, 1 - y) + line(other, 1 - y)).astype(BF16)
+            arrived = self.flip(send, 2)
+            values, (arrived, self.out_pieces) = tie(values, (arrived, self.out_pieces))
+            self.d_p01 = (line(own, y) + line(other, y) + arrived.astype(F32)).astype(BF16)
         return values[0] if single else values
 
     def halve(self, parts, plane_rows):
-        keep, send = split_cores(parts, plane_rows, 4, self.core_ref)
-        return (keep, self.flip(send, 1))
+        return split_cores(parts, plane_rows, 4, self.core_ref)
 
     def across(self, keep, other):
         result = []
@@ -428,17 +463,20 @@
         return result
 
     def gathered(self, arrived):
-        total = arrived[0].astype(F32)
-        for block in arrived[1:]:
-            total = total + block.astype(F32)
-        return total.astype(BF16)
+        return self.added(arrived).astype(BF16)
 
     def along(self, planes):
         every = jnp.stack(planes, axis=0)
-        total = lax.dynamic_index_in_dim(every, self.plane, 0, keepdims=False).astype(F32)
+        pieces = [lax.dynamic_index_in_dim(every, self.plane, 0, keepdims=False)]
         for step in (1, 2, 3):
             block = lax.dynamic_index_in_dim(every, (self.plane + step) % 4, 0, keepdims=False)
-            total = total + self.shift(block, step).astype(F32)
+            pieces.append(self.shift(block, step))
+        return pieces
+
+    def added(self, pieces):
+        total = pieces[0].astype(F32)
+        for piece in pieces[1:]:
+            total = total + piece.astype(F32)
         return total
 
     def sum_small(self, small):
@@ -451,16 +489,9 @@
         return jnp.sum(slots, axis=0).reshape(-1)[: count * share].reshape(count, share)
 
     def total(self, small):
-        rows_in, rows_out = (self.rows_in, self.rows_out)
-        a, b = (self.part_a, self.part_b)
-        out_planes = [b[rows_in : rows_in + rows_out], b[rows_in + rows_out :], a[:rows_out], a[rows_out : 2 * rows_out]]
-        arrived = self.across(*self.part_c)
-        small, arrived[0] = tie(small, arrived[0])
-        summed_out = self.along(out_planes)
-        owned = self.sum_small(small)
-        c = self.gathered(arrived)
-        summed_in = self.along([c[:rows_in], c[rows_in:], b[:rows_in], a[2 * rows_out :]])
-        return (summed_in, summed_out, owned)
+        last, rows_in = (self.d_p01, self.rows_in)
+        pieces = self.along([last[:rows_in], last[rows_in:], self.d_p2, self.d_p3])
+        return (self.added(pieces), self.added(self.out_pieces), self.sum_small(small))
 
 
 def norm_parts(values):
@@ -531,10 +562,12 @@
 
     grad_out = grad_low.astype(F32)
     grads["out_m"] = tn(hidden, grad_low).astype(BF16)
+    grad_low = feed.tick("out_m", grad_low)
     s_dense = column_sum(grad_low)
     grad_pre = (nt(grad_low, feed.out_m) * slope.astype(F32)).astype(BF16)
+    grad_pre = feed.tick("grad_pre", grad_pre)
     grads["in_m"] = tn(grad_pre, normed_m).astype(BF16)
-    grad_pre = feed.tick("grad_hidden", grad_pre)
+    grad_pre = feed.tick("in_m", grad_pre)
     s_hidden = column_sum(grad_pre).reshape(-1, width)
     part, g_m, b_m = norm_backward(after_s, gains32[2], nn(grad_pre, feed.in_m))
     grad_s = grad_out + part
@@ -546,9 +579,11 @@
     grad_qk, grad_v = attention_call(
         backward_kernel, 2, project_s + [cube(grad_mixed_s)], (2 * width, width), False, patches
     )
-    grad_qk, grad_v = (flat(grad_qk), flat(grad_v))
-    grads["in_qk"] = tn(grad_qk, normed_s).astype(BF16)
+    grad_qk, grad_v = feed.tick("grad_s", flat(grad_qk), flat(grad_v))
     grads["in_v"] = tn(grad_v, normed_s).astype(BF16)
+    grad_qk, grad_v = feed.tick("in_v", grad_qk, grad_v)
+    d_in_qk = tn(grad_qk, normed_s).astype(BF16)
+    grads["in_qk"], grad_qk, grad_v = feed.tick("in_qk", d_in_qk, grad_qk, grad_v)
     part, g_s, b_s = norm_backward(after_t, gains32[1], nn(grad_qk, feed.in_qk) + nn(grad_v, feed.in_v))
     grad_t = grad_s + part
     grad_branch_t = feed.tick("grad_t", grad_t.astype(BF16))
@@ -556,17 +591,18 @@
     s_fc = column_sum(grad_branch_t)
     grad_projected = nt(grad_branch_t, feed.out_f).astype(BF16)
     grads["out_t"] = tn(mixed_t, grad_projected).astype(BF16)
-    grad_projected = feed.tick("grad_projected", grad_projected)
+    grad_projected = feed.tick("out_t", grad_projected)
     s_time = column_sum(grad_projected)
     grad_mixed_t = feed.tick("grad_mixed_t", nt(grad_projected, feed.out_t).astype(BF16))
     grad_project_t = attention_call(
         backward_kernel, 2, project_t + [cube(grad_mixed_t)], (3 * width,), True, patches
     )[0]
-    grad_project_t = flat(grad_project_t)
+    grad_project_t = feed.tick("grad_project_t", flat(grad_project_t))
     grads["in_t"] = tn(grad_project_t, normed_t).astype(BF16)
-    grad_project_t = feed.tick("grad_in_t", grad_project_t)
+    grad_project_t = feed.tick("in_t", grad_project_t)
     part, g_t, b_t = norm_backward(start, gains32[0], nn(grad_project_t, feed.in_t))
     grad_clip = (grad_t + part.astype(BF16).astype(F32)).astype(BF16)
+    grad_clip, g_t, b_t, s_time = feed.tick("grad_clip", grad_clip, g_t, b_t, s_time)
     small = jnp.concatenate(
         [
             jnp.stack([g_t, g_s, g_m, b_t, b_s, b_m, s_time, s_fc, s_space], axis=0),
@@ -600,7 +636,7 @@
     feed = (Staged if staged else Whole)(both, weights_in, weights_out, packed, width)
     clip = enter(clips_in)
     if staged:
-        clip = feed.begin(clip)
+        feed.begin()
     live = lax.dynamic_slice(clip_live, (lax.axis_index("seq") * own,), (own,)).astype(BF16)
 
     def target(after):

time: 714 us -> 684 us (0.958)
  waiting for transfers between devices: 175 us -> 122 us
  matrix products: 197 us -> 183 us
  other arithmetic: 44.4 us -> 56.3 us
  local copies, waits for them, and re-layouts: 48.5 us -> 60 us
  starting transfers between devices: 81.3 us -> 90.7 us
    ppermute x54 -> x61, waiting for transfers between devices: 103 us -> 76.7 us  [flip(): return lax.ppermute(x, self.axes, [(d, d ^ bits) for d in range(32)])]
    all_to_all x1, waiting for transfers between devices: 20.9 us -> 4.81 us  [sum_small(): slots = lax.all_to_all(slots, self.axes, split_axis=0, concat_axis=0)]
    unnamed x214 -> x232, local copies, waits for them, and re-layouts: 22.4 us -> 36.7 us
    ppermute x12, waiting for transfers between devices: 48.1 us -> 40.9 us  [shift(): lax.ppermute(x, self.axes, [(d, (d + 8 * step) % 32) for d in range(32)])]
    ppermute x54 -> x61, starting transfers between devices: 39.8 us -> 45.2 us  [flip(): return lax.ppermute(x, self.axes, [(d, d ^ bits) for d in range(32)])]
    pallas_call x3 -> x5, Pallas kernels: 26.6 us -> 29.9 us  [split_cores(): pl.pallas_call(partial(split_kernel, spans, tuple(plane_rows), squares),...]
  transfers between devices with their start and end apart: 71 -> 78, of which waited for: 14 -> 18; matrix products, arithmetic and copies ran while one was open for 34% -> 33% of each run, Pallas kernels for 13% -> 19%
where the time goes in v4:
time: 684 us; the launch traced here: 674 us
  matrix products  183 us (27%)
  Pallas kernels  157 us (23%)
  waiting for transfers between devices  122 us (18%)
  starting transfers between devices  90.7 us (13%)
  local copies, waits for them, and re-layouts  60 us (9%)
  other arithmetic  56.3 us (8%)
    pallas_call x4, Pallas kernels, attention_call(): pl.pallas_call(partial(kernel, group, patches, count), grid=(clips, steps...  84.6 us
    ppermute x61, waiting for transfers between devices, flip(): return lax.ppermute(x, self.axes, [(d, d ^ bits) for d in range(32)])  76.7 us
    dot_general x8, matrix products, nn(): lax.dot_general(left, right, (((1,), (0,)), ((), ())), preferred_element_...  65 us
    dot_general x9, matrix products, nt(): lax.dot_general(left, right, (((1,), (1,)), ((), ())), preferred_element_...  64.9 us
    dot_general x8, matrix products, tn(): lax.dot_general(left, right, (((0,), (0,)), ((), ())), preferred_element_...  53.4 us
    ppermute x61, starting transfers between devices, flip(): return lax.ppermute(x, self.axes, [(d, d ^ bits) for d in range(32)])  45.2 us
    pallas_call x8, Pallas kernels, place(): pl.pallas_call(partial(place_kernel, tuple((tuple(e) for e in outs_plan))...  42.6 us
    ppermute x12, waiting for transfers between devices, shift(): lax.ppermute(x, self.axes, [(d, (d + 8 * step) % 32) for d in range(32)])  40.9 us
  transfers between devices with their start and end apart: 78, of which 18 were waited for; matrix products, arithmetic and copies ran while one was open for 33% of the time, Pallas kernels for 19%

profile of v4, /device:TPU:0, one launch (start us, length us, event | category | flops | bytes accessed | tf_op | source)
XLA Modules:
  0.0 673.7 jit_solution(9609544302073342472)
XLA Ops:
  15.0 17.7 %collective-permute-done.1 = bf16[248,768]{1,0:T(8,128)(2,1)S(1)} collective-permute-done((bf16[248,768]{1,0:T(8,128)(2,1)S(1)}, bf16[248,768]{1,0:T(8,128)(2,1)S(1)}, u32[]{:S(2)}, u32[]{:S(2)}) %collective-permute-start.1) | collective-permute-done | bytes 380960 | tf_op jit(solution)/shard_map/ppermute | solution.py:308
  40.1 9.9 %collective-permute-done.5 = bf16[272,768]{1,0:T(8,128)(2,1)S(1)} collective-permute-done((bf16[272,768]{1,0:T(8,128)(2,1)S(1)}, bf16[272,768]{1,0:T(8,128)(2,1)S(1)}, u32[]{:S(2)}, u32[]{:S(2)}) %collective-permute-start.5) | collective-permute-done | bytes 417824 | tf_op jit(solution)/shard_map/ppermute | solution.py:305
  55.6 6.2 collective-permute-done.3
  85.0 7.3 %convolution_convert_fusion = bf16[1664,1920]{1,0:T(8,128)(2,1)} fusion(bf16[1664,768]{1,0:T(8,128)(2,1)S(1)} %bitcast.395, bf16[1920,768]{1,0:T(8,128)(2,1)S(1)} %bitcast.365), kind=kOutput, calls=%fused_computation.10 | convolution fusion | flops 4910530560 | bytes 11894784 | tf_op jit(solution)/shard_map/dot_general | solution.py:22
  95.7 6.2 collective-permute-done.10
  124.4 15.7 %shard_map.138 = bf16[1,8,208,768]{3,2,1,0:T(8,128)(2,1)} custom-call(bf16[1,8,208,1920]{3,2,1,0:T(8,128)(2,1)} %bitcast.406, bf16[1,8,208,384]{3,2,1,0:T(8,128)(2,1)} %bitcast.426), custom_call_target="tpu_custom_call" | custom-call | flops 14976000000 | tf_op jit(solution)/shard_map/pallas_call | solution.py:134
  145.2 9.7 %shard_map.140 = bf16[2,8,21,8,768]{4,3,2,1,0:T(8,128)(2,1)S(1)} custom-call(s32[8]{0:T(128)S(1)} %iota_xor_fusion.dest_ref, bf16[42,8,768]{2,1,0:T(8,128)(2,1)S(1)} %bitcast.310, bf16[42,8,768]{2,1,0:T(8,128)(2,1)S(1)} %bitcast.332, bf16[42,8,768]{2,1,0:T(8,128)(2,1)S(1)} %bitcast.330, bf16[42,8,768]{2,1,0:T(8,128)(2,1)} %bitcast.43.refs_3_, ...), custom_call_target="tpu_custom_call" | custom-call | bytes 16515072 | tf_op jit(solution)/shard_map/pallas_call | solution.py:181
  164.2 8.4 %convolution_convert_fusion.1 = bf16[1664,1536]{1,0:T(8,128)(2,1)} fusion(bf16[1664,768]{1,0:T(8,128)(2,1)S(1)} %add_convert_fusion.3, bf16[3840,768]{1,0:T(8,128)(2,1)} %bitcast.297), kind=kOutput, calls=%fused_computation.11 | convolution fusion | flops 3928424448 | bytes 10027008 | tf_op jit(solution)/shard_map/dot_general | solution.py:22
  188.8 16.3 %shard_map.142 = bf16[1,8,208,768]{3,2,1,0:T(8,128)(2,1)} custom-call(bf16[1,8,208,1536]{3,2,1,0:T(8,128)(2,1)} %bitcast.408, bf16[1,8,208,768]{3,2,1,0:T(8,128)(2,1)} %bitcast.420), custom_call_target="tpu_custom_call" | custom-call | flops 14976000000 | tf_op jit(solution)/shard_map/pallas_call | solution.py:134
  213.5 6.4 fusion.84
  225.8 17.1 %fusion.4 = (bf16[1664,3072]{1,0:T(8,128)(2,1)}, bf16[1664,3072]{1,0:T(8,128)(2,1)}) fusion(f32[3072]{0:T(1024)S(1)} %add.448, bf16[3840,768]{1,0:T(8,128)(2,1)S(1)} %bitcast.302, f32[1664,768]{1,0:T(8,128)S(1)} %get-tuple-element.340, f32[768]{0:T(1024)S(1)} %add.445, f32[768]{0:T(1024)S(1)} %mul.247, f32[1664]{0:T(1024)S(1)} %add_rsqrt_fusion, ...), kind=kOutput, calls=%fused_computation.5 | convolution fusion | flops 7919468544 | bytes 30314496 | tf_op jit(solution)/shard_map/dot_general | solution.py:22
  242.9 17.8 %collective-permute-done.41 = bf16[336,768]{1,0:T(8,128)(2,1)} collective-permute-done((bf16[336,768]{1,0:T(8,128)(2,1)}, bf16[336,768]{1,0:T(8,128)(2,1)}, u32[]{:S(2)}, u32[]{:S(2)}) %collective-permute-start.41) | collective-permute-done | bytes 516128 | tf_op jit(solution)/shard_map/ppermute | solution.py:305
  265.2 11.5 %shard_map.145 = bf16[3,8,21,8,768]{4,3,2,1,0:T(8,128)(2,1)S(1)} custom-call(s32[8]{0:T(128)S(1)} %iota_xor_fusion.dest_ref, bf16[42,8,768]{2,1,0:T(8,128)(2,1)S(1)} %bitcast.311, bf16[42,8,768]{2,1,0:T(8,128)(2,1)S(1)} %bitcast.333, bf16[42,8,768]{2,1,0:T(8,128)(2,1)S(1)} %bitcast.331, bf16[42,8,768]{2,1,0:T(8,128)(2,1)} %bitcast.43.refs_3_, ...), custom_call_target="tpu_custom_call" | custom-call | bytes 24772608 | tf_op jit(solution)/shard_map/pallas_call | solution.py:181
  281.9 13.0 %fusion.35.refs_0_.refs_3_ = bf16[384,8,768]{2,1,0:T(8,128)(2,1)S(1)} fusion(bf16[1664,3072]{1,0:T(8,128)(2,1)} %get-tuple-element.169, bf16[1664,768]{1,0:T(8,128)(2,1)S(1)} %bitcast.381), kind=kOutput, calls=%fused_computation.81 | convolution fusion | flops 7854096384 | bytes 17498112 | tf_op jit(solution)/shard_map/dot_general | solution.py:30
  294.8 8.7 %shard_map.144 = (bf16[4,42,8,768]{3,2,1,0:T(8,128)(2,1)S(1)}, bf16[4,42,8,768]{3,2,1,0:T(8,128)(2,1)}) custom-call(s32[1]{0:T(128)} %bitcast.66.core_ref, bf16[384,8,768]{2,1,0:T(8,128)(2,1)S(1)} %fusion.35.refs_0_.refs_3_), custom_call_target="tpu_custom_call" | custom-call | bytes 16515072 | tf_op jit(solution)/shard_map/pallas_call | solution.py:240
  305.8 10.7 %add_convert_fusion.1 = bf16[1664,768]{1,0:T(8,128)(2,1)S(1)} fusion(f32[1664,768]{1,0:T(8,128)S(1)} %bitcast.387, bf16[1664,3072]{1,0:T(8,128)(2,1)} %get-tuple-element.169, bf16[4032,768]{1,0:T(8,128)(2,1)S(1)} %bitcast.295, f32[768]{0:T(1024)S(1)} %add.455), kind=kOutput, calls=%fused_computation.43 | convolution fusion | flops 7855570944 | bytes 22614016 | tf_op jit(solution)/shard_map/dot_general | solution.py:26
  322.9 14.8 %multiply_convert_fusion = bf16[1664,3072]{1,0:T(8,128)(2,1)} fusion(bf16[1664,3072]{1,0:T(8,128)(2,1)} %get-tuple-element.176, bf16[1664,768]{1,0:T(8,128)(2,1)} %bitcast.382, bf16[4032,768]{1,0:T(8,128)(2,1)} %bitcast.292), kind=kOutput, calls=%fused_computation.7 | convolution fusion | flops 7867072512 | bytes 27721728 | tf_op jit(solution)/shard_map/dot_general | solution.py:22
  344.7 13.8 %fusion.36.refs_0_.refs_1_ = bf16[384,8,768]{2,1,0:T(8,128)(2,1)S(1)} fusion(bf16[1664,3072]{1,0:T(8,128)(2,1)} %multiply_convert_fusion, f32[1664,768]{1,0:T(8,128)} %copy-done.32, f32[768]{0:T(1024)S(1)} %add.445, f32[768]{0:T(1024)S(1)} %mul.247, f32[1664]{0:T(1024)S(1)} %add_rsqrt_fusion, f32[1664]{0:T(1024)S(1)} %broadcast_multiply_fusion.6), kind=kOutput, calls=%fused_computation.82 | convolution fusion | flops 7860486144 | bytes 20073472 | tf_op jit(solution)/shard_map/dot_general | solution.py:30
  363.4 15.2 %multiply_reduce_fusion = (f32[768]{0:T(1024)}, f32[1664]{0:T(1024)S(1)}, f32[1664]{0:T(1024)S(1)}, f32[768]{0:T(1024)}, f32[1664,768]{1,0:T(8,128)}) fusion(f32[1664,768]{1,0:T(8,128)S(1)} %bitcast.389, f32[1664]{0:T(1024)S(1)} %add_rsqrt_fusion, f32[1664]{0:T(1024)S(1)} %broadcast_multiply_fusion.6, f32[768]{0:T(1024)S(1)} %mul.247, ...), kind=kOutput, calls=%fused_computation.37 | convolution fusion | flops 7863233536 | bytes 25205760 | tf_op jit(solution)/shard_map/dot_general | solution.py:26
  397.2 26.3 %shard_map.147 = (bf16[1,8,208,1536]{3,2,1,0:T(8,128)(2,1)}, bf16[1,8,208,768]{3,2,1,0:T(8,128)(2,1)}) custom-call(bf16[1,8,208,1536]{3,2,1,0:T(8,128)(2,1)} %bitcast.409, bf16[1,8,208,768]{3,2,1,0:T(8,128)(2,1)} %bitcast.421, bf16[1,8,208,768]{3,2,1,0:T(8,128)(2,1)} %bitcast.424), custom_call_target="tpu_custom_call" | custom-call | flops 23296000000 | tf_op jit(solution)/shard_map/pallas_call | solution.py:134
  435.4 6.0 convolution_convert_fusion.9
  446.2 5.8 fusion.47
  452.1 9.0 %multiply_reduce_fusion.1 = (f32[768]{0:T(1024)S(1)}, f32[1664]{0:T(1024)S(1)}, f32[1664]{0:T(1024)S(1)}, f32[768]{0:T(1024)S(1)}, f32[1664,768]{1,0:T(8,128)S(1)}) fusion(f32[1664]{0:T(1024)S(1)} %copy-done.66, f32[1664]{0:T(1024)S(1)} %copy-done.60, bf16[1664,768]{1,0:T(8,128)(2,1)S(1)} %copy-done.27, bf16[1,8,196,768]{3,2,1,0:T(8,128)(2,1)S(1)} %bitcast.377, ...), kind=kOutput, calls=%fused_computation.38 | convolution fusion | flops 3942477056 | bytes 22694912 | tf_op jit(solution)/shard_map/dot_general | solution.py:26
  473.8 11.0 %shard_map.149 = (bf16[4,42,8,768]{3,2,1,0:T(8,128)(2,1)S(1)}, bf16[4,42,8,768]{3,2,1,0:T(8,128)(2,1)S(1)}) custom-call(s32[1]{0:T(128)} %bitcast.66.core_ref, bf16[96,8,768]{2,1,0:T(8,128)(2,1)S(1)} %fusion.42.refs_0_, bf16[96,8,768]{2,1,0:T(8,128)(2,1)S(1)} %fusion.43.refs_1_, bf16[96,8,768]{2,1,0:T(8,128)(2,1)S(1)} %fusion.44.refs_2_, ...), custom_call_target="tpu_custom_call" | custom-call | bytes 16515072 | tf_op jit(solution)/shard_map/pallas_call | solution.py:240
  494.2 26.3 %shard_map.150 = bf16[1,8,208,2304]{3,2,1,0:T(8,128)(2,1)} custom-call(bf16[1,8,208,1920]{3,2,1,0:T(8,128)(2,1)} %bitcast.407, bf16[1,8,208,384]{3,2,1,0:T(8,128)(2,1)} %bitcast.427, bf16[1,8,208,768]{3,2,1,0:T(8,128)(2,1)} %bitcast.425), custom_call_target="tpu_custom_call" | custom-call | flops 23296000000 | tf_op jit(solution)/shard_map/pallas_call | solution.py:134
  521.3 9.3 %fusion.39.refs_0_ = bf16[288,8,768]{2,1,0:T(8,128)(2,1)S(1)} fusion(bf16[1664,2304]{1,0:T(8,128)(2,1)} %bitcast.404, bf16[1664,768]{1,0:T(8,128)(2,1)S(1)} %copy-done.38), kind=kOutput, calls=%fused_computation.85 | convolution fusion | flops 5890572288 | bytes 13762560 | tf_op jit(solution)/shard_map/dot_general | solution.py:30
  552.2 13.4 %fusion.22 = (f32[768]{0:T(1024)S(1)}, f32[1664]{0:T(1024)S(1)}, f32[1664]{0:T(1024)S(1)}, f32[768]{0:T(1024)S(1)}, f32[1664,768]{1,0:T(8,128)}) fusion(f32[1664]{0:T(1024)S(1)} %copy-done.64, f32[1664]{0:T(1024)S(1)} %copy-done.62, bf16[1,8,196,768]{3,2,1,0:T(8,128)(2,1)S(1)} %bitcast.379, f32[768]{0:T(1024)S(1)} %copy-done.68, ...), kind=kOutput, calls=%fused_computation.33 | convolution fusion | flops 5901577216 | bytes 18816000 | tf_op jit(solution)/shard_map/dot_general | solution.py:26
  570.3 14.5 %collective-permute-done.65 = bf16[2,480,768]{2,1,0:T(8,128)(2,1)S(1)} collective-permute-done((bf16[2,480,768]{2,1,0:T(8,128)(2,1)}, bf16[2,480,768]{2,1,0:T(8,128)(2,1)S(1)}, u32[]{:S(2)}, u32[]{:S(2)}) %collective-permute-start.65) | collective-permute-done | bytes 1474592 | tf_op jit(solution)/shard_map/ppermute | solution.py:305
  591.8 13.0 %collective-permute-done.66 = bf16[480,768]{1,0:T(8,128)(2,1)} collective-permute-done((bf16[480,768]{1,0:T(8,128)(2,1)}, bf16[480,768]{1,0:T(8,128)(2,1)}, u32[]{:S(2)}, u32[]{:S(2)}) %collective-permute-start.66) | collective-permute-done | bytes 737312 | tf_op jit(solution)/shard_map/ppermute | solution.py:305
  606.1 5.8 all-to-all-start.4
  645.1 6.6 collective-permute-done.72
  651.6 15.3 %collective-permute-done.71 = bf16[240,768]{1,0:T(8,128)(2,1)} collective-permute-done((bf16[240,768]{1,0:T(8,128)(2,1)S(1)}, bf16[240,768]{1,0:T(8,128)(2,1)}, u32[]{:S(2)}, u32[]{:S(2)}) %collective-permute-start.71) | collective-permute-done | bytes 368672 | tf_op jit(solution)/shard_map/ppermute | solution.py:308
  (507 shorter events, 281.1 us)
Async XLA Ops:
  2.5 30.2 %collective-permute-start.1 = (bf16[248,768]{1,0:T(8,128)(2,1)S(1)}, bf16[248,768]{1,0:T(8,128)(2,1)S(1)}, u32[]{:S(2)}, u32[]{:S(2)}) collective-permute-start(bf16[248,768]{1,0:T(8,128)(2,1)S(1)} %get-tuple-element.335), channel_id=1, source_target_pairs={{0,16},{1,17},{2,18},{3,19},{4,20},{5,21},{6,22},{7,23},{8,24},{9,... | collective-permute-start | bytes 1142792 | tf_op jit(solution)/shard_map/ppermute | solution.py:308
  10.5 69.8 %all-to-all-start = ((bf16[4,2,196,768]{3,1,2,0:T(2,128)(2,1)}), bf16[4,2,196,768]{3,1,2,0:T(2,128)(2,1)}, u32[]{:S(2)}, u32[]{:S(2)}) async-start(bf16[4,2,196,768]{3,1,2,0:T(2,128)(2,1)} %param.8), calls=%async_computation | async-start | bytes 4816896 | tf_op jit(solution)/shard_map/all_to_all | solution.py:628
  62.9 29.6 %collective-permute-start.15 = (bf16[168,768]{1,0:T(8,128)(2,1)S(1)}, bf16[168,768]{1,0:T(8,128)(2,1)}, u32[]{:S(2)}, u32[]{:S(2)}) collective-permute-start(bf16[168,768]{1,0:T(8,128)(2,1)S(1)} %copy-done.19), channel_id=1, source_target_pairs={{0,24},{1,25},{2,26},{3,27},{4,28},{5,29},{6,30},{7,31},{8,0},{9,1... | collective-permute-start | bytes 774152 | tf_op jit(solution)/shard_map/ppermute | solution.py:308
  63.6 32.1 %collective-permute-start.14 = (bf16[168,768]{1,0:T(8,128)(2,1)S(1)}, bf16[168,768]{1,0:T(8,128)(2,1)}, u32[]{:S(2)}, u32[]{:S(2)}) collective-permute-start(bf16[168,768]{1,0:T(8,128)(2,1)S(1)} %copy-done.19), channel_id=1, source_target_pairs={{0,16},{1,17},{2,18},{3,19},{4,20},{5,21},{6,22},{7,23},{8,24},{9,... | collective-permute-start | bytes 774152 | tf_op jit(solution)/shard_map/ppermute | solution.py:308
  69.2 26.5 %collective-permute-start.13 = (bf16[168,768]{1,0:T(8,128)(2,1)S(1)}, bf16[168,768]{1,0:T(8,128)(2,1)}, u32[]{:S(2)}, u32[]{:S(2)}) collective-permute-start(bf16[168,768]{1,0:T(8,128)(2,1)S(1)} %copy-done.19), channel_id=1, source_target_pairs={{0,8},{1,9},{2,10},{3,11},{4,12},{5,13},{6,14},{7,15},{8,16},{9,17... | collective-permute-start | bytes 774152 | tf_op jit(solution)/shard_map/ppermute | solution.py:308
  106.7 33.5 %collective-permute-start.22 = (bf16[336,768]{1,0:T(8,128)(2,1)S(1)}, bf16[336,768]{1,0:T(8,128)(2,1)S(1)}, u32[]{:S(2)}, u32[]{:S(2)}) collective-permute-start(bf16[336,768]{1,0:T(8,128)(2,1)S(1)} %bitcast.306), channel_id=1, source_target_pairs={{0,6},{1,7},{2,4},{3,5},{4,2},{5,3},{6,0},{7,1},{8,14},{9,15},{10,... | collective-permute-start | bytes 1548296 | tf_op jit(solution)/shard_map/ppermute | solution.py:305
  108.3 31.8 %collective-permute-start.21 = (bf16[336,768]{1,0:T(8,128)(2,1)S(1)}, bf16[336,768]{1,0:T(8,128)(2,1)S(1)}, u32[]{:S(2)}, u32[]{:S(2)}) collective-permute-start(bf16[336,768]{1,0:T(8,128)(2,1)S(1)} %bitcast.307), channel_id=1, source_target_pairs={{0,4},{1,5},{2,6},{3,7},{4,0},{5,1},{6,2},{7,3},{8,12},{9,13},{10,... | collective-permute-start | bytes 1548296 | tf_op jit(solution)/shard_map/ppermute | solution.py:305
  108.8 31.3 %collective-permute-start.20 = (bf16[336,768]{1,0:T(8,128)(2,1)S(1)}, bf16[336,768]{1,0:T(8,128)(2,1)S(1)}, u32[]{:S(2)}, u32[]{:S(2)}) collective-permute-start(bf16[336,768]{1,0:T(8,128)(2,1)S(1)} %bitcast.308), channel_id=1, source_target_pairs={{0,2},{1,3},{2,0},{3,1},{4,6},{5,7},{6,4},{7,5},{8,10},{9,11},{10,... | collective-permute-start | bytes 1548296 | tf_op jit(solution)/shard_map/ppermute | solution.py:305
  141.7 31.0 %collective-permute-start.29 = (bf16[240,768]{1,0:T(8,128)(2,1)S(1)}, bf16[240,768]{1,0:T(8,128)(2,1)}, u32[]{:S(2)}, u32[]{:S(2)}) collective-permute-start(bf16[240,768]{1,0:T(8,128)(2,1)S(1)} %get-tuple-element.157), channel_id=1, source_target_pairs={{0,6},{1,7},{2,4},{3,5},{4,2},{5,3},{6,0},{7,1},{8,14},{9,15},{10,... | collective-permute-start | bytes 1105928 | tf_op jit(solution)/shard_map/ppermute | solution.py:305
  143.4 29.3 %collective-permute-start.28 = (bf16[240,768]{1,0:T(8,128)(2,1)S(1)}, bf16[240,768]{1,0:T(8,128)(2,1)}, u32[]{:S(2)}, u32[]{:S(2)}) collective-permute-start(bf16[240,768]{1,0:T(8,128)(2,1)S(1)} %get-tuple-element.157), channel_id=1, source_target_pairs={{0,4},{1,5},{2,6},{3,7},{4,0},{5,1},{6,2},{7,3},{8,12},{9,13},{10,... | collective-permute-start | bytes 1105928 | tf_op jit(solution)/shard_map/ppermute | solution.py:305
  143.9 28.8 %collective-permute-start.27 = (bf16[240,768]{1,0:T(8,128)(2,1)S(1)}, bf16[240,768]{1,0:T(8,128)(2,1)}, u32[]{:S(2)}, u32[]{:S(2)}) collective-permute-start(bf16[240,768]{1,0:T(8,128)(2,1)S(1)} %get-tuple-element.157), channel_id=1, source_target_pairs={{0,2},{1,3},{2,0},{3,1},{4,6},{5,7},{6,4},{7,5},{8,10},{9,11},{10,... | collective-permute-start | bytes 1105928 | tf_op jit(solution)/shard_map/ppermute | solution.py:305
  178.6 26.5 %collective-permute-start.36 = (bf16[240,768]{1,0:T(8,128)(2,1)S(1)}, bf16[240,768]{1,0:T(8,128)(2,1)}, u32[]{:S(2)}, u32[]{:S(2)}) collective-permute-start(bf16[240,768]{1,0:T(8,128)(2,1)S(1)} %copy-done.18), channel_id=1, source_target_pairs={{0,6},{1,7},{2,4},{3,5},{4,2},{5,3},{6,0},{7,1},{8,14},{9,15},{10,... | collective-permute-start | bytes 1105928 | tf_op jit(solution)/shard_map/ppermute | solution.py:305
  205.1 74.3 %all-to-all-start.1 = ((bf16[4,2,196,768]{3,1,2,0:T(2,128)(2,1)}), bf16[4,2,196,768]{3,1,2,0:T(2,128)(2,1)}, u32[]{:S(2)}, u32[]{:S(2)}) async-start(bf16[4,2,196,768]{3,1,2,0:T(2,128)(2,1)} %param.9), calls=%async_computation.1 | async-start | bytes 4816896 | tf_op jit(solution)/shard_map/all_to_all | solution.py:628
  210.7 32.2 %collective-permute-start.43 = (bf16[336,768]{1,0:T(8,128)(2,1)}, bf16[336,768]{1,0:T(8,128)(2,1)}, u32[]{:S(2)}, u32[]{:S(2)}) collective-permute-start(bf16[336,768]{1,0:T(8,128)(2,1)} %bitcast.61), channel_id=1, source_target_pairs={{0,6},{1,7},{2,4},{3,5},{4,2},{5,3},{6,0},{7,1},{8,14},{9,15},{10,... | collective-permute-start | bytes 1548296 | tf_op jit(solution)/shard_map/ppermute | solution.py:305
  221.3 39.5 %collective-permute-start.41 = (bf16[336,768]{1,0:T(8,128)(2,1)}, bf16[336,768]{1,0:T(8,128)(2,1)}, u32[]{:S(2)}, u32[]{:S(2)}) collective-permute-start(bf16[336,768]{1,0:T(8,128)(2,1)} %bitcast.61), channel_id=1, source_target_pairs={{0,2},{1,3},{2,0},{3,1},{4,6},{5,7},{6,4},{7,5},{8,10},{9,11},{10,... | collective-permute-start | bytes 1548296 | tf_op jit(solution)/shard_map/ppermute | solution.py:305
  305.6 32.1 %collective-permute-start.48 = (bf16[4,336,768]{2,1,0:T(8,128)(2,1)}, bf16[4,336,768]{2,1,0:T(8,128)(2,1)}, u32[]{:S(2)}, u32[]{:S(2)}) collective-permute-start(bf16[4,336,768]{2,1,0:T(8,128)(2,1)} %bitcast.77), channel_id=1, source_target_pairs={{0,1},{1,0},{2,3},{3,2},{4,5},{5,4},{6,7},{7,6},{8,9},{9,8},{10,11... | collective-permute-start | bytes 6193160 | tf_op jit(solution)/shard_map/ppermute | solution.py:305
  318.2 72.7 %all-to-all-start.2 = ((bf16[1,8,196,768]{3,2,0,1:T(8,128)(2,1)}), bf16[1,8,196,768]{3,2,0,1:T(8,128)(2,1)}, u32[]{:S(2)}, u32[]{:S(2)}) async-start(bf16[1,8,196,768]{3,2,0,1:T(8,128)(2,1)} %slice.224), calls=%async_computation.2 | async-start | bytes 4915200 | tf_op jit(solution)/shard_map/all_to_all | solution.py:633
  341.2 49.7 %collective-permute-start.51 = (bf16[336,768]{1,0:T(8,128)(2,1)}, bf16[336,768]{1,0:T(8,128)(2,1)S(1)}, u32[]{:S(2)}, u32[]{:S(2)}) collective-permute-start(bf16[336,768]{1,0:T(8,128)(2,1)} %get-tuple-element.304), channel_id=1, source_target_pairs={{0,6},{1,7},{2,4},{3,5},{4,2},{5,3},{6,0},{7,1},{8,14},{9,15},{10,... | collective-permute-start | bytes 1548296 | tf_op jit(solution)/shard_map/ppermute | solution.py:305
  344.1 46.7 %collective-permute-start.50 = (bf16[336,768]{1,0:T(8,128)(2,1)}, bf16[336,768]{1,0:T(8,128)(2,1)}, u32[]{:S(2)}, u32[]{:S(2)}) collective-permute-start(bf16[336,768]{1,0:T(8,128)(2,1)} %get-tuple-element.305), channel_id=1, source_target_pairs={{0,4},{1,5},{2,6},{3,7},{4,0},{5,1},{6,2},{7,3},{8,12},{9,13},{10,... | collective-permute-start | bytes 1548296 | tf_op jit(solution)/shard_map/ppermute | solution.py:305
  344.6 46.2 %collective-permute-start.49 = (bf16[336,768]{1,0:T(8,128)(2,1)}, bf16[336,768]{1,0:T(8,128)(2,1)}, u32[]{:S(2)}, u32[]{:S(2)}) collective-permute-start(bf16[336,768]{1,0:T(8,128)(2,1)} %get-tuple-element.306), channel_id=1, source_target_pairs={{0,2},{1,3},{2,0},{3,1},{4,6},{5,7},{6,4},{7,5},{8,10},{9,11},{10,... | collective-permute-start | bytes 1548296 | tf_op jit(solution)/shard_map/ppermute | solution.py:305
  393.7 29.9 %collective-permute-start.55 = (bf16[240,768]{1,0:T(8,128)(2,1)}, bf16[240,768]{1,0:T(8,128)(2,1)S(1)}, u32[]{:S(2)}, u32[]{:S(2)}) collective-permute-start(bf16[240,768]{1,0:T(8,128)(2,1)} %get-tuple-element.312), channel_id=1, source_target_pairs={{0,6},{1,7},{2,4},{3,5},{4,2},{5,3},{6,0},{7,1},{8,14},{9,15},{10,... | collective-permute-start | bytes 1105928 | tf_op jit(solution)/shard_map/ppermute | solution.py:305
  396.5 27.1 %collective-permute-start.54 = (bf16[240,768]{1,0:T(8,128)(2,1)}, bf16[240,768]{1,0:T(8,128)(2,1)}, u32[]{:S(2)}, u32[]{:S(2)}) collective-permute-start(bf16[240,768]{1,0:T(8,128)(2,1)} %get-tuple-element.313), channel_id=1, source_target_pairs={{0,4},{1,5},{2,6},{3,7},{4,0},{5,1},{6,2},{7,3},{8,12},{9,13},{10,... | collective-permute-start | bytes 1105928 | tf_op jit(solution)/shard_map/ppermute | solution.py:305
  397.1 26.6 %collective-permute-start.53 = (bf16[240,768]{1,0:T(8,128)(2,1)}, bf16[240,768]{1,0:T(8,128)(2,1)}, u32[]{:S(2)}, u32[]{:S(2)}) collective-permute-start(bf16[240,768]{1,0:T(8,128)(2,1)} %get-tuple-element.314), channel_id=1, source_target_pairs={{0,2},{1,3},{2,0},{3,1},{4,6},{5,7},{6,4},{7,5},{8,10},{9,11},{10,... | collective-permute-start | bytes 1105928 | tf_op jit(solution)/shard_map/ppermute | solution.py:305
  490.7 29.8 %collective-permute-start.63 = (bf16[336,768]{1,0:T(8,128)(2,1)}, bf16[336,768]{1,0:T(8,128)(2,1)S(1)}, u32[]{:S(2)}, u32[]{:S(2)}) collective-permute-start(bf16[336,768]{1,0:T(8,128)(2,1)} %get-tuple-element.300), channel_id=1, source_target_pairs={{0,6},{1,7},{2,4},{3,5},{4,2},{5,3},{6,0},{7,1},{8,14},{9,15},{10,... | collective-permute-start | bytes 1548296 | tf_op jit(solution)/shard_map/ppermute | solution.py:305
  493.3 27.1 %collective-permute-start.62 = (bf16[336,768]{1,0:T(8,128)(2,1)}, bf16[336,768]{1,0:T(8,128)(2,1)}, u32[]{:S(2)}, u32[]{:S(2)}) collective-permute-start(bf16[336,768]{1,0:T(8,128)(2,1)} %get-tuple-element.301), channel_id=1, source_target_pairs={{0,4},{1,5},{2,6},{3,7},{4,0},{5,1},{6,2},{7,3},{8,12},{9,13},{10,... | collective-permute-start | bytes 1548296 | tf_op jit(solution)/shard_map/ppermute | solution.py:305
  493.9 26.6 %collective-permute-start.61 = (bf16[336,768]{1,0:T(8,128)(2,1)}, bf16[336,768]{1,0:T(8,128)(2,1)}, u32[]{:S(2)}, u32[]{:S(2)}) collective-permute-start(bf16[336,768]{1,0:T(8,128)(2,1)} %get-tuple-element.302), channel_id=1, source_target_pairs={{0,2},{1,3},{2,0},{3,1},{4,6},{5,7},{6,4},{7,5},{8,10},{9,11},{10,... | collective-permute-start | bytes 1548296 | tf_op jit(solution)/shard_map/ppermute | solution.py:305
  543.2 48.5 %collective-permute-start.69 = (bf16[168,768]{1,0:T(8,128)(2,1)}, bf16[168,768]{1,0:T(8,128)(2,1)}, u32[]{:S(2)}, u32[]{:S(2)}) collective-permute-start(bf16[168,768]{1,0:T(8,128)(2,1)} %get-tuple-element.323), channel_id=1, source_target_pairs={{0,24},{1,25},{2,26},{3,27},{4,28},{5,29},{6,30},{7,31},{8,0},{9,1... | collective-permute-start | bytes 774152 | tf_op jit(solution)/shard_map/ppermute | solution.py:308
  546.1 45.6 %collective-permute-start.68 = (bf16[168,768]{1,0:T(8,128)(2,1)}, bf16[168,768]{1,0:T(8,128)(2,1)}, u32[]{:S(2)}, u32[]{:S(2)}) collective-permute-start(bf16[168,768]{1,0:T(8,128)(2,1)} %get-tuple-element.324), channel_id=1, source_target_pairs={{0,16},{1,17},{2,18},{3,19},{4,20},{5,21},{6,22},{7,23},{8,24},{9,... | collective-permute-start | bytes 774152 | tf_op jit(solution)/shard_map/ppermute | solution.py:308
  546.1 45.6 %collective-permute-start.67 = (bf16[168,768]{1,0:T(8,128)(2,1)}, bf16[168,768]{1,0:T(8,128)(2,1)}, u32[]{:S(2)}, u32[]{:S(2)}) collective-permute-start(bf16[168,768]{1,0:T(8,128)(2,1)} %get-tuple-element.325), channel_id=1, source_target_pairs={{0,8},{1,9},{2,10},{3,11},{4,12},{5,13},{6,14},{7,15},{8,16},{9,17... | collective-permute-start | bytes 774152 | tf_op jit(solution)/shard_map/ppermute | solution.py:308
  550.6 34.3 %collective-permute-start.65 = (bf16[2,480,768]{2,1,0:T(8,128)(2,1)}, bf16[2,480,768]{2,1,0:T(8,128)(2,1)S(1)}, u32[]{:S(2)}, u32[]{:S(2)}) collective-permute-start(bf16[2,480,768]{2,1,0:T(8,128)(2,1)} %get-tuple-element.217), channel_id=1, source_target_pairs={{0,4},{1,5},{2,6},{3,7},{4,0},{5,1},{6,2},{7,3},{8,12},{9,13},{10,... | collective-permute-start | bytes 4423688 | tf_op jit(solution)/shard_map/ppermute | solution.py:305
  620.8 48.5 %all-to-all-start.3 = ((bf16[1,8,196,768]{3,2,0,1:T(8,128)(2,1)}), bf16[1,8,196,768]{3,2,0,1:T(8,128)(2,1)S(1)}, u32[]{:S(2)}, u32[]{:S(2)}) async-start(bf16[1,8,196,768]{3,2,0,1:T(8,128)(2,1)} %slice.230), calls=%async_computation.3 | async-start | bytes 4915200 | tf_op jit(solution)/shard_map/all_to_all | solution.py:633
  635.3 31.6 %collective-permute-start.71 = (bf16[240,768]{1,0:T(8,128)(2,1)S(1)}, bf16[240,768]{1,0:T(8,128)(2,1)}, u32[]{:S(2)}, u32[]{:S(2)}) collective-permute-start(bf16[240,768]{1,0:T(8,128)(2,1)S(1)} %get-tuple-element.318), channel_id=1, source_target_pairs={{0,16},{1,17},{2,18},{3,19},{4,20},{5,21},{6,22},{7,23},{8,24},{9,... | collective-permute-start | bytes 1105928 | tf_op jit(solution)/shard_map/ppermute | solution.py:308
  (155 other events, 1777.8 us)

commit v5 on v4

--- a/solution.py
+++ b/solution.py
@@ -14,6 +14,7 @@
 LANES = 2 * HEAD_DIM
 SUB = 16
 NEG = -1e30
+COPY_VMEM = 60 << 20
 F32 = jnp.float32
 BF16 = jnp.bfloat16
 
@@ -185,7 +186,7 @@
         out_shape=[jax.ShapeDtypeStruct(s, BF16) for s in shapes],
         scratch_shapes=[pltpu.VMEM(s, BF16) for s in shapes]
         + [pltpu.SemaphoreType.DMA((slots,)), pltpu.SemaphoreType.DMA((slots,))],
-        compiler_params=pltpu.CompilerParams(vmem_limit_bytes=size + (2 << 20)),
+        compiler_params=pltpu.CompilerParams(vmem_limit_bytes=COPY_VMEM),
         cost_estimate=pl.CostEstimate(flops=0, bytes_accessed=4 * size, transcendentals=0),
     )(dest, *flat)
     return [out.reshape(out.shape[:2] + (-1, width)) for out in outs]
@@ -244,10 +245,33 @@
         out_shape=[half, half],
         scratch_shapes=[pltpu.VMEM((2 * squares, rows // 8, 8, width), BF16) for rows in plane_rows]
         + [pltpu.SemaphoreType.DMA((slots + len(parts),)), pltpu.SemaphoreType.DMA((slots,))],
-        compiler_params=pltpu.CompilerParams(vmem_limit_bytes=size + (2 << 20)),
+        compiler_params=pltpu.CompilerParams(vmem_limit_bytes=COPY_VMEM),
         cost_estimate=pl.CostEstimate(flops=0, bytes_accessed=4 * size, transcendentals=0),
     )(core, *arrays)
     return [out.reshape(squares, -1, width) for out in outs]
+
+
+def pack_kernel(devices, *refs):
+    parts, out_ref, held = (refs[:-2], refs[-2], refs[-1])
+    held[...] = jnp.zeros_like(held)
+    out_ref[...] = jnp.zeros_like(out_ref)
+    row = 0
+    for part in parts:
+        held[row : row + part.shape[0], :] = part[...]
+        row += part.shape[0]
+    share = held.shape[1] // devices
+    for device in range(devices):
+        out_ref[device, :, :share] = held[:, device * share : (device + 1) * share]
+
+
+def pack(parts, devices):
+    rows = -(-sum(part.shape[0] for part in parts) // 8) * 8
+    width = parts[0].shape[1]
+    return pl.pallas_call(
+        partial(pack_kernel, devices),
+        out_shape=jax.ShapeDtypeStruct((devices, rows, LANES), F32),
+        scratch_shapes=[pltpu.VMEM((rows, width), F32)],
+    )(*parts)
 
 
 def tie(values, others):
@@ -274,8 +298,8 @@
     def tick(self, name, *values):
         return values[0] if len(values) == 1 else values
 
-    def total(self, small):
-        g = self.grads
+    def total(self, parts):
+        g, small = (self.grads, jnp.concatenate(parts, axis=0))
         d_in = jnp.concatenate([g["in_t"], g["in_qk"], g["in_v"], g["in_m"]], axis=0)
         d_out = jnp.concatenate([g["out_t"], g["out_f"], g["out_s"], g["out_m"]], axis=0)
         summed_in = lax.psum_scatter(d_in, self.axes, scatter_dimension=0, tiled=True).astype(F32)
@@ -317,6 +341,10 @@
             row += size
         return [out[0] for out in place([pieces], plan, self.planes)]
 
+    def planes_exchange(self, blocks):
+        groups = [[spot + 8 * plane for plane in range(4)] for spot in range(8)]
+        return lax.all_to_all(blocks, self.axes, split_axis=0, concat_axis=0, axis_index_groups=groups)
+
     def over(self, piece):
         return [piece] + [self.flip(piece, bits) for bits in (2, 4, 6)]
 
@@ -330,22 +358,25 @@
         out = place(groups, [entries], self.spots)[0]
         return out.reshape(-1, self.width)
 
-    def begin(self):
+    def begin(self, clip):
         rows_in, rows_out, width = (self.rows_in, self.rows_out, self.width)
         smalls = self.column_small.reshape(-1, width)
         first = jnp.concatenate([self.column_in[0], smalls], axis=0)
         self.p1, self.p2, self.p3 = (self.column_in[k] for k in (1, 2, 3))
         p0 = self.over(first)
-        p0[0], weights_out = tie(first, self.weights_out)
-        self.q = self.shifted(weights_out)
-        p0, self.p1 = tie(p0, self.p1)
-        self.p1 = self.over(self.p1)
+        first, weights_out = tie(first, self.weights_out)
+        column = self.planes_exchange(jnp.broadcast_to(weights_out[None], (4,) + weights_out.shape))
+        p0, (clip, column) = tie(p0, (clip, column))
+        self.q01, self.q23 = (column[:2].reshape(-1, width), column[2:].reshape(-1, width))
         self.p0 = self.cores(p0)
         low, small = place([self.p0], [[(0, 0, rows_in)], [(0, rows_in, 32)]], self.spots)
+        low, self.p1 = tie(low, self.p1)
+        self.p1 = self.over(self.p1)
         self.in_a = low.reshape(-1, width)
         share = width // 32
         small = small.reshape(8, 4, 8, width)[:, :, 0, : self.count * share].reshape(8, 4, self.count, share)
         self.small = small.transpose(2, 1, 0, 3).reshape(self.count, width)
+        return clip
 
     def tick(self, name, *values):
         single = len(values) == 1
@@ -353,9 +384,7 @@
         g = self.grads
         whole = lambda key: (g[key], 0, g[key].shape[0])
         if name == "query_t":
-            values, (self.p1, self.q) = tie(values, (self.p1, self.q))
-            column = self.columns(self.q, (rows_out,))[0]
-            self.q01, self.q23 = (column[:2].reshape(-1, width), column[2:].reshape(-1, width))
+            values, (self.p1, self.q01) = tie(values, (self.p1, self.q01))
             self.q01 = self.over(self.q01)
             self.p1 = self.cores(self.p1)
             low = self.lay([self.p0, self.p1], [(0, 0, rows_in), (1, 0, rows_in)])
@@ -416,7 +445,13 @@
         elif name == "grad_t":
             values, self.d_p2 = tie(values, self.d_p2)
             self.d_p2 = self.gathered(self.d_p2)
+            late = jnp.zeros((8 * rows_in - 2 * width, width), BF16)
+            self.kept, send = self.halve([(late, 0, late.shape[0]), whole("in_qk")], (rows_in,))
+            values, send = tie(values, send)
+            self.other = self.flip(send, 1)
         elif name == "out_t":
+            values, (self.kept, self.other) = tie(values, (self.kept, self.other))
+            self.d_p1 = self.across(self.kept, self.other)
             start = 16 * rows_out - 3 * width
             self.kept, send = self.halve(
                 [whole("out_t"), whole("out_f"), whole("out_s"), (g["out_m"], 0, start)], (rows_out, rows_out)
@@ -427,27 +462,37 @@
             values, (self.kept, self.other) = tie(values, (self.kept, self.other))
             self.d_q01 = self.across(self.kept, self.other)
         elif name == "grad_project_t":
-            values, self.d_q01 = tie(values, self.d_q01)
-            self.d_q01 = self.gathered(self.d_q01)
-            planes = [a[k * rows_out : (k + 1) * rows_out] for a in (self.d_q01, self.d_q23) for k in range(2)]
-            self.out_pieces = self.along(planes)
+            values, self.d_p1 = tie(values, self.d_p1)
+            self.d_p1 = self.gathered(self.d_p1)
+            planes = [jnp.zeros_like(self.d_p1), self.d_p1, self.d_p2, self.d_p3]
+            self.in_pieces = self.planes_exchange(jnp.stack(planes, axis=0))
         elif name == "in_t":
-            kept, send = self.halve([whole("in_t"), whole("in_qk")], (rows_in, rows_in))
+            d_in_t = g["in_t"]
+            kept, send = self.halve([whole("in_t")], (rows_in, d_in_t.shape[0] // 8 - rows_in))
+            values, send = tie(values, send)
             half = lambda a, x: lax.dynamic_slice_in_dim(a, 2 * x, 2, 0).astype(F32)
             other = self.flip(send, 1)
             x = self.square // 2
             send = (half(kept, 1 - x) + half(other, 1 - x)).astype(BF16)
             own = (half(kept, x) + half(other, x)).astype(BF16)
-            values, (own, send) = tie(values, (own, send))
+            values, (own, send, self.d_q01) = tie(values, (own, send, self.d_q01))
             self.last = (own, self.flip(send, 4))
-        elif name == "grad_clip":
-            values, (own, other) = tie(values, self.last)
+            self.d_q01 = self.gathered(self.d_q01)
+            planes = [a[k * rows_out : (k + 1) * rows_out] for a in (self.d_q01, self.d_q23) for k in range(2)]
+            self.out_pieces = self.planes_exchange(jnp.stack(planes, axis=0))
+        elif name == "dx_t":
+            values, (own, other, self.in_pieces) = tie(values, self.last + (self.in_pieces,))
             y = self.square % 2
             line = lambda a, y: lax.dynamic_index_in_dim(a, y, 0, keepdims=False).astype(F32)
             send = (line(own, 1 - y) + line(other, 1 - y)).astype(BF16)
-            arrived = self.flip(send, 2)
-            values, (arrived, self.out_pieces) = tie(values, (arrived, self.out_pieces))
-            self.d_p01 = (line(own, y) + line(other, y) + arrived.astype(F32)).astype(BF16)
+            own = (line(own, y) + line(other, y)).astype(BF16)
+            self.last = (own, self.flip(send, 2))
+        elif name == "grad_clip":
+            small = lax.all_to_all(pack(values[1:], 32), self.axes, split_axis=0, concat_axis=0)
+            tied = tie(values[0], self.last + (small, self.out_pieces))
+            clip, (own, arrived, self.small_sums, self.out_pieces) = tied
+            values = (clip,) + tuple(values[1:])
+            self.d_last = self.gathered([own, arrived])
         return values[0] if single else values
 
     def halve(self, parts, plane_rows):
@@ -465,12 +510,11 @@
     def gathered(self, arrived):
         return self.added(arrived).astype(BF16)
 
-    def along(self, planes):
-        every = jnp.stack(planes, axis=0)
-        pieces = [lax.dynamic_index_in_dim(every, self.plane, 0, keepdims=False)]
+    def towards(self, block, plane):
+        pieces = [block]
         for step in (1, 2, 3):
-            block = lax.dynamic_index_in_dim(every, (self.plane + step) % 4, 0, keepdims=False)
-            pieces.append(self.shift(block, step))
+            pairs = [(d, (d + 8 * step) % 32) for d in range(32) if (d // 8 + step) % 4 == plane]
+            pieces.append(lax.ppermute(block, self.axes, pairs))
         return pieces
 
     def added(self, pieces):
@@ -479,19 +523,23 @@
             total = total + piece.astype(F32)
         return total
 
-    def sum_small(self, small):
-        count, width = small.shape
-        share = width // 32
-        tiles = -(-count * share // (8 * LANES))
-        slots = small.reshape(count, 32, share).transpose(1, 0, 2).reshape(32, count * share)
-        slots = jnp.pad(slots, ((0, 0), (0, tiles * 8 * LANES - count * share))).reshape(32, tiles * 8, LANES)
-        slots = lax.all_to_all(slots, self.axes, split_axis=0, concat_axis=0)
-        return jnp.sum(slots, axis=0).reshape(-1)[: count * share].reshape(count, share)
-
-    def total(self, small):
-        last, rows_in = (self.d_p01, self.rows_in)
-        pieces = self.along([last[:rows_in], last[rows_in:], self.d_p2, self.d_p3])
-        return (self.added(pieces), self.added(self.out_pieces), self.sum_small(small))
+    def total(self, parts):
+        rows, last = (self.rows_in, self.d_last)
+        extra, first = tie(self.towards(last[rows:], 1), last[:rows])
+        first = self.added(self.towards(first, 0))
+        extra = self.added(extra).astype(BF16)
+        extra = jnp.concatenate([extra, self.flip(extra, 1)], axis=0)
+        blocks = [extra]
+        for bits in (2, 4, 6):
+            blocks.append(lax.ppermute(extra, self.axes, [(8 + bits + core, 8 + core) for core in range(2)]))
+        extra = jnp.concatenate(blocks, axis=0).reshape(8, -1, self.width)
+        swapped = jnp.stack([extra[4], extra[7], extra[6]], axis=0).reshape(-1, self.width)
+        swapped = jnp.pad(swapped, ((0, rows - swapped.shape[0]), (0, 0)))
+        extra = jnp.where(self.core == 0, extra.reshape(-1, self.width)[:rows], swapped).astype(F32)
+        extra = jnp.where((self.plane == 1) & (self.square == 0), extra, 0.0)
+        summed_in = jnp.where(self.plane == 0, first, jnp.sum(self.in_pieces.astype(F32), axis=0) + extra)
+        small = jnp.sum(self.small_sums, axis=0)[: self.count, : self.width // 32]
+        return (summed_in, jnp.sum(self.out_pieces.astype(F32), axis=0), small)
 
 
 def norm_parts(values):
@@ -505,13 +553,15 @@
     return (norm_parts(values)[0] * gains + shifts).astype(BF16)
 
 
-def norm_backward(values, gains, grad):
+def norm_backward(values, gains, grad, hook=lambda *sums: sums):
     normed, scale = norm_parts(values)
     scaled = grad * gains
     first = jnp.mean(scaled, axis=-1, keepdims=True)
     second = jnp.mean(scaled * normed, axis=-1, keepdims=True)
-    inner = (scaled - first - normed * second) * scale
-    return (inner, jnp.sum(grad * normed, axis=0), jnp.sum(grad, axis=0))
+    sums = (first, second, jnp.sum(grad * normed, axis=0), jnp.sum(grad, axis=0))
+    grad, first, second, d_gain, d_shift = hook(grad, *sums)
+    inner = (grad * gains - first - normed * second) * scale
+    return (inner, d_gain, d_shift)
 
 
 def gelu_parts(values):
@@ -541,6 +591,7 @@
     project_t = [cube(project_a), cube(project_b)]
     mixed_t = attention_call(forward_kernel, 2, project_t, (width,), True, patches)[0]
     mixed_t = flat(feed.tick("mixed_t", mixed_t))
+    grad_low = flat(target(mixed_t))
     projected_t = (nn(mixed_t, feed.out_t) + shifts32[3]).astype(BF16)
     branch_t = (nn(projected_t, feed.out_f) + shifts32[4]).astype(BF16)
     after_t = start + branch_t.astype(F32)
@@ -551,7 +602,6 @@
     project_s = [cube(project_qk), cube(project_v)]
     mixed_s = attention_call(forward_kernel, 2, project_s, (width,), False, patches)[0]
     mixed_s = flat(feed.tick("mixed_s", mixed_s))
-    grad_low = flat(target(mixed_s))
     after_s = after_t + (nn(mixed_s, feed.out_s) + shifts32[5])
     normed_m = layer_norm(after_s, gains32[2], shifts32[2])
     hidden_pre = nt(normed_m, feed.in_m) + shifts32[6:].reshape(-1)
@@ -600,18 +650,12 @@
     grad_project_t = feed.tick("grad_project_t", flat(grad_project_t))
     grads["in_t"] = tn(grad_project_t, normed_t).astype(BF16)
     grad_project_t = feed.tick("in_t", grad_project_t)
-    part, g_t, b_t = norm_backward(start, gains32[0], nn(grad_project_t, feed.in_t))
+    hook = lambda *sums: feed.tick("dx_t", *sums)
+    part, g_t, b_t = norm_backward(start, gains32[0], nn(grad_project_t, feed.in_t), hook)
     grad_clip = (grad_t + part.astype(BF16).astype(F32)).astype(BF16)
-    grad_clip, g_t, b_t, s_time = feed.tick("grad_clip", grad_clip, g_t, b_t, s_time)
-    small = jnp.concatenate(
-        [
-            jnp.stack([g_t, g_s, g_m, b_t, b_s, b_m, s_time, s_fc, s_space], axis=0),
-            s_hidden,
-            s_dense[None, :],
-        ],
-        axis=0,
-    )
-    return (output, leave(grad_clip.reshape(shape)).astype(F32)) + feed.total(small)
+    parts = [g_t, g_s, g_m, b_t, b_s, b_m, s_time, s_fc, s_space, s_hidden, s_dense]
+    grad_clip, *parts = feed.tick("grad_clip", grad_clip, *[part.reshape(-1, width) for part in parts])
+    return (output, leave(grad_clip.reshape(shape)).astype(F32)) + feed.total(parts)
 
 
 def shards(clips_in, cotangent, clip_live, weights_in, weights_out, norm_gain, shift_rows, dense_shift):
@@ -636,7 +680,7 @@
     feed = (Staged if staged else Whole)(both, weights_in, weights_out, packed, width)
     clip = enter(clips_in)
     if staged:
-        feed.begin()
+        clip = feed.begin(clip)
     live = lax.dynamic_slice(clip_live, (lax.axis_index("seq") * own,), (own,)).astype(BF16)
 
     def target(after):

time: 684 us -> 719 us (1.051)
  matrix products: 183 us -> 211 us
  other arithmetic: 56.3 us -> 77.9 us
  Pallas kernels: 157 us -> 139 us
  starting transfers between devices: 90.7 us -> 105 us
  local copies, waits for them, and re-layouts: 60 us -> 46.4 us
    ppermute x0 -> x9, waiting for transfers between devices: none -> 23.4 us  [the longest x6 23.4 us: towards(): pieces.append(lax.ppermute(block, self.axes, pairs))]
    ppermute x61 -> x66, waiting for transfers between devices: 76.7 us -> 57.1 us  [flip(): return lax.ppermute(x, self.axes, [(d, d ^ bits) for d in range(32)])]
    unnamed x232 -> x134, local copies, waits for them, and re-layouts: 36.7 us -> 17.2 us
    ppermute x12 -> x3, waiting for transfers between devices: 40.9 us -> 23.2 us  [shift(): lax.ppermute(x, self.axes, [(d, (d + 8 * step) % 32) for d in range(32)])]
    all_to_all x1 -> x4, starting transfers between devices: 5.82 us -> 23.2 us  [the longest x3 19.7 us: planes_exchange(): lax.all_to_all(blocks, self.axes, split_axis=0, concat_axis=0, axis_index...]
    all_to_all x1 -> x4, waiting for transfers between devices: 4.81 us -> 21.7 us  [the longest x3 15.2 us: planes_exchange(): lax.all_to_all(blocks, self.axes, split_axis=0, concat_axis=0, axis_index...]
    ppermute x12 -> x3, starting transfers between devices: 22.2 us -> 7.27 us  [shift(): lax.ppermute(x, self.axes, [(d, (d + 8 * step) % 32) for d in range(32)])]
    dot_general x8, matrix products: 53.4 us -> 64.8 us  [tn(): lax.dot_general(left, right, (((0,), (0,)), ((), ())), preferred_element_...]
  transfers between devices with their start and end apart: 78 -> 86, of which waited for: 18 -> 16; matrix products, arithmetic and copies ran while one was open for 33% -> 42% of each run, Pallas kernels for 19% -> 18%
where the time goes in v5:
time: 719 us; the launch traced here: 708 us
  matrix products  211 us (29%)
  Pallas kernels  139 us (19%)
  waiting for transfers between devices  125 us (17%)
  starting transfers between devices  105 us (15%)
  other arithmetic  77.9 us (11%)
  local copies, waits for them, and re-layouts  46.4 us (6%)
    pallas_call x4, Pallas kernels, attention_call(): pl.pallas_call(partial(kernel, group, patches, count), grid=(clips, steps...  84.7 us
    dot_general x9, matrix products, nt(): lax.dot_general(left, right, (((1,), (1,)), ((), ())), preferred_element_...  75.1 us
    dot_general x8, matrix products, nn(): lax.dot_general(left, right, (((1,), (0,)), ((), ())), preferred_element_...  71 us
    dot_general x8, matrix products, tn(): lax.dot_general(left, right, (((0,), (0,)), ((), ())), preferred_element_...  64.8 us
    ppermute x66, waiting for transfers between devices, flip(): return lax.ppermute(x, self.axes, [(d, d ^ bits) for d in range(32)])  57.1 us
    ppermute x66, starting transfers between devices, flip(): return lax.ppermute(x, self.axes, [(d, d ^ bits) for d in range(32)])  48.2 us
    pallas_call x7, Pallas kernels, place(): pl.pallas_call(partial(place_kernel, tuple((tuple(e) for e in outs_plan))...  33.1 us
    ppermute x6, waiting for transfers between devices, towards(): pieces.append(lax.ppermute(block, self.axes, pairs))  23.4 us
  transfers between devices with their start and end apart: 86, of which 16 were waited for; matrix products, arithmetic and copies ran while one was open for 42% of the time, Pallas kernels for 18%

profile of v5, /device:TPU:0, one launch (start us, length us, event | category | flops | bytes accessed | tf_op | source)
XLA Modules:
  0.0 708.5 jit_solution(2855261685334411966)
XLA Ops:
  15.3 21.7 %collective-permute-done.1 = bf16[248,768]{1,0:T(8,128)(2,1)S(1)} collective-permute-done((bf16[248,768]{1,0:T(8,128)(2,1)S(1)}, bf16[248,768]{1,0:T(8,128)(2,1)S(1)}, u32[]{:S(2)}, u32[]{:S(2)}) %collective-permute-start.1) | collective-permute-done | bytes 380960 | tf_op jit(solution)/shard_map/ppermute | solution.py:332
  45.8 11.0 %all-to-all-start.1 = ((bf16[4,168,768]{2,1,0:T(8,128)(2,1)}), bf16[4,168,768]{2,1,0:T(8,128)(2,1)}, u32[]{:S(2)}, u32[]{:S(2)}) async-start(bf16[4,168,768]{2,1,0:T(8,128)(2,1)} %broadcast_in_dim.8), calls=%async_computation.1 | async-start | bytes 2064384 | tf_op jit(solution)/shard_map/all_to_all | solution.py:346
  61.3 9.1 %collective-permute-done.5 = bf16[272,768]{1,0:T(8,128)(2,1)} collective-permute-done((bf16[272,768]{1,0:T(8,128)(2,1)S(1)}, bf16[272,768]{1,0:T(8,128)(2,1)}, u32[]{:S(2)}, u32[]{:S(2)}) %collective-permute-start.5) | collective-permute-done | bytes 417824 | tf_op jit(solution)/shard_map/ppermute | solution.py:329
  70.3 7.9 %collective-permute-done.4 = bf16[272,768]{1,0:T(8,128)(2,1)} collective-permute-done((bf16[272,768]{1,0:T(8,128)(2,1)S(1)}, bf16[272,768]{1,0:T(8,128)(2,1)}, u32[]{:S(2)}, u32[]{:S(2)}) %collective-permute-start.4) | collective-permute-done | bytes 417824 | tf_op jit(solution)/shard_map/ppermute | solution.py:329
  99.6 7.5 %convolution_convert_fusion = bf16[1664,1920]{1,0:T(8,128)(2,1)} fusion(bf16[1664,768]{1,0:T(8,128)(2,1)S(1)} %bitcast.316, bf16[1920,768]{1,0:T(8,128)(2,1)S(1)} %bitcast.347), kind=kOutput, calls=%fused_computation.10 | convolution fusion | flops 4910530560 | bytes 11894784 | tf_op jit(solution)/shard_map/dot_general | solution.py:23
  116.5 6.0 shard_map.137
  126.9 16.0 %shard_map.138 = bf16[1,8,208,768]{3,2,1,0:T(8,128)(2,1)} custom-call(bf16[1,8,208,1920]{3,2,1,0:T(8,128)(2,1)} %bitcast.355, bf16[1,8,208,384]{3,2,1,0:T(8,128)(2,1)} %bitcast.373), custom_call_target="tpu_custom_call" | custom-call | flops 14976000000 | tf_op jit(solution)/shard_map/pallas_call | solution.py:135
  166.8 8.4 %convolution_convert_fusion.1 = bf16[1664,1536]{1,0:T(8,128)(2,1)} fusion(bf16[1664,768]{1,0:T(8,128)(2,1)S(1)} %add_convert_fusion.3, bf16[3840,768]{1,0:T(8,128)(2,1)} %bitcast.293), kind=kOutput, calls=%fused_computation.11 | convolution fusion | flops 3928424448 | bytes 10027008 | tf_op jit(solution)/shard_map/dot_general | solution.py:23
  196.7 15.9 %shard_map.141 = bf16[1,8,208,768]{3,2,1,0:T(8,128)(2,1)} custom-call(bf16[1,8,208,1536]{3,2,1,0:T(8,128)(2,1)} %bitcast.357, bf16[1,8,208,768]{3,2,1,0:T(8,128)(2,1)} %bitcast.367), custom_call_target="tpu_custom_call" | custom-call | flops 14976000000 | tf_op jit(solution)/shard_map/pallas_call | solution.py:135
  212.6 16.2 %collective-permute-done.31 = bf16[240,768]{1,0:T(8,128)(2,1)} collective-permute-done((bf16[240,768]{1,0:T(8,128)(2,1)}, bf16[240,768]{1,0:T(8,128)(2,1)}, u32[]{:S(2)}, u32[]{:S(2)}) %collective-permute-start.31) | collective-permute-done | bytes 368672 | tf_op jit(solution)/shard_map/ppermute | solution.py:329
  243.4 5.9 shard_map.142
  249.3 19.9 %fusion.4 = (bf16[1664,3072]{1,0:T(8,128)(2,1)}, bf16[1664,3072]{1,0:T(8,128)(2,1)}) fusion(f32[3072]{0:T(1024)S(1)} %add.443, bf16[3840,768]{1,0:T(8,128)(2,1)} %bitcast.296, f32[1664,768]{1,0:T(8,128)} %copy-done.5, f32[768]{0:T(1024)S(1)} %add.440, f32[768]{0:T(1024)S(1)} %mul.263, f32[1664]{0:T(1024)S(1)} %add_rsqrt_fusion, ...), kind=kOutput, calls=%fused_computation.5 | convolution fusion | flops 7919468544 | bytes 30309376 | tf_op jit(solution)/shard_map/dot_general | solution.py:23
  272.8 13.9 %fusion.35.refs_0_.refs_3_ = bf16[384,8,768]{2,1,0:T(8,128)(2,1)} fusion(bf16[1664,3072]{1,0:T(8,128)(2,1)} %get-tuple-element.183, bf16[1664,768]{1,0:T(8,128)(2,1)S(1)} %bitcast.281), kind=kOutput, calls=%fused_computation.80 | convolution fusion | flops 7854096384 | bytes 17498112 | tf_op jit(solution)/shard_map/dot_general | solution.py:31
  290.9 6.2 shard_map.144
  297.1 12.9 %add_convert_fusion.1 = bf16[1664,768]{1,0:T(8,128)(2,1)S(1)} fusion(f32[1664,768]{1,0:T(8,128)} %copy-done.5, bf16[1664,3072]{1,0:T(8,128)(2,1)} %get-tuple-element.183, bf16[4032,768]{1,0:T(8,128)(2,1)} %bitcast.290, f32[768]{0:T(1024)S(1)} %add.450), kind=kOutput, calls=%fused_computation.43 | convolution fusion | flops 7855570944 | bytes 22612992 | tf_op jit(solution)/shard_map/dot_general | solution.py:27
  316.4 14.7 %multiply_convert_fusion = bf16[1664,3072]{1,0:T(8,128)(2,1)} fusion(bf16[1664,3072]{1,0:T(8,128)(2,1)} %get-tuple-element.190, bf16[1664,768]{1,0:T(8,128)(2,1)S(1)} %bitcast.282, bf16[4032,768]{1,0:T(8,128)(2,1)} %bitcast.291), kind=kOutput, calls=%fused_computation.7 | convolution fusion | flops 7867072512 | bytes 27721728 | tf_op jit(solution)/shard_map/dot_general | solution.py:23
  337.6 15.1 %fusion.36.refs_0_.refs_1_ = bf16[384,8,768]{2,1,0:T(8,128)(2,1)} fusion(bf16[1664,3072]{1,0:T(8,128)(2,1)} %multiply_convert_fusion, f32[1664,768]{1,0:T(8,128)} %copy-done.5, f32[768]{0:T(1024)S(1)} %add.440, f32[768]{0:T(1024)S(1)} %mul.263, f32[1664]{0:T(1024)S(1)} %add_rsqrt_fusion, f32[1664]{0:T(1024)S(1)} %broadcast_multiply_fusion.6), kind=kOutput, calls=%fused_computation.81 | convolution fusion | flops 7860486144 | bytes 20073472 | tf_op jit(solution)/shard_map/dot_general | solution.py:31
  355.5 15.5 %multiply_reduce_fusion = (f32[768]{0:T(1024)S(1)}, f32[1664]{0:T(1024)S(1)}, f32[1664]{0:T(1024)S(1)}, f32[768]{0:T(1024)S(1)}, f32[1664,768]{1,0:T(8,128)S(1)}) fusion(f32[1664,768]{1,0:T(8,128)} %copy-done.5, f32[1664]{0:T(1024)S(1)} %add_rsqrt_fusion, f32[1664]{0:T(1024)S(1)} %broadcast_multiply_fusion.6, f32[768]{0:T(1024)S(1)} %mul.263, ...), kind=kOutput, calls=%fused_computation.38 | convolution fusion | flops 7863233536 | bytes 25201664 | tf_op jit(solution)/shard_map/dot_general | solution.py:27
  388.9 26.3 %shard_map.146 = (bf16[1,8,208,1536]{3,2,1,0:T(8,128)(2,1)}, bf16[1,8,208,768]{3,2,1,0:T(8,128)(2,1)}) custom-call(bf16[1,8,208,1536]{3,2,1,0:T(8,128)(2,1)} %bitcast.358, bf16[1,8,208,768]{3,2,1,0:T(8,128)(2,1)} %bitcast.368, bf16[1,8,208,768]{3,2,1,0:T(8,128)(2,1)} %bitcast.371), custom_call_target="tpu_custom_call" | custom-call | flops 23296000000 | tf_op jit(solution)/shard_map/pallas_call | solution.py:135
  423.4 6.7 fusion.43.refs_2_
  430.2 6.0 convolution_convert_fusion.9
  441.2 5.8 fusion.46
  447.0 8.8 %multiply_reduce_fusion.1 = (f32[768]{0:T(1024)S(1)}, f32[1664]{0:T(1024)S(1)}, f32[1664]{0:T(1024)S(1)}, f32[768]{0:T(1024)S(1)}, f32[1664,768]{1,0:T(8,128)S(1)}) fusion(f32[1664]{0:T(1024)S(1)} %copy-done.48, f32[1664]{0:T(1024)S(1)} %copy-done.42, bf16[1664,768]{1,0:T(8,128)(2,1)S(1)} %copy-done.3, bf16[1,8,208,768]{3,2,1,0:T(8,128)(2,1)S(1)} %copy-done.1, ...), kind=kOutput, calls=%fused_computation.39 | convolution fusion | flops 3942477056 | bytes 22842368 | tf_op jit(solution)/shard_map/dot_general | solution.py:27
  505.7 26.5 %shard_map.150 = bf16[1,8,208,2304]{3,2,1,0:T(8,128)(2,1)} custom-call(bf16[1,8,208,1920]{3,2,1,0:T(8,128)(2,1)} %bitcast.356, bf16[1,8,208,384]{3,2,1,0:T(8,128)(2,1)} %bitcast.374, bf16[1,8,208,768]{3,2,1,0:T(8,128)(2,1)} %bitcast.372), custom_call_target="tpu_custom_call" | custom-call | flops 23296000000 | tf_op jit(solution)/shard_map/pallas_call | solution.py:135
  532.9 11.0 %fusion.39.refs_0_ = bf16[288,8,768]{2,1,0:T(8,128)(2,1)} fusion(bf16[1664,2304]{1,0:T(8,128)(2,1)} %bitcast.353, bf16[1664,768]{1,0:T(8,128)(2,1)} %fusion.17), kind=kOutput, calls=%fused_computation.85 | convolution fusion | flops 5890572288 | bytes 13762560 | tf_op jit(solution)/shard_map/dot_general | solution.py:31
  575.7 10.5 %collective-permute-done.64 = bf16[336,768]{1,0:T(8,128)(2,1)} collective-permute-done((bf16[336,768]{1,0:T(8,128)(2,1)}, bf16[336,768]{1,0:T(8,128)(2,1)}, u32[]{:S(2)}, u32[]{:S(2)}) %collective-permute-start.64) | collective-permute-done | bytes 516128 | tf_op jit(solution)/shard_map/ppermute | solution.py:329
  587.6 13.7 %fusion.19 = (f32[768]{0:T(1024)S(1)}, f32[1664]{0:T(1024)S(1)}, f32[1664]{0:T(1024)S(1)}, f32[768]{0:T(1024)S(1)}, f32[1664,768]{1,0:T(8,128)}) fusion(bf16[1,8,208,768]{3,2,1,0:T(8,128)(2,1)S(1)} %copy-done.1, f32[1664]{0:T(1024)S(1)} %copy-done.46, f32[1664]{0:T(1024)S(1)} %copy-done.44, f32[768]{0:T(1024)S(1)} %copy-done.50, ...), kind=kOutput, calls=%fused_computation.30 | convolution fusion | flops 5901577216 | bytes 18910208 | tf_op jit(solution)/shard_map/dot_general | solution.py:27
  617.9 6.5 all-to-all-done.5
  636.2 6.0 add_convert_fusion
  642.1 5.8 collective-permute-done.67
  647.9 6.6 all-to-all-done.6
  678.6 23.4 %collective-permute-done.73 = bf16[240,768]{1,0:T(8,128)(2,1)S(1)} collective-permute-done((bf16[240,768]{1,0:T(8,128)(2,1)}, bf16[240,768]{1,0:T(8,128)(2,1)S(1)}, u32[]{:S(2)}, u32[]{:S(2)}) %collective-permute-start.73) | collective-permute-done | bytes 368672 | tf_op jit(solution)/shard_map/ppermute | solution.py:517
  (427 shorter events, 317.9 us)
Async XLA Ops:
  0.6 44.1 %all-to-all-start = ((bf16[4,2,196,768]{3,1,2,0:T(2,128)(2,1)}), bf16[4,2,196,768]{3,1,2,0:T(2,128)(2,1)S(1)}, u32[]{:S(2)}, u32[]{:S(2)}) async-start(bf16[4,2,196,768]{3,1,2,0:T(2,128)(2,1)} %param.8), calls=%async_computation | async-start | bytes 4816896 | tf_op jit(solution)/shard_map/all_to_all | solution.py:672
  7.5 29.5 %collective-permute-start.1 = (bf16[248,768]{1,0:T(8,128)(2,1)S(1)}, bf16[248,768]{1,0:T(8,128)(2,1)S(1)}, u32[]{:S(2)}, u32[]{:S(2)}) collective-permute-start(bf16[248,768]{1,0:T(8,128)(2,1)S(1)} %get-tuple-element.362), channel_id=1, source_target_pairs={{0,16},{1,17},{2,18},{3,19},{4,20},{5,21},{6,22},{7,23},{8,24},{9,... | collective-permute-start | bytes 1142792 | tf_op jit(solution)/shard_map/ppermute | solution.py:332
  45.8 37.3 %all-to-all-start.1 = ((bf16[4,168,768]{2,1,0:T(8,128)(2,1)}), bf16[4,168,768]{2,1,0:T(8,128)(2,1)}, u32[]{:S(2)}, u32[]{:S(2)}) async-start(bf16[4,168,768]{2,1,0:T(8,128)(2,1)} %broadcast_in_dim.8), calls=%async_computation.1 | async-start | bytes 2064384 | tf_op jit(solution)/shard_map/all_to_all | solution.py:346
  112.9 29.9 %collective-permute-start.19 = (bf16[336,768]{1,0:T(8,128)(2,1)S(1)}, bf16[336,768]{1,0:T(8,128)(2,1)}, u32[]{:S(2)}, u32[]{:S(2)}) collective-permute-start(bf16[336,768]{1,0:T(8,128)(2,1)S(1)} %bitcast.298), channel_id=1, source_target_pairs={{0,6},{1,7},{2,4},{3,5},{4,2},{5,3},{6,0},{7,1},{8,14},{9,15},{10,... | collective-permute-start | bytes 1548296 | tf_op jit(solution)/shard_map/ppermute | solution.py:329
  115.3 27.6 %collective-permute-start.18 = (bf16[336,768]{1,0:T(8,128)(2,1)S(1)}, bf16[336,768]{1,0:T(8,128)(2,1)}, u32[]{:S(2)}, u32[]{:S(2)}) collective-permute-start(bf16[336,768]{1,0:T(8,128)(2,1)S(1)} %bitcast.299), channel_id=1, source_target_pairs={{0,4},{1,5},{2,6},{3,7},{4,0},{5,1},{6,2},{7,3},{8,12},{9,13},{10,... | collective-permute-start | bytes 1548296 | tf_op jit(solution)/shard_map/ppermute | solution.py:329
  115.8 27.1 %collective-permute-start.17 = (bf16[336,768]{1,0:T(8,128)(2,1)S(1)}, bf16[336,768]{1,0:T(8,128)(2,1)}, u32[]{:S(2)}, u32[]{:S(2)}) collective-permute-start(bf16[336,768]{1,0:T(8,128)(2,1)S(1)} %bitcast.300), channel_id=1, source_target_pairs={{0,2},{1,3},{2,0},{3,1},{4,6},{5,7},{6,4},{7,5},{8,10},{9,11},{10,... | collective-permute-start | bytes 1548296 | tf_op jit(solution)/shard_map/ppermute | solution.py:329
  146.2 29.0 %collective-permute-start.26 = (bf16[240,768]{1,0:T(8,128)(2,1)S(1)}, bf16[240,768]{1,0:T(8,128)(2,1)}, u32[]{:S(2)}, u32[]{:S(2)}) collective-permute-start(bf16[240,768]{1,0:T(8,128)(2,1)S(1)} %copy-done.10), channel_id=1, source_target_pairs={{0,6},{1,7},{2,4},{3,5},{4,2},{5,3},{6,0},{7,1},{8,14},{9,15},{10,... | collective-permute-start | bytes 1105928 | tf_op jit(solution)/shard_map/ppermute | solution.py:329
  148.6 26.7 %collective-permute-start.25 = (bf16[240,768]{1,0:T(8,128)(2,1)S(1)}, bf16[240,768]{1,0:T(8,128)(2,1)S(1)}, u32[]{:S(2)}, u32[]{:S(2)}) collective-permute-start(bf16[240,768]{1,0:T(8,128)(2,1)S(1)} %copy-done.10), channel_id=1, source_target_pairs={{0,4},{1,5},{2,6},{3,7},{4,0},{5,1},{6,2},{7,3},{8,12},{9,13},{10,... | collective-permute-start | bytes 1105928 | tf_op jit(solution)/shard_map/ppermute | solution.py:329
  149.1 26.2 %collective-permute-start.24 = (bf16[240,768]{1,0:T(8,128)(2,1)S(1)}, bf16[240,768]{1,0:T(8,128)(2,1)}, u32[]{:S(2)}, u32[]{:S(2)}) collective-permute-start(bf16[240,768]{1,0:T(8,128)(2,1)S(1)} %copy-done.10), channel_id=1, source_target_pairs={{0,2},{1,3},{2,0},{3,1},{4,6},{5,7},{6,4},{7,5},{8,10},{9,11},{10,... | collective-permute-start | bytes 1105928 | tf_op jit(solution)/shard_map/ppermute | solution.py:329
  179.0 91.3 %all-to-all-start.2 = ((bf16[4,2,196,768]{3,1,2,0:T(2,128)(2,1)}), bf16[4,2,196,768]{3,1,2,0:T(2,128)(2,1)}, u32[]{:S(2)}, u32[]{:S(2)}) async-start(bf16[4,2,196,768]{3,1,2,0:T(2,128)(2,1)} %param.9), calls=%async_computation.2 | async-start | bytes 4816896 | tf_op jit(solution)/shard_map/all_to_all | solution.py:672
  184.0 28.6 %collective-permute-start.33 = (bf16[240,768]{1,0:T(8,128)(2,1)}, bf16[240,768]{1,0:T(8,128)(2,1)}, u32[]{:S(2)}, u32[]{:S(2)}) collective-permute-start(bf16[240,768]{1,0:T(8,128)(2,1)} %get-tuple-element.178), channel_id=1, source_target_pairs={{0,6},{1,7},{2,4},{3,5},{4,2},{5,3},{6,0},{7,1},{8,14},{9,15},{10,... | collective-permute-start | bytes 1105928 | tf_op jit(solution)/shard_map/ppermute | solution.py:329
  187.5 41.3 %collective-permute-start.31 = (bf16[240,768]{1,0:T(8,128)(2,1)}, bf16[240,768]{1,0:T(8,128)(2,1)}, u32[]{:S(2)}, u32[]{:S(2)}) collective-permute-start(bf16[240,768]{1,0:T(8,128)(2,1)} %get-tuple-element.178), channel_id=1, source_target_pairs={{0,2},{1,3},{2,0},{3,1},{4,6},{5,7},{6,4},{7,5},{8,10},{9,11},{10,... | collective-permute-start | bytes 1105928 | tf_op jit(solution)/shard_map/ppermute | solution.py:329
  229.8 39.4 %collective-permute-start.40 = (bf16[336,768]{1,0:T(8,128)(2,1)S(1)}, bf16[336,768]{1,0:T(8,128)(2,1)}, u32[]{:S(2)}, u32[]{:S(2)}) collective-permute-start(bf16[336,768]{1,0:T(8,128)(2,1)S(1)} %bitcast.320), channel_id=1, source_target_pairs={{0,6},{1,7},{2,4},{3,5},{4,2},{5,3},{6,0},{7,1},{8,14},{9,15},{10,... | collective-permute-start | bytes 1548296 | tf_op jit(solution)/shard_map/ppermute | solution.py:329
  239.5 29.7 %collective-permute-start.39 = (bf16[336,768]{1,0:T(8,128)(2,1)S(1)}, bf16[336,768]{1,0:T(8,128)(2,1)}, u32[]{:S(2)}, u32[]{:S(2)}) collective-permute-start(bf16[336,768]{1,0:T(8,128)(2,1)S(1)} %bitcast.321), channel_id=1, source_target_pairs={{0,4},{1,5},{2,6},{3,7},{4,0},{5,1},{6,2},{7,3},{8,12},{9,13},{10,... | collective-permute-start | bytes 1548296 | tf_op jit(solution)/shard_map/ppermute | solution.py:329
  240.2 29.0 %collective-permute-start.38 = (bf16[336,768]{1,0:T(8,128)(2,1)S(1)}, bf16[336,768]{1,0:T(8,128)(2,1)}, u32[]{:S(2)}, u32[]{:S(2)}) collective-permute-start(bf16[336,768]{1,0:T(8,128)(2,1)S(1)} %bitcast.322), channel_id=1, source_target_pairs={{0,2},{1,3},{2,0},{3,1},{4,6},{5,7},{6,4},{7,5},{8,10},{9,11},{10,... | collective-permute-start | bytes 1548296 | tf_op jit(solution)/shard_map/ppermute | solution.py:329
  290.8 40.3 %collective-permute-start.45 = (bf16[4,336,768]{2,1,0:T(8,128)(2,1)}, bf16[4,336,768]{2,1,0:T(8,128)(2,1)}, u32[]{:S(2)}, u32[]{:S(2)}) collective-permute-start(bf16[4,336,768]{2,1,0:T(8,128)(2,1)} %bitcast.349), channel_id=1, source_target_pairs={{0,1},{1,0},{2,3},{3,2},{4,5},{5,4},{6,7},{7,6},{8,9},{9,8},{10,11... | collective-permute-start | bytes 6193160 | tf_op jit(solution)/shard_map/ppermute | solution.py:329
  311.6 71.2 %all-to-all-start.3 = ((bf16[1,8,196,768]{3,2,0,1:T(8,128)(2,1)}), bf16[1,8,196,768]{3,2,0,1:T(8,128)(2,1)}, u32[]{:S(2)}, u32[]{:S(2)}) async-start(bf16[1,8,196,768]{3,2,0,1:T(8,128)(2,1)} %slice.239), calls=%async_computation.3 | async-start | bytes 4915200 | tf_op jit(solution)/shard_map/all_to_all | solution.py:677
  334.1 48.8 %collective-permute-start.48 = (bf16[336,768]{1,0:T(8,128)(2,1)}, bf16[336,768]{1,0:T(8,128)(2,1)}, u32[]{:S(2)}, u32[]{:S(2)}) collective-permute-start(bf16[336,768]{1,0:T(8,128)(2,1)} %get-tuple-element.332), channel_id=1, source_target_pairs={{0,6},{1,7},{2,4},{3,5},{4,2},{5,3},{6,0},{7,1},{8,14},{9,15},{10,... | collective-permute-start | bytes 1548296 | tf_op jit(solution)/shard_map/ppermute | solution.py:329
  336.9 45.9 %collective-permute-start.47 = (bf16[336,768]{1,0:T(8,128)(2,1)}, bf16[336,768]{1,0:T(8,128)(2,1)}, u32[]{:S(2)}, u32[]{:S(2)}) collective-permute-start(bf16[336,768]{1,0:T(8,128)(2,1)} %get-tuple-element.333), channel_id=1, source_target_pairs={{0,4},{1,5},{2,6},{3,7},{4,0},{5,1},{6,2},{7,3},{8,12},{9,13},{10,... | collective-permute-start | bytes 1548296 | tf_op jit(solution)/shard_map/ppermute | solution.py:329
  337.5 45.3 %collective-permute-start.46 = (bf16[336,768]{1,0:T(8,128)(2,1)}, bf16[336,768]{1,0:T(8,128)(2,1)}, u32[]{:S(2)}, u32[]{:S(2)}) collective-permute-start(bf16[336,768]{1,0:T(8,128)(2,1)} %get-tuple-element.334), channel_id=1, source_target_pairs={{0,2},{1,3},{2,0},{3,1},{4,6},{5,7},{6,4},{7,5},{8,10},{9,11},{10,... | collective-permute-start | bytes 1548296 | tf_op jit(solution)/shard_map/ppermute | solution.py:329
  385.4 29.8 %collective-permute-start.52 = (bf16[240,768]{1,0:T(8,128)(2,1)}, bf16[240,768]{1,0:T(8,128)(2,1)}, u32[]{:S(2)}, u32[]{:S(2)}) collective-permute-start(bf16[240,768]{1,0:T(8,128)(2,1)} %get-tuple-element.346), channel_id=1, source_target_pairs={{0,6},{1,7},{2,4},{3,5},{4,2},{5,3},{6,0},{7,1},{8,14},{9,15},{10,... | collective-permute-start | bytes 1105928 | tf_op jit(solution)/shard_map/ppermute | solution.py:329
  388.3 27.0 %collective-permute-start.51 = (bf16[240,768]{1,0:T(8,128)(2,1)}, bf16[240,768]{1,0:T(8,128)(2,1)}, u32[]{:S(2)}, u32[]{:S(2)}) collective-permute-start(bf16[240,768]{1,0:T(8,128)(2,1)} %get-tuple-element.347), channel_id=1, source_target_pairs={{0,4},{1,5},{2,6},{3,7},{4,0},{5,1},{6,2},{7,3},{8,12},{9,13},{10,... | collective-permute-start | bytes 1105928 | tf_op jit(solution)/shard_map/ppermute | solution.py:329
  388.9 26.4 %collective-permute-start.50 = (bf16[240,768]{1,0:T(8,128)(2,1)}, bf16[240,768]{1,0:T(8,128)(2,1)}, u32[]{:S(2)}, u32[]{:S(2)}) collective-permute-start(bf16[240,768]{1,0:T(8,128)(2,1)} %get-tuple-element.348), channel_id=1, source_target_pairs={{0,2},{1,3},{2,0},{3,1},{4,6},{5,7},{6,4},{7,5},{8,10},{9,11},{10,... | collective-permute-start | bytes 1105928 | tf_op jit(solution)/shard_map/ppermute | solution.py:329
  437.6 26.6 %collective-permute-start.56 = (bf16[240,768]{1,0:T(8,128)(2,1)}, bf16[240,768]{1,0:T(8,128)(2,1)S(1)}, u32[]{:S(2)}, u32[]{:S(2)}) collective-permute-start(bf16[240,768]{1,0:T(8,128)(2,1)} %get-tuple-element.342), channel_id=1, source_target_pairs={{0,6},{1,7},{2,4},{3,5},{4,2},{5,3},{6,0},{7,1},{8,14},{9,15},{10,... | collective-permute-start | bytes 1105928 | tf_op jit(solution)/shard_map/ppermute | solution.py:329
  497.1 35.0 %collective-permute-start.61 = (bf16[240,768]{1,0:T(8,128)(2,1)}, bf16[240,768]{1,0:T(8,128)(2,1)S(1)}, u32[]{:S(2)}, u32[]{:S(2)}) collective-permute-start(bf16[240,768]{1,0:T(8,128)(2,1)} %get-tuple-element.338), channel_id=1, source_target_pairs={{0,6},{1,7},{2,4},{3,5},{4,2},{5,3},{6,0},{7,1},{8,14},{9,15},{10,... | collective-permute-start | bytes 1105928 | tf_op jit(solution)/shard_map/ppermute | solution.py:329
  500.1 32.1 %collective-permute-start.60 = (bf16[240,768]{1,0:T(8,128)(2,1)}, bf16[240,768]{1,0:T(8,128)(2,1)}, u32[]{:S(2)}, u32[]{:S(2)}) collective-permute-start(bf16[240,768]{1,0:T(8,128)(2,1)} %get-tuple-element.339), channel_id=1, source_target_pairs={{0,4},{1,5},{2,6},{3,7},{4,0},{5,1},{6,2},{7,3},{8,12},{9,13},{10,... | collective-permute-start | bytes 1105928 | tf_op jit(solution)/shard_map/ppermute | solution.py:329
  500.7 31.5 %collective-permute-start.59 = (bf16[240,768]{1,0:T(8,128)(2,1)}, bf16[240,768]{1,0:T(8,128)(2,1)}, u32[]{:S(2)}, u32[]{:S(2)}) collective-permute-start(bf16[240,768]{1,0:T(8,128)(2,1)} %get-tuple-element.340), channel_id=1, source_target_pairs={{0,2},{1,3},{2,0},{3,1},{4,6},{5,7},{6,4},{7,5},{8,10},{9,11},{10,... | collective-permute-start | bytes 1105928 | tf_op jit(solution)/shard_map/ppermute | solution.py:329
  565.9 39.1 %all-to-all-start.4 = ((bf16[4,240,768]{2,1,0:T(8,128)(2,1)}), bf16[4,240,768]{2,1,0:T(8,128)(2,1)}, u32[]{:S(2)}, u32[]{:S(2)}) async-start(bf16[4,240,768]{2,1,0:T(8,128)(2,1)} %pad_maximum_fusion), calls=%async_computation.4 | async-start | bytes 2949120 | tf_op jit(solution)/shard_map/all_to_all | solution.py:346
  624.5 30.0 %all-to-all-start.6 = ((bf16[4,168,768]{2,1,0:T(8,128)(2,1)}), bf16[4,168,768]{2,1,0:T(8,128)(2,1)}, u32[]{:S(2)}, u32[]{:S(2)}) async-start(bf16[4,168,768]{2,1,0:T(8,128)(2,1)} %pad_maximum_fusion.1), calls=%async_computation.6 | async-start | bytes 2064384 | tf_op jit(solution)/shard_map/all_to_all | solution.py:346
  657.8 46.4 %all-to-all-start.7 = ((bf16[1,8,196,768]{3,2,0,1:T(8,128)(2,1)}), bf16[1,8,196,768]{3,2,0,1:T(8,128)(2,1)S(1)}, u32[]{:S(2)}, u32[]{:S(2)}) async-start(bf16[1,8,196,768]{3,2,0,1:T(8,128)(2,1)} %slice.245), calls=%async_computation.7 | async-start | bytes 4915200 | tf_op jit(solution)/shard_map/all_to_all | solution.py:677
  673.2 28.7 %collective-permute-start.73 = (bf16[240,768]{1,0:T(8,128)(2,1)}, bf16[240,768]{1,0:T(8,128)(2,1)S(1)}, u32[]{:S(2)}, u32[]{:S(2)}) collective-permute-start(bf16[240,768]{1,0:T(8,128)(2,1)} %slice.247), channel_id=1, source_target_pairs={{8,0},{9,1},{10,2},{11,3},{12,4},{13,5},{14,6},{15,7}} | collective-permute-start | bytes 1105928 | tf_op jit(solution)/shard_map/ppermute | solution.py:517
  674.5 27.4 %collective-permute-start.72 = (bf16[240,768]{1,0:T(8,128)(2,1)}, bf16[240,768]{1,0:T(8,128)(2,1)S(1)}, u32[]{:S(2)}, u32[]{:S(2)}) collective-permute-start(bf16[240,768]{1,0:T(8,128)(2,1)} %slice.247), channel_id=1, source_target_pairs={{16,0},{17,1},{18,2},{19,3},{20,4},{21,5},{22,6},{23,7}} | collective-permute-start | bytes 1105928 | tf_op jit(solution)/shard_map/ppermute | solution.py:517
  (120 other events, 1655.5 us)

commit v6 on v5

--- a/solution.py
+++ b/solution.py
@@ -186,7 +186,7 @@
         out_shape=[jax.ShapeDtypeStruct(s, BF16) for s in shapes],
         scratch_shapes=[pltpu.VMEM(s, BF16) for s in shapes]
         + [pltpu.SemaphoreType.DMA((slots,)), pltpu.SemaphoreType.DMA((slots,))],
-        compiler_params=pltpu.CompilerParams(vmem_limit_bytes=COPY_VMEM),
+        compiler_params=pltpu.CompilerParams(vmem_limit_bytes=size + (2 << 20)),
         cost_estimate=pl.CostEstimate(flops=0, bytes_accessed=4 * size, transcendentals=0),
     )(dest, *flat)
     return [out.reshape(out.shape[:2] + (-1, width)) for out in outs]
@@ -245,10 +245,46 @@
         out_shape=[half, half],
         scratch_shapes=[pltpu.VMEM((2 * squares, rows // 8, 8, width), BF16) for rows in plane_rows]
         + [pltpu.SemaphoreType.DMA((slots + len(parts),)), pltpu.SemaphoreType.DMA((slots,))],
-        compiler_params=pltpu.CompilerParams(vmem_limit_bytes=COPY_VMEM),
+        compiler_params=pltpu.CompilerParams(vmem_limit_bytes=size + (2 << 20)),
         cost_estimate=pl.CostEstimate(flops=0, bytes_accessed=4 * size, transcendentals=0),
     )(core, *arrays)
     return [out.reshape(squares, -1, width) for out in outs]
+
+
+def join_kernel(chunks, *refs):
+    parts, (out, held, in_sem, out_sem) = (refs[:-4], refs[-4:])
+    moves = []
+    for slot, (part, row) in enumerate(chunks):
+        size = held.shape[1]
+        fetch = pltpu.make_async_copy(parts[part].at[pl.ds(row, size)], held.at[slot], in_sem.at[slot])
+        fetch.start()
+        moves.append((fetch, pltpu.make_async_copy(held.at[slot], out.at[pl.ds(slot * size, size)], out_sem.at[slot])))
+    for fetch, write in moves:
+        fetch.wait()
+        write.start()
+    for _, write in moves:
+        write.wait()
+
+
+def join(parts, rows):
+    width = parts[0].shape[1]
+    chunks = [(k, row // 8) for k, part in enumerate(parts) for row in range(0, part.shape[0], rows)]
+    count = len(chunks)
+    anywhere = pl.BlockSpec(memory_space=pl.ANY)
+    out = pl.pallas_call(
+        partial(join_kernel, tuple(chunks)),
+        in_specs=[anywhere] * len(parts),
+        out_specs=anywhere,
+        out_shape=jax.ShapeDtypeStruct((count * rows // 8, 8, width), BF16),
+        scratch_shapes=[
+            pltpu.VMEM((count, rows // 8, 8, width), BF16),
+            pltpu.SemaphoreType.DMA((count,)),
+            pltpu.SemaphoreType.DMA((count,)),
+        ],
+        compiler_params=pltpu.CompilerParams(vmem_limit_bytes=COPY_VMEM),
+        cost_estimate=pl.CostEstimate(flops=0, bytes_accessed=8 * count * rows * width, transcendentals=0),
+    )(*[eights(part) for part in parts])
+    return out.reshape(-1, width)
 
 
 def pack_kernel(devices, *refs):
@@ -317,8 +353,10 @@
         self.spots = jnp.bitwise_xor(jnp.arange(8, dtype=jnp.int32), self.spot)
         self.planes = (self.plane + 4 - jnp.arange(4, dtype=jnp.int32)) % 4
         self.core_ref = self.core.astype(jnp.int32).reshape(1)
-        self.rows_in, self.rows_out = (weights_in.shape[0], weights_out.shape[0])
-        self.weights_out, self.count = (weights_out, packed.shape[0])
+        self.rows_in, self.count = (weights_in.shape[0], packed.shape[0])
+        full_out = lax.all_gather(weights_out, axes, axis=0, tiled=True)
+        self.out_t, self.out_f = (full_out[:width], full_out[width : 2 * width])
+        self.out_s, self.out_m = (full_out[2 * width : 3 * width], full_out[3 * width :])
         self.grads = {}
         flat = packed.reshape(1, -1)
         tail = jnp.pad(flat, ((0, 7), (0, width - flat.shape[1])))
@@ -359,15 +397,12 @@
         return out.reshape(-1, self.width)
 
     def begin(self, clip):
-        rows_in, rows_out, width = (self.rows_in, self.rows_out, self.width)
+        rows_in, width = (self.rows_in, self.width)
         smalls = self.column_small.reshape(-1, width)
         first = jnp.concatenate([self.column_in[0], smalls], axis=0)
         self.p1, self.p2, self.p3 = (self.column_in[k] for k in (1, 2, 3))
         p0 = self.over(first)
-        first, weights_out = tie(first, self.weights_out)
-        column = self.planes_exchange(jnp.broadcast_to(weights_out[None], (4,) + weights_out.shape))
-        p0, (clip, column) = tie(p0, (clip, column))
-        self.q01, self.q23 = (column[:2].reshape(-1, width), column[2:].reshape(-1, width))
+        p0, clip = tie(p0, clip)
         self.p0 = self.cores(p0)
         low, small = place([self.p0], [[(0, 0, rows_in)], [(0, rows_in, 32)]], self.spots)
         low, self.p1 = tie(low, self.p1)
@@ -380,47 +415,29 @@
 
     def tick(self, name, *values):
         single = len(values) == 1
-        rows_in, rows_out, width = (self.rows_in, self.rows_out, self.width)
+        rows_in, width = (self.rows_in, self.width)
         g = self.grads
         whole = lambda key: (g[key], 0, g[key].shape[0])
         if name == "query_t":
-            values, (self.p1, self.q01) = tie(values, (self.p1, self.q01))
-            self.q01 = self.over(self.q01)
+            values, (self.p1, self.p2) = tie(values, (self.p1, self.p2))
+            self.p2 = self.over(self.p2)
             self.p1 = self.cores(self.p1)
             low = self.lay([self.p0, self.p1], [(0, 0, rows_in), (1, 0, rows_in)])
             self.in_t, self.in_qk = (low[: 3 * width], low[3 * width :])
             self.in_b = self.in_t[5 * width // 2 :]
         elif name == "mixed_t":
-            values, (self.q01, self.p2) = tie(values, (self.q01, self.p2))
-            self.p2 = self.over(self.p2)
-            self.q01 = self.cores(self.q01)
-            early = self.lay([self.q01], [(0, 0, rows_out), (0, rows_out, rows_out)])
-            self.out_t, self.out_f, self.out_s = (early[k * width : (k + 1) * width] for k in range(3))
-        elif name == "query_s":
             values, (self.p2, self.p3) = tie(values, (self.p2, self.p3))
             self.p3 = self.over(self.p3)
+        elif name == "query_s":
             self.p2 = self.cores(self.p2)
             self.in_v = self.lay([self.p2], [(0, 0, rows_in)])[:width]
         elif name == "mixed_s":
-            values, (self.p3, self.q23) = tie(values, (self.p3, self.q23))
-            self.q23 = self.over(self.q23)
+            values, self.p3 = tie(values, self.p3)
             self.p3 = self.cores(self.p3)
             high = self.lay([self.p2, self.p3], [(0, 0, rows_in), (1, 0, rows_in)])
             self.in_m = high[width:]
         elif name == "hidden":
-            values, self.q23 = tie(values, self.q23)
-            self.q23 = self.cores(self.q23)
-            entries = [(0, rows_out, rows_out), (1, 0, rows_out), (1, rows_out, rows_out)]
-            self.out_m = self.lay([self.q01, self.q23], entries)[3 * width - 8 * rows_out :]
-        elif name == "out_m":
-            start = 16 * rows_out - 3 * width
-            d_out_m = g["out_m"]
-            self.kept, send = self.halve([(d_out_m, start, d_out_m.shape[0] - start)], (rows_out, rows_out))
-            values, send = tie(values, send)
-            self.other = self.flip(send, 1)
-        elif name == "grad_pre":
-            values, (self.kept, self.other) = tie(values, (self.kept, self.other))
-            self.d_q23 = self.across(self.kept, self.other)
+            values = lax.optimization_barrier(values)
         elif name == "in_m":
             start = 24 * rows_in - 6 * width
             d_in_m = g["in_m"]
@@ -428,8 +445,7 @@
             values, send = tie(values, send)
             self.other = self.flip(send, 1)
         elif name == "grad_mixed_s":
-            values, (self.d_q23, self.kept, self.other) = tie(values, (self.d_q23, self.kept, self.other))
-            self.d_q23 = self.gathered(self.d_q23)
+            values, (self.kept, self.other) = tie(values, (self.kept, self.other))
             self.d_p3 = self.across(self.kept, self.other)
         elif name == "grad_s":
             values, self.d_p3 = tie(values, self.d_p3)
@@ -452,15 +468,9 @@
         elif name == "out_t":
             values, (self.kept, self.other) = tie(values, (self.kept, self.other))
             self.d_p1 = self.across(self.kept, self.other)
-            start = 16 * rows_out - 3 * width
-            self.kept, send = self.halve(
-                [whole("out_t"), whole("out_f"), whole("out_s"), (g["out_m"], 0, start)], (rows_out, rows_out)
-            )
-            values, send = tie(values, send)
-            self.other = self.flip(send, 1)
-        elif name == "grad_mixed_t":
-            values, (self.kept, self.other) = tie(values, (self.kept, self.other))
-            self.d_q01 = self.across(self.kept, self.other)
+            d_out = join([g["out_t"], g["out_f"], g["out_s"], g["out_m"]], width // 2)
+            values, d_out = tie(values, d_out)
+            self.summed_out = lax.psum_scatter(d_out, self.axes, scatter_dimension=0, tiled=True).astype(F32)
         elif name == "grad_project_t":
             values, self.d_p1 = tie(values, self.d_p1)
             self.d_p1 = self.gathered(self.d_p1)
@@ -475,11 +485,8 @@
             x = self.square // 2
             send = (half(kept, 1 - x) + half(other, 1 - x)).astype(BF16)
             own = (half(kept, x) + half(other, x)).astype(BF16)
-            values, (own, send, self.d_q01) = tie(values, (own, send, self.d_q01))
+            values, (own, send) = tie(values, (own, send))
             self.last = (own, self.flip(send, 4))
-            self.d_q01 = self.gathered(self.d_q01)
-            planes = [a[k * rows_out : (k + 1) * rows_out] for a in (self.d_q01, self.d_q23) for k in range(2)]
-            self.out_pieces = self.planes_exchange(jnp.stack(planes, axis=0))
         elif name == "dx_t":
             values, (own, other, self.in_pieces) = tie(values, self.last + (self.in_pieces,))
             y = self.square % 2
@@ -489,8 +496,7 @@
             self.last = (own, self.flip(send, 2))
         elif name == "grad_clip":
             small = lax.all_to_all(pack(values[1:], 32), self.axes, split_axis=0, concat_axis=0)
-            tied = tie(values[0], self.last + (small, self.out_pieces))
-            clip, (own, arrived, self.small_sums, self.out_pieces) = tied
+            clip, (own, arrived, self.small_sums) = tie(values[0], self.last + (small,))
             values = (clip,) + tuple(values[1:])
             self.d_last = self.gathered([own, arrived])
         return values[0] if single else values
@@ -539,7 +545,7 @@
         extra = jnp.where((self.plane == 1) & (self.square == 0), extra, 0.0)
         summed_in = jnp.where(self.plane == 0, first, jnp.sum(self.in_pieces.astype(F32), axis=0) + extra)
         small = jnp.sum(self.small_sums, axis=0)[: self.count, : self.width // 32]
-        return (summed_in, jnp.sum(self.out_pieces.astype(F32), axis=0), small)
+        return (summed_in, self.summed_out, small)
 
 
 def norm_parts(values):
@@ -591,7 +597,6 @@
     project_t = [cube(project_a), cube(project_b)]
     mixed_t = attention_call(forward_kernel, 2, project_t, (width,), True, patches)[0]
     mixed_t = flat(feed.tick("mixed_t", mixed_t))
-    grad_low = flat(target(mixed_t))
     projected_t = (nn(mixed_t, feed.out_t) + shifts32[3]).astype(BF16)
     branch_t = (nn(projected_t, feed.out_f) + shifts32[4]).astype(BF16)
     after_t = start + branch_t.astype(F32)
@@ -602,11 +607,12 @@
     project_s = [cube(project_qk), cube(project_v)]
     mixed_s = attention_call(forward_kernel, 2, project_s, (width,), False, patches)[0]
     mixed_s = flat(feed.tick("mixed_s", mixed_s))
+    grad_low = flat(target(mixed_s))
     after_s = after_t + (nn(mixed_s, feed.out_s) + shifts32[5])
     normed_m = layer_norm(after_s, gains32[2], shifts32[2])
     hidden_pre = nt(normed_m, feed.in_m) + shifts32[6:].reshape(-1)
     hidden32, slope32 = gelu_parts(hidden_pre)
-    hidden, slope = feed.tick("hidden", hidden32.astype(BF16), slope32.astype(BF16))
+    hidden, slope, grad_low = feed.tick("hidden", hidden32.astype(BF16), slope32.astype(BF16), grad_low)
     output = (after_s + (nn(hidden, feed.out_m) + dense32)).astype(BF16)
     output = leave(output.reshape(shape))
 

time: 719 us -> 663 us (0.922)
  other arithmetic: 77.9 us -> 55.7 us
  starting transfers between devices: 105 us -> 85.3 us
  Pallas kernels: 139 us -> 125 us
  between operations: 3.11 us -> 16.5 us
  waiting for transfers between devices: 125 us -> 115 us
  matrix products: 211 us -> 202 us
    ppermute x66 -> x44, waiting for transfers between devices: 57.1 us -> 33.2 us  [flip(): return lax.ppermute(x, self.axes, [(d, d ^ bits) for d in range(32)])]
    ppermute x66 -> x44, starting transfers between devices: 48.2 us -> 33.3 us  [flip(): return lax.ppermute(x, self.axes, [(d, d ^ bits) for d in range(32)])]
    all_to_all x3 -> x1, waiting for transfers between devices: 15.2 us -> 28.8 us  [planes_exchange(): lax.all_to_all(blocks, self.axes, split_axis=0, concat_axis=0, axis_index...]
    pallas_call x7 -> x5, Pallas kernels: 33.1 us -> 20 us  [place(): pl.pallas_call(partial(place_kernel, tuple((tuple(e) for e in outs_plan))...]
    all_to_all x3 -> x1, starting transfers between devices: 19.7 us -> 10.7 us  [planes_exchange(): lax.all_to_all(blocks, self.axes, split_axis=0, concat_axis=0, axis_index...]
    convert_element_type x5 -> x3, other arithmetic: 13.3 us -> 5.33 us  [across(): summed = (take(keep) + take(other)).astype(BF16)]
    dot_general x8, matrix products: 64.8 us -> 57 us  [tn(): lax.dot_general(left, right, (((0,), (0,)), ((), ())), preferred_element_...]
    pallas_call x6 -> x4, Pallas kernels: 20 us -> 12.9 us  [split_cores(): pl.pallas_call(partial(split_kernel, spans, tuple(plane_rows), squares),...]
  transfers between devices with their start and end apart: 86 -> 64, of which waited for: 16 -> 9; matrix products, arithmetic and copies ran while one was open for 42% -> 41% of each run, Pallas kernels for 18% -> 19%
where the time goes in v6:
time: 663 us; the launch traced here: 652 us
  matrix products  202 us (30%)
  Pallas kernels  125 us (19%)
  waiting for transfers between devices  115 us (17%)
  starting transfers between devices  85.3 us (13%)
  other arithmetic  55.7 us (8%)
  local copies, waits for them, and re-layouts  52.3 us (8%)
  between operations  16.5 us (2%)
    pallas_call x4, Pallas kernels, attention_call(): pl.pallas_call(partial(kernel, group, patches, count), grid=(clips, steps...  84.3 us
    dot_general x8, matrix products, nn(): lax.dot_general(left, right, (((1,), (0,)), ((), ())), preferred_element_...  74.2 us
    dot_general x9, matrix products, nt(): lax.dot_general(left, right, (((1,), (1,)), ((), ())), preferred_element_...  70.7 us
    dot_general x8, matrix products, tn(): lax.dot_general(left, right, (((0,), (0,)), ((), ())), preferred_element_...  57 us
    ppermute x44, starting transfers between devices, flip(): return lax.ppermute(x, self.axes, [(d, d ^ bits) for d in range(32)])  33.3 us
    ppermute x44, waiting for transfers between devices, flip(): return lax.ppermute(x, self.axes, [(d, d ^ bits) for d in range(32)])  33.2 us
    ppermute x3, waiting for transfers between devices, shift(): lax.ppermute(x, self.axes, [(d, (d + 8 * step) % 32) for d in range(32)])  29.1 us
    all_to_all x1, waiting for transfers between devices, planes_exchange(): lax.all_to_all(blocks, self.axes, split_axis=0, concat_axis=0, axis_index...  28.8 us
  transfers between devices with their start and end apart: 64, of which 9 were waited for; matrix products, arithmetic and copies ran while one was open for 41% of the time, Pallas kernels for 19%

profile of v6, /device:TPU:0, one launch (start us, length us, event | category | flops | bytes accessed | tf_op | source)
XLA Modules:
  0.0 652.0 jit_solution(11198873173078928808)
XLA Ops:
  21.3 27.7 %collective-permute-done.1 = bf16[248,768]{1,0:T(8,128)(2,1)S(1)} collective-permute-done((bf16[248,768]{1,0:T(8,128)(2,1)S(1)}, bf16[248,768]{1,0:T(8,128)(2,1)S(1)}, u32[]{:S(2)}, u32[]{:S(2)}) %collective-permute-start.1) | collective-permute-done | bytes 380960 | tf_op jit(solution)/shard_map/ppermute | solution.py:370
  59.2 14.2 %collective-permute-done.5 = bf16[272,768]{1,0:T(8,128)(2,1)S(1)} collective-permute-done((bf16[272,768]{1,0:T(8,128)(2,1)S(1)}, bf16[272,768]{1,0:T(8,128)(2,1)S(1)}, u32[]{:S(2)}, u32[]{:S(2)}) %collective-permute-start.5) | collective-permute-done | bytes 417824 | tf_op jit(solution)/shard_map/ppermute | solution.py:367
  73.4 7.0 %collective-permute-done.4 = bf16[272,768]{1,0:T(8,128)(2,1)S(1)} collective-permute-done((bf16[272,768]{1,0:T(8,128)(2,1)S(1)}, bf16[272,768]{1,0:T(8,128)(2,1)S(1)}, u32[]{:S(2)}, u32[]{:S(2)}) %collective-permute-start.4) | collective-permute-done | bytes 417824 | tf_op jit(solution)/shard_map/ppermute | solution.py:367
  102.4 7.3 %convolution_convert_fusion = bf16[1664,1920]{1,0:T(8,128)(2,1)} fusion(bf16[1664,768]{1,0:T(8,128)(2,1)S(1)} %bitcast.306, bf16[1920,768]{1,0:T(8,128)(2,1)S(1)} %bitcast.289), kind=kOutput, calls=%fused_computation.10 | convolution fusion | flops 4910530560 | bytes 11894784 | tf_op jit(solution)/shard_map/dot_general | solution.py:23
  119.6 5.3 shard_map.137
  130.0 15.8 %shard_map.138 = bf16[1,8,208,768]{3,2,1,0:T(8,128)(2,1)} custom-call(bf16[1,8,208,1920]{3,2,1,0:T(8,128)(2,1)} %bitcast.314, bf16[1,8,208,384]{3,2,1,0:T(8,128)(2,1)} %bitcast.334), custom_call_target="tpu_custom_call" | custom-call | flops 14976000000 | tf_op jit(solution)/shard_map/pallas_call | solution.py:135
  171.2 8.4 %convolution_convert_fusion.1 = bf16[1664,1536]{1,0:T(8,128)(2,1)} fusion(bf16[1664,768]{1,0:T(8,128)(2,1)S(1)} %add_convert_fusion.3, bf16[3840,768]{1,0:T(8,128)(2,1)} %bitcast.233), kind=kOutput, calls=%fused_computation.11 | convolution fusion | flops 3928424448 | bytes 10027008 | tf_op jit(solution)/shard_map/dot_general | solution.py:23
  184.5 15.9 %shard_map.140 = bf16[1,8,208,768]{3,2,1,0:T(8,128)(2,1)} custom-call(bf16[1,8,208,1536]{3,2,1,0:T(8,128)(2,1)} %bitcast.316, bf16[1,8,208,768]{3,2,1,0:T(8,128)(2,1)} %bitcast.328), custom_call_target="tpu_custom_call" | custom-call | flops 14976000000 | tf_op jit(solution)/shard_map/pallas_call | solution.py:135
  206.5 6.4 fusion.79
  213.7 5.5 shard_map.141
  221.6 17.2 %fusion.4 = (bf16[1664,3072]{1,0:T(8,128)(2,1)}, bf16[1664,3072]{1,0:T(8,128)(2,1)}) fusion(f32[3072]{0:T(1024)S(1)} %add.376, bf16[3840,768]{1,0:T(8,128)(2,1)S(1)} %bitcast.236, f32[1664,768]{1,0:T(8,128)S(1)} %get-tuple-element.288, f32[768]{0:T(1024)S(1)} %add.373, f32[768]{0:T(1024)S(1)} %mul.260, f32[1664]{0:T(1024)S(1)} %add_rsqrt_fusion, ...), kind=kOutput, calls=%fused_computation.5 | convolution fusion | flops 7919468544 | bytes 30314496 | tf_op jit(solution)/shard_map/dot_general | solution.py:23
  242.0 12.5 %add_convert_fusion.1 = bf16[1664,768]{1,0:T(8,128)(2,1)S(1)} fusion(f32[1664,768]{1,0:T(8,128)S(1)} %copy-done.18, bf16[1664,3072]{1,0:T(8,128)(2,1)} %get-tuple-element.143, bf16[5376,768]{1,0:T(8,128)(2,1)} %all-gather.2.cloned.1.call-done, f32[768]{0:T(1024)S(1)} %add.385), kind=kOutput, calls=%fused_computation.44 | convolution fusion | flops 7855570944 | bytes 22612992 | tf_op jit(solution)/shard_map/dot_general | solution.py:27
  260.7 14.8 %multiply_convert_fusion = bf16[1664,3072]{1,0:T(8,128)(2,1)} fusion(bf16[1664,3072]{1,0:T(8,128)(2,1)} %get-tuple-element.140, bf16[1664,768]{1,0:T(8,128)(2,1)S(1)} %bitcast.297, bf16[5376,768]{1,0:T(8,128)(2,1)} %all-gather.2.cloned.1.call-done), kind=kOutput, calls=%fused_computation.7 | convolution fusion | flops 7867072512 | bytes 27721728 | tf_op jit(solution)/shard_map/dot_general | solution.py:23
  275.6 13.8 %fusion.35.refs_0_.refs_1_ = bf16[384,8,768]{2,1,0:T(8,128)(2,1)S(1)} fusion(bf16[1664,3072]{1,0:T(8,128)(2,1)} %multiply_convert_fusion, f32[1664,768]{1,0:T(8,128)} %copy-done.17, f32[768]{0:T(1024)S(1)} %add.373, f32[768]{0:T(1024)S(1)} %mul.260, f32[1664]{0:T(1024)S(1)} %add_rsqrt_fusion, f32[1664]{0:T(1024)S(1)} %broadcast_multiply_fusion.6), kind=kOutput, calls=%fused_computation.80 | convolution fusion | flops 7860486144 | bytes 20073472 | tf_op jit(solution)/shard_map/dot_general | solution.py:31
  294.2 17.2 %multiply_reduce_fusion = (f32[768]{0:T(1024)}, f32[1664]{0:T(1024)S(1)}, f32[1664]{0:T(1024)S(1)}, f32[768]{0:T(1024)}, f32[1664,768]{1,0:T(8,128)}) fusion(f32[1664,768]{1,0:T(8,128)} %copy-done.17, f32[1664]{0:T(1024)S(1)} %add_rsqrt_fusion, f32[1664]{0:T(1024)S(1)} %broadcast_multiply_fusion.6, f32[768]{0:T(1024)S(1)} %mul.260, ...), kind=kOutput, calls=%fused_computation.39 | convolution fusion | flops 7863233536 | bytes 25205760 | tf_op jit(solution)/shard_map/dot_general | solution.py:27
  311.9 5.4 convert_reduce_fusion.3
  317.4 5.8 convolution_convert_fusion.7
  323.2 13.1 %fusion.36.refs_3_ = bf16[384,8,768]{2,1,0:T(8,128)(2,1)} fusion(bf16[1664,3072]{1,0:T(8,128)(2,1)} %get-tuple-element.143, bf16[1664,768]{1,0:T(8,128)(2,1)S(1)} %bitcast.299), kind=kOutput, calls=%fused_computation.81 | convolution fusion | flops 7854096384 | bytes 17498112 | tf_op jit(solution)/shard_map/dot_general | solution.py:31
  341.2 26.3 %shard_map.143 = (bf16[1,8,208,1536]{3,2,1,0:T(8,128)(2,1)}, bf16[1,8,208,768]{3,2,1,0:T(8,128)(2,1)}) custom-call(bf16[1,8,208,1536]{3,2,1,0:T(8,128)(2,1)} %bitcast.317, bf16[1,8,208,768]{3,2,1,0:T(8,128)(2,1)} %bitcast.329, bf16[1,8,208,768]{3,2,1,0:T(8,128)(2,1)} %bitcast.332), custom_call_target="tpu_custom_call" | custom-call | flops 23296000000 | tf_op jit(solution)/shard_map/pallas_call | solution.py:135
  380.5 5.0 convolution_convert_fusion.9
  390.3 5.9 fusion.46
  396.3 9.5 %multiply_reduce_fusion.1 = (f32[768]{0:T(1024)}, f32[1664]{0:T(1024)S(1)}, f32[1664]{0:T(1024)S(1)}, f32[768]{0:T(1024)}, f32[1664,768]{1,0:T(8,128)S(1)}) fusion(f32[1664]{0:T(1024)S(1)} %copy-done.49, f32[1664]{0:T(1024)S(1)} %copy-done.43, bf16[1664,768]{1,0:T(8,128)(2,1)S(1)} %copy-done.16, bf16[1,8,208,768]{3,2,1,0:T(8,128)(2,1)S(1)} %copy-done.12, ...), kind=kOutput, calls=%fused_computation.40 | convolution fusion | flops 3942477056 | bytes 22842368 | tf_op jit(solution)/shard_map/dot_general | solution.py:27
  424.0 6.3 shard_map.146
  436.6 5.7 convolution_convert_fusion.5
  442.4 26.4 %shard_map.147 = bf16[1,8,208,2304]{3,2,1,0:T(8,128)(2,1)} custom-call(bf16[1,8,208,1920]{3,2,1,0:T(8,128)(2,1)} %bitcast.315, bf16[1,8,208,384]{3,2,1,0:T(8,128)(2,1)} %bitcast.335, bf16[1,8,208,768]{3,2,1,0:T(8,128)(2,1)} %bitcast.333), custom_call_target="tpu_custom_call" | custom-call | flops 23296000000 | tf_op jit(solution)/shard_map/pallas_call | solution.py:135
  469.6 10.4 %fusion.39.refs_0_ = bf16[288,8,768]{2,1,0:T(8,128)(2,1)S(1)} fusion(bf16[1664,2304]{1,0:T(8,128)(2,1)} %bitcast.312, bf16[1664,768]{1,0:T(8,128)(2,1)S(1)} %copy-done.25), kind=kOutput, calls=%fused_computation.84 | convolution fusion | flops 5890572288 | bytes 13762560 | tf_op jit(solution)/shard_map/dot_general | solution.py:31
  502.1 10.7 %all-to-all-start.3 = ((bf16[4,240,768]{2,1,0:T(8,128)(2,1)}), bf16[4,240,768]{2,1,0:T(8,128)(2,1)}, u32[]{:S(2)}, u32[]{:S(2)}) async-start(bf16[4,240,768]{2,1,0:T(8,128)(2,1)} %pad_maximum_fusion), calls=%async_computation.3 | async-start | bytes 2949120 | tf_op jit(solution)/shard_map/all_to_all | solution.py:384
  517.6 13.7 %fusion.19 = (f32[768]{0:T(1024)S(1)}, f32[1664]{0:T(1024)S(1)}, f32[1664]{0:T(1024)S(1)}, f32[768]{0:T(1024)S(1)}, f32[1664,768]{1,0:T(8,128)}) fusion(bf16[1,8,208,768]{3,2,1,0:T(8,128)(2,1)S(1)} %copy-done.13, f32[1664]{0:T(1024)S(1)} %copy-done.47, f32[1664]{0:T(1024)S(1)} %copy-done.45, f32[768]{0:T(1024)S(1)} %copy-done.51, ...), kind=kOutput, calls=%fused_computation.32 | convolution fusion | flops 5901577216 | bytes 18910208 | tf_op jit(solution)/shard_map/dot_general | solution.py:27
  531.4 28.8 %all-to-all-done.3 = bf16[4,240,768]{2,1,0:T(8,128)(2,1)} async-done(((bf16[4,240,768]{2,1,0:T(8,128)(2,1)}), bf16[4,240,768]{2,1,0:T(8,128)(2,1)}, u32[]{:S(2)}, u32[]{:S(2)}) %all-to-all-start.3) | async-done | bytes 1474592 | tf_op jit(solution)/shard_map/all_to_all | solution.py:384
  570.3 6.0 add_convert_fusion
  576.3 6.4 collective-permute-done.45
  613.5 23.4 %collective-permute-done.51 = bf16[240,768]{1,0:T(8,128)(2,1)S(1)} collective-permute-done((bf16[240,768]{1,0:T(8,128)(2,1)}, bf16[240,768]{1,0:T(8,128)(2,1)S(1)}, u32[]{:S(2)}, u32[]{:S(2)}) %collective-permute-start.51) | collective-permute-done | bytes 368672 | tf_op jit(solution)/shard_map/ppermute | solution.py:523
  (393 shorter events, 237.6 us)
Async XLA Ops:
  7.2 151.4 %all-gather.2.cloned.1.call-start = ((), (), s32[]{:S(2)}) async-start(), calls=%async_computation.7 | async-start | bytes 8515584 | tf_op jit(solution)/shard_map/all_gather | solution.py:357
  7.9 49.1 %all-to-all-start = ((bf16[4,2,196,768]{3,1,2,0:T(2,128)(2,1)}), bf16[4,2,196,768]{3,1,2,0:T(2,128)(2,1)}, u32[]{:S(2)}, u32[]{:S(2)}) async-start(bf16[4,2,196,768]{3,1,2,0:T(2,128)(2,1)} %param.8), calls=%async_computation | async-start | bytes 4816896 | tf_op jit(solution)/shard_map/all_to_all | solution.py:678
  13.4 35.7 %collective-permute-start.1 = (bf16[248,768]{1,0:T(8,128)(2,1)S(1)}, bf16[248,768]{1,0:T(8,128)(2,1)S(1)}, u32[]{:S(2)}, u32[]{:S(2)}) collective-permute-start(bf16[248,768]{1,0:T(8,128)(2,1)S(1)} %get-tuple-element.281), channel_id=1, source_target_pairs={{0,16},{1,17},{2,18},{3,19},{4,20},{5,21},{6,22},{7,23},{8,24},{9,... | collective-permute-start | bytes 1142792 | tf_op jit(solution)/shard_map/ppermute | solution.py:370
  17.5 31.6 %collective-permute-start = (bf16[248,768]{1,0:T(8,128)(2,1)S(1)}, bf16[248,768]{1,0:T(8,128)(2,1)S(1)}, u32[]{:S(2)}, u32[]{:S(2)}) collective-permute-start(bf16[248,768]{1,0:T(8,128)(2,1)S(1)} %get-tuple-element.281), channel_id=1, source_target_pairs={{0,8},{1,9},{2,10},{3,11},{4,12},{5,13},{6,14},{7,15},{8,16},{9,17... | collective-permute-start | bytes 1142792 | tf_op jit(solution)/shard_map/ppermute | solution.py:370
  19.1 31.3 %collective-permute-start.2 = (bf16[248,768]{1,0:T(8,128)(2,1)S(1)}, bf16[248,768]{1,0:T(8,128)(2,1)S(1)}, u32[]{:S(2)}, u32[]{:S(2)}) collective-permute-start(bf16[248,768]{1,0:T(8,128)(2,1)S(1)} %get-tuple-element.281), channel_id=1, source_target_pairs={{0,24},{1,25},{2,26},{3,27},{4,28},{5,29},{6,30},{7,31},{8,0},{9,1... | collective-permute-start | bytes 1142792 | tf_op jit(solution)/shard_map/ppermute | solution.py:370
  56.2 24.3 %collective-permute-start.4 = (bf16[272,768]{1,0:T(8,128)(2,1)S(1)}, bf16[272,768]{1,0:T(8,128)(2,1)S(1)}, u32[]{:S(2)}, u32[]{:S(2)}) collective-permute-start(bf16[272,768]{1,0:T(8,128)(2,1)S(1)} %pad_maximum_fusion.1), channel_id=1, source_target_pairs={{0,4},{1,5},{2,6},{3,7},{4,0},{5,1},{6,2},{7,3},{8,12},{9,13},{10,... | collective-permute-start | bytes 1253384 | tf_op jit(solution)/shard_map/ppermute | solution.py:367
  56.6 23.8 %collective-permute-start.3 = (bf16[272,768]{1,0:T(8,128)(2,1)S(1)}, bf16[272,768]{1,0:T(8,128)(2,1)S(1)}, u32[]{:S(2)}, u32[]{:S(2)}) collective-permute-start(bf16[272,768]{1,0:T(8,128)(2,1)S(1)} %pad_maximum_fusion.1), channel_id=1, source_target_pairs={{0,2},{1,3},{2,0},{3,1},{4,6},{5,7},{6,4},{7,5},{8,10},{9,11},{10,... | collective-permute-start | bytes 1253384 | tf_op jit(solution)/shard_map/ppermute | solution.py:367
  116.1 29.6 %collective-permute-start.19 = (bf16[240,768]{1,0:T(8,128)(2,1)S(1)}, bf16[240,768]{1,0:T(8,128)(2,1)}, u32[]{:S(2)}, u32[]{:S(2)}) collective-permute-start(bf16[240,768]{1,0:T(8,128)(2,1)S(1)} %get-tuple-element.128), channel_id=1, source_target_pairs={{0,6},{1,7},{2,4},{3,5},{4,2},{5,3},{6,0},{7,1},{8,14},{9,15},{10,... | collective-permute-start | bytes 1105928 | tf_op jit(solution)/shard_map/ppermute | solution.py:367
  117.6 28.1 %collective-permute-start.18 = (bf16[240,768]{1,0:T(8,128)(2,1)S(1)}, bf16[240,768]{1,0:T(8,128)(2,1)}, u32[]{:S(2)}, u32[]{:S(2)}) collective-permute-start(bf16[240,768]{1,0:T(8,128)(2,1)S(1)} %get-tuple-element.128), channel_id=1, source_target_pairs={{0,4},{1,5},{2,6},{3,7},{4,0},{5,1},{6,2},{7,3},{8,12},{9,13},{10,... | collective-permute-start | bytes 1105928 | tf_op jit(solution)/shard_map/ppermute | solution.py:367
  119.1 26.7 %collective-permute-start.17 = (bf16[240,768]{1,0:T(8,128)(2,1)S(1)}, bf16[240,768]{1,0:T(8,128)(2,1)}, u32[]{:S(2)}, u32[]{:S(2)}) collective-permute-start(bf16[240,768]{1,0:T(8,128)(2,1)S(1)} %get-tuple-element.128), channel_id=1, source_target_pairs={{0,2},{1,3},{2,0},{3,1},{4,6},{5,7},{6,4},{7,5},{8,10},{9,11},{10,... | collective-permute-start | bytes 1105928 | tf_op jit(solution)/shard_map/ppermute | solution.py:367
  150.4 50.0 %collective-permute-start.26 = (bf16[240,768]{1,0:T(8,128)(2,1)S(1)}, bf16[240,768]{1,0:T(8,128)(2,1)S(1)}, u32[]{:S(2)}, u32[]{:S(2)}) collective-permute-start(bf16[240,768]{1,0:T(8,128)(2,1)S(1)} %copy-done.6), channel_id=1, source_target_pairs={{0,6},{1,7},{2,4},{3,5},{4,2},{5,3},{6,0},{7,1},{8,14},{9,15},{10,... | collective-permute-start | bytes 1105928 | tf_op jit(solution)/shard_map/ppermute | solution.py:367
  151.9 48.5 %collective-permute-start.25 = (bf16[240,768]{1,0:T(8,128)(2,1)S(1)}, bf16[240,768]{1,0:T(8,128)(2,1)S(1)}, u32[]{:S(2)}, u32[]{:S(2)}) collective-permute-start(bf16[240,768]{1,0:T(8,128)(2,1)S(1)} %copy-done.6), channel_id=1, source_target_pairs={{0,4},{1,5},{2,6},{3,7},{4,0},{5,1},{6,2},{7,3},{8,12},{9,13},{10,... | collective-permute-start | bytes 1105928 | tf_op jit(solution)/shard_map/ppermute | solution.py:367
  153.4 47.0 %collective-permute-start.24 = (bf16[240,768]{1,0:T(8,128)(2,1)S(1)}, bf16[240,768]{1,0:T(8,128)(2,1)S(1)}, u32[]{:S(2)}, u32[]{:S(2)}) collective-permute-start(bf16[240,768]{1,0:T(8,128)(2,1)S(1)} %copy-done.6), channel_id=1, source_target_pairs={{0,2},{1,3},{2,0},{3,1},{4,6},{5,7},{6,4},{7,5},{8,10},{9,11},{10,... | collective-permute-start | bytes 1105928 | tf_op jit(solution)/shard_map/ppermute | solution.py:367
  200.4 38.4 %all-to-all-start.1 = ((bf16[4,2,196,768]{3,1,2,0:T(2,128)(2,1)}), bf16[4,2,196,768]{3,1,2,0:T(2,128)(2,1)}, u32[]{:S(2)}, u32[]{:S(2)}) async-start(bf16[4,2,196,768]{3,1,2,0:T(2,128)(2,1)} %param.9), calls=%async_computation.1 | async-start | bytes 4816896 | tf_op jit(solution)/shard_map/all_to_all | solution.py:678
  256.1 80.2 %all-to-all-start.2 = ((bf16[1,8,196,768]{3,2,0,1:T(8,128)(2,1)}), bf16[1,8,196,768]{3,2,0,1:T(8,128)(2,1)}, u32[]{:S(2)}, u32[]{:S(2)}) async-start(bf16[1,8,196,768]{3,2,0,1:T(8,128)(2,1)} %slice.215), calls=%async_computation.2 | async-start | bytes 4915200 | tf_op jit(solution)/shard_map/all_to_all | solution.py:683
  260.7 382.5 %reduce-scatter.2.cloned.1.call-start = ((), (), s32[]{:S(2)}) async-start(), calls=%async_computation.8 | async-start | bytes 8515584 | tf_op jit(solution)/shard_map/reduce_scatter | solution.py:473
  311.5 24.8 %collective-permute-start.31 = (bf16[4,240,768]{2,1,0:T(8,128)(2,1)S(1)}, bf16[4,240,768]{2,1,0:T(8,128)(2,1)S(1)}, u32[]{:S(2)}, u32[]{:S(2)}) collective-permute-start(bf16[4,240,768]{2,1,0:T(8,128)(2,1)S(1)} %bitcast.291), channel_id=1, source_target_pairs={{0,1},{1,0},{2,3},{3,2},{4,5},{5,4},{6,7},{7,6},{8,9},{9,8},{10,11... | collective-permute-start | bytes 4423688 | tf_op jit(solution)/shard_map/ppermute | solution.py:367
  337.7 29.8 %collective-permute-start.34 = (bf16[240,768]{1,0:T(8,128)(2,1)}, bf16[240,768]{1,0:T(8,128)(2,1)S(1)}, u32[]{:S(2)}, u32[]{:S(2)}) collective-permute-start(bf16[240,768]{1,0:T(8,128)(2,1)} %get-tuple-element.270), channel_id=1, source_target_pairs={{0,6},{1,7},{2,4},{3,5},{4,2},{5,3},{6,0},{7,1},{8,14},{9,15},{10,... | collective-permute-start | bytes 1105928 | tf_op jit(solution)/shard_map/ppermute | solution.py:367
  340.3 27.3 %collective-permute-start.33 = (bf16[240,768]{1,0:T(8,128)(2,1)}, bf16[240,768]{1,0:T(8,128)(2,1)S(1)}, u32[]{:S(2)}, u32[]{:S(2)}) collective-permute-start(bf16[240,768]{1,0:T(8,128)(2,1)} %get-tuple-element.271), channel_id=1, source_target_pairs={{0,4},{1,5},{2,6},{3,7},{4,0},{5,1},{6,2},{7,3},{8,12},{9,13},{10,... | collective-permute-start | bytes 1105928 | tf_op jit(solution)/shard_map/ppermute | solution.py:367
  340.9 26.7 %collective-permute-start.32 = (bf16[240,768]{1,0:T(8,128)(2,1)}, bf16[240,768]{1,0:T(8,128)(2,1)}, u32[]{:S(2)}, u32[]{:S(2)}) collective-permute-start(bf16[240,768]{1,0:T(8,128)(2,1)} %get-tuple-element.272), channel_id=1, source_target_pairs={{0,2},{1,3},{2,0},{3,1},{4,6},{5,7},{6,4},{7,5},{8,10},{9,11},{10,... | collective-permute-start | bytes 1105928 | tf_op jit(solution)/shard_map/ppermute | solution.py:367
  386.7 26.2 %collective-permute-start.38 = (bf16[240,768]{1,0:T(8,128)(2,1)S(1)}, bf16[240,768]{1,0:T(8,128)(2,1)S(1)}, u32[]{:S(2)}, u32[]{:S(2)}) collective-permute-start(bf16[240,768]{1,0:T(8,128)(2,1)S(1)} %get-tuple-element.266), channel_id=1, source_target_pairs={{0,6},{1,7},{2,4},{3,5},{4,2},{5,3},{6,0},{7,1},{8,14},{9,15},{10,... | collective-permute-start | bytes 1105928 | tf_op jit(solution)/shard_map/ppermute | solution.py:367
  389.3 23.7 %collective-permute-start.37 = (bf16[240,768]{1,0:T(8,128)(2,1)S(1)}, bf16[240,768]{1,0:T(8,128)(2,1)S(1)}, u32[]{:S(2)}, u32[]{:S(2)}) collective-permute-start(bf16[240,768]{1,0:T(8,128)(2,1)S(1)} %get-tuple-element.267), channel_id=1, source_target_pairs={{0,4},{1,5},{2,6},{3,7},{4,0},{5,1},{6,2},{7,3},{8,12},{9,13},{10,... | collective-permute-start | bytes 1105928 | tf_op jit(solution)/shard_map/ppermute | solution.py:367
  433.2 35.6 %collective-permute-start.42 = (bf16[240,768]{1,0:T(8,128)(2,1)}, bf16[240,768]{1,0:T(8,128)(2,1)S(1)}, u32[]{:S(2)}, u32[]{:S(2)}) collective-permute-start(bf16[240,768]{1,0:T(8,128)(2,1)} %get-tuple-element.262), channel_id=1, source_target_pairs={{0,6},{1,7},{2,4},{3,5},{4,2},{5,3},{6,0},{7,1},{8,14},{9,15},{10,... | collective-permute-start | bytes 1105928 | tf_op jit(solution)/shard_map/ppermute | solution.py:367
  435.6 33.2 %collective-permute-start.41 = (bf16[240,768]{1,0:T(8,128)(2,1)}, bf16[240,768]{1,0:T(8,128)(2,1)S(1)}, u32[]{:S(2)}, u32[]{:S(2)}) collective-permute-start(bf16[240,768]{1,0:T(8,128)(2,1)} %get-tuple-element.263), channel_id=1, source_target_pairs={{0,4},{1,5},{2,6},{3,7},{4,0},{5,1},{6,2},{7,3},{8,12},{9,13},{10,... | collective-permute-start | bytes 1105928 | tf_op jit(solution)/shard_map/ppermute | solution.py:367
  436.1 32.6 %collective-permute-start.40 = (bf16[240,768]{1,0:T(8,128)(2,1)}, bf16[240,768]{1,0:T(8,128)(2,1)}, u32[]{:S(2)}, u32[]{:S(2)}) collective-permute-start(bf16[240,768]{1,0:T(8,128)(2,1)} %get-tuple-element.264), channel_id=1, source_target_pairs={{0,2},{1,3},{2,0},{3,1},{4,6},{5,7},{6,4},{7,5},{8,10},{9,11},{10,... | collective-permute-start | bytes 1105928 | tf_op jit(solution)/shard_map/ppermute | solution.py:367
  484.4 28.4 %collective-permute-start.43 = (bf16[4,288,768]{2,1,0:T(8,128)(2,1)S(1)}, bf16[4,288,768]{2,1,0:T(8,128)(2,1)}, u32[]{:S(2)}, u32[]{:S(2)}) collective-permute-start(bf16[4,288,768]{2,1,0:T(8,128)(2,1)S(1)} %bitcast.290), channel_id=1, source_target_pairs={{0,1},{1,0},{2,3},{3,2},{4,5},{5,4},{6,7},{7,6},{8,9},{9,8},{10,11... | collective-permute-start | bytes 5308424 | tf_op jit(solution)/shard_map/ppermute | solution.py:367
  502.1 58.0 %all-to-all-start.3 = ((bf16[4,240,768]{2,1,0:T(8,128)(2,1)}), bf16[4,240,768]{2,1,0:T(8,128)(2,1)}, u32[]{:S(2)}, u32[]{:S(2)}) async-start(bf16[4,240,768]{2,1,0:T(8,128)(2,1)} %pad_maximum_fusion), calls=%async_computation.3 | async-start | bytes 2949120 | tf_op jit(solution)/shard_map/all_to_all | solution.py:384
  515.8 44.3 %collective-permute-start.44 = (bf16[2,288,768]{2,1,0:T(8,128)(2,1)}, bf16[2,288,768]{2,1,0:T(8,128)(2,1)}, u32[]{:S(2)}, u32[]{:S(2)}) collective-permute-start(bf16[2,288,768]{2,1,0:T(8,128)(2,1)} %get-tuple-element.180), channel_id=1, source_target_pairs={{0,4},{1,5},{2,6},{3,7},{4,0},{5,1},{6,2},{7,3},{8,12},{9,13},{10,... | collective-permute-start | bytes 2654216 | tf_op jit(solution)/shard_map/ppermute | solution.py:367
  586.0 53.1 %all-to-all-start.5 = ((bf16[1,8,196,768]{3,2,0,1:T(8,128)(2,1)}), bf16[1,8,196,768]{3,2,0,1:T(8,128)(2,1)S(1)}, u32[]{:S(2)}, u32[]{:S(2)}) async-start(bf16[1,8,196,768]{3,2,0,1:T(8,128)(2,1)} %slice.217), calls=%async_computation.5 | async-start | bytes 4915200 | tf_op jit(solution)/shard_map/all_to_all | solution.py:683
  608.1 28.7 %collective-permute-start.51 = (bf16[240,768]{1,0:T(8,128)(2,1)}, bf16[240,768]{1,0:T(8,128)(2,1)S(1)}, u32[]{:S(2)}, u32[]{:S(2)}) collective-permute-start(bf16[240,768]{1,0:T(8,128)(2,1)} %slice.219), channel_id=1, source_target_pairs={{8,0},{9,1},{10,2},{11,3},{12,4},{13,5},{14,6},{15,7}} | collective-permute-start | bytes 1105928 | tf_op jit(solution)/shard_map/ppermute | solution.py:523
  609.4 27.4 %collective-permute-start.50 = (bf16[240,768]{1,0:T(8,128)(2,1)}, bf16[240,768]{1,0:T(8,128)(2,1)S(1)}, u32[]{:S(2)}, u32[]{:S(2)}) collective-permute-start(bf16[240,768]{1,0:T(8,128)(2,1)} %slice.219), channel_id=1, source_target_pairs={{16,0},{17,1},{18,2},{19,3},{20,4},{21,5},{22,6},{23,7}} | collective-permute-start | bytes 1105928 | tf_op jit(solution)/shard_map/ppermute | solution.py:523
  610.7 26.1 %collective-permute-start.49 = (bf16[240,768]{1,0:T(8,128)(2,1)}, bf16[240,768]{1,0:T(8,128)(2,1)S(1)}, u32[]{:S(2)}, u32[]{:S(2)}) collective-permute-start(bf16[240,768]{1,0:T(8,128)(2,1)} %slice.219), channel_id=1, source_target_pairs={{24,0},{25,1},{26,2},{27,3},{28,4},{29,5},{30,6},{31,7}} | collective-permute-start | bytes 1105928 | tf_op jit(solution)/shard_map/ppermute | solution.py:523
  (107 other events, 1094.0 us)
Sparse Core Ops, SparseCore 0:
  10.9 106.0 all-gather.1
  430.6 150.6 reduce-scatter.1

commit v7 on v6

--- a/solution.py
+++ b/solution.py
@@ -246,7 +246,7 @@
         scratch_shapes=[pltpu.VMEM((2 * squares, rows // 8, 8, width), BF16) for rows in plane_rows]
         + [pltpu.SemaphoreType.DMA((slots + len(parts),)), pltpu.SemaphoreType.DMA((slots,))],
         compiler_params=pltpu.CompilerParams(vmem_limit_bytes=size + (2 << 20)),
-        cost_estimate=pl.CostEstimate(flops=0, bytes_accessed=4 * size, transcendentals=0),
+        cost_estimate=pl.CostEstimate(flops=0, bytes_accessed=size // 8, transcendentals=0),
     )(core, *arrays)
     return [out.reshape(squares, -1, width) for out in outs]
 
@@ -307,6 +307,7 @@
         partial(pack_kernel, devices),
         out_shape=jax.ShapeDtypeStruct((devices, rows, LANES), F32),
         scratch_shapes=[pltpu.VMEM((rows, width), F32)],
+        cost_estimate=pl.CostEstimate(flops=0, bytes_accessed=8 * rows * width, transcendentals=0),
     )(*parts)
 
 
@@ -334,15 +335,18 @@
     def tick(self, name, *values):
         return values[0] if len(values) == 1 else values
 
-    def total(self, parts):
-        g, small = (self.grads, jnp.concatenate(parts, axis=0))
+    def total(self, sums, arrays, clip):
+        g = self.grads
+        parts = sums + [column_sum(array) for array in arrays]
+        small = jnp.concatenate([part.reshape(-1, self.width) for part in parts], axis=0)
         d_in = jnp.concatenate([g["in_t"], g["in_qk"], g["in_v"], g["in_m"]], axis=0)
         d_out = jnp.concatenate([g["out_t"], g["out_f"], g["out_s"], g["out_m"]], axis=0)
         summed_in = lax.psum_scatter(d_in, self.axes, scatter_dimension=0, tiled=True).astype(F32)
         summed_out = lax.psum_scatter(d_out, self.axes, scatter_dimension=0, tiled=True).astype(F32)
         share = self.width // lax.axis_size(self.axes)
         at = (0, lax.axis_index(self.axes) * share)
-        return (summed_in, summed_out, lax.dynamic_slice(lax.psum(small, self.axes), at, (small.shape[0], share)))
+        clip = clip.astype(F32)
+        return (clip, summed_in, summed_out, lax.dynamic_slice(lax.psum(small, self.axes), at, (small.shape[0], share)))
 
 
 class Staged:
@@ -354,13 +358,14 @@
         self.planes = (self.plane + 4 - jnp.arange(4, dtype=jnp.int32)) % 4
         self.core_ref = self.core.astype(jnp.int32).reshape(1)
         self.rows_in, self.count = (weights_in.shape[0], packed.shape[0])
-        full_out = lax.all_gather(weights_out, axes, axis=0, tiled=True)
-        self.out_t, self.out_f = (full_out[:width], full_out[width : 2 * width])
-        self.out_s, self.out_m = (full_out[2 * width : 3 * width], full_out[3 * width :])
         self.grads = {}
         flat = packed.reshape(1, -1)
         tail = jnp.pad(flat, ((0, 7), (0, width - flat.shape[1])))
         pieces = self.shifted(jnp.concatenate([weights_in, tail], axis=0))
+        pieces, weights_out = tie(pieces, weights_out)
+        full_out = lax.all_gather(weights_out, axes, axis=0, tiled=True)
+        self.out_t, self.out_f = (full_out[:width], full_out[width : 2 * width])
+        self.out_s, self.out_m = (full_out[2 * width : 3 * width], full_out[3 * width :])
         self.column_in, self.column_small = self.columns(pieces, (self.rows_in, 8))
 
     def flip(self, x, bits):
@@ -378,10 +383,6 @@
             plan.append([(0, row, size)])
             row += size
         return [out[0] for out in place([pieces], plan, self.planes)]
-
-    def planes_exchange(self, blocks):
-        groups = [[spot + 8 * plane for plane in range(4)] for spot in range(8)]
-        return lax.all_to_all(blocks, self.axes, split_axis=0, concat_axis=0, axis_index_groups=groups)
 
     def over(self, piece):
         return [piece] + [self.flip(piece, bits) for bits in (2, 4, 6)]
@@ -470,12 +471,10 @@
             self.d_p1 = self.across(self.kept, self.other)
             d_out = join([g["out_t"], g["out_f"], g["out_s"], g["out_m"]], width // 2)
             values, d_out = tie(values, d_out)
-            self.summed_out = lax.psum_scatter(d_out, self.axes, scatter_dimension=0, tiled=True).astype(F32)
+            self.summed_out = lax.psum_scatter(d_out, self.axes, scatter_dimension=0, tiled=True)
         elif name == "grad_project_t":
             values, self.d_p1 = tie(values, self.d_p1)
             self.d_p1 = self.gathered(self.d_p1)
-            planes = [jnp.zeros_like(self.d_p1), self.d_p1, self.d_p2, self.d_p3]
-            self.in_pieces = self.planes_exchange(jnp.stack(planes, axis=0))
         elif name == "in_t":
             d_in_t = g["in_t"]
             kept, send = self.halve([whole("in_t")], (rows_in, d_in_t.shape[0] // 8 - rows_in))
@@ -488,17 +487,15 @@
             values, (own, send) = tie(values, (own, send))
             self.last = (own, self.flip(send, 4))
         elif name == "dx_t":
-            values, (own, other, self.in_pieces) = tie(values, self.last + (self.in_pieces,))
+            values, (own, other) = tie(values, self.last)
             y = self.square % 2
             line = lambda a, y: lax.dynamic_index_in_dim(a, y, 0, keepdims=False).astype(F32)
             send = (line(own, 1 - y) + line(other, 1 - y)).astype(BF16)
             own = (line(own, y) + line(other, y)).astype(BF16)
             self.last = (own, self.flip(send, 2))
         elif name == "grad_clip":
-            small = lax.all_to_all(pack(values[1:], 32), self.axes, split_axis=0, concat_axis=0)
-            clip, (own, arrived, self.small_sums) = tie(values[0], self.last + (small,))
-            values = (clip,) + tuple(values[1:])
-            self.d_last = self.gathered([own, arrived])
+            values, last = tie(values, self.last)
+            self.d_last = self.gathered(last)
         return values[0] if single else values
 
     def halve(self, parts, plane_rows):
@@ -529,12 +526,17 @@
             total = total + piece.astype(F32)
         return total
 
-    def total(self, parts):
+    def total(self, sums, arrays, clip):
         rows, last = (self.rows_in, self.d_last)
         extra, first = tie(self.towards(last[rows:], 1), last[:rows])
-        first = self.added(self.towards(first, 0))
+        every = jnp.stack([first, self.d_p1, self.d_p2, self.d_p3], axis=0)
+        terms = [lax.dynamic_index_in_dim(every, self.plane, 0, keepdims=False)]
+        for step in (1, 2, 3):
+            block = lax.dynamic_index_in_dim(every, (self.plane + step) % 4, 0, keepdims=False)
+            terms.append(self.shift(block, step))
         extra = self.added(extra).astype(BF16)
-        extra = jnp.concatenate([extra, self.flip(extra, 1)], axis=0)
+        beside, arrays = tie(self.flip(extra, 1), arrays)
+        extra = jnp.concatenate([extra, beside], axis=0)
         blocks = [extra]
         for bits in (2, 4, 6):
             blocks.append(lax.ppermute(extra, self.axes, [(8 + bits + core, 8 + core) for core in range(2)]))
@@ -543,9 +545,13 @@
         swapped = jnp.pad(swapped, ((0, rows - swapped.shape[0]), (0, 0)))
         extra = jnp.where(self.core == 0, extra.reshape(-1, self.width)[:rows], swapped).astype(F32)
         extra = jnp.where((self.plane == 1) & (self.square == 0), extra, 0.0)
-        summed_in = jnp.where(self.plane == 0, first, jnp.sum(self.in_pieces.astype(F32), axis=0) + extra)
-        small = jnp.sum(self.small_sums, axis=0)[: self.count, : self.width // 32]
-        return (summed_in, self.summed_out, small)
+        clip, self.summed_out = tie(clip, self.summed_out)
+        summed_in = self.added(terms) + extra
+        parts = sums + [column_sum(array) for array in arrays]
+        parts, clip = tie([part.reshape(-1, self.width) for part in parts], clip)
+        small = lax.all_to_all(pack(parts, 32), self.axes, split_axis=0, concat_axis=0)
+        small = jnp.sum(small, axis=0)[: self.count, : self.width // 32]
+        return (clip.astype(F32), summed_in, self.summed_out.astype(F32), small)
 
 
 def norm_parts(values):
@@ -619,17 +625,14 @@
     grad_out = grad_low.astype(F32)
     grads["out_m"] = tn(hidden, grad_low).astype(BF16)
     grad_low = feed.tick("out_m", grad_low)
-    s_dense = column_sum(grad_low)
     grad_pre = (nt(grad_low, feed.out_m) * slope.astype(F32)).astype(BF16)
     grad_pre = feed.tick("grad_pre", grad_pre)
     grads["in_m"] = tn(grad_pre, normed_m).astype(BF16)
     grad_pre = feed.tick("in_m", grad_pre)
-    s_hidden = column_sum(grad_pre).reshape(-1, width)
     part, g_m, b_m = norm_backward(after_s, gains32[2], nn(grad_pre, feed.in_m))
     grad_s = grad_out + part
     grad_branch_s = grad_s.astype(BF16)
     grads["out_s"] = tn(mixed_s, grad_branch_s).astype(BF16)
-    s_space = column_sum(grad_branch_s)
     grad_mixed_s = nt(grad_branch_s, feed.out_s).astype(BF16)
     grad_mixed_s, output = feed.tick("grad_mixed_s", grad_mixed_s, output)
     grad_qk, grad_v = attention_call(
@@ -644,11 +647,9 @@
     grad_t = grad_s + part
     grad_branch_t = feed.tick("grad_t", grad_t.astype(BF16))
     grads["out_f"] = tn(projected_t, grad_branch_t).astype(BF16)
-    s_fc = column_sum(grad_branch_t)
     grad_projected = nt(grad_branch_t, feed.out_f).astype(BF16)
     grads["out_t"] = tn(mixed_t, grad_projected).astype(BF16)
     grad_projected = feed.tick("out_t", grad_projected)
-    s_time = column_sum(grad_projected)
     grad_mixed_t = feed.tick("grad_mixed_t", nt(grad_projected, feed.out_t).astype(BF16))
     grad_project_t = attention_call(
         backward_kernel, 2, project_t + [cube(grad_mixed_t)], (3 * width,), True, patches
@@ -659,9 +660,10 @@
     hook = lambda *sums: feed.tick("dx_t", *sums)
     part, g_t, b_t = norm_backward(start, gains32[0], nn(grad_project_t, feed.in_t), hook)
     grad_clip = (grad_t + part.astype(BF16).astype(F32)).astype(BF16)
-    parts = [g_t, g_s, g_m, b_t, b_s, b_m, s_time, s_fc, s_space, s_hidden, s_dense]
-    grad_clip, *parts = feed.tick("grad_clip", grad_clip, *[part.reshape(-1, width) for part in parts])
-    return (output, leave(grad_clip.reshape(shape)).astype(F32)) + feed.total(parts)
+    rows = (grad_projected, grad_branch_t, grad_branch_s, grad_pre, grad_low)
+    grad_clip, *rows = feed.tick("grad_clip", grad_clip, *rows)
+    sums = [g_t, g_s, g_m, b_t, b_s, b_m]
+    return (output,) + feed.total(sums, rows, leave(grad_clip.reshape(shape)))
 
 
 def shards(clips_in, cotangent, clip_live, weights_in, weights_out, norm_gain, shift_rows, dense_shift):

time: 663 us -> 657 us (level)
  starting transfers between devices: 85.3 us -> 74.2 us
  waiting for transfers between devices: 115 us -> 125 us
    all_to_all x2, waiting for transfers between devices: 0.01 us -> 37.4 us  [enter(): x = lax.all_to_all(x, 'seq', split_axis=0, concat_axis=1, tiled=True)]
    all_to_all x2 -> x1, waiting for transfers between devices: 28.8 us -> 0.01 us  [total(): lax.all_to_all(pack(parts, 32), self.axes, split_axis=0, concat_axis=0)]
    ppermute x6 -> x3, waiting for transfers between devices: 23.4 us -> 0.01 us  [towards(): pieces.append(lax.ppermute(block, self.axes, pairs))]
    ppermute x3 -> x6, waiting for transfers between devices: 29.1 us -> 40.9 us  [shift(): lax.ppermute(x, self.axes, [(d, (d + 8 * step) % 32) for d in range(32)])]
    all_to_all x2 -> x1, starting transfers between devices: 14.2 us -> 4.39 us  [total(): lax.all_to_all(pack(parts, 32), self.axes, split_axis=0, concat_axis=0)]
  transfers between devices with their start and end apart: 64 -> 63, of which waited for: 9 -> 12; matrix products, arithmetic and copies ran while one was open for 41% -> 41% of each run, Pallas kernels for 19% -> 19%
where the time goes in v7:
time: 657 us; the launch traced here: 646 us
  matrix products  196 us (30%)
  waiting for transfers between devices  125 us (19%)
  Pallas kernels  124 us (19%)
  starting transfers between devices  74.2 us (11%)
  other arithmetic  58.9 us (9%)
  local copies, waits for them, and re-layouts  51.4 us (8%)
  between operations  16.8 us (3%)
    pallas_call x4, Pallas kernels, attention_call(): pl.pallas_call(partial(kernel, group, patches, count), grid=(clips, steps...  84 us
    dot_general x9, matrix products, nt(): lax.dot_general(left, right, (((1,), (1,)), ((), ())), preferred_element_...  71 us
    dot_general x8, matrix products, nn(): lax.dot_general(left, right, (((1,), (0,)), ((), ())), preferred_element_...  69.4 us
    dot_general x8, matrix products, tn(): lax.dot_general(left, right, (((0,), (0,)), ((), ())), preferred_element_...  55.9 us
    ppermute x6, waiting for transfers between devices, shift(): lax.ppermute(x, self.axes, [(d, (d + 8 * step) % 32) for d in range(32)])  40.9 us
    ppermute x44, waiting for transfers between devices, flip(): return lax.ppermute(x, self.axes, [(d, d ^ bits) for d in range(32)])  39.6 us
    all_to_all x2, waiting for transfers between devices, enter(): x = lax.all_to_all(x, 'seq', split_axis=0, concat_axis=1, tiled=True)  37.4 us
    ppermute x44, starting transfers between devices, flip(): return lax.ppermute(x, self.axes, [(d, d ^ bits) for d in range(32)])  33.7 us
  transfers between devices with their start and end apart: 63, of which 12 were waited for; matrix products, arithmetic and copies ran while one was open for 41% of the time, Pallas kernels for 19%

profile of v7, /device:TPU:0, one launch (start us, length us, event | category | flops | bytes accessed | tf_op | source)
XLA Modules:
  0.0 646.3 jit_solution(1716596245795256870)
XLA Ops:
  15.2 8.3 %collective-permute-done.2 = bf16[248,768]{1,0:T(8,128)(2,1)S(1)} collective-permute-done((bf16[248,768]{1,0:T(8,128)(2,1)S(1)}, bf16[248,768]{1,0:T(8,128)(2,1)S(1)}, u32[]{:S(2)}, u32[]{:S(2)}) %collective-permute-start.2) | collective-permute-done | bytes 380960 | tf_op jit(solution)/shard_map/ppermute | solution.py:375
  23.5 23.2 %collective-permute-done.1 = bf16[248,768]{1,0:T(8,128)(2,1)S(1)} collective-permute-done((bf16[248,768]{1,0:T(8,128)(2,1)S(1)}, bf16[248,768]{1,0:T(8,128)(2,1)S(1)}, u32[]{:S(2)}, u32[]{:S(2)}) %collective-permute-start.1) | collective-permute-done | bytes 380960 | tf_op jit(solution)/shard_map/ppermute | solution.py:375
  58.0 37.4 %all-to-all-done = bf16[4,2,196,768]{3,1,2,0:T(2,128)(2,1)} async-done(((bf16[4,2,196,768]{3,1,2,0:T(2,128)(2,1)}), bf16[4,2,196,768]{3,1,2,0:T(2,128)(2,1)}, u32[]{:S(2)}, u32[]{:S(2)}) %all-to-all-start) | async-done | bytes 2408480 | tf_op jit(solution)/shard_map/all_to_all | solution.py:680
  97.6 6.1 collective-permute-done.3
  125.5 7.3 %convolution_convert_fusion = bf16[1664,1920]{1,0:T(8,128)(2,1)} fusion(bf16[1664,768]{1,0:T(8,128)(2,1)S(1)} %bitcast.314, bf16[1920,768]{1,0:T(8,128)(2,1)S(1)} %bitcast.297), kind=kOutput, calls=%fused_computation.10 | convolution fusion | flops 4910530560 | bytes 11894784 | tf_op jit(solution)/shard_map/dot_general | solution.py:23
  153.5 15.8 %shard_map.138 = bf16[1,8,208,768]{3,2,1,0:T(8,128)(2,1)} custom-call(bf16[1,8,208,1920]{3,2,1,0:T(8,128)(2,1)} %bitcast.323, bf16[1,8,208,384]{3,2,1,0:T(8,128)(2,1)} %bitcast.341), custom_call_target="tpu_custom_call" | custom-call | flops 14976000000 | tf_op jit(solution)/shard_map/pallas_call | solution.py:135
  194.3 8.4 %convolution_convert_fusion.1 = bf16[1664,1536]{1,0:T(8,128)(2,1)} fusion(bf16[1664,768]{1,0:T(8,128)(2,1)S(1)} %add_convert_fusion.3, bf16[3840,768]{1,0:T(8,128)(2,1)} %bitcast.240), kind=kOutput, calls=%fused_computation.11 | convolution fusion | flops 3928424448 | bytes 10027008 | tf_op jit(solution)/shard_map/dot_general | solution.py:23
  207.7 15.9 %shard_map.140 = bf16[1,8,208,768]{3,2,1,0:T(8,128)(2,1)} custom-call(bf16[1,8,208,1536]{3,2,1,0:T(8,128)(2,1)} %bitcast.325, bf16[1,8,208,768]{3,2,1,0:T(8,128)(2,1)} %bitcast.335), custom_call_target="tpu_custom_call" | custom-call | flops 14976000000 | tf_op jit(solution)/shard_map/pallas_call | solution.py:135
  229.4 6.2 fusion.80
  236.4 5.5 shard_map.141
  244.3 17.2 %fusion.4 = (bf16[1664,3072]{1,0:T(8,128)(2,1)}, bf16[1664,3072]{1,0:T(8,128)(2,1)}) fusion(f32[3072]{0:T(1024)S(1)} %add.404, bf16[3840,768]{1,0:T(8,128)(2,1)S(1)} %bitcast.243, f32[1664,768]{1,0:T(8,128)S(1)} %get-tuple-element.344, f32[768]{0:T(1024)S(1)} %add.401, f32[768]{0:T(1024)S(1)} %mul.260, f32[1664]{0:T(1024)S(1)} %add_rsqrt_fusion, ...), kind=kOutput, calls=%fused_computation.5 | convolution fusion | flops 7919468544 | bytes 30314496 | tf_op jit(solution)/shard_map/dot_general | solution.py:23
  264.7 12.5 %add_convert_fusion.1 = bf16[1664,768]{1,0:T(8,128)(2,1)S(1)} fusion(f32[1664,768]{1,0:T(8,128)S(1)} %copy-done.21, bf16[1664,3072]{1,0:T(8,128)(2,1)} %get-tuple-element.176, bf16[5376,768]{1,0:T(8,128)(2,1)} %all-gather.2.cloned.1.call-done, f32[768]{0:T(1024)S(1)} %add.413), kind=kOutput, calls=%fused_computation.43 | convolution fusion | flops 7855570944 | bytes 22612992 | tf_op jit(solution)/shard_map/dot_general | solution.py:27
  283.4 15.1 %multiply_convert_fusion = bf16[1664,3072]{1,0:T(8,128)(2,1)} fusion(bf16[1664,3072]{1,0:T(8,128)(2,1)} %get-tuple-element.173, bf16[1664,768]{1,0:T(8,128)(2,1)S(1)} %bitcast.302, bf16[5376,768]{1,0:T(8,128)(2,1)} %all-gather.2.cloned.1.call-done), kind=kOutput, calls=%fused_computation.7 | convolution fusion | flops 7867072512 | bytes 27721728 | tf_op jit(solution)/shard_map/dot_general | solution.py:23
  298.5 13.8 %fusion.35.refs_0_.refs_1_ = bf16[384,8,768]{2,1,0:T(8,128)(2,1)S(1)} fusion(bf16[1664,3072]{1,0:T(8,128)(2,1)} %multiply_convert_fusion, f32[1664,768]{1,0:T(8,128)} %copy-done.20, f32[768]{0:T(1024)S(1)} %add.401, f32[768]{0:T(1024)S(1)} %mul.260, f32[1664]{0:T(1024)S(1)} %add_rsqrt_fusion, f32[1664]{0:T(1024)S(1)} %broadcast_multiply_fusion.6), kind=kOutput, calls=%fused_computation.79 | convolution fusion | flops 7860486144 | bytes 20073472 | tf_op jit(solution)/shard_map/dot_general | solution.py:31
  317.2 15.1 %multiply_reduce_fusion = (f32[768]{0:T(1024)S(1)}, f32[1664]{0:T(1024)S(1)}, f32[1664]{0:T(1024)S(1)}, f32[768]{0:T(1024)S(1)}, f32[1664,768]{1,0:T(8,128)}) fusion(f32[1664,768]{1,0:T(8,128)} %copy-done.20, f32[1664]{0:T(1024)S(1)} %add_rsqrt_fusion, f32[1664]{0:T(1024)S(1)} %broadcast_multiply_fusion.6, f32[768]{0:T(1024)S(1)} %mul.260, ...), kind=kOutput, calls=%fused_computation.39 | convolution fusion | flops 7863233536 | bytes 25205760 | tf_op jit(solution)/shard_map/dot_general | solution.py:27
  332.7 5.6 fusion.79
  338.3 5.8 convolution_convert_fusion.7
  344.1 13.0 %fusion.36.refs_3_ = bf16[384,8,768]{2,1,0:T(8,128)(2,1)} fusion(bf16[1664,3072]{1,0:T(8,128)(2,1)} %get-tuple-element.176, bf16[1664,768]{1,0:T(8,128)(2,1)S(1)} %bitcast.304), kind=kOutput, calls=%fused_computation.80 | convolution fusion | flops 7854096384 | bytes 17498112 | tf_op jit(solution)/shard_map/dot_general | solution.py:31
  362.1 26.1 %shard_map.143 = (bf16[1,8,208,1536]{3,2,1,0:T(8,128)(2,1)}, bf16[1,8,208,768]{3,2,1,0:T(8,128)(2,1)}) custom-call(bf16[1,8,208,1536]{3,2,1,0:T(8,128)(2,1)} %bitcast.326, bf16[1,8,208,768]{3,2,1,0:T(8,128)(2,1)} %bitcast.336, bf16[1,8,208,768]{3,2,1,0:T(8,128)(2,1)} %bitcast.339), custom_call_target="tpu_custom_call" | custom-call | flops 23296000000 | tf_op jit(solution)/shard_map/pallas_call | solution.py:135
  411.9 6.0 fusion.46
  417.9 9.2 %multiply_reduce_fusion.1 = (f32[768]{0:T(1024)S(1)}, f32[1664]{0:T(1024)S(1)}, f32[1664]{0:T(1024)S(1)}, f32[768]{0:T(1024)S(1)}, f32[1664,768]{1,0:T(8,128)S(1)}) fusion(f32[1664]{0:T(1024)S(1)} %copy-done.54, f32[1664]{0:T(1024)S(1)} %copy-done.48, bf16[1664,768]{1,0:T(8,128)(2,1)S(1)} %copy-done.16, bf16[1,8,208,768]{3,2,1,0:T(8,128)(2,1)S(1)} %copy-done.12, ...), kind=kOutput, calls=%fused_computation.40 | convolution fusion | flops 3942477056 | bytes 22842368 | tf_op jit(solution)/shard_map/dot_general | solution.py:27
  445.3 6.3 shard_map.146
  457.9 5.8 convolution_convert_fusion.5
  463.7 26.3 %shard_map.147 = bf16[1,8,208,2304]{3,2,1,0:T(8,128)(2,1)} custom-call(bf16[1,8,208,1920]{3,2,1,0:T(8,128)(2,1)} %bitcast.324, bf16[1,8,208,384]{3,2,1,0:T(8,128)(2,1)} %bitcast.342, bf16[1,8,208,768]{3,2,1,0:T(8,128)(2,1)} %bitcast.340), custom_call_target="tpu_custom_call" | custom-call | flops 23296000000 | tf_op jit(solution)/shard_map/pallas_call | solution.py:135
  490.9 9.2 %fusion.39.refs_0_ = bf16[288,8,768]{2,1,0:T(8,128)(2,1)S(1)} fusion(bf16[1664,2304]{1,0:T(8,128)(2,1)} %bitcast.321, bf16[1664,768]{1,0:T(8,128)(2,1)S(1)} %copy-done.29), kind=kOutput, calls=%fused_computation.83 | convolution fusion | flops 5890572288 | bytes 13762560 | tf_op jit(solution)/shard_map/dot_general | solution.py:31
  519.2 11.4 %fusion.19 = (f32[768]{0:T(1024)S(1)}, f32[1664]{0:T(1024)S(1)}, f32[1664]{0:T(1024)S(1)}, f32[768]{0:T(1024)S(1)}, f32[1664,768]{1,0:T(8,128)}) fusion(bf16[1,8,208,768]{3,2,1,0:T(8,128)(2,1)S(1)} %copy-done.13, f32[1664]{0:T(1024)S(1)} %copy-done.52, f32[1664]{0:T(1024)S(1)} %copy-done.50, f32[768]{0:T(1024)S(1)} %copy-done.56, ...), kind=kOutput, calls=%fused_computation.30 | convolution fusion | flops 5901577216 | bytes 18910208 | tf_op jit(solution)/shard_map/dot_general | solution.py:27
  530.7 16.2 %collective-permute-done.44 = bf16[2,288,768]{2,1,0:T(8,128)(2,1)} collective-permute-done((bf16[2,288,768]{2,1,0:T(8,128)(2,1)S(1)}, bf16[2,288,768]{2,1,0:T(8,128)(2,1)}, u32[]{:S(2)}, u32[]{:S(2)}) %collective-permute-start.44) | collective-permute-done | bytes 884768 | tf_op jit(solution)/shard_map/ppermute | solution.py:372
  550.4 5.5 add_convert_fusion
  555.9 11.2 %collective-permute-done.45 = bf16[288,768]{1,0:T(8,128)(2,1)S(1)} collective-permute-done((bf16[288,768]{1,0:T(8,128)(2,1)S(1)}, bf16[288,768]{1,0:T(8,128)(2,1)S(1)}, u32[]{:S(2)}, u32[]{:S(2)}) %collective-permute-start.45) | collective-permute-done | bytes 442400 | tf_op jit(solution)/shard_map/ppermute | solution.py:372
  596.5 5.9 convert_reduce_fusion
  606.0 6.5 %all-to-all-done.3 = bf16[1,8,196,768]{3,2,0,1:T(8,128)(2,1)S(1)} async-done(((bf16[1,8,196,768]{3,2,0,1:T(8,128)(2,1)}), bf16[1,8,196,768]{3,2,0,1:T(8,128)(2,1)S(1)}, u32[]{:S(2)}, u32[]{:S(2)}) %all-to-all-start.3) | async-done | bytes 2408480 | tf_op jit(solution)/shard_map/all_to_all | solution.py:685
  619.5 9.4 %collective-permute-done.51 = bf16[240,768]{1,0:T(8,128)(2,1)} collective-permute-done((bf16[240,768]{1,0:T(8,128)(2,1)S(1)}, bf16[240,768]{1,0:T(8,128)(2,1)}, u32[]{:S(2)}, u32[]{:S(2)}) %collective-permute-start.51) | collective-permute-done | bytes 368672 | tf_op jit(solution)/shard_map/ppermute | solution.py:375
  (391 shorter events, 242.4 us)
Async XLA Ops:
  7.2 174.4 %all-gather.2.cloned.1.call-start = ((), (), s32[]{:S(2)}) async-start(), calls=%async_computation.6 | async-start | bytes 8515584 | tf_op jit(solution)/shard_map/all_gather | solution.py:366
  14.2 32.5 %collective-permute-start.1 = (bf16[248,768]{1,0:T(8,128)(2,1)S(1)}, bf16[248,768]{1,0:T(8,128)(2,1)S(1)}, u32[]{:S(2)}, u32[]{:S(2)}) collective-permute-start(bf16[248,768]{1,0:T(8,128)(2,1)S(1)} %fusion.60), channel_id=1, source_target_pairs={{0,16},{1,17},{2,18},{3,19},{4,20},{5,21},{6,22},{7,23},{8,24},{9,... | collective-permute-start | bytes 1142792 | tf_op jit(solution)/shard_map/ppermute | solution.py:375
  14.2 32.5 %collective-permute-start = (bf16[248,768]{1,0:T(8,128)(2,1)S(1)}, bf16[248,768]{1,0:T(8,128)(2,1)S(1)}, u32[]{:S(2)}, u32[]{:S(2)}) collective-permute-start(bf16[248,768]{1,0:T(8,128)(2,1)S(1)} %fusion.60), channel_id=1, source_target_pairs={{0,8},{1,9},{2,10},{3,11},{4,12},{5,13},{6,14},{7,15},{8,16},{9,17... | collective-permute-start | bytes 1142792 | tf_op jit(solution)/shard_map/ppermute | solution.py:375
  46.7 48.7 %all-to-all-start = ((bf16[4,2,196,768]{3,1,2,0:T(2,128)(2,1)}), bf16[4,2,196,768]{3,1,2,0:T(2,128)(2,1)}, u32[]{:S(2)}, u32[]{:S(2)}) async-start(bf16[4,2,196,768]{3,1,2,0:T(2,128)(2,1)} %param.8), calls=%async_computation | async-start | bytes 4816896 | tf_op jit(solution)/shard_map/all_to_all | solution.py:680
  54.4 43.2 %collective-permute-start.5 = (bf16[272,768]{1,0:T(8,128)(2,1)S(1)}, bf16[272,768]{1,0:T(8,128)(2,1)S(1)}, u32[]{:S(2)}, u32[]{:S(2)}) collective-permute-start(bf16[272,768]{1,0:T(8,128)(2,1)S(1)} %pad_maximum_fusion.1), channel_id=1, source_target_pairs={{0,6},{1,7},{2,4},{3,5},{4,2},{5,3},{6,0},{7,1},{8,14},{9,15},{10,... | collective-permute-start | bytes 1253384 | tf_op jit(solution)/shard_map/ppermute | solution.py:372
  57.3 40.3 %collective-permute-start.4 = (bf16[272,768]{1,0:T(8,128)(2,1)S(1)}, bf16[272,768]{1,0:T(8,128)(2,1)S(1)}, u32[]{:S(2)}, u32[]{:S(2)}) collective-permute-start(bf16[272,768]{1,0:T(8,128)(2,1)S(1)} %pad_maximum_fusion.1), channel_id=1, source_target_pairs={{0,4},{1,5},{2,6},{3,7},{4,0},{5,1},{6,2},{7,3},{8,12},{9,13},{10,... | collective-permute-start | bytes 1253384 | tf_op jit(solution)/shard_map/ppermute | solution.py:372
  57.8 45.8 %collective-permute-start.3 = (bf16[272,768]{1,0:T(8,128)(2,1)S(1)}, bf16[272,768]{1,0:T(8,128)(2,1)S(1)}, u32[]{:S(2)}, u32[]{:S(2)}) collective-permute-start(bf16[272,768]{1,0:T(8,128)(2,1)S(1)} %pad_maximum_fusion.1), channel_id=1, source_target_pairs={{0,2},{1,3},{2,0},{3,1},{4,6},{5,7},{6,4},{7,5},{8,10},{9,11},{10,... | collective-permute-start | bytes 1253384 | tf_op jit(solution)/shard_map/ppermute | solution.py:372
  139.2 30.1 %collective-permute-start.19 = (bf16[240,768]{1,0:T(8,128)(2,1)S(1)}, bf16[240,768]{1,0:T(8,128)(2,1)}, u32[]{:S(2)}, u32[]{:S(2)}) collective-permute-start(bf16[240,768]{1,0:T(8,128)(2,1)S(1)} %get-tuple-element.161), channel_id=1, source_target_pairs={{0,6},{1,7},{2,4},{3,5},{4,2},{5,3},{6,0},{7,1},{8,14},{9,15},{10,... | collective-permute-start | bytes 1105928 | tf_op jit(solution)/shard_map/ppermute | solution.py:372
  140.7 28.6 %collective-permute-start.18 = (bf16[240,768]{1,0:T(8,128)(2,1)S(1)}, bf16[240,768]{1,0:T(8,128)(2,1)}, u32[]{:S(2)}, u32[]{:S(2)}) collective-permute-start(bf16[240,768]{1,0:T(8,128)(2,1)S(1)} %get-tuple-element.161), channel_id=1, source_target_pairs={{0,4},{1,5},{2,6},{3,7},{4,0},{5,1},{6,2},{7,3},{8,12},{9,13},{10,... | collective-permute-start | bytes 1105928 | tf_op jit(solution)/shard_map/ppermute | solution.py:372
  142.1 27.2 %collective-permute-start.17 = (bf16[240,768]{1,0:T(8,128)(2,1)S(1)}, bf16[240,768]{1,0:T(8,128)(2,1)}, u32[]{:S(2)}, u32[]{:S(2)}) collective-permute-start(bf16[240,768]{1,0:T(8,128)(2,1)S(1)} %get-tuple-element.161), channel_id=1, source_target_pairs={{0,2},{1,3},{2,0},{3,1},{4,6},{5,7},{6,4},{7,5},{8,10},{9,11},{10,... | collective-permute-start | bytes 1105928 | tf_op jit(solution)/shard_map/ppermute | solution.py:372
  173.4 50.1 %collective-permute-start.26 = (bf16[240,768]{1,0:T(8,128)(2,1)S(1)}, bf16[240,768]{1,0:T(8,128)(2,1)S(1)}, u32[]{:S(2)}, u32[]{:S(2)}) collective-permute-start(bf16[240,768]{1,0:T(8,128)(2,1)S(1)} %copy-done.6), channel_id=1, source_target_pairs={{0,6},{1,7},{2,4},{3,5},{4,2},{5,3},{6,0},{7,1},{8,14},{9,15},{10,... | collective-permute-start | bytes 1105928 | tf_op jit(solution)/shard_map/ppermute | solution.py:372
  174.9 48.7 %collective-permute-start.25 = (bf16[240,768]{1,0:T(8,128)(2,1)S(1)}, bf16[240,768]{1,0:T(8,128)(2,1)S(1)}, u32[]{:S(2)}, u32[]{:S(2)}) collective-permute-start(bf16[240,768]{1,0:T(8,128)(2,1)S(1)} %copy-done.6), channel_id=1, source_target_pairs={{0,4},{1,5},{2,6},{3,7},{4,0},{5,1},{6,2},{7,3},{8,12},{9,13},{10,... | collective-permute-start | bytes 1105928 | tf_op jit(solution)/shard_map/ppermute | solution.py:372
  175.9 47.6 %collective-permute-start.24 = (bf16[240,768]{1,0:T(8,128)(2,1)S(1)}, bf16[240,768]{1,0:T(8,128)(2,1)S(1)}, u32[]{:S(2)}, u32[]{:S(2)}) collective-permute-start(bf16[240,768]{1,0:T(8,128)(2,1)S(1)} %copy-done.6), channel_id=1, source_target_pairs={{0,2},{1,3},{2,0},{3,1},{4,6},{5,7},{6,4},{7,5},{8,10},{9,11},{10,... | collective-permute-start | bytes 1105928 | tf_op jit(solution)/shard_map/ppermute | solution.py:372
  223.6 37.9 %all-to-all-start.1 = ((bf16[4,2,196,768]{3,1,2,0:T(2,128)(2,1)}), bf16[4,2,196,768]{3,1,2,0:T(2,128)(2,1)}, u32[]{:S(2)}, u32[]{:S(2)}) async-start(bf16[4,2,196,768]{3,1,2,0:T(2,128)(2,1)} %param.9), calls=%async_computation.1 | async-start | bytes 4816896 | tf_op jit(solution)/shard_map/all_to_all | solution.py:680
  278.8 78.4 %all-to-all-start.2 = ((bf16[1,8,196,768]{3,2,0,1:T(8,128)(2,1)}), bf16[1,8,196,768]{3,2,0,1:T(8,128)(2,1)}, u32[]{:S(2)}, u32[]{:S(2)}) async-start(bf16[1,8,196,768]{3,2,0,1:T(8,128)(2,1)} %slice.215), calls=%async_computation.2 | async-start | bytes 4915200 | tf_op jit(solution)/shard_map/all_to_all | solution.py:685
  283.4 329.1 %reduce-scatter.2.cloned.1.call-start = ((), (), s32[]{:S(2)}) async-start(), calls=%async_computation.7 | async-start | bytes 8515584 | tf_op jit(solution)/shard_map/reduce_scatter | solution.py:474
  332.3 24.9 %collective-permute-start.31 = (bf16[4,240,768]{2,1,0:T(8,128)(2,1)S(1)}, bf16[4,240,768]{2,1,0:T(8,128)(2,1)S(1)}, u32[]{:S(2)}, u32[]{:S(2)}) collective-permute-start(bf16[4,240,768]{2,1,0:T(8,128)(2,1)S(1)} %bitcast.298), channel_id=1, source_target_pairs={{0,1},{1,0},{2,3},{3,2},{4,5},{5,4},{6,7},{7,6},{8,9},{9,8},{10,11... | collective-permute-start | bytes 4423688 | tf_op jit(solution)/shard_map/ppermute | solution.py:372
  358.6 29.6 %collective-permute-start.34 = (bf16[240,768]{1,0:T(8,128)(2,1)}, bf16[240,768]{1,0:T(8,128)(2,1)S(1)}, u32[]{:S(2)}, u32[]{:S(2)}) collective-permute-start(bf16[240,768]{1,0:T(8,128)(2,1)} %get-tuple-element.326), channel_id=1, source_target_pairs={{0,6},{1,7},{2,4},{3,5},{4,2},{5,3},{6,0},{7,1},{8,14},{9,15},{10,... | collective-permute-start | bytes 1105928 | tf_op jit(solution)/shard_map/ppermute | solution.py:372
  361.5 26.7 %collective-permute-start.33 = (bf16[240,768]{1,0:T(8,128)(2,1)}, bf16[240,768]{1,0:T(8,128)(2,1)S(1)}, u32[]{:S(2)}, u32[]{:S(2)}) collective-permute-start(bf16[240,768]{1,0:T(8,128)(2,1)} %get-tuple-element.327), channel_id=1, source_target_pairs={{0,4},{1,5},{2,6},{3,7},{4,0},{5,1},{6,2},{7,3},{8,12},{9,13},{10,... | collective-permute-start | bytes 1105928 | tf_op jit(solution)/shard_map/ppermute | solution.py:372
  361.7 26.5 %collective-permute-start.32 = (bf16[240,768]{1,0:T(8,128)(2,1)}, bf16[240,768]{1,0:T(8,128)(2,1)}, u32[]{:S(2)}, u32[]{:S(2)}) collective-permute-start(bf16[240,768]{1,0:T(8,128)(2,1)} %get-tuple-element.328), channel_id=1, source_target_pairs={{0,2},{1,3},{2,0},{3,1},{4,6},{5,7},{6,4},{7,5},{8,10},{9,11},{10,... | collective-permute-start | bytes 1105928 | tf_op jit(solution)/shard_map/ppermute | solution.py:372
  408.3 26.1 %collective-permute-start.38 = (bf16[240,768]{1,0:T(8,128)(2,1)S(1)}, bf16[240,768]{1,0:T(8,128)(2,1)S(1)}, u32[]{:S(2)}, u32[]{:S(2)}) collective-permute-start(bf16[240,768]{1,0:T(8,128)(2,1)S(1)} %get-tuple-element.322), channel_id=1, source_target_pairs={{0,6},{1,7},{2,4},{3,5},{4,2},{5,3},{6,0},{7,1},{8,14},{9,15},{10,... | collective-permute-start | bytes 1105928 | tf_op jit(solution)/shard_map/ppermute | solution.py:372
  411.2 23.2 %collective-permute-start.37 = (bf16[240,768]{1,0:T(8,128)(2,1)S(1)}, bf16[240,768]{1,0:T(8,128)(2,1)S(1)}, u32[]{:S(2)}, u32[]{:S(2)}) collective-permute-start(bf16[240,768]{1,0:T(8,128)(2,1)S(1)} %get-tuple-element.323), channel_id=1, source_target_pairs={{0,4},{1,5},{2,6},{3,7},{4,0},{5,1},{6,2},{7,3},{8,12},{9,13},{10,... | collective-permute-start | bytes 1105928 | tf_op jit(solution)/shard_map/ppermute | solution.py:372
  454.4 35.6 %collective-permute-start.42 = (bf16[240,768]{1,0:T(8,128)(2,1)}, bf16[240,768]{1,0:T(8,128)(2,1)S(1)}, u32[]{:S(2)}, u32[]{:S(2)}) collective-permute-start(bf16[240,768]{1,0:T(8,128)(2,1)} %get-tuple-element.318), channel_id=1, source_target_pairs={{0,6},{1,7},{2,4},{3,5},{4,2},{5,3},{6,0},{7,1},{8,14},{9,15},{10,... | collective-permute-start | bytes 1105928 | tf_op jit(solution)/shard_map/ppermute | solution.py:372
  457.3 32.7 %collective-permute-start.41 = (bf16[240,768]{1,0:T(8,128)(2,1)}, bf16[240,768]{1,0:T(8,128)(2,1)S(1)}, u32[]{:S(2)}, u32[]{:S(2)}) collective-permute-start(bf16[240,768]{1,0:T(8,128)(2,1)} %get-tuple-element.319), channel_id=1, source_target_pairs={{0,4},{1,5},{2,6},{3,7},{4,0},{5,1},{6,2},{7,3},{8,12},{9,13},{10,... | collective-permute-start | bytes 1105928 | tf_op jit(solution)/shard_map/ppermute | solution.py:372
  457.6 32.4 %collective-permute-start.40 = (bf16[240,768]{1,0:T(8,128)(2,1)}, bf16[240,768]{1,0:T(8,128)(2,1)}, u32[]{:S(2)}, u32[]{:S(2)}) collective-permute-start(bf16[240,768]{1,0:T(8,128)(2,1)} %get-tuple-element.320), channel_id=1, source_target_pairs={{0,2},{1,3},{2,0},{3,1},{4,6},{5,7},{6,4},{7,5},{8,10},{9,11},{10,... | collective-permute-start | bytes 1105928 | tf_op jit(solution)/shard_map/ppermute | solution.py:372
  517.4 29.5 %collective-permute-start.44 = (bf16[2,288,768]{2,1,0:T(8,128)(2,1)S(1)}, bf16[2,288,768]{2,1,0:T(8,128)(2,1)}, u32[]{:S(2)}, u32[]{:S(2)}) collective-permute-start(bf16[2,288,768]{2,1,0:T(8,128)(2,1)S(1)} %get-tuple-element.213), channel_id=1, source_target_pairs={{0,4},{1,5},{2,6},{3,7},{4,0},{5,1},{6,2},{7,3},{8,12},{9,13},{10,... | collective-permute-start | bytes 2654216 | tf_op jit(solution)/shard_map/ppermute | solution.py:372
  578.3 34.2 %all-to-all-start.3 = ((bf16[1,8,196,768]{3,2,0,1:T(8,128)(2,1)}), bf16[1,8,196,768]{3,2,0,1:T(8,128)(2,1)S(1)}, u32[]{:S(2)}, u32[]{:S(2)}) async-start(bf16[1,8,196,768]{3,2,0,1:T(8,128)(2,1)} %slice.219), calls=%async_computation.3 | async-start | bytes 4915200 | tf_op jit(solution)/shard_map/all_to_all | solution.py:685
  587.5 32.0 %collective-permute-start.50 = (bf16[240,768]{1,0:T(8,128)(2,1)}, bf16[240,768]{1,0:T(8,128)(2,1)}, u32[]{:S(2)}, u32[]{:S(2)}) collective-permute-start(bf16[240,768]{1,0:T(8,128)(2,1)} %get-tuple-element.332), channel_id=1, source_target_pairs={{0,8},{1,9},{2,10},{3,11},{4,12},{5,13},{6,14},{7,15},{8,16},{9,17... | collective-permute-start | bytes 1105928 | tf_op jit(solution)/shard_map/ppermute | solution.py:375
  587.5 32.0 %collective-permute-start.52 = (bf16[240,768]{1,0:T(8,128)(2,1)}, bf16[240,768]{1,0:T(8,128)(2,1)}, u32[]{:S(2)}, u32[]{:S(2)}) collective-permute-start(bf16[240,768]{1,0:T(8,128)(2,1)} %get-tuple-element.333), channel_id=1, source_target_pairs={{0,24},{1,25},{2,26},{3,27},{4,28},{5,29},{6,30},{7,31},{8,0},{9,1... | collective-permute-start | bytes 1105928 | tf_op jit(solution)/shard_map/ppermute | solution.py:375
  591.4 37.6 %collective-permute-start.51 = (bf16[240,768]{1,0:T(8,128)(2,1)S(1)}, bf16[240,768]{1,0:T(8,128)(2,1)}, u32[]{:S(2)}, u32[]{:S(2)}) collective-permute-start(bf16[240,768]{1,0:T(8,128)(2,1)S(1)} %get-tuple-element.334), channel_id=1, source_target_pairs={{0,16},{1,17},{2,18},{3,19},{4,20},{5,21},{6,22},{7,23},{8,24},{9,... | collective-permute-start | bytes 1105928 | tf_op jit(solution)/shard_map/ppermute | solution.py:375
  592.7 25.8 %collective-permute-start.54 = (bf16[96,768]{1,0:T(8,128)(2,1)}, bf16[96,768]{1,0:T(8,128)(2,1)S(1)}, u32[]{:S(2)}, u32[]{:S(2)}) collective-permute-start(bf16[96,768]{1,0:T(8,128)(2,1)} %pad_maximum_fusion.6), channel_id=1, source_target_pairs={{12,8},{13,9}} | collective-permute-start | bytes 442376 | tf_op jit(solution)/shard_map/ppermute | solution.py:542
  614.1 23.2 %all-to-all-start.4 = ((f32[32,16,128]{2,1,0:T(8,128)}), f32[32,16,128]{2,1,0:T(8,128)S(1)}, u32[]{:S(2)}, u32[]{:S(2)}) async-start(f32[32,16,128]{2,1,0:T(8,128)} %shard_map.149), calls=%async_computation.5 | async-start | bytes 524288 | tf_op jit(solution)/shard_map/all_to_all | solution.py:552
  (106 other events, 1078.4 us)
Sparse Core Ops, SparseCore 0:
  46.8 98.4 all-gather.1
  451.8 153.3 reduce-scatter.1

commit v8 on v7

--- a/solution.py
+++ b/solution.py
@@ -45,12 +45,12 @@
 
 def pair_forward(queries, keys, values, keep):
     stacked = split_heads(queries * jnp.asarray(HEAD_DIM**-0.5, BF16))
-    scores = jnp.where(keep, nt(stacked, keys), NEG)
-    top = jnp.max(scores, axis=1, keepdims=True)
+    scores = jnp.where(keep, nt(keys, stacked), NEG)
+    top = jnp.max(scores, axis=0, keepdims=True)
     weights = jnp.exp(scores - top)
-    total = jnp.sum(weights, axis=1, keepdims=True)
+    total = jnp.sum(weights, axis=0, keepdims=True)
     probs = (weights * (1.0 / total)).astype(BF16)
-    return join_heads(nn(probs, values)).astype(BF16)
+    return join_heads(tn(probs, values)).astype(BF16)
 
 
 def pair_backward(queries, keys, values, grad, keep):
@@ -106,7 +106,7 @@
 def forward_kernel(group, patches, count, *refs):
     project, mixed = (refs[:count], refs[count:])
     rows = project[0].size // project[0].shape[-1]
-    keep = keep_mask((2 * rows, rows), 1, group, patches)
+    keep = keep_mask((rows, 2 * rows), 0, group, patches)
     for pair in range(PAIRS):
         block = pair_forward(*[load(project, kind, pair) for kind in range(3)], keep)
         store(mixed, 0, pair, block)
@@ -316,8 +316,8 @@
 
 
 class Whole:
-    def __init__(self, axes, weights_in, weights_out, packed, width):
-        self.axes, self.width = (axes, width)
+    def __init__(self, axes, weights_in, weights_out, packed, width, clip):
+        self.axes, self.width, self.clip = (axes, width, clip)
         full_in = lax.all_gather(weights_in, axes, axis=0, tiled=True)
         full_out = lax.all_gather(weights_out, axes, axis=0, tiled=True)
         devices = lax.axis_size(axes)
@@ -350,7 +350,7 @@
 
 
 class Staged:
-    def __init__(self, axes, weights_in, weights_out, packed, width):
+    def __init__(self, axes, weights_in, weights_out, packed, width, clip):
         self.axes, self.width = (axes, width)
         me = lax.axis_index(axes)
         self.plane, self.spot, self.square, self.core = (me // 8, me % 8, me % 8 // 2, me % 2)
@@ -362,7 +362,7 @@
         flat = packed.reshape(1, -1)
         tail = jnp.pad(flat, ((0, 7), (0, width - flat.shape[1])))
         pieces = self.shifted(jnp.concatenate([weights_in, tail], axis=0))
-        pieces, weights_out = tie(pieces, weights_out)
+        pieces, (weights_out, self.clip) = tie(pieces, (weights_out, clip))
         full_out = lax.all_gather(weights_out, axes, axis=0, tiled=True)
         self.out_t, self.out_f = (full_out[:width], full_out[width : 2 * width])
         self.out_s, self.out_m = (full_out[2 * width : 3 * width], full_out[3 * width :])
@@ -528,15 +528,15 @@
 
     def total(self, sums, arrays, clip):
         rows, last = (self.rows_in, self.d_last)
-        extra, first = tie(self.towards(last[rows:], 1), last[:rows])
-        every = jnp.stack([first, self.d_p1, self.d_p2, self.d_p3], axis=0)
-        terms = [lax.dynamic_index_in_dim(every, self.plane, 0, keepdims=False)]
-        for step in (1, 2, 3):
-            block = lax.dynamic_index_in_dim(every, (self.plane + step) % 4, 0, keepdims=False)
-            terms.append(self.shift(block, step))
+        every = jnp.stack([last[:rows], self.d_p1, self.d_p2, self.d_p3], axis=0)
+        blocks = [
+            lax.dynamic_index_in_dim(every, (self.plane + step) % 4, 0, keepdims=False) for step in range(4)
+        ]
+        blocks, extra = tie(blocks, last[rows:])
+        terms = blocks[:1] + [self.shift(blocks[step], step) for step in (1, 2, 3)]
+        beside, arrays = tie(self.flip(extra, 1), arrays)
+        extra = self.towards(jnp.concatenate([extra, beside], axis=0), 1)
         extra = self.added(extra).astype(BF16)
-        beside, arrays = tie(self.flip(extra, 1), arrays)
-        extra = jnp.concatenate([extra, beside], axis=0)
         blocks = [extra]
         for bits in (2, 4, 6):
             blocks.append(lax.ppermute(extra, self.axes, [(8 + bits + core, 8 + core) for core in range(2)]))
@@ -676,8 +676,10 @@
     shift_count = shift_rows.shape[0]
     staged = lax.axis_size(both) == 32 and group == 4 and weights_in.shape[0] == 240 and weights_out.shape[0] == 168
 
-    def enter(x):
-        x = lax.all_to_all(x, "seq", split_axis=0, concat_axis=1, tiled=True)
+    def exchange(x):
+        return lax.all_to_all(x, "seq", split_axis=0, concat_axis=1, tiled=True)
+
+    def widen(x):
         return jnp.pad(x, ((0, 0), (0, 0), (0, rows - patches), (0, 0)))
 
     def leave(x):
@@ -685,8 +687,8 @@
         return lax.all_to_all(x, "seq", split_axis=1, concat_axis=0, tiled=True)
 
     packed = jnp.concatenate([norm_gain, shift_rows, dense_shift[None, :]], axis=0)
-    feed = (Staged if staged else Whole)(both, weights_in, weights_out, packed, width)
-    clip = enter(clips_in)
+    feed = (Staged if staged else Whole)(both, weights_in, weights_out, packed, width, exchange(clips_in))
+    clip = widen(feed.clip)
     if staged:
         clip = feed.begin(clip)
     live = lax.dynamic_slice(clip_live, (lax.axis_index("seq") * own,), (own,)).astype(BF16)
@@ -695,7 +697,7 @@
         gradient = cotangent * 1
         if staged:
             gradient = tie(gradient, after)[0]
-        return enter(gradient) * live[:, None, None, None]
+        return widen(exchange(gradient)) * live[:, None, None, None]
 
     output, grad_clip, summed_in, summed_out, owned = block(clip, target, leave, feed, gain_count, patches)
     return (

time: 657 us -> 627 us (0.954)
  waiting for transfers between devices: 125 us -> 93.9 us
    ppermute x6, waiting for transfers between devices: 40.9 us -> 6.94 us  [shift(): lax.ppermute(x, self.axes, [(d, (d + 8 * step) % 32) for d in range(32)])]
    all_to_all x2, waiting for transfers between devices: 37.4 us -> 21.7 us  [exchange(): return lax.all_to_all(x, 'seq', split_axis=0, concat_axis=1, tiled=True)]
    ppermute x44, waiting for transfers between devices: 39.6 us -> 50.6 us  [flip(): return lax.ppermute(x, self.axes, [(d, d ^ bits) for d in range(32)])]
    unnamed x152 -> x167, local copies, waits for them, and re-layouts: 26.3 us -> 26.1 us
  transfers between devices with their start and end apart: 63 -> 63, of which waited for: 12 -> 14; matrix products, arithmetic and copies ran while one was open for 41% -> 43% of each run, Pallas kernels for 19% -> 19%
where the time goes in v8:
time: 627 us; the launch traced here: 617 us
  matrix products  198 us (32%)
  Pallas kernels  120 us (19%)
  waiting for transfers between devices  93.9 us (15%)
  starting transfers between devices  77.3 us (12%)
  other arithmetic  55.1 us (9%)
  local copies, waits for them, and re-layouts  54.4 us (9%)
  between operations  17 us (3%)
    pallas_call x4, Pallas kernels, attention_call(): pl.pallas_call(partial(kernel, group, patches, count), grid=(clips, steps...  79.3 us
    dot_general x8, matrix products, nn(): lax.dot_general(left, right, (((1,), (0,)), ((), ())), preferred_element_...  71.3 us
    dot_general x9, matrix products, nt(): lax.dot_general(left, right, (((1,), (1,)), ((), ())), preferred_element_...  71.2 us
    dot_general x8, matrix products, tn(): lax.dot_general(left, right, (((0,), (0,)), ((), ())), preferred_element_...  55.9 us
    ppermute x44, waiting for transfers between devices, flip(): return lax.ppermute(x, self.axes, [(d, d ^ bits) for d in range(32)])  50.6 us
    ppermute x44, starting transfers between devices, flip(): return lax.ppermute(x, self.axes, [(d, d ^ bits) for d in range(32)])  33.1 us
    unnamed x167, local copies, waits for them, and re-layouts  26.1 us
    all_to_all x2, waiting for transfers between devices, exchange(): return lax.all_to_all(x, 'seq', split_axis=0, concat_axis=1, tiled=True)  21.7 us
  transfers between devices with their start and end apart: 63, of which 14 were waited for; matrix products, arithmetic and copies ran while one was open for 43% of the time, Pallas kernels for 19%

profile of v8, /device:TPU:0, one launch (start us, length us, event | category | flops | bytes accessed | tf_op | source)
XLA Modules:
  0.0 616.5 jit_solution(8648188809564679173)
XLA Ops:
  19.8 21.7 %all-to-all-done = bf16[4,2,196,768]{3,1,2,0:T(2,128)(2,1)} async-done(((bf16[4,2,196,768]{3,1,2,0:T(2,128)(2,1)}), bf16[4,2,196,768]{3,1,2,0:T(2,128)(2,1)}, u32[]{:S(2)}, u32[]{:S(2)}) %all-to-all-start) | async-done | bytes 2408480 | tf_op jit(solution)/shard_map/all_to_all | solution.py:680
  44.9 6.9 %collective-permute-done.1 = bf16[248,768]{1,0:T(8,128)(2,1)S(1)} collective-permute-done((bf16[248,768]{1,0:T(8,128)(2,1)S(1)}, bf16[248,768]{1,0:T(8,128)(2,1)S(1)}, u32[]{:S(2)}, u32[]{:S(2)}) %collective-permute-start.1) | collective-permute-done | bytes 380960 | tf_op jit(solution)/shard_map/ppermute | solution.py:375
  60.4 9.9 %collective-permute-done.5 = bf16[272,768]{1,0:T(8,128)(2,1)S(1)} collective-permute-done((bf16[272,768]{1,0:T(8,128)(2,1)S(1)}, bf16[272,768]{1,0:T(8,128)(2,1)S(1)}, u32[]{:S(2)}, u32[]{:S(2)}) %collective-permute-start.5) | collective-permute-done | bytes 417824 | tf_op jit(solution)/shard_map/ppermute | solution.py:372
  70.3 7.4 %collective-permute-done.4 = bf16[272,768]{1,0:T(8,128)(2,1)S(1)} collective-permute-done((bf16[272,768]{1,0:T(8,128)(2,1)S(1)}, bf16[272,768]{1,0:T(8,128)(2,1)S(1)}, u32[]{:S(2)}, u32[]{:S(2)}) %collective-permute-start.4) | collective-permute-done | bytes 417824 | tf_op jit(solution)/shard_map/ppermute | solution.py:372
  97.6 7.3 %convolution_convert_fusion = bf16[1664,1920]{1,0:T(8,128)(2,1)} fusion(bf16[1664,768]{1,0:T(8,128)(2,1)S(1)} %bitcast.316, bf16[1920,768]{1,0:T(8,128)(2,1)S(1)} %bitcast.299), kind=kOutput, calls=%fused_computation.10 | convolution fusion | flops 4910530560 | bytes 11894784 | tf_op jit(solution)/shard_map/dot_general | solution.py:23
  123.4 14.9 %shard_map.138 = bf16[1,8,208,768]{3,2,1,0:T(8,128)(2,1)} custom-call(bf16[1,8,208,1920]{3,2,1,0:T(8,128)(2,1)} %bitcast.324, bf16[1,8,208,384]{3,2,1,0:T(8,128)(2,1)} %bitcast.342), custom_call_target="tpu_custom_call" | custom-call | flops 14976000000 | tf_op jit(solution)/shard_map/pallas_call | solution.py:135
  168.8 8.4 %convolution_convert_fusion.1 = bf16[1664,1536]{1,0:T(8,128)(2,1)} fusion(bf16[1664,768]{1,0:T(8,128)(2,1)S(1)} %add_convert_fusion.3, bf16[3840,768]{1,0:T(8,128)(2,1)} %bitcast.240), kind=kOutput, calls=%fused_computation.11 | convolution fusion | flops 3928424448 | bytes 10027008 | tf_op jit(solution)/shard_map/dot_general | solution.py:23
  182.2 12.0 %shard_map.140 = bf16[1,8,208,768]{3,2,1,0:T(8,128)(2,1)} custom-call(bf16[1,8,208,1536]{3,2,1,0:T(8,128)(2,1)} %bitcast.326, bf16[1,8,208,768]{3,2,1,0:T(8,128)(2,1)} %bitcast.336), custom_call_target="tpu_custom_call" | custom-call | flops 14976000000 | tf_op jit(solution)/shard_map/pallas_call | solution.py:135
  200.1 6.4 %fusion.77 = (f32[1664]{0:T(1024)S(1)}, f32[1664,768]{1,0:T(8,128)S(1)}) fusion(f32[768]{0:T(1024)S(1)} %add.401, bf16[1664,768]{1,0:T(8,128)(2,1)} %bitcast.334, bf16[5376,768]{1,0:T(8,128)(2,1)} %all-gather.2.cloned.1.call-done, bf16[1664,768]{1,0:T(8,128)(2,1)} %copy-done.15, bf16[1,8,208,768]{3,2,1,0:T(8,128)(2,1)} %copy-done.9), kind=kOutput, calls=%fused_computation.196 | convolution fusion | flops 1970600320 | bytes 13968896 | tf_op jit(solution)/shard_map/dot_general | solution.py:27
  207.3 5.5 shard_map.141
  215.2 17.2 %fusion.4 = (bf16[1664,3072]{1,0:T(8,128)(2,1)}, bf16[1664,3072]{1,0:T(8,128)(2,1)}) fusion(f32[3072]{0:T(1024)S(1)} %add.409, bf16[3840,768]{1,0:T(8,128)(2,1)S(1)} %bitcast.245, f32[1664,768]{1,0:T(8,128)S(1)} %get-tuple-element.347, f32[768]{0:T(1024)S(1)} %add.406, f32[768]{0:T(1024)S(1)} %mul.260, f32[1664]{0:T(1024)S(1)} %add_rsqrt_fusion, ...), kind=kOutput, calls=%fused_computation.5 | convolution fusion | flops 7919468544 | bytes 30314496 | tf_op jit(solution)/shard_map/dot_general | solution.py:23
  235.6 12.5 %add_convert_fusion.1 = bf16[1664,768]{1,0:T(8,128)(2,1)S(1)} fusion(f32[1664,768]{1,0:T(8,128)S(1)} %copy-done.21, bf16[1664,3072]{1,0:T(8,128)(2,1)} %get-tuple-element.178, bf16[5376,768]{1,0:T(8,128)(2,1)} %all-gather.2.cloned.1.call-done, f32[768]{0:T(1024)S(1)} %add.418), kind=kOutput, calls=%fused_computation.43 | convolution fusion | flops 7855570944 | bytes 22612992 | tf_op jit(solution)/shard_map/dot_general | solution.py:27
  254.3 15.1 %multiply_convert_fusion = bf16[1664,3072]{1,0:T(8,128)(2,1)} fusion(bf16[1664,3072]{1,0:T(8,128)(2,1)} %get-tuple-element.175, bf16[1664,768]{1,0:T(8,128)(2,1)S(1)} %bitcast.305, bf16[5376,768]{1,0:T(8,128)(2,1)} %all-gather.2.cloned.1.call-done), kind=kOutput, calls=%fused_computation.7 | convolution fusion | flops 7867072512 | bytes 27721728 | tf_op jit(solution)/shard_map/dot_general | solution.py:23
  269.4 13.8 %fusion.35.refs_0_.refs_1_ = bf16[384,8,768]{2,1,0:T(8,128)(2,1)S(1)} fusion(bf16[1664,3072]{1,0:T(8,128)(2,1)} %multiply_convert_fusion, f32[1664,768]{1,0:T(8,128)} %copy-done.20, f32[768]{0:T(1024)S(1)} %add.406, f32[768]{0:T(1024)S(1)} %mul.260, f32[1664]{0:T(1024)S(1)} %add_rsqrt_fusion, f32[1664]{0:T(1024)S(1)} %broadcast_multiply_fusion.6), kind=kOutput, calls=%fused_computation.79 | convolution fusion | flops 7860486144 | bytes 20073472 | tf_op jit(solution)/shard_map/dot_general | solution.py:31
  288.0 15.1 %multiply_reduce_fusion = (f32[768]{0:T(1024)S(1)}, f32[1664]{0:T(1024)S(1)}, f32[1664]{0:T(1024)S(1)}, f32[768]{0:T(1024)S(1)}, f32[1664,768]{1,0:T(8,128)}) fusion(f32[1664,768]{1,0:T(8,128)} %copy-done.20, f32[1664]{0:T(1024)S(1)} %add_rsqrt_fusion, f32[1664]{0:T(1024)S(1)} %broadcast_multiply_fusion.6, f32[768]{0:T(1024)S(1)} %mul.260, ...), kind=kOutput, calls=%fused_computation.39 | convolution fusion | flops 7863233536 | bytes 25205760 | tf_op jit(solution)/shard_map/dot_general | solution.py:27
  303.6 5.5 fusion.76
  309.2 5.8 convolution_convert_fusion.7
  315.0 13.1 %fusion.36.refs_3_ = bf16[384,8,768]{2,1,0:T(8,128)(2,1)} fusion(bf16[1664,3072]{1,0:T(8,128)(2,1)} %get-tuple-element.178, bf16[1664,768]{1,0:T(8,128)(2,1)S(1)} %bitcast.307), kind=kOutput, calls=%fused_computation.80 | convolution fusion | flops 7854096384 | bytes 17498112 | tf_op jit(solution)/shard_map/dot_general | solution.py:31
  332.9 26.1 %shard_map.143 = (bf16[1,8,208,1536]{3,2,1,0:T(8,128)(2,1)}, bf16[1,8,208,768]{3,2,1,0:T(8,128)(2,1)}) custom-call(bf16[1,8,208,1536]{3,2,1,0:T(8,128)(2,1)} %bitcast.327, bf16[1,8,208,768]{3,2,1,0:T(8,128)(2,1)} %bitcast.337, bf16[1,8,208,768]{3,2,1,0:T(8,128)(2,1)} %bitcast.340), custom_call_target="tpu_custom_call" | custom-call | flops 23296000000 | tf_op jit(solution)/shard_map/pallas_call | solution.py:135
  382.0 5.9 fusion.46
  387.9 9.6 %multiply_reduce_fusion.1 = (f32[768]{0:T(1024)}, f32[1664]{0:T(1024)S(1)}, f32[1664]{0:T(1024)S(1)}, f32[768]{0:T(1024)}, f32[1664,768]{1,0:T(8,128)S(1)}) fusion(f32[1664]{0:T(1024)S(1)} %copy-done.59, f32[1664]{0:T(1024)S(1)} %copy-done.53, bf16[1664,768]{1,0:T(8,128)(2,1)S(1)} %copy-done.16, bf16[1,8,208,768]{3,2,1,0:T(8,128)(2,1)S(1)} %copy-done.12, ...), kind=kOutput, calls=%fused_computation.40 | convolution fusion | flops 3942477056 | bytes 22842368 | tf_op jit(solution)/shard_map/dot_general | solution.py:27
  415.8 6.3 %shard_map.146 = bf16[672,8,768]{2,1,0:T(8,128)(2,1)} custom-call(bf16[96,8,768]{2,1,0:T(8,128)(2,1)} %fusion.41.refs_0_, bf16[96,8,768]{2,1,0:T(8,128)(2,1)} %fusion.42.refs_1_, bf16[96,8,768]{2,1,0:T(8,128)(2,1)} %fusion.43.refs_2_, bf16[384,8,768]{2,1,0:T(8,128)(2,1)} %fusion.36.refs_3_), custom_call_target="tpu_custom_call" | custom-call | bytes 33030144 | tf_op jit(solution)/shard_map/pallas_call | solution.py:274
  428.4 5.9 convolution_convert_fusion.5
  434.3 26.3 %shard_map.147 = bf16[1,8,208,2304]{3,2,1,0:T(8,128)(2,1)} custom-call(bf16[1,8,208,1920]{3,2,1,0:T(8,128)(2,1)} %bitcast.325, bf16[1,8,208,384]{3,2,1,0:T(8,128)(2,1)} %bitcast.343, bf16[1,8,208,768]{3,2,1,0:T(8,128)(2,1)} %bitcast.341), custom_call_target="tpu_custom_call" | custom-call | flops 23296000000 | tf_op jit(solution)/shard_map/pallas_call | solution.py:135
  461.5 9.2 %fusion.39.refs_0_ = bf16[288,8,768]{2,1,0:T(8,128)(2,1)S(1)} fusion(bf16[1664,2304]{1,0:T(8,128)(2,1)} %bitcast.322, bf16[1664,768]{1,0:T(8,128)(2,1)S(1)} %copy-done.28), kind=kOutput, calls=%fused_computation.83 | convolution fusion | flops 5890572288 | bytes 13762560 | tf_op jit(solution)/shard_map/dot_general | solution.py:31
  493.7 12.9 %fusion.19 = (f32[768]{0:T(1024)S(1)}, f32[1664]{0:T(1024)S(1)}, f32[1664]{0:T(1024)S(1)}, f32[768]{0:T(1024)S(1)}, f32[1664,768]{1,0:T(8,128)}) fusion(bf16[1,8,208,768]{3,2,1,0:T(8,128)(2,1)S(1)} %copy-done.13, f32[1664]{0:T(1024)S(1)} %copy-done.57, f32[1664]{0:T(1024)S(1)} %copy-done.55, f32[768]{0:T(1024)S(1)} %copy-done.61, ...), kind=kOutput, calls=%fused_computation.30 | convolution fusion | flops 5901577216 | bytes 18914304 | tf_op jit(solution)/shard_map/dot_general | solution.py:27
  506.6 14.6 %collective-permute-done.44 = bf16[2,288,768]{2,1,0:T(8,128)(2,1)} collective-permute-done((bf16[2,288,768]{2,1,0:T(8,128)(2,1)S(1)}, bf16[2,288,768]{2,1,0:T(8,128)(2,1)}, u32[]{:S(2)}, u32[]{:S(2)}) %collective-permute-start.44) | collective-permute-done | bytes 884768 | tf_op jit(solution)/shard_map/ppermute | solution.py:372
  530.9 10.8 %collective-permute-done.45 = bf16[288,768]{1,0:T(8,128)(2,1)S(1)} collective-permute-done((bf16[288,768]{1,0:T(8,128)(2,1)S(1)}, bf16[288,768]{1,0:T(8,128)(2,1)S(1)}, u32[]{:S(2)}, u32[]{:S(2)}) %collective-permute-start.45) | collective-permute-done | bytes 442400 | tf_op jit(solution)/shard_map/ppermute | solution.py:372
  562.2 5.9 convert_reduce_fusion
  574.7 9.8 %all-to-all-done.3 = bf16[1,8,196,768]{3,2,0,1:T(8,128)(2,1)} async-done(((bf16[1,8,196,768]{3,2,0,1:T(8,128)(2,1)}), bf16[1,8,196,768]{3,2,0,1:T(8,128)(2,1)}, u32[]{:S(2)}, u32[]{:S(2)}) %all-to-all-start.3) | async-done | bytes 2408480 | tf_op jit(solution)/shard_map/all_to_all | solution.py:687
  590.2 6.7 %all-to-all-start.4 = ((f32[32,16,128]{2,1,0:T(8,128)}), f32[32,16,128]{2,1,0:T(8,128)S(1)}, u32[]{:S(2)}, u32[]{:S(2)}) async-start(f32[32,16,128]{2,1,0:T(8,128)} %shard_map.149), calls=%async_computation.5 | async-start | bytes 524288 | tf_op jit(solution)/shard_map/all_to_all | solution.py:552
  601.1 5.8 copy.36
  (407 shorter events, 245.3 us)
Async XLA Ops:
  7.2 34.3 %all-to-all-start = ((bf16[4,2,196,768]{3,1,2,0:T(2,128)(2,1)}), bf16[4,2,196,768]{3,1,2,0:T(2,128)(2,1)}, u32[]{:S(2)}, u32[]{:S(2)}) async-start(bf16[4,2,196,768]{3,1,2,0:T(2,128)(2,1)} %param.8), calls=%async_computation | async-start | bytes 4816896 | tf_op jit(solution)/shard_map/all_to_all | solution.py:680
  11.7 144.4 %all-gather.2.cloned.1.call-start = ((), (), s32[]{:S(2)}) async-start(), calls=%async_computation.6 | async-start | bytes 8515584 | tf_op jit(solution)/shard_map/all_gather | solution.py:366
  13.6 31.3 %collective-permute-start.2 = (bf16[248,768]{1,0:T(8,128)(2,1)S(1)}, bf16[248,768]{1,0:T(8,128)(2,1)S(1)}, u32[]{:S(2)}, u32[]{:S(2)}) collective-permute-start(bf16[248,768]{1,0:T(8,128)(2,1)S(1)} %fusion.57), channel_id=1, source_target_pairs={{0,24},{1,25},{2,26},{3,27},{4,28},{5,29},{6,30},{7,31},{8,0},{9,1... | collective-permute-start | bytes 1142792 | tf_op jit(solution)/shard_map/ppermute | solution.py:375
  18.7 33.1 %collective-permute-start.1 = (bf16[248,768]{1,0:T(8,128)(2,1)S(1)}, bf16[248,768]{1,0:T(8,128)(2,1)S(1)}, u32[]{:S(2)}, u32[]{:S(2)}) collective-permute-start(bf16[248,768]{1,0:T(8,128)(2,1)S(1)} %fusion.57), channel_id=1, source_target_pairs={{0,16},{1,17},{2,18},{3,19},{4,20},{5,21},{6,22},{7,23},{8,24},{9,... | collective-permute-start | bytes 1142792 | tf_op jit(solution)/shard_map/ppermute | solution.py:375
  18.7 33.1 %collective-permute-start = (bf16[248,768]{1,0:T(8,128)(2,1)S(1)}, bf16[248,768]{1,0:T(8,128)(2,1)S(1)}, u32[]{:S(2)}, u32[]{:S(2)}) collective-permute-start(bf16[248,768]{1,0:T(8,128)(2,1)S(1)} %fusion.57), channel_id=1, source_target_pairs={{0,8},{1,9},{2,10},{3,11},{4,12},{5,13},{6,14},{7,15},{8,16},{9,17... | collective-permute-start | bytes 1142792 | tf_op jit(solution)/shard_map/ppermute | solution.py:375
  57.6 20.2 %collective-permute-start.4 = (bf16[272,768]{1,0:T(8,128)(2,1)S(1)}, bf16[272,768]{1,0:T(8,128)(2,1)S(1)}, u32[]{:S(2)}, u32[]{:S(2)}) collective-permute-start(bf16[272,768]{1,0:T(8,128)(2,1)S(1)} %pad_maximum_fusion.1), channel_id=1, source_target_pairs={{0,4},{1,5},{2,6},{3,7},{4,0},{5,1},{6,2},{7,3},{8,12},{9,13},{10,... | collective-permute-start | bytes 1253384 | tf_op jit(solution)/shard_map/ppermute | solution.py:372
  109.6 28.7 %collective-permute-start.19 = (bf16[240,768]{1,0:T(8,128)(2,1)S(1)}, bf16[240,768]{1,0:T(8,128)(2,1)}, u32[]{:S(2)}, u32[]{:S(2)}) collective-permute-start(bf16[240,768]{1,0:T(8,128)(2,1)S(1)} %get-tuple-element.163), channel_id=1, source_target_pairs={{0,6},{1,7},{2,4},{3,5},{4,2},{5,3},{6,0},{7,1},{8,14},{9,15},{10,... | collective-permute-start | bytes 1105928 | tf_op jit(solution)/shard_map/ppermute | solution.py:372
  111.0 32.6 %collective-permute-start.18 = (bf16[240,768]{1,0:T(8,128)(2,1)S(1)}, bf16[240,768]{1,0:T(8,128)(2,1)}, u32[]{:S(2)}, u32[]{:S(2)}) collective-permute-start(bf16[240,768]{1,0:T(8,128)(2,1)S(1)} %get-tuple-element.163), channel_id=1, source_target_pairs={{0,4},{1,5},{2,6},{3,7},{4,0},{5,1},{6,2},{7,3},{8,12},{9,13},{10,... | collective-permute-start | bytes 1105928 | tf_op jit(solution)/shard_map/ppermute | solution.py:372
  112.4 31.3 %collective-permute-start.17 = (bf16[240,768]{1,0:T(8,128)(2,1)S(1)}, bf16[240,768]{1,0:T(8,128)(2,1)}, u32[]{:S(2)}, u32[]{:S(2)}) collective-permute-start(bf16[240,768]{1,0:T(8,128)(2,1)S(1)} %get-tuple-element.163), channel_id=1, source_target_pairs={{0,2},{1,3},{2,0},{3,1},{4,6},{5,7},{6,4},{7,5},{8,10},{9,11},{10,... | collective-permute-start | bytes 1105928 | tf_op jit(solution)/shard_map/ppermute | solution.py:372
  147.7 46.6 %collective-permute-start.26 = (bf16[240,768]{1,0:T(8,128)(2,1)S(1)}, bf16[240,768]{1,0:T(8,128)(2,1)S(1)}, u32[]{:S(2)}, u32[]{:S(2)}) collective-permute-start(bf16[240,768]{1,0:T(8,128)(2,1)S(1)} %copy-done.6), channel_id=1, source_target_pairs={{0,6},{1,7},{2,4},{3,5},{4,2},{5,3},{6,0},{7,1},{8,14},{9,15},{10,... | collective-permute-start | bytes 1105928 | tf_op jit(solution)/shard_map/ppermute | solution.py:372
  149.2 45.1 %collective-permute-start.25 = (bf16[240,768]{1,0:T(8,128)(2,1)S(1)}, bf16[240,768]{1,0:T(8,128)(2,1)S(1)}, u32[]{:S(2)}, u32[]{:S(2)}) collective-permute-start(bf16[240,768]{1,0:T(8,128)(2,1)S(1)} %copy-done.6), channel_id=1, source_target_pairs={{0,4},{1,5},{2,6},{3,7},{4,0},{5,1},{6,2},{7,3},{8,12},{9,13},{10,... | collective-permute-start | bytes 1105928 | tf_op jit(solution)/shard_map/ppermute | solution.py:372
  149.9 44.4 %collective-permute-start.24 = (bf16[240,768]{1,0:T(8,128)(2,1)S(1)}, bf16[240,768]{1,0:T(8,128)(2,1)S(1)}, u32[]{:S(2)}, u32[]{:S(2)}) collective-permute-start(bf16[240,768]{1,0:T(8,128)(2,1)S(1)} %copy-done.6), channel_id=1, source_target_pairs={{0,2},{1,3},{2,0},{3,1},{4,6},{5,7},{6,4},{7,5},{8,10},{9,11},{10,... | collective-permute-start | bytes 1105928 | tf_op jit(solution)/shard_map/ppermute | solution.py:372
  194.3 38.1 %all-to-all-start.1 = ((bf16[4,2,196,768]{3,1,2,0:T(2,128)(2,1)}), bf16[4,2,196,768]{3,1,2,0:T(2,128)(2,1)}, u32[]{:S(2)}, u32[]{:S(2)}) async-start(bf16[4,2,196,768]{3,1,2,0:T(2,128)(2,1)} %param.9), calls=%async_computation.1 | async-start | bytes 4816896 | tf_op jit(solution)/shard_map/all_to_all | solution.py:680
  249.7 78.3 %all-to-all-start.2 = ((bf16[1,8,196,768]{3,2,0,1:T(8,128)(2,1)}), bf16[1,8,196,768]{3,2,0,1:T(8,128)(2,1)}, u32[]{:S(2)}, u32[]{:S(2)}) async-start(bf16[1,8,196,768]{3,2,0,1:T(8,128)(2,1)} %slice.215), calls=%async_computation.2 | async-start | bytes 4915200 | tf_op jit(solution)/shard_map/all_to_all | solution.py:687
  254.2 334.3 %reduce-scatter.2.cloned.1.call-start = ((), (), s32[]{:S(2)}) async-start(), calls=%async_computation.7 | async-start | bytes 8515584 | tf_op jit(solution)/shard_map/reduce_scatter | solution.py:474
  303.2 24.9 %collective-permute-start.31 = (bf16[4,240,768]{2,1,0:T(8,128)(2,1)S(1)}, bf16[4,240,768]{2,1,0:T(8,128)(2,1)S(1)}, u32[]{:S(2)}, u32[]{:S(2)}) collective-permute-start(bf16[4,240,768]{2,1,0:T(8,128)(2,1)S(1)} %bitcast.301), channel_id=1, source_target_pairs={{0,1},{1,0},{2,3},{3,2},{4,5},{5,4},{6,7},{7,6},{8,9},{9,8},{10,11... | collective-permute-start | bytes 4423688 | tf_op jit(solution)/shard_map/ppermute | solution.py:372
  329.4 29.6 %collective-permute-start.34 = (bf16[240,768]{1,0:T(8,128)(2,1)}, bf16[240,768]{1,0:T(8,128)(2,1)S(1)}, u32[]{:S(2)}, u32[]{:S(2)}) collective-permute-start(bf16[240,768]{1,0:T(8,128)(2,1)} %get-tuple-element.328), channel_id=1, source_target_pairs={{0,6},{1,7},{2,4},{3,5},{4,2},{5,3},{6,0},{7,1},{8,14},{9,15},{10,... | collective-permute-start | bytes 1105928 | tf_op jit(solution)/shard_map/ppermute | solution.py:372
  332.3 26.7 %collective-permute-start.33 = (bf16[240,768]{1,0:T(8,128)(2,1)}, bf16[240,768]{1,0:T(8,128)(2,1)S(1)}, u32[]{:S(2)}, u32[]{:S(2)}) collective-permute-start(bf16[240,768]{1,0:T(8,128)(2,1)} %get-tuple-element.329), channel_id=1, source_target_pairs={{0,4},{1,5},{2,6},{3,7},{4,0},{5,1},{6,2},{7,3},{8,12},{9,13},{10,... | collective-permute-start | bytes 1105928 | tf_op jit(solution)/shard_map/ppermute | solution.py:372
  332.5 26.5 %collective-permute-start.32 = (bf16[240,768]{1,0:T(8,128)(2,1)}, bf16[240,768]{1,0:T(8,128)(2,1)}, u32[]{:S(2)}, u32[]{:S(2)}) collective-permute-start(bf16[240,768]{1,0:T(8,128)(2,1)} %get-tuple-element.330), channel_id=1, source_target_pairs={{0,2},{1,3},{2,0},{3,1},{4,6},{5,7},{6,4},{7,5},{8,10},{9,11},{10,... | collective-permute-start | bytes 1105928 | tf_op jit(solution)/shard_map/ppermute | solution.py:372
  378.4 26.3 %collective-permute-start.38 = (bf16[240,768]{1,0:T(8,128)(2,1)S(1)}, bf16[240,768]{1,0:T(8,128)(2,1)S(1)}, u32[]{:S(2)}, u32[]{:S(2)}) collective-permute-start(bf16[240,768]{1,0:T(8,128)(2,1)S(1)} %get-tuple-element.324), channel_id=1, source_target_pairs={{0,6},{1,7},{2,4},{3,5},{4,2},{5,3},{6,0},{7,1},{8,14},{9,15},{10,... | collective-permute-start | bytes 1105928 | tf_op jit(solution)/shard_map/ppermute | solution.py:372
  381.3 23.4 %collective-permute-start.37 = (bf16[240,768]{1,0:T(8,128)(2,1)S(1)}, bf16[240,768]{1,0:T(8,128)(2,1)S(1)}, u32[]{:S(2)}, u32[]{:S(2)}) collective-permute-start(bf16[240,768]{1,0:T(8,128)(2,1)S(1)} %get-tuple-element.325), channel_id=1, source_target_pairs={{0,4},{1,5},{2,6},{3,7},{4,0},{5,1},{6,2},{7,3},{8,12},{9,13},{10,... | collective-permute-start | bytes 1105928 | tf_op jit(solution)/shard_map/ppermute | solution.py:372
  381.5 23.2 %collective-permute-start.36 = (bf16[240,768]{1,0:T(8,128)(2,1)S(1)}, bf16[240,768]{1,0:T(8,128)(2,1)S(1)}, u32[]{:S(2)}, u32[]{:S(2)}) collective-permute-start(bf16[240,768]{1,0:T(8,128)(2,1)S(1)} %get-tuple-element.326), channel_id=1, source_target_pairs={{0,2},{1,3},{2,0},{3,1},{4,6},{5,7},{6,4},{7,5},{8,10},{9,11},{10,... | collective-permute-start | bytes 1105928 | tf_op jit(solution)/shard_map/ppermute | solution.py:372
  424.9 35.7 %collective-permute-start.42 = (bf16[240,768]{1,0:T(8,128)(2,1)}, bf16[240,768]{1,0:T(8,128)(2,1)S(1)}, u32[]{:S(2)}, u32[]{:S(2)}) collective-permute-start(bf16[240,768]{1,0:T(8,128)(2,1)} %get-tuple-element.320), channel_id=1, source_target_pairs={{0,6},{1,7},{2,4},{3,5},{4,2},{5,3},{6,0},{7,1},{8,14},{9,15},{10,... | collective-permute-start | bytes 1105928 | tf_op jit(solution)/shard_map/ppermute | solution.py:372
  427.7 32.9 %collective-permute-start.41 = (bf16[240,768]{1,0:T(8,128)(2,1)}, bf16[240,768]{1,0:T(8,128)(2,1)S(1)}, u32[]{:S(2)}, u32[]{:S(2)}) collective-permute-start(bf16[240,768]{1,0:T(8,128)(2,1)} %get-tuple-element.321), channel_id=1, source_target_pairs={{0,4},{1,5},{2,6},{3,7},{4,0},{5,1},{6,2},{7,3},{8,12},{9,13},{10,... | collective-permute-start | bytes 1105928 | tf_op jit(solution)/shard_map/ppermute | solution.py:372
  428.1 32.5 %collective-permute-start.40 = (bf16[240,768]{1,0:T(8,128)(2,1)}, bf16[240,768]{1,0:T(8,128)(2,1)}, u32[]{:S(2)}, u32[]{:S(2)}) collective-permute-start(bf16[240,768]{1,0:T(8,128)(2,1)} %get-tuple-element.322), channel_id=1, source_target_pairs={{0,2},{1,3},{2,0},{3,1},{4,6},{5,7},{6,4},{7,5},{8,10},{9,11},{10,... | collective-permute-start | bytes 1105928 | tf_op jit(solution)/shard_map/ppermute | solution.py:372
  491.8 29.5 %collective-permute-start.44 = (bf16[2,288,768]{2,1,0:T(8,128)(2,1)S(1)}, bf16[2,288,768]{2,1,0:T(8,128)(2,1)}, u32[]{:S(2)}, u32[]{:S(2)}) collective-permute-start(bf16[2,288,768]{2,1,0:T(8,128)(2,1)S(1)} %get-tuple-element.215), channel_id=1, source_target_pairs={{0,4},{1,5},{2,6},{3,7},{4,0},{5,1},{6,2},{7,3},{8,12},{9,13},{10,... | collective-permute-start | bytes 2654216 | tf_op jit(solution)/shard_map/ppermute | solution.py:372
  543.0 53.9 %collective-permute-start.47 = (bf16[240,768]{1,0:T(8,128)(2,1)}, bf16[240,768]{1,0:T(8,128)(2,1)}, u32[]{:S(2)}, u32[]{:S(2)}) collective-permute-start(bf16[240,768]{1,0:T(8,128)(2,1)} %get-tuple-element.253), channel_id=1, source_target_pairs={{0,8},{1,9},{2,10},{3,11},{4,12},{5,13},{6,14},{7,15},{8,16},{9,17... | collective-permute-start | bytes 1105928 | tf_op jit(solution)/shard_map/ppermute | solution.py:375
  544.5 52.5 %collective-permute-start.48 = (bf16[240,768]{1,0:T(8,128)(2,1)}, bf16[240,768]{1,0:T(8,128)(2,1)}, u32[]{:S(2)}, u32[]{:S(2)}) collective-permute-start(bf16[240,768]{1,0:T(8,128)(2,1)} %get-tuple-element.254), channel_id=1, source_target_pairs={{0,16},{1,17},{2,18},{3,19},{4,20},{5,21},{6,22},{7,23},{8,24},{9,... | collective-permute-start | bytes 1105928 | tf_op jit(solution)/shard_map/ppermute | solution.py:375
  548.2 36.2 %all-to-all-start.3 = ((bf16[1,8,196,768]{3,2,0,1:T(8,128)(2,1)}), bf16[1,8,196,768]{3,2,0,1:T(8,128)(2,1)}, u32[]{:S(2)}, u32[]{:S(2)}) async-start(bf16[1,8,196,768]{3,2,0,1:T(8,128)(2,1)} %slice.219), calls=%async_computation.3 | async-start | bytes 4915200 | tf_op jit(solution)/shard_map/all_to_all | solution.py:687
  569.2 27.8 %collective-permute-start.49 = (bf16[240,768]{1,0:T(8,128)(2,1)S(1)}, bf16[240,768]{1,0:T(8,128)(2,1)S(1)}, u32[]{:S(2)}, u32[]{:S(2)}) collective-permute-start(bf16[240,768]{1,0:T(8,128)(2,1)S(1)} %get-tuple-element.255), channel_id=1, source_target_pairs={{0,24},{1,25},{2,26},{3,27},{4,28},{5,29},{6,30},{7,31},{8,0},{9,1... | collective-permute-start | bytes 1105928 | tf_op jit(solution)/shard_map/ppermute | solution.py:375
  573.3 23.6 %collective-permute-start.54 = (bf16[96,768]{1,0:T(8,128)(2,1)S(1)}, bf16[96,768]{1,0:T(8,128)(2,1)S(1)}, u32[]{:S(2)}, u32[]{:S(2)}) collective-permute-start(bf16[96,768]{1,0:T(8,128)(2,1)S(1)} %add_convert_fusion.26), channel_id=1, source_target_pairs={{12,8},{13,9}} | collective-permute-start | bytes 442376 | tf_op jit(solution)/shard_map/ppermute | solution.py:542
  574.0 23.0 %collective-permute-start.53 = (bf16[96,768]{1,0:T(8,128)(2,1)S(1)}, bf16[96,768]{1,0:T(8,128)(2,1)S(1)}, u32[]{:S(2)}, u32[]{:S(2)}) collective-permute-start(bf16[96,768]{1,0:T(8,128)(2,1)S(1)} %add_convert_fusion.26), channel_id=1, source_target_pairs={{10,8},{11,9}} | collective-permute-start | bytes 442376 | tf_op jit(solution)/shard_map/ppermute | solution.py:542
  (113 other events, 1183.3 us)
Sparse Core Ops, SparseCore 0:
  52.0 104.1 all-gather.1
  422.3 166.2 reduce-scatter.1

commit v9 on v8

--- a/solution.py
+++ b/solution.py
@@ -362,7 +362,7 @@
         flat = packed.reshape(1, -1)
         tail = jnp.pad(flat, ((0, 7), (0, width - flat.shape[1])))
         pieces = self.shifted(jnp.concatenate([weights_in, tail], axis=0))
-        pieces, (weights_out, self.clip) = tie(pieces, (weights_out, clip))
+        pieces, self.clip = tie(pieces, clip)
         full_out = lax.all_gather(weights_out, axes, axis=0, tiled=True)
         self.out_t, self.out_f = (full_out[:width], full_out[width : 2 * width])
         self.out_s, self.out_m = (full_out[2 * width : 3 * width], full_out[3 * width :])
@@ -401,7 +401,7 @@
         rows_in, width = (self.rows_in, self.width)
         smalls = self.column_small.reshape(-1, width)
         first = jnp.concatenate([self.column_in[0], smalls], axis=0)
-        self.p1, self.p2, self.p3 = (self.column_in[k] for k in (1, 2, 3))
+        self.p1, self.p23 = (self.column_in[1], self.column_in[2:].reshape(-1, width))
         p0 = self.over(first)
         p0, clip = tie(p0, clip)
         self.p0 = self.cores(p0)
@@ -420,23 +420,17 @@
         g = self.grads
         whole = lambda key: (g[key], 0, g[key].shape[0])
         if name == "query_t":
-            values, (self.p1, self.p2) = tie(values, (self.p1, self.p2))
-            self.p2 = self.over(self.p2)
+            values, (self.p1, self.p23) = tie(values, (self.p1, self.p23))
+            self.p23 = self.over(self.p23)
             self.p1 = self.cores(self.p1)
             low = self.lay([self.p0, self.p1], [(0, 0, rows_in), (1, 0, rows_in)])
             self.in_t, self.in_qk = (low[: 3 * width], low[3 * width :])
             self.in_b = self.in_t[5 * width // 2 :]
-        elif name == "mixed_t":
-            values, (self.p2, self.p3) = tie(values, (self.p2, self.p3))
-            self.p3 = self.over(self.p3)
         elif name == "query_s":
-            self.p2 = self.cores(self.p2)
-            self.in_v = self.lay([self.p2], [(0, 0, rows_in)])[:width]
-        elif name == "mixed_s":
-            values, self.p3 = tie(values, self.p3)
-            self.p3 = self.cores(self.p3)
-            high = self.lay([self.p2, self.p3], [(0, 0, rows_in), (1, 0, rows_in)])
-            self.in_m = high[width:]
+            values, self.p23 = tie(values, self.p23)
+            self.p23 = self.cores(self.p23)
+            high = self.lay([self.p23], [(0, 0, rows_in), (0, rows_in, rows_in)])
+            self.in_v, self.in_m = (high[:width], high[width:])
         elif name == "hidden":
             values = lax.optimization_barrier(values)
         elif name == "in_m":

time: 627 us -> 638 us (1.018)
  waiting for transfers between devices: 93.9 us -> 112 us
    ppermute x44 -> x37, waiting for transfers between devices: 50.6 us -> 57.7 us  [flip(): return lax.ppermute(x, self.axes, [(d, d ^ bits) for d in range(32)])]
    ppermute x44 -> x37, starting transfers between devices: 33.1 us -> 27.8 us  [flip(): return lax.ppermute(x, self.axes, [(d, d ^ bits) for d in range(32)])]
    pallas_call x5 -> x4, Pallas kernels: 20.1 us -> 15 us  [place(): pl.pallas_call(partial(place_kernel, tuple((tuple(e) for e in outs_plan))...]
    unnamed x167 -> x173, local copies, waits for them, and re-layouts: 26.1 us -> 24.3 us
  transfers between devices with their start and end apart: 63 -> 56, of which waited for: 14 -> 18; matrix products, arithmetic and copies ran while one was open for 43% -> 40% of each run, Pallas kernels for 19% -> 15%
where the time goes in v9:
time: 638 us; the launch traced here: 628 us
  matrix products  199 us (31%)
  Pallas kernels  115 us (18%)
  waiting for transfers between devices  112 us (18%)
  starting transfers between devices  72.4 us (11%)
  other arithmetic  58.2 us (9%)
  local copies, waits for them, and re-layouts  54.9 us (9%)
  between operations  16.9 us (3%)
    pallas_call x4, Pallas kernels, attention_call(): pl.pallas_call(partial(kernel, group, patches, count), grid=(clips, steps...  79.3 us
    dot_general x8, matrix products, nn(): lax.dot_general(left, right, (((1,), (0,)), ((), ())), preferred_element_...  74 us
    dot_general x9, matrix products, nt(): lax.dot_general(left, right, (((1,), (1,)), ((), ())), preferred_element_...  69.5 us
    ppermute x37, waiting for transfers between devices, flip(): return lax.ppermute(x, self.axes, [(d, d ^ bits) for d in range(32)])  57.7 us
    dot_general x8, matrix products, tn(): lax.dot_general(left, right, (((0,), (0,)), ((), ())), preferred_element_...  55.9 us
    all_to_all x2, waiting for transfers between devices, exchange(): return lax.all_to_all(x, 'seq', split_axis=0, concat_axis=1, tiled=True)  27.9 us
    ppermute x37, starting transfers between devices, flip(): return lax.ppermute(x, self.axes, [(d, d ^ bits) for d in range(32)])  27.8 us
    unnamed x173, local copies, waits for them, and re-layouts  24.3 us
  transfers between devices with their start and end apart: 56, of which 18 were waited for; matrix products, arithmetic and copies ran while one was open for 40% of the time, Pallas kernels for 15%

profile of v9, /device:TPU:0, one launch (start us, length us, event | category | flops | bytes accessed | tf_op | source)
XLA Modules:
  0.0 627.9 jit_solution(15985811017575050877)
XLA Ops:
  19.5 24.5 %all-to-all-done = bf16[4,2,196,768]{3,1,2,0:T(2,128)(2,1)} async-done(((bf16[4,2,196,768]{3,1,2,0:T(2,128)(2,1)}), bf16[4,2,196,768]{3,1,2,0:T(2,128)(2,1)}, u32[]{:S(2)}, u32[]{:S(2)}) %all-to-all-start) | async-done | bytes 2408480 | tf_op jit(solution)/shard_map/all_to_all | solution.py:674
  47.5 9.7 %collective-permute-done.1 = bf16[248,768]{1,0:T(8,128)(2,1)S(1)} collective-permute-done((bf16[248,768]{1,0:T(8,128)(2,1)S(1)}, bf16[248,768]{1,0:T(8,128)(2,1)S(1)}, u32[]{:S(2)}, u32[]{:S(2)}) %collective-permute-start.1) | collective-permute-done | bytes 380960 | tf_op jit(solution)/shard_map/ppermute | solution.py:375
  66.7 8.4 %collective-permute-done.5 = bf16[272,768]{1,0:T(8,128)(2,1)S(1)} collective-permute-done((bf16[272,768]{1,0:T(8,128)(2,1)S(1)}, bf16[272,768]{1,0:T(8,128)(2,1)S(1)}, u32[]{:S(2)}, u32[]{:S(2)}) %collective-permute-start.5) | collective-permute-done | bytes 417824 | tf_op jit(solution)/shard_map/ppermute | solution.py:372
  75.1 7.6 %collective-permute-done.4 = bf16[272,768]{1,0:T(8,128)(2,1)S(1)} collective-permute-done((bf16[272,768]{1,0:T(8,128)(2,1)S(1)}, bf16[272,768]{1,0:T(8,128)(2,1)S(1)}, u32[]{:S(2)}, u32[]{:S(2)}) %collective-permute-start.4) | collective-permute-done | bytes 417824 | tf_op jit(solution)/shard_map/ppermute | solution.py:372
  105.0 7.3 %convolution_convert_fusion = bf16[1664,1920]{1,0:T(8,128)(2,1)} fusion(bf16[1664,768]{1,0:T(8,128)(2,1)S(1)} %bitcast.287, bf16[1920,768]{1,0:T(8,128)(2,1)S(1)} %bitcast.272), kind=kOutput, calls=%fused_computation.10 | convolution fusion | flops 4910530560 | bytes 11894784 | tf_op jit(solution)/shard_map/dot_general | solution.py:23
  133.7 15.0 %shard_map.138 = bf16[1,8,208,768]{3,2,1,0:T(8,128)(2,1)} custom-call(bf16[1,8,208,1920]{3,2,1,0:T(8,128)(2,1)} %bitcast.295, bf16[1,8,208,384]{3,2,1,0:T(8,128)(2,1)} %bitcast.311), custom_call_target="tpu_custom_call" | custom-call | flops 14976000000 | tf_op jit(solution)/shard_map/pallas_call | solution.py:135
  161.5 8.5 %convolution_convert_fusion.1 = bf16[1664,1536]{1,0:T(8,128)(2,1)} fusion(bf16[1664,768]{1,0:T(8,128)(2,1)S(1)} %add_convert_fusion.3, bf16[3840,768]{1,0:T(8,128)(2,1)} %bitcast.228), kind=kOutput, calls=%fused_computation.11 | convolution fusion | flops 3928424448 | bytes 10027008 | tf_op jit(solution)/shard_map/dot_general | solution.py:23
  184.0 12.0 %shard_map.140 = bf16[1,8,208,768]{3,2,1,0:T(8,128)(2,1)} custom-call(bf16[1,8,208,1536]{3,2,1,0:T(8,128)(2,1)} %bitcast.297, bf16[1,8,208,768]{3,2,1,0:T(8,128)(2,1)} %bitcast.305), custom_call_target="tpu_custom_call" | custom-call | flops 14976000000 | tf_op jit(solution)/shard_map/pallas_call | solution.py:135
  200.9 6.4 %fusion.77 = (f32[1664]{0:T(1024)S(1)}, f32[1664,768]{1,0:T(8,128)S(1)}) fusion(f32[768]{0:T(1024)S(1)} %add.401, bf16[1664,768]{1,0:T(8,128)(2,1)} %bitcast.303, bf16[5376,768]{1,0:T(8,128)(2,1)} %all-gather.2.cloned.1.call-done, bf16[1664,768]{1,0:T(8,128)(2,1)} %copy-done.13, bf16[1,8,208,768]{3,2,1,0:T(8,128)(2,1)} %copy-done.7), kind=kOutput, calls=%fused_computation.194 | convolution fusion | flops 1970600320 | bytes 13968896 | tf_op jit(solution)/shard_map/dot_general | solution.py:27
  209.5 17.1 %fusion.4 = (bf16[1664,3072]{1,0:T(8,128)(2,1)}, bf16[1664,3072]{1,0:T(8,128)(2,1)}) fusion(f32[3072]{0:T(1024)S(1)} %add.409, bf16[3840,768]{1,0:T(8,128)(2,1)S(1)} %bitcast.237, f32[1664,768]{1,0:T(8,128)S(1)} %get-tuple-element.333, f32[768]{0:T(1024)S(1)} %add.406, f32[768]{0:T(1024)S(1)} %mul.260, f32[1664]{0:T(1024)S(1)} %add_rsqrt_fusion, ...), kind=kOutput, calls=%fused_computation.5 | convolution fusion | flops 7919468544 | bytes 30314496 | tf_op jit(solution)/shard_map/dot_general | solution.py:23
  233.1 12.5 %add_convert_fusion.1 = bf16[1664,768]{1,0:T(8,128)(2,1)S(1)} fusion(f32[1664,768]{1,0:T(8,128)S(1)} %copy-done.19, bf16[1664,3072]{1,0:T(8,128)(2,1)} %get-tuple-element.166, bf16[5376,768]{1,0:T(8,128)(2,1)} %all-gather.2.cloned.1.call-done, f32[768]{0:T(1024)S(1)} %add.418), kind=kOutput, calls=%fused_computation.43 | convolution fusion | flops 7855570944 | bytes 22612992 | tf_op jit(solution)/shard_map/dot_general | solution.py:27
  252.2 14.9 %multiply_convert_fusion = bf16[1664,3072]{1,0:T(8,128)(2,1)} fusion(bf16[1664,3072]{1,0:T(8,128)(2,1)} %get-tuple-element.163, bf16[1664,768]{1,0:T(8,128)(2,1)S(1)} %bitcast.276, bf16[5376,768]{1,0:T(8,128)(2,1)} %all-gather.2.cloned.1.call-done), kind=kOutput, calls=%fused_computation.7 | convolution fusion | flops 7867072512 | bytes 27721728 | tf_op jit(solution)/shard_map/dot_general | solution.py:23
  267.1 13.8 %fusion.35.refs_0_.refs_1_ = bf16[384,8,768]{2,1,0:T(8,128)(2,1)S(1)} fusion(bf16[1664,3072]{1,0:T(8,128)(2,1)} %multiply_convert_fusion, f32[1664,768]{1,0:T(8,128)} %copy-done.18, f32[768]{0:T(1024)S(1)} %add.406, f32[768]{0:T(1024)S(1)} %mul.260, f32[1664]{0:T(1024)S(1)} %add_rsqrt_fusion, f32[1664]{0:T(1024)S(1)} %broadcast_multiply_fusion.6), kind=kOutput, calls=%fused_computation.79 | convolution fusion | flops 7860486144 | bytes 20073472 | tf_op jit(solution)/shard_map/dot_general | solution.py:31
  286.2 16.6 %multiply_reduce_fusion = (f32[768]{0:T(1024)S(1)}, f32[1664]{0:T(1024)S(1)}, f32[1664]{0:T(1024)S(1)}, f32[768]{0:T(1024)S(1)}, f32[1664,768]{1,0:T(8,128)}) fusion(f32[1664,768]{1,0:T(8,128)} %copy-done.18, f32[1664]{0:T(1024)S(1)} %add_rsqrt_fusion, f32[1664]{0:T(1024)S(1)} %broadcast_multiply_fusion.6, f32[768]{0:T(1024)S(1)} %mul.260, ...), kind=kOutput, calls=%fused_computation.39 | convolution fusion | flops 7863233536 | bytes 25205760 | tf_op jit(solution)/shard_map/dot_general | solution.py:27
  308.3 5.8 convolution_convert_fusion.7
  314.1 13.0 %fusion.36.refs_3_ = bf16[384,8,768]{2,1,0:T(8,128)(2,1)} fusion(bf16[1664,3072]{1,0:T(8,128)(2,1)} %get-tuple-element.166, bf16[1664,768]{1,0:T(8,128)(2,1)S(1)} %bitcast.278), kind=kOutput, calls=%fused_computation.80 | convolution fusion | flops 7854096384 | bytes 17498112 | tf_op jit(solution)/shard_map/dot_general | solution.py:31
  333.3 26.1 %shard_map.142 = (bf16[1,8,208,1536]{3,2,1,0:T(8,128)(2,1)}, bf16[1,8,208,768]{3,2,1,0:T(8,128)(2,1)}) custom-call(bf16[1,8,208,1536]{3,2,1,0:T(8,128)(2,1)} %bitcast.298, bf16[1,8,208,768]{3,2,1,0:T(8,128)(2,1)} %bitcast.306, bf16[1,8,208,768]{3,2,1,0:T(8,128)(2,1)} %bitcast.309), custom_call_target="tpu_custom_call" | custom-call | flops 23296000000 | tf_op jit(solution)/shard_map/pallas_call | solution.py:135
  378.3 5.9 fusion.46
  384.2 10.8 %multiply_reduce_fusion.1 = (f32[768]{0:T(1024)S(1)}, f32[1664]{0:T(1024)S(1)}, f32[1664]{0:T(1024)S(1)}, f32[768]{0:T(1024)S(1)}, f32[1664,768]{1,0:T(8,128)S(1)}) fusion(f32[1664]{0:T(1024)S(1)} %copy-done.59, f32[1664]{0:T(1024)S(1)} %copy-done.53, bf16[1664,768]{1,0:T(8,128)(2,1)S(1)} %copy-done.14, bf16[1,8,208,768]{3,2,1,0:T(8,128)(2,1)S(1)} %copy-done.10, ...), kind=kOutput, calls=%fused_computation.40 | convolution fusion | flops 3942477056 | bytes 22842368 | tf_op jit(solution)/shard_map/dot_general | solution.py:27
  408.5 7.6 %collective-permute-done.30 = bf16[240,768]{1,0:T(8,128)(2,1)S(1)} collective-permute-done((bf16[240,768]{1,0:T(8,128)(2,1)S(1)}, bf16[240,768]{1,0:T(8,128)(2,1)S(1)}, u32[]{:S(2)}, u32[]{:S(2)}) %collective-permute-start.30) | collective-permute-done | bytes 368672 | tf_op jit(solution)/shard_map/ppermute | solution.py:372
  427.0 6.3 %shard_map.145 = bf16[672,8,768]{2,1,0:T(8,128)(2,1)} custom-call(bf16[96,8,768]{2,1,0:T(8,128)(2,1)} %fusion.41.refs_0_, bf16[96,8,768]{2,1,0:T(8,128)(2,1)} %fusion.42.refs_1_, bf16[96,8,768]{2,1,0:T(8,128)(2,1)} %fusion.43.refs_2_, bf16[384,8,768]{2,1,0:T(8,128)(2,1)} %fusion.36.refs_3_), custom_call_target="tpu_custom_call" | custom-call | bytes 33030144 | tf_op jit(solution)/shard_map/pallas_call | solution.py:274
  439.6 5.8 convolution_convert_fusion.5
  445.5 26.3 %shard_map.146 = bf16[1,8,208,2304]{3,2,1,0:T(8,128)(2,1)} custom-call(bf16[1,8,208,1920]{3,2,1,0:T(8,128)(2,1)} %bitcast.296, bf16[1,8,208,384]{3,2,1,0:T(8,128)(2,1)} %bitcast.312, bf16[1,8,208,768]{3,2,1,0:T(8,128)(2,1)} %bitcast.310), custom_call_target="tpu_custom_call" | custom-call | flops 23296000000 | tf_op jit(solution)/shard_map/pallas_call | solution.py:135
  472.6 9.2 %fusion.39.refs_0_ = bf16[288,8,768]{2,1,0:T(8,128)(2,1)S(1)} fusion(bf16[1664,2304]{1,0:T(8,128)(2,1)} %bitcast.293, bf16[1664,768]{1,0:T(8,128)(2,1)S(1)} %copy-done.26), kind=kOutput, calls=%fused_computation.83 | convolution fusion | flops 5890572288 | bytes 13762560 | tf_op jit(solution)/shard_map/dot_general | solution.py:31
  503.6 12.9 %fusion.19 = (f32[768]{0:T(1024)S(1)}, f32[1664]{0:T(1024)S(1)}, f32[1664]{0:T(1024)S(1)}, f32[768]{0:T(1024)S(1)}, f32[1664,768]{1,0:T(8,128)}) fusion(bf16[1,8,208,768]{3,2,1,0:T(8,128)(2,1)S(1)} %copy-done.11, f32[1664]{0:T(1024)S(1)} %copy-done.57, f32[1664]{0:T(1024)S(1)} %copy-done.55, f32[768]{0:T(1024)S(1)} %copy-done.61, ...), kind=kOutput, calls=%fused_computation.30 | convolution fusion | flops 5901577216 | bytes 18914304 | tf_op jit(solution)/shard_map/dot_general | solution.py:27
  516.5 14.8 %collective-permute-done.37 = bf16[2,288,768]{2,1,0:T(8,128)(2,1)} collective-permute-done((bf16[2,288,768]{2,1,0:T(8,128)(2,1)S(1)}, bf16[2,288,768]{2,1,0:T(8,128)(2,1)}, u32[]{:S(2)}, u32[]{:S(2)}) %collective-permute-start.37) | collective-permute-done | bytes 884768 | tf_op jit(solution)/shard_map/ppermute | solution.py:372
  534.3 5.7 add_convert_fusion
  541.2 10.8 %collective-permute-done.38 = bf16[288,768]{1,0:T(8,128)(2,1)S(1)} collective-permute-done((bf16[288,768]{1,0:T(8,128)(2,1)S(1)}, bf16[288,768]{1,0:T(8,128)(2,1)S(1)}, u32[]{:S(2)}, u32[]{:S(2)}) %collective-permute-start.38) | collective-permute-done | bytes 442400 | tf_op jit(solution)/shard_map/ppermute | solution.py:372
  572.5 5.9 convert_reduce_fusion
  584.9 10.3 %all-to-all-done.3 = bf16[1,8,196,768]{3,2,0,1:T(8,128)(2,1)} async-done(((bf16[1,8,196,768]{3,2,0,1:T(8,128)(2,1)}), bf16[1,8,196,768]{3,2,0,1:T(8,128)(2,1)}, u32[]{:S(2)}, u32[]{:S(2)}) %all-to-all-start.3) | async-done | bytes 2408480 | tf_op jit(solution)/shard_map/all_to_all | solution.py:681
  601.7 6.6 %all-to-all-start.4 = ((f32[32,16,128]{2,1,0:T(8,128)}), f32[32,16,128]{2,1,0:T(8,128)S(1)}, u32[]{:S(2)}, u32[]{:S(2)}) async-start(f32[32,16,128]{2,1,0:T(8,128)} %shard_map.148), calls=%async_computation.5 | async-start | bytes 524288 | tf_op jit(solution)/shard_map/all_to_all | solution.py:546
  612.4 5.8 copy.36
  (399 shorter events, 247.4 us)
Async XLA Ops:
  7.2 141.5 %all-gather.2.cloned.1.call-start = ((), (), s32[]{:S(2)}) async-start(), calls=%async_computation.6 | async-start | bytes 8515584 | tf_op jit(solution)/shard_map/all_gather | solution.py:366
  7.9 36.1 %all-to-all-start = ((bf16[4,2,196,768]{3,1,2,0:T(2,128)(2,1)}), bf16[4,2,196,768]{3,1,2,0:T(2,128)(2,1)}, u32[]{:S(2)}, u32[]{:S(2)}) async-start(bf16[4,2,196,768]{3,1,2,0:T(2,128)(2,1)} %param.8), calls=%async_computation | async-start | bytes 4816896 | tf_op jit(solution)/shard_map/all_to_all | solution.py:674
  13.4 34.1 %collective-permute-start.2 = (bf16[248,768]{1,0:T(8,128)(2,1)S(1)}, bf16[248,768]{1,0:T(8,128)(2,1)S(1)}, u32[]{:S(2)}, u32[]{:S(2)}) collective-permute-start(bf16[248,768]{1,0:T(8,128)(2,1)S(1)} %fusion.57), channel_id=1, source_target_pairs={{0,24},{1,25},{2,26},{3,27},{4,28},{5,29},{6,30},{7,31},{8,0},{9,1... | collective-permute-start | bytes 1142792 | tf_op jit(solution)/shard_map/ppermute | solution.py:375
  18.5 38.6 %collective-permute-start.1 = (bf16[248,768]{1,0:T(8,128)(2,1)S(1)}, bf16[248,768]{1,0:T(8,128)(2,1)S(1)}, u32[]{:S(2)}, u32[]{:S(2)}) collective-permute-start(bf16[248,768]{1,0:T(8,128)(2,1)S(1)} %fusion.57), channel_id=1, source_target_pairs={{0,16},{1,17},{2,18},{3,19},{4,20},{5,21},{6,22},{7,23},{8,24},{9,... | collective-permute-start | bytes 1142792 | tf_op jit(solution)/shard_map/ppermute | solution.py:375
  18.5 38.6 %collective-permute-start = (bf16[248,768]{1,0:T(8,128)(2,1)S(1)}, bf16[248,768]{1,0:T(8,128)(2,1)S(1)}, u32[]{:S(2)}, u32[]{:S(2)}) collective-permute-start(bf16[248,768]{1,0:T(8,128)(2,1)S(1)} %fusion.57), channel_id=1, source_target_pairs={{0,8},{1,9},{2,10},{3,11},{4,12},{5,13},{6,14},{7,15},{8,16},{9,17... | collective-permute-start | bytes 1142792 | tf_op jit(solution)/shard_map/ppermute | solution.py:375
  62.7 20.0 %collective-permute-start.4 = (bf16[272,768]{1,0:T(8,128)(2,1)S(1)}, bf16[272,768]{1,0:T(8,128)(2,1)S(1)}, u32[]{:S(2)}, u32[]{:S(2)}) collective-permute-start(bf16[272,768]{1,0:T(8,128)(2,1)S(1)} %pad_maximum_fusion.1), channel_id=1, source_target_pairs={{0,4},{1,5},{2,6},{3,7},{4,0},{5,1},{6,2},{7,3},{8,12},{9,13},{10,... | collective-permute-start | bytes 1253384 | tf_op jit(solution)/shard_map/ppermute | solution.py:372
  63.3 19.5 %collective-permute-start.3 = (bf16[272,768]{1,0:T(8,128)(2,1)S(1)}, bf16[272,768]{1,0:T(8,128)(2,1)S(1)}, u32[]{:S(2)}, u32[]{:S(2)}) collective-permute-start(bf16[272,768]{1,0:T(8,128)(2,1)S(1)} %pad_maximum_fusion.1), channel_id=1, source_target_pairs={{0,2},{1,3},{2,0},{3,1},{4,6},{5,7},{6,4},{7,5},{8,10},{9,11},{10,... | collective-permute-start | bytes 1253384 | tf_op jit(solution)/shard_map/ppermute | solution.py:372
  94.6 20.1 %collective-permute-start.12 = (bf16[240,768]{1,0:T(8,128)(2,1)}, bf16[240,768]{1,0:T(8,128)(2,1)}, u32[]{:S(2)}, u32[]{:S(2)}) collective-permute-start(bf16[240,768]{1,0:T(8,128)(2,1)} %get-tuple-element.150), channel_id=1, source_target_pairs={{0,6},{1,7},{2,4},{3,5},{4,2},{5,3},{6,0},{7,1},{8,14},{9,15},{10,... | collective-permute-start | bytes 1105928 | tf_op jit(solution)/shard_map/ppermute | solution.py:372
  95.9 20.5 %collective-permute-start.11 = (bf16[240,768]{1,0:T(8,128)(2,1)}, bf16[240,768]{1,0:T(8,128)(2,1)}, u32[]{:S(2)}, u32[]{:S(2)}) collective-permute-start(bf16[240,768]{1,0:T(8,128)(2,1)} %get-tuple-element.150), channel_id=1, source_target_pairs={{0,4},{1,5},{2,6},{3,7},{4,0},{5,1},{6,2},{7,3},{8,12},{9,13},{10,... | collective-permute-start | bytes 1105928 | tf_op jit(solution)/shard_map/ppermute | solution.py:372
  97.7 18.8 %collective-permute-start.10 = (bf16[240,768]{1,0:T(8,128)(2,1)}, bf16[240,768]{1,0:T(8,128)(2,1)}, u32[]{:S(2)}, u32[]{:S(2)}) collective-permute-start(bf16[240,768]{1,0:T(8,128)(2,1)} %get-tuple-element.150), channel_id=1, source_target_pairs={{0,2},{1,3},{2,0},{3,1},{4,6},{5,7},{6,4},{7,5},{8,10},{9,11},{10,... | collective-permute-start | bytes 1105928 | tf_op jit(solution)/shard_map/ppermute | solution.py:372
  120.7 49.3 %collective-permute-start.19 = (bf16[480,768]{1,0:T(8,128)(2,1)S(1)}, bf16[480,768]{1,0:T(8,128)(2,1)}, u32[]{:S(2)}, u32[]{:S(2)}) collective-permute-start(bf16[480,768]{1,0:T(8,128)(2,1)S(1)} %bitcast.243), channel_id=1, source_target_pairs={{0,6},{1,7},{2,4},{3,5},{4,2},{5,3},{6,0},{7,1},{8,14},{9,15},{10,... | collective-permute-start | bytes 2211848 | tf_op jit(solution)/shard_map/ppermute | solution.py:372
  122.3 47.7 %collective-permute-start.18 = (bf16[480,768]{1,0:T(8,128)(2,1)S(1)}, bf16[480,768]{1,0:T(8,128)(2,1)}, u32[]{:S(2)}, u32[]{:S(2)}) collective-permute-start(bf16[480,768]{1,0:T(8,128)(2,1)S(1)} %bitcast.244), channel_id=1, source_target_pairs={{0,4},{1,5},{2,6},{3,7},{4,0},{5,1},{6,2},{7,3},{8,12},{9,13},{10,... | collective-permute-start | bytes 2211848 | tf_op jit(solution)/shard_map/ppermute | solution.py:372
  123.7 46.3 %collective-permute-start.17 = (bf16[480,768]{1,0:T(8,128)(2,1)S(1)}, bf16[480,768]{1,0:T(8,128)(2,1)}, u32[]{:S(2)}, u32[]{:S(2)}) collective-permute-start(bf16[480,768]{1,0:T(8,128)(2,1)S(1)} %bitcast.245), channel_id=1, source_target_pairs={{0,2},{1,3},{2,0},{3,1},{4,6},{5,7},{6,4},{7,5},{8,10},{9,11},{10,... | collective-permute-start | bytes 2211848 | tf_op jit(solution)/shard_map/ppermute | solution.py:372
  196.0 33.9 %all-to-all-start.1 = ((bf16[4,2,196,768]{3,1,2,0:T(2,128)(2,1)}), bf16[4,2,196,768]{3,1,2,0:T(2,128)(2,1)}, u32[]{:S(2)}, u32[]{:S(2)}) async-start(bf16[4,2,196,768]{3,1,2,0:T(2,128)(2,1)} %param.9), calls=%async_computation.1 | async-start | bytes 4816896 | tf_op jit(solution)/shard_map/all_to_all | solution.py:674
  247.2 79.9 %all-to-all-start.2 = ((bf16[1,8,196,768]{3,2,0,1:T(8,128)(2,1)}), bf16[1,8,196,768]{3,2,0,1:T(8,128)(2,1)}, u32[]{:S(2)}, u32[]{:S(2)}) async-start(bf16[1,8,196,768]{3,2,0,1:T(8,128)(2,1)} %slice.210), calls=%async_computation.2 | async-start | bytes 4915200 | tf_op jit(solution)/shard_map/all_to_all | solution.py:681
  251.8 348.2 %reduce-scatter.2.cloned.1.call-start = ((), (), s32[]{:S(2)}) async-start(), calls=%async_computation.7 | async-start | bytes 8515584 | tf_op jit(solution)/shard_map/reduce_scatter | solution.py:468
  285.8 41.3 %collective-permute-start.24 = (bf16[4,240,768]{2,1,0:T(8,128)(2,1)S(1)}, bf16[4,240,768]{2,1,0:T(8,128)(2,1)}, u32[]{:S(2)}, u32[]{:S(2)}) collective-permute-start(bf16[4,240,768]{2,1,0:T(8,128)(2,1)S(1)} %bitcast.273), channel_id=1, source_target_pairs={{0,1},{1,0},{2,3},{3,2},{4,5},{5,4},{6,7},{7,6},{8,9},{9,8},{10,11... | collective-permute-start | bytes 4423688 | tf_op jit(solution)/shard_map/ppermute | solution.py:372
  329.8 29.6 %collective-permute-start.27 = (bf16[240,768]{1,0:T(8,128)(2,1)}, bf16[240,768]{1,0:T(8,128)(2,1)S(1)}, u32[]{:S(2)}, u32[]{:S(2)}) collective-permute-start(bf16[240,768]{1,0:T(8,128)(2,1)} %get-tuple-element.316), channel_id=1, source_target_pairs={{0,6},{1,7},{2,4},{3,5},{4,2},{5,3},{6,0},{7,1},{8,14},{9,15},{10,... | collective-permute-start | bytes 1105928 | tf_op jit(solution)/shard_map/ppermute | solution.py:372
  332.3 27.0 %collective-permute-start.26 = (bf16[240,768]{1,0:T(8,128)(2,1)}, bf16[240,768]{1,0:T(8,128)(2,1)S(1)}, u32[]{:S(2)}, u32[]{:S(2)}) collective-permute-start(bf16[240,768]{1,0:T(8,128)(2,1)} %get-tuple-element.317), channel_id=1, source_target_pairs={{0,4},{1,5},{2,6},{3,7},{4,0},{5,1},{6,2},{7,3},{8,12},{9,13},{10,... | collective-permute-start | bytes 1105928 | tf_op jit(solution)/shard_map/ppermute | solution.py:372
  332.9 26.5 %collective-permute-start.25 = (bf16[240,768]{1,0:T(8,128)(2,1)}, bf16[240,768]{1,0:T(8,128)(2,1)}, u32[]{:S(2)}, u32[]{:S(2)}) collective-permute-start(bf16[240,768]{1,0:T(8,128)(2,1)} %get-tuple-element.318), channel_id=1, source_target_pairs={{0,2},{1,3},{2,0},{3,1},{4,6},{5,7},{6,4},{7,5},{8,10},{9,11},{10,... | collective-permute-start | bytes 1105928 | tf_op jit(solution)/shard_map/ppermute | solution.py:372
  398.6 17.4 %collective-permute-start.30 = (bf16[240,768]{1,0:T(8,128)(2,1)S(1)}, bf16[240,768]{1,0:T(8,128)(2,1)S(1)}, u32[]{:S(2)}, u32[]{:S(2)}) collective-permute-start(bf16[240,768]{1,0:T(8,128)(2,1)S(1)} %get-tuple-element.313), channel_id=1, source_target_pairs={{0,4},{1,5},{2,6},{3,7},{4,0},{5,1},{6,2},{7,3},{8,12},{9,13},{10,... | collective-permute-start | bytes 1105928 | tf_op jit(solution)/shard_map/ppermute | solution.py:372
  436.2 35.6 %collective-permute-start.35 = (bf16[240,768]{1,0:T(8,128)(2,1)}, bf16[240,768]{1,0:T(8,128)(2,1)S(1)}, u32[]{:S(2)}, u32[]{:S(2)}) collective-permute-start(bf16[240,768]{1,0:T(8,128)(2,1)} %get-tuple-element.308), channel_id=1, source_target_pairs={{0,6},{1,7},{2,4},{3,5},{4,2},{5,3},{6,0},{7,1},{8,14},{9,15},{10,... | collective-permute-start | bytes 1105928 | tf_op jit(solution)/shard_map/ppermute | solution.py:372
  438.3 33.5 %collective-permute-start.34 = (bf16[240,768]{1,0:T(8,128)(2,1)}, bf16[240,768]{1,0:T(8,128)(2,1)S(1)}, u32[]{:S(2)}, u32[]{:S(2)}) collective-permute-start(bf16[240,768]{1,0:T(8,128)(2,1)} %get-tuple-element.309), channel_id=1, source_target_pairs={{0,4},{1,5},{2,6},{3,7},{4,0},{5,1},{6,2},{7,3},{8,12},{9,13},{10,... | collective-permute-start | bytes 1105928 | tf_op jit(solution)/shard_map/ppermute | solution.py:372
  438.8 33.0 %collective-permute-start.33 = (bf16[240,768]{1,0:T(8,128)(2,1)}, bf16[240,768]{1,0:T(8,128)(2,1)}, u32[]{:S(2)}, u32[]{:S(2)}) collective-permute-start(bf16[240,768]{1,0:T(8,128)(2,1)} %get-tuple-element.310), channel_id=1, source_target_pairs={{0,2},{1,3},{2,0},{3,1},{4,6},{5,7},{6,4},{7,5},{8,10},{9,11},{10,... | collective-permute-start | bytes 1105928 | tf_op jit(solution)/shard_map/ppermute | solution.py:372
  502.0 29.3 %collective-permute-start.37 = (bf16[2,288,768]{2,1,0:T(8,128)(2,1)S(1)}, bf16[2,288,768]{2,1,0:T(8,128)(2,1)}, u32[]{:S(2)}, u32[]{:S(2)}) collective-permute-start(bf16[2,288,768]{2,1,0:T(8,128)(2,1)S(1)} %get-tuple-element.203), channel_id=1, source_target_pairs={{0,4},{1,5},{2,6},{3,7},{4,0},{5,1},{6,2},{7,3},{8,12},{9,13},{10,... | collective-permute-start | bytes 2654216 | tf_op jit(solution)/shard_map/ppermute | solution.py:372
  533.0 19.0 %collective-permute-start.38 = (bf16[288,768]{1,0:T(8,128)(2,1)S(1)}, bf16[288,768]{1,0:T(8,128)(2,1)S(1)}, u32[]{:S(2)}, u32[]{:S(2)}) collective-permute-start(bf16[288,768]{1,0:T(8,128)(2,1)S(1)} %get-tuple-element.320), channel_id=1, source_target_pairs={{0,2},{1,3},{2,0},{3,1},{4,6},{5,7},{6,4},{7,5},{8,10},{9,11},{10,... | collective-permute-start | bytes 1327112 | tf_op jit(solution)/shard_map/ppermute | solution.py:372
  553.4 55.0 %collective-permute-start.40 = (bf16[240,768]{1,0:T(8,128)(2,1)}, bf16[240,768]{1,0:T(8,128)(2,1)}, u32[]{:S(2)}, u32[]{:S(2)}) collective-permute-start(bf16[240,768]{1,0:T(8,128)(2,1)} %get-tuple-element.241), channel_id=1, source_target_pairs={{0,8},{1,9},{2,10},{3,11},{4,12},{5,13},{6,14},{7,15},{8,16},{9,17... | collective-permute-start | bytes 1105928 | tf_op jit(solution)/shard_map/ppermute | solution.py:375
  555.0 53.3 %collective-permute-start.41 = (bf16[240,768]{1,0:T(8,128)(2,1)}, bf16[240,768]{1,0:T(8,128)(2,1)}, u32[]{:S(2)}, u32[]{:S(2)}) collective-permute-start(bf16[240,768]{1,0:T(8,128)(2,1)} %get-tuple-element.242), channel_id=1, source_target_pairs={{0,16},{1,17},{2,18},{3,19},{4,20},{5,21},{6,22},{7,23},{8,24},{9,... | collective-permute-start | bytes 1105928 | tf_op jit(solution)/shard_map/ppermute | solution.py:375
  559.0 36.2 %all-to-all-start.3 = ((bf16[1,8,196,768]{3,2,0,1:T(8,128)(2,1)}), bf16[1,8,196,768]{3,2,0,1:T(8,128)(2,1)}, u32[]{:S(2)}, u32[]{:S(2)}) async-start(bf16[1,8,196,768]{3,2,0,1:T(8,128)(2,1)} %slice.214), calls=%async_computation.3 | async-start | bytes 4915200 | tf_op jit(solution)/shard_map/all_to_all | solution.py:681
  579.4 29.0 %collective-permute-start.42 = (bf16[240,768]{1,0:T(8,128)(2,1)}, bf16[240,768]{1,0:T(8,128)(2,1)S(1)}, u32[]{:S(2)}, u32[]{:S(2)}) collective-permute-start(bf16[240,768]{1,0:T(8,128)(2,1)} %get-tuple-element.243), channel_id=1, source_target_pairs={{0,24},{1,25},{2,26},{3,27},{4,28},{5,29},{6,30},{7,31},{8,0},{9,1... | collective-permute-start | bytes 1105928 | tf_op jit(solution)/shard_map/ppermute | solution.py:375
  583.5 24.7 %collective-permute-start.47 = (bf16[96,768]{1,0:T(8,128)(2,1)S(1)}, bf16[96,768]{1,0:T(8,128)(2,1)S(1)}, u32[]{:S(2)}, u32[]{:S(2)}) collective-permute-start(bf16[96,768]{1,0:T(8,128)(2,1)S(1)} %add_convert_fusion.26), channel_id=1, source_target_pairs={{12,8},{13,9}} | collective-permute-start | bytes 442376 | tf_op jit(solution)/shard_map/ppermute | solution.py:536
  584.2 24.2 %collective-permute-start.46 = (bf16[96,768]{1,0:T(8,128)(2,1)S(1)}, bf16[96,768]{1,0:T(8,128)(2,1)S(1)}, u32[]{:S(2)}, u32[]{:S(2)}) collective-permute-start(bf16[96,768]{1,0:T(8,128)(2,1)S(1)} %add_convert_fusion.26), channel_id=1, source_target_pairs={{10,8},{11,9}} | collective-permute-start | bytes 442376 | tf_op jit(solution)/shard_map/ppermute | solution.py:536
  (109 other events, 1113.8 us)
Sparse Core Ops, SparseCore 0:
  10.9 108.5 all-gather.1
  433.6 166.3 reduce-scatter.1

commit v10 on v9

--- a/solution.py
+++ b/solution.py
@@ -431,7 +431,7 @@
             self.p23 = self.cores(self.p23)
             high = self.lay([self.p23], [(0, 0, rows_in), (0, rows_in, rows_in)])
             self.in_v, self.in_m = (high[:width], high[width:])
-        elif name == "hidden":
+        elif name in ("hidden", "end"):
             values = lax.optimization_barrier(values)
         elif name == "in_m":
             start = 24 * rows_in - 6 * width
@@ -454,13 +454,13 @@
             values, (self.kept, self.other) = tie(values, (self.kept, self.other))
             self.d_p2 = self.across(self.kept, self.other)
         elif name == "grad_t":
-            values, self.d_p2 = tie(values, self.d_p2)
-            self.d_p2 = self.gathered(self.d_p2)
             late = jnp.zeros((8 * rows_in - 2 * width, width), BF16)
             self.kept, send = self.halve([(late, 0, late.shape[0]), whole("in_qk")], (rows_in,))
             values, send = tie(values, send)
             self.other = self.flip(send, 1)
         elif name == "out_t":
+            values, self.d_p2 = tie(values, self.d_p2)
+            self.d_p2 = self.gathered(self.d_p2)
             values, (self.kept, self.other) = tie(values, (self.kept, self.other))
             self.d_p1 = self.across(self.kept, self.other)
             d_out = join([g["out_t"], g["out_f"], g["out_s"], g["out_m"]], width // 2)
@@ -657,7 +657,8 @@
     rows = (grad_projected, grad_branch_t, grad_branch_s, grad_pre, grad_low)
     grad_clip, *rows = feed.tick("grad_clip", grad_clip, *rows)
     sums = [g_t, g_s, g_m, b_t, b_s, b_m]
-    return (output,) + feed.total(sums, rows, leave(grad_clip.reshape(shape)))
+    clip, output = feed.tick("end", leave(grad_clip.reshape(shape)), output)
+    return (output,) + feed.total(sums, rows, clip)
 
 
 def shards(clips_in, cotangent, clip_live, weights_in, weights_out, norm_gain, shift_rows, dense_shift):

time: 638 us -> 637 us (level)
  waiting for transfers between devices: 112 us -> 95.2 us
  starting transfers between devices: 72.4 us -> 86.7 us
    all_to_all x1, starting transfers between devices: 6.62 us -> 20.2 us  [total(): lax.all_to_all(pack(parts, 32), self.axes, split_axis=0, concat_axis=0)]
    all_to_all x2, waiting for transfers between devices: 10.3 us -> 0.01 us  [leave(): return lax.all_to_all(x, 'seq', split_axis=1, concat_axis=0, tiled=True)]
    ppermute x37, waiting for transfers between devices: 57.7 us -> 47.5 us  [flip(): return lax.ppermute(x, self.axes, [(d, d ^ bits) for d in range(32)])]
    unnamed x173 -> x153, local copies, waits for them, and re-layouts: 24.3 us -> 23.1 us
  transfers between devices with their start and end apart: 56 -> 56, of which waited for: 18 -> 15; matrix products, arithmetic and copies ran while one was open for 40% -> 40% of each run, Pallas kernels for 15% -> 15%
where the time goes in v10:
time: 637 us; the launch traced here: 626 us
  matrix products  199 us (31%)
  Pallas kernels  115 us (18%)
  waiting for transfers between devices  95.2 us (15%)
  starting transfers between devices  86.7 us (14%)
  other arithmetic  59.6 us (9%)
  local copies, waits for them, and re-layouts  54.5 us (9%)
  between operations  16.8 us (3%)
    pallas_call x4, Pallas kernels, attention_call(): pl.pallas_call(partial(kernel, group, patches, count), grid=(clips, steps...  79.4 us
    dot_general x8, matrix products, nn(): lax.dot_general(left, right, (((1,), (0,)), ((), ())), preferred_element_...  73.2 us
    dot_general x9, matrix products, nt(): lax.dot_general(left, right, (((1,), (1,)), ((), ())), preferred_element_...  70 us
    dot_general x8, matrix products, tn(): lax.dot_general(left, right, (((0,), (0,)), ((), ())), preferred_element_...  56 us
    ppermute x37, waiting for transfers between devices, flip(): return lax.ppermute(x, self.axes, [(d, d ^ bits) for d in range(32)])  47.5 us
    ppermute x37, starting transfers between devices, flip(): return lax.ppermute(x, self.axes, [(d, d ^ bits) for d in range(32)])  28.7 us
    all_to_all x2, waiting for transfers between devices, exchange(): return lax.all_to_all(x, 'seq', split_axis=0, concat_axis=1, tiled=True)  27.9 us
    unnamed x153, local copies, waits for them, and re-layouts  23.1 us
  transfers between devices with their start and end apart: 56, of which 15 were waited for; matrix products, arithmetic and copies ran while one was open for 40% of the time, Pallas kernels for 15%

profile of v10, /device:TPU:0, one launch (start us, length us, event | category | flops | bytes accessed | tf_op | source)
XLA Modules:
  0.0 626.5 jit_solution(2711030707209479823)
XLA Ops:
  13.3 5.1 collective-permute-start.2
  19.5 24.6 %all-to-all-done = bf16[4,2,196,768]{3,1,2,0:T(2,128)(2,1)} async-done(((bf16[4,2,196,768]{3,1,2,0:T(2,128)(2,1)}), bf16[4,2,196,768]{3,1,2,0:T(2,128)(2,1)}, u32[]{:S(2)}, u32[]{:S(2)}) %all-to-all-start) | async-done | bytes 2408480 | tf_op jit(solution)/shard_map/all_to_all | solution.py:675
  47.5 9.6 %collective-permute-done.1 = bf16[248,768]{1,0:T(8,128)(2,1)S(1)} collective-permute-done((bf16[248,768]{1,0:T(8,128)(2,1)S(1)}, bf16[248,768]{1,0:T(8,128)(2,1)S(1)}, u32[]{:S(2)}, u32[]{:S(2)}) %collective-permute-start.1) | collective-permute-done | bytes 380960 | tf_op jit(solution)/shard_map/ppermute | solution.py:375
  66.7 8.5 %collective-permute-done.5 = bf16[272,768]{1,0:T(8,128)(2,1)S(1)} collective-permute-done((bf16[272,768]{1,0:T(8,128)(2,1)S(1)}, bf16[272,768]{1,0:T(8,128)(2,1)S(1)}, u32[]{:S(2)}, u32[]{:S(2)}) %collective-permute-start.5) | collective-permute-done | bytes 417824 | tf_op jit(solution)/shard_map/ppermute | solution.py:372
  75.2 7.6 %collective-permute-done.4 = bf16[272,768]{1,0:T(8,128)(2,1)S(1)} collective-permute-done((bf16[272,768]{1,0:T(8,128)(2,1)S(1)}, bf16[272,768]{1,0:T(8,128)(2,1)S(1)}, u32[]{:S(2)}, u32[]{:S(2)}) %collective-permute-start.4) | collective-permute-done | bytes 417824 | tf_op jit(solution)/shard_map/ppermute | solution.py:372
  105.0 7.3 %convolution_convert_fusion = bf16[1664,1920]{1,0:T(8,128)(2,1)} fusion(bf16[1664,768]{1,0:T(8,128)(2,1)S(1)} %bitcast.286, bf16[1920,768]{1,0:T(8,128)(2,1)S(1)} %bitcast.270), kind=kOutput, calls=%fused_computation.10 | convolution fusion | flops 4910530560 | bytes 11894784 | tf_op jit(solution)/shard_map/dot_general | solution.py:23
  133.8 14.9 %shard_map.138 = bf16[1,8,208,768]{3,2,1,0:T(8,128)(2,1)} custom-call(bf16[1,8,208,1920]{3,2,1,0:T(8,128)(2,1)} %bitcast.294, bf16[1,8,208,384]{3,2,1,0:T(8,128)(2,1)} %bitcast.310), custom_call_target="tpu_custom_call" | custom-call | flops 14976000000 | tf_op jit(solution)/shard_map/pallas_call | solution.py:135
  161.5 8.4 %convolution_convert_fusion.1 = bf16[1664,1536]{1,0:T(8,128)(2,1)} fusion(bf16[1664,768]{1,0:T(8,128)(2,1)S(1)} %add_convert_fusion.3, bf16[3840,768]{1,0:T(8,128)(2,1)} %bitcast.228), kind=kOutput, calls=%fused_computation.11 | convolution fusion | flops 3928424448 | bytes 10027008 | tf_op jit(solution)/shard_map/dot_general | solution.py:23
  184.0 12.0 %shard_map.140 = bf16[1,8,208,768]{3,2,1,0:T(8,128)(2,1)} custom-call(bf16[1,8,208,1536]{3,2,1,0:T(8,128)(2,1)} %bitcast.296, bf16[1,8,208,768]{3,2,1,0:T(8,128)(2,1)} %bitcast.304), custom_call_target="tpu_custom_call" | custom-call | flops 14976000000 | tf_op jit(solution)/shard_map/pallas_call | solution.py:135
  200.9 6.3 %fusion.77 = (f32[1664]{0:T(1024)S(1)}, f32[1664,768]{1,0:T(8,128)S(1)}) fusion(f32[768]{0:T(1024)S(1)} %add.401, bf16[1664,768]{1,0:T(8,128)(2,1)} %bitcast.302, bf16[5376,768]{1,0:T(8,128)(2,1)} %all-gather.2.cloned.1.call-done, bf16[1664,768]{1,0:T(8,128)(2,1)} %copy-done.13, bf16[1,8,208,768]{3,2,1,0:T(8,128)(2,1)} %copy-done.7), kind=kOutput, calls=%fused_computation.194 | convolution fusion | flops 1970600320 | bytes 13968896 | tf_op jit(solution)/shard_map/dot_general | solution.py:27
  209.5 17.1 %fusion.4 = (bf16[1664,3072]{1,0:T(8,128)(2,1)}, bf16[1664,3072]{1,0:T(8,128)(2,1)}) fusion(f32[3072]{0:T(1024)S(1)} %add.409, bf16[3840,768]{1,0:T(8,128)(2,1)S(1)} %bitcast.235, f32[1664,768]{1,0:T(8,128)S(1)} %get-tuple-element.337, f32[768]{0:T(1024)S(1)} %add.406, f32[768]{0:T(1024)S(1)} %mul.260, f32[1664]{0:T(1024)S(1)} %add_rsqrt_fusion, ...), kind=kOutput, calls=%fused_computation.5 | convolution fusion | flops 7919468544 | bytes 30314496 | tf_op jit(solution)/shard_map/dot_general | solution.py:23
  233.1 12.5 %add_convert_fusion.1 = bf16[1664,768]{1,0:T(8,128)(2,1)S(1)} fusion(f32[1664,768]{1,0:T(8,128)S(1)} %copy-done.19, bf16[1664,3072]{1,0:T(8,128)(2,1)} %get-tuple-element.168, bf16[5376,768]{1,0:T(8,128)(2,1)} %all-gather.2.cloned.1.call-done, f32[768]{0:T(1024)S(1)} %add.418), kind=kOutput, calls=%fused_computation.43 | convolution fusion | flops 7855570944 | bytes 22612992 | tf_op jit(solution)/shard_map/dot_general | solution.py:27
  252.3 14.8 %multiply_convert_fusion = bf16[1664,3072]{1,0:T(8,128)(2,1)} fusion(bf16[1664,3072]{1,0:T(8,128)(2,1)} %get-tuple-element.165, bf16[1664,768]{1,0:T(8,128)(2,1)S(1)} %bitcast.274, bf16[5376,768]{1,0:T(8,128)(2,1)} %all-gather.2.cloned.1.call-done), kind=kOutput, calls=%fused_computation.7 | convolution fusion | flops 7867072512 | bytes 27721728 | tf_op jit(solution)/shard_map/dot_general | solution.py:23
  267.1 13.8 %fusion.35.refs_0_.refs_1_ = bf16[384,8,768]{2,1,0:T(8,128)(2,1)S(1)} fusion(bf16[1664,3072]{1,0:T(8,128)(2,1)} %multiply_convert_fusion, f32[1664,768]{1,0:T(8,128)} %copy-done.18, f32[768]{0:T(1024)S(1)} %add.406, f32[768]{0:T(1024)S(1)} %mul.260, f32[1664]{0:T(1024)S(1)} %add_rsqrt_fusion, f32[1664]{0:T(1024)S(1)} %broadcast_multiply_fusion.6), kind=kOutput, calls=%fused_computation.79 | convolution fusion | flops 7860486144 | bytes 20073472 | tf_op jit(solution)/shard_map/dot_general | solution.py:31
  286.2 16.7 %multiply_reduce_fusion = (f32[768]{0:T(1024)S(1)}, f32[1664]{0:T(1024)S(1)}, f32[1664]{0:T(1024)S(1)}, f32[768]{0:T(1024)S(1)}, f32[1664,768]{1,0:T(8,128)}) fusion(f32[1664,768]{1,0:T(8,128)} %copy-done.18, f32[1664]{0:T(1024)S(1)} %add_rsqrt_fusion, f32[1664]{0:T(1024)S(1)} %broadcast_multiply_fusion.6, f32[768]{0:T(1024)S(1)} %mul.260, ...), kind=kOutput, calls=%fused_computation.38 | convolution fusion | flops 7863233536 | bytes 25205760 | tf_op jit(solution)/shard_map/dot_general | solution.py:27
  302.9 5.6 fusion.76
  308.5 5.8 convolution_convert_fusion.7
  314.3 13.0 %fusion.36.refs_3_ = bf16[384,8,768]{2,1,0:T(8,128)(2,1)} fusion(bf16[1664,3072]{1,0:T(8,128)(2,1)} %get-tuple-element.168, bf16[1664,768]{1,0:T(8,128)(2,1)S(1)} %bitcast.276), kind=kOutput, calls=%fused_computation.80 | convolution fusion | flops 7854096384 | bytes 17498112 | tf_op jit(solution)/shard_map/dot_general | solution.py:31
  333.5 26.0 %shard_map.142 = (bf16[1,8,208,1536]{3,2,1,0:T(8,128)(2,1)}, bf16[1,8,208,768]{3,2,1,0:T(8,128)(2,1)}) custom-call(bf16[1,8,208,1536]{3,2,1,0:T(8,128)(2,1)} %bitcast.297, bf16[1,8,208,768]{3,2,1,0:T(8,128)(2,1)} %bitcast.305, bf16[1,8,208,768]{3,2,1,0:T(8,128)(2,1)} %bitcast.308), custom_call_target="tpu_custom_call" | custom-call | flops 23296000000 | tf_op jit(solution)/shard_map/pallas_call | solution.py:135
  373.1 5.2 convolution_convert_fusion.9
  378.4 5.9 fusion.46
  384.4 10.8 %multiply_reduce_fusion.1 = (f32[768]{0:T(1024)S(1)}, f32[1664]{0:T(1024)S(1)}, f32[1664]{0:T(1024)S(1)}, f32[768]{0:T(1024)S(1)}, f32[1664,768]{1,0:T(8,128)S(1)}) fusion(f32[1664]{0:T(1024)S(1)} %copy-done.50, f32[1664]{0:T(1024)S(1)} %copy-done.44, bf16[1664,768]{1,0:T(8,128)(2,1)S(1)} %copy-done.14, bf16[1,8,208,768]{3,2,1,0:T(8,128)(2,1)S(1)} %copy-done.10, ...), kind=kOutput, calls=%fused_computation.39 | convolution fusion | flops 3942477056 | bytes 22842368 | tf_op jit(solution)/shard_map/dot_general | solution.py:27
  418.5 6.3 %shard_map.145 = bf16[672,8,768]{2,1,0:T(8,128)(2,1)} custom-call(bf16[96,8,768]{2,1,0:T(8,128)(2,1)} %fusion.41.refs_0_, bf16[96,8,768]{2,1,0:T(8,128)(2,1)} %fusion.42.refs_1_, bf16[96,8,768]{2,1,0:T(8,128)(2,1)} %fusion.43.refs_2_, bf16[384,8,768]{2,1,0:T(8,128)(2,1)} %fusion.36.refs_3_), custom_call_target="tpu_custom_call" | custom-call | bytes 33030144 | tf_op jit(solution)/shard_map/pallas_call | solution.py:274
  431.1 5.8 convolution_convert_fusion.5
  436.8 26.4 %shard_map.146 = bf16[1,8,208,2304]{3,2,1,0:T(8,128)(2,1)} custom-call(bf16[1,8,208,1920]{3,2,1,0:T(8,128)(2,1)} %bitcast.295, bf16[1,8,208,384]{3,2,1,0:T(8,128)(2,1)} %bitcast.311, bf16[1,8,208,768]{3,2,1,0:T(8,128)(2,1)} %bitcast.309), custom_call_target="tpu_custom_call" | custom-call | flops 23296000000 | tf_op jit(solution)/shard_map/pallas_call | solution.py:135
  464.1 9.3 %fusion.39.refs_0_ = bf16[288,8,768]{2,1,0:T(8,128)(2,1)S(1)} fusion(bf16[1664,2304]{1,0:T(8,128)(2,1)} %bitcast.292, bf16[1664,768]{1,0:T(8,128)(2,1)S(1)} %copy-done.26), kind=kOutput, calls=%fused_computation.83 | convolution fusion | flops 5890572288 | bytes 13762560 | tf_op jit(solution)/shard_map/dot_general | solution.py:31
  490.8 11.9 %fusion.19 = (f32[768]{0:T(1024)S(1)}, f32[1664]{0:T(1024)S(1)}, f32[1664]{0:T(1024)S(1)}, f32[768]{0:T(1024)S(1)}, f32[1664,768]{1,0:T(8,128)}) fusion(bf16[1,8,208,768]{3,2,1,0:T(8,128)(2,1)S(1)} %copy-done.11, f32[1664]{0:T(1024)S(1)} %copy-done.48, f32[1664]{0:T(1024)S(1)} %copy-done.46, f32[768]{0:T(1024)S(1)} %copy-done.52, ...), kind=kOutput, calls=%fused_computation.30 | convolution fusion | flops 5901577216 | bytes 18910208 | tf_op jit(solution)/shard_map/dot_general | solution.py:27
  502.8 15.8 %collective-permute-done.37 = bf16[2,288,768]{2,1,0:T(8,128)(2,1)} collective-permute-done((bf16[2,288,768]{2,1,0:T(8,128)(2,1)S(1)}, bf16[2,288,768]{2,1,0:T(8,128)(2,1)}, u32[]{:S(2)}, u32[]{:S(2)}) %collective-permute-start.37) | collective-permute-done | bytes 884768 | tf_op jit(solution)/shard_map/ppermute | solution.py:372
  528.2 9.0 %collective-permute-done.38 = bf16[288,768]{1,0:T(8,128)(2,1)S(1)} collective-permute-done((bf16[288,768]{1,0:T(8,128)(2,1)S(1)}, bf16[288,768]{1,0:T(8,128)(2,1)S(1)}, u32[]{:S(2)}, u32[]{:S(2)}) %collective-permute-start.38) | collective-permute-done | bytes 442400 | tf_op jit(solution)/shard_map/ppermute | solution.py:372
  559.1 5.9 convert_reduce_fusion
  567.8 5.3 collective-permute-done.43
  583.9 20.2 %all-to-all-start.4 = ((f32[32,16,128]{2,1,0:T(8,128)}), f32[32,16,128]{2,1,0:T(8,128)S(1)}, u32[]{:S(2)}, u32[]{:S(2)}) async-start(f32[32,16,128]{2,1,0:T(8,128)} %shard_map.148), calls=%async_computation.5 | async-start | bytes 524288 | tf_op jit(solution)/shard_map/all_to_all | solution.py:546
  (378 shorter events, 242.0 us)
Async XLA Ops:
  7.2 141.6 %all-gather.2.cloned.1.call-start = ((), (), s32[]{:S(2)}) async-start(), calls=%async_computation.6 | async-start | bytes 8515584 | tf_op jit(solution)/shard_map/all_gather | solution.py:366
  7.9 36.1 %all-to-all-start = ((bf16[4,2,196,768]{3,1,2,0:T(2,128)(2,1)}), bf16[4,2,196,768]{3,1,2,0:T(2,128)(2,1)}, u32[]{:S(2)}, u32[]{:S(2)}) async-start(bf16[4,2,196,768]{3,1,2,0:T(2,128)(2,1)} %param.8), calls=%async_computation | async-start | bytes 4816896 | tf_op jit(solution)/shard_map/all_to_all | solution.py:675
  13.3 34.2 %collective-permute-start.2 = (bf16[248,768]{1,0:T(8,128)(2,1)S(1)}, bf16[248,768]{1,0:T(8,128)(2,1)S(1)}, u32[]{:S(2)}, u32[]{:S(2)}) collective-permute-start(bf16[248,768]{1,0:T(8,128)(2,1)S(1)} %fusion.57), channel_id=1, source_target_pairs={{0,24},{1,25},{2,26},{3,27},{4,28},{5,29},{6,30},{7,31},{8,0},{9,1... | collective-permute-start | bytes 1142792 | tf_op jit(solution)/shard_map/ppermute | solution.py:375
  18.4 38.6 %collective-permute-start.1 = (bf16[248,768]{1,0:T(8,128)(2,1)S(1)}, bf16[248,768]{1,0:T(8,128)(2,1)S(1)}, u32[]{:S(2)}, u32[]{:S(2)}) collective-permute-start(bf16[248,768]{1,0:T(8,128)(2,1)S(1)} %fusion.57), channel_id=1, source_target_pairs={{0,16},{1,17},{2,18},{3,19},{4,20},{5,21},{6,22},{7,23},{8,24},{9,... | collective-permute-start | bytes 1142792 | tf_op jit(solution)/shard_map/ppermute | solution.py:375
  18.4 38.6 %collective-permute-start = (bf16[248,768]{1,0:T(8,128)(2,1)S(1)}, bf16[248,768]{1,0:T(8,128)(2,1)S(1)}, u32[]{:S(2)}, u32[]{:S(2)}) collective-permute-start(bf16[248,768]{1,0:T(8,128)(2,1)S(1)} %fusion.57), channel_id=1, source_target_pairs={{0,8},{1,9},{2,10},{3,11},{4,12},{5,13},{6,14},{7,15},{8,16},{9,17... | collective-permute-start | bytes 1142792 | tf_op jit(solution)/shard_map/ppermute | solution.py:375
  62.7 20.1 %collective-permute-start.4 = (bf16[272,768]{1,0:T(8,128)(2,1)S(1)}, bf16[272,768]{1,0:T(8,128)(2,1)S(1)}, u32[]{:S(2)}, u32[]{:S(2)}) collective-permute-start(bf16[272,768]{1,0:T(8,128)(2,1)S(1)} %pad_maximum_fusion.1), channel_id=1, source_target_pairs={{0,4},{1,5},{2,6},{3,7},{4,0},{5,1},{6,2},{7,3},{8,12},{9,13},{10,... | collective-permute-start | bytes 1253384 | tf_op jit(solution)/shard_map/ppermute | solution.py:372
  96.0 20.5 %collective-permute-start.11 = (bf16[240,768]{1,0:T(8,128)(2,1)}, bf16[240,768]{1,0:T(8,128)(2,1)}, u32[]{:S(2)}, u32[]{:S(2)}) collective-permute-start(bf16[240,768]{1,0:T(8,128)(2,1)} %get-tuple-element.152), channel_id=1, source_target_pairs={{0,4},{1,5},{2,6},{3,7},{4,0},{5,1},{6,2},{7,3},{8,12},{9,13},{10,... | collective-permute-start | bytes 1105928 | tf_op jit(solution)/shard_map/ppermute | solution.py:372
  120.8 49.2 %collective-permute-start.19 = (bf16[480,768]{1,0:T(8,128)(2,1)S(1)}, bf16[480,768]{1,0:T(8,128)(2,1)}, u32[]{:S(2)}, u32[]{:S(2)}) collective-permute-start(bf16[480,768]{1,0:T(8,128)(2,1)S(1)} %bitcast.241), channel_id=1, source_target_pairs={{0,6},{1,7},{2,4},{3,5},{4,2},{5,3},{6,0},{7,1},{8,14},{9,15},{10,... | collective-permute-start | bytes 2211848 | tf_op jit(solution)/shard_map/ppermute | solution.py:372
  122.3 47.7 %collective-permute-start.18 = (bf16[480,768]{1,0:T(8,128)(2,1)S(1)}, bf16[480,768]{1,0:T(8,128)(2,1)}, u32[]{:S(2)}, u32[]{:S(2)}) collective-permute-start(bf16[480,768]{1,0:T(8,128)(2,1)S(1)} %bitcast.242), channel_id=1, source_target_pairs={{0,4},{1,5},{2,6},{3,7},{4,0},{5,1},{6,2},{7,3},{8,12},{9,13},{10,... | collective-permute-start | bytes 2211848 | tf_op jit(solution)/shard_map/ppermute | solution.py:372
  123.8 46.2 %collective-permute-start.17 = (bf16[480,768]{1,0:T(8,128)(2,1)S(1)}, bf16[480,768]{1,0:T(8,128)(2,1)}, u32[]{:S(2)}, u32[]{:S(2)}) collective-permute-start(bf16[480,768]{1,0:T(8,128)(2,1)S(1)} %bitcast.243), channel_id=1, source_target_pairs={{0,2},{1,3},{2,0},{3,1},{4,6},{5,7},{6,4},{7,5},{8,10},{9,11},{10,... | collective-permute-start | bytes 2211848 | tf_op jit(solution)/shard_map/ppermute | solution.py:372
  196.0 33.9 %all-to-all-start.1 = ((bf16[4,2,196,768]{3,1,2,0:T(2,128)(2,1)}), bf16[4,2,196,768]{3,1,2,0:T(2,128)(2,1)}, u32[]{:S(2)}, u32[]{:S(2)}) async-start(bf16[4,2,196,768]{3,1,2,0:T(2,128)(2,1)} %param.9), calls=%async_computation.1 | async-start | bytes 4816896 | tf_op jit(solution)/shard_map/all_to_all | solution.py:675
  247.2 80.0 %all-to-all-start.2 = ((bf16[1,8,196,768]{3,2,0,1:T(8,128)(2,1)}), bf16[1,8,196,768]{3,2,0,1:T(8,128)(2,1)}, u32[]{:S(2)}, u32[]{:S(2)}) async-start(bf16[1,8,196,768]{3,2,0,1:T(8,128)(2,1)} %slice.210), calls=%async_computation.2 | async-start | bytes 4915200 | tf_op jit(solution)/shard_map/all_to_all | solution.py:682
  251.8 330.5 %reduce-scatter.2.cloned.1.call-start = ((), (), s32[]{:S(2)}) async-start(), calls=%async_computation.7 | async-start | bytes 8515584 | tf_op jit(solution)/shard_map/reduce_scatter | solution.py:468
  285.8 41.5 %collective-permute-start.24 = (bf16[4,240,768]{2,1,0:T(8,128)(2,1)S(1)}, bf16[4,240,768]{2,1,0:T(8,128)(2,1)}, u32[]{:S(2)}, u32[]{:S(2)}) collective-permute-start(bf16[4,240,768]{2,1,0:T(8,128)(2,1)S(1)} %bitcast.271), channel_id=1, source_target_pairs={{0,1},{1,0},{2,3},{3,2},{4,5},{5,4},{6,7},{7,6},{8,9},{9,8},{10,11... | collective-permute-start | bytes 4423688 | tf_op jit(solution)/shard_map/ppermute | solution.py:372
  330.0 29.5 %collective-permute-start.27 = (bf16[240,768]{1,0:T(8,128)(2,1)}, bf16[240,768]{1,0:T(8,128)(2,1)S(1)}, u32[]{:S(2)}, u32[]{:S(2)}) collective-permute-start(bf16[240,768]{1,0:T(8,128)(2,1)} %get-tuple-element.320), channel_id=1, source_target_pairs={{0,6},{1,7},{2,4},{3,5},{4,2},{5,3},{6,0},{7,1},{8,14},{9,15},{10,... | collective-permute-start | bytes 1105928 | tf_op jit(solution)/shard_map/ppermute | solution.py:372
  332.6 27.0 %collective-permute-start.26 = (bf16[240,768]{1,0:T(8,128)(2,1)}, bf16[240,768]{1,0:T(8,128)(2,1)S(1)}, u32[]{:S(2)}, u32[]{:S(2)}) collective-permute-start(bf16[240,768]{1,0:T(8,128)(2,1)} %get-tuple-element.321), channel_id=1, source_target_pairs={{0,4},{1,5},{2,6},{3,7},{4,0},{5,1},{6,2},{7,3},{8,12},{9,13},{10,... | collective-permute-start | bytes 1105928 | tf_op jit(solution)/shard_map/ppermute | solution.py:372
  333.1 26.5 %collective-permute-start.25 = (bf16[240,768]{1,0:T(8,128)(2,1)}, bf16[240,768]{1,0:T(8,128)(2,1)}, u32[]{:S(2)}, u32[]{:S(2)}) collective-permute-start(bf16[240,768]{1,0:T(8,128)(2,1)} %get-tuple-element.322), channel_id=1, source_target_pairs={{0,2},{1,3},{2,0},{3,1},{4,6},{5,7},{6,4},{7,5},{8,10},{9,11},{10,... | collective-permute-start | bytes 1105928 | tf_op jit(solution)/shard_map/ppermute | solution.py:372
  396.3 28.5 %collective-permute-start.31 = (bf16[240,768]{1,0:T(8,128)(2,1)S(1)}, bf16[240,768]{1,0:T(8,128)(2,1)}, u32[]{:S(2)}, u32[]{:S(2)}) collective-permute-start(bf16[240,768]{1,0:T(8,128)(2,1)S(1)} %get-tuple-element.316), channel_id=1, source_target_pairs={{0,6},{1,7},{2,4},{3,5},{4,2},{5,3},{6,0},{7,1},{8,14},{9,15},{10,... | collective-permute-start | bytes 1105928 | tf_op jit(solution)/shard_map/ppermute | solution.py:372
  398.9 25.9 %collective-permute-start.30 = (bf16[240,768]{1,0:T(8,128)(2,1)S(1)}, bf16[240,768]{1,0:T(8,128)(2,1)}, u32[]{:S(2)}, u32[]{:S(2)}) collective-permute-start(bf16[240,768]{1,0:T(8,128)(2,1)S(1)} %get-tuple-element.317), channel_id=1, source_target_pairs={{0,4},{1,5},{2,6},{3,7},{4,0},{5,1},{6,2},{7,3},{8,12},{9,13},{10,... | collective-permute-start | bytes 1105928 | tf_op jit(solution)/shard_map/ppermute | solution.py:372
  399.4 25.4 %collective-permute-start.29 = (bf16[240,768]{1,0:T(8,128)(2,1)S(1)}, bf16[240,768]{1,0:T(8,128)(2,1)}, u32[]{:S(2)}, u32[]{:S(2)}) collective-permute-start(bf16[240,768]{1,0:T(8,128)(2,1)S(1)} %get-tuple-element.318), channel_id=1, source_target_pairs={{0,2},{1,3},{2,0},{3,1},{4,6},{5,7},{6,4},{7,5},{8,10},{9,11},{10,... | collective-permute-start | bytes 1105928 | tf_op jit(solution)/shard_map/ppermute | solution.py:372
  427.6 35.6 %collective-permute-start.35 = (bf16[240,768]{1,0:T(8,128)(2,1)}, bf16[240,768]{1,0:T(8,128)(2,1)S(1)}, u32[]{:S(2)}, u32[]{:S(2)}) collective-permute-start(bf16[240,768]{1,0:T(8,128)(2,1)} %get-tuple-element.312), channel_id=1, source_target_pairs={{0,6},{1,7},{2,4},{3,5},{4,2},{5,3},{6,0},{7,1},{8,14},{9,15},{10,... | collective-permute-start | bytes 1105928 | tf_op jit(solution)/shard_map/ppermute | solution.py:372
  430.2 33.0 %collective-permute-start.34 = (bf16[240,768]{1,0:T(8,128)(2,1)}, bf16[240,768]{1,0:T(8,128)(2,1)S(1)}, u32[]{:S(2)}, u32[]{:S(2)}) collective-permute-start(bf16[240,768]{1,0:T(8,128)(2,1)} %get-tuple-element.313), channel_id=1, source_target_pairs={{0,4},{1,5},{2,6},{3,7},{4,0},{5,1},{6,2},{7,3},{8,12},{9,13},{10,... | collective-permute-start | bytes 1105928 | tf_op jit(solution)/shard_map/ppermute | solution.py:372
  430.7 32.5 %collective-permute-start.33 = (bf16[240,768]{1,0:T(8,128)(2,1)}, bf16[240,768]{1,0:T(8,128)(2,1)}, u32[]{:S(2)}, u32[]{:S(2)}) collective-permute-start(bf16[240,768]{1,0:T(8,128)(2,1)} %get-tuple-element.314), channel_id=1, source_target_pairs={{0,2},{1,3},{2,0},{3,1},{4,6},{5,7},{6,4},{7,5},{8,10},{9,11},{10,... | collective-permute-start | bytes 1105928 | tf_op jit(solution)/shard_map/ppermute | solution.py:372
  489.2 29.4 %collective-permute-start.37 = (bf16[2,288,768]{2,1,0:T(8,128)(2,1)S(1)}, bf16[2,288,768]{2,1,0:T(8,128)(2,1)}, u32[]{:S(2)}, u32[]{:S(2)}) collective-permute-start(bf16[2,288,768]{2,1,0:T(8,128)(2,1)S(1)} %get-tuple-element.204), channel_id=1, source_target_pairs={{0,4},{1,5},{2,6},{3,7},{4,0},{5,1},{6,2},{7,3},{8,12},{9,13},{10,... | collective-permute-start | bytes 2654216 | tf_op jit(solution)/shard_map/ppermute | solution.py:372
  539.6 38.5 %all-to-all-start.3 = ((bf16[1,8,196,768]{3,2,0,1:T(8,128)(2,1)}), bf16[1,8,196,768]{3,2,0,1:T(8,128)(2,1)S(1)}, u32[]{:S(2)}, u32[]{:S(2)}) async-start(bf16[1,8,196,768]{3,2,0,1:T(8,128)(2,1)} %slice.212), calls=%async_computation.3 | async-start | bytes 4915200 | tf_op jit(solution)/shard_map/all_to_all | solution.py:682
  547.8 57.3 %collective-permute-start.40 = (bf16[240,768]{1,0:T(8,128)(2,1)}, bf16[240,768]{1,0:T(8,128)(2,1)}, u32[]{:S(2)}, u32[]{:S(2)}) collective-permute-start(bf16[240,768]{1,0:T(8,128)(2,1)} %get-tuple-element.245), channel_id=1, source_target_pairs={{0,8},{1,9},{2,10},{3,11},{4,12},{5,13},{6,14},{7,15},{8,16},{9,17... | collective-permute-start | bytes 1105928 | tf_op jit(solution)/shard_map/ppermute | solution.py:375
  549.0 56.2 %collective-permute-start.41 = (bf16[240,768]{1,0:T(8,128)(2,1)}, bf16[240,768]{1,0:T(8,128)(2,1)}, u32[]{:S(2)}, u32[]{:S(2)}) collective-permute-start(bf16[240,768]{1,0:T(8,128)(2,1)} %get-tuple-element.246), channel_id=1, source_target_pairs={{0,16},{1,17},{2,18},{3,19},{4,20},{5,21},{6,22},{7,23},{8,24},{9,... | collective-permute-start | bytes 1105928 | tf_op jit(solution)/shard_map/ppermute | solution.py:375
  552.7 20.3 %collective-permute-start.43 = (bf16[96,768]{1,0:T(8,128)(2,1)S(1)}, bf16[96,768]{1,0:T(8,128)(2,1)S(1)}, u32[]{:S(2)}, u32[]{:S(2)}) collective-permute-start(bf16[96,768]{1,0:T(8,128)(2,1)S(1)} %constant_dynamic-update-slice_fusion), channel_id=1, source_target_pairs={{0,8},{1,9},{2,10},{3,11},{4,12},{5,13},{6,14},{7,15}} | collective-permute-start | bytes 442376 | tf_op jit(solution)/shard_map/ppermute | solution.py:514
  566.0 39.1 %collective-permute-start.42 = (bf16[240,768]{1,0:T(8,128)(2,1)}, bf16[240,768]{1,0:T(8,128)(2,1)}, u32[]{:S(2)}, u32[]{:S(2)}) collective-permute-start(bf16[240,768]{1,0:T(8,128)(2,1)} %get-tuple-element.247), channel_id=1, source_target_pairs={{0,24},{1,25},{2,26},{3,27},{4,28},{5,29},{6,30},{7,31},{8,0},{9,1... | collective-permute-start | bytes 1105928 | tf_op jit(solution)/shard_map/ppermute | solution.py:375
  575.4 28.7 %collective-permute-start.47 = (bf16[96,768]{1,0:T(8,128)(2,1)S(1)}, bf16[96,768]{1,0:T(8,128)(2,1)S(1)}, u32[]{:S(2)}, u32[]{:S(2)}) collective-permute-start(bf16[96,768]{1,0:T(8,128)(2,1)S(1)} %add_convert_fusion.26), channel_id=1, source_target_pairs={{12,8},{13,9}} | collective-permute-start | bytes 442376 | tf_op jit(solution)/shard_map/ppermute | solution.py:536
  576.1 29.1 %collective-permute-start.46 = (bf16[96,768]{1,0:T(8,128)(2,1)S(1)}, bf16[96,768]{1,0:T(8,128)(2,1)}, u32[]{:S(2)}, u32[]{:S(2)}) collective-permute-start(bf16[96,768]{1,0:T(8,128)(2,1)S(1)} %add_convert_fusion.26), channel_id=1, source_target_pairs={{10,8},{11,9}} | collective-permute-start | bytes 442376 | tf_op jit(solution)/shard_map/ppermute | solution.py:536
  583.9 33.5 %all-to-all-start.4 = ((f32[32,16,128]{2,1,0:T(8,128)}), f32[32,16,128]{2,1,0:T(8,128)S(1)}, u32[]{:S(2)}, u32[]{:S(2)}) async-start(f32[32,16,128]{2,1,0:T(8,128)} %shard_map.148), calls=%async_computation.5 | async-start | bytes 524288 | tf_op jit(solution)/shard_map/all_to_all | solution.py:546
  (99 other events, 1001.5 us)
Sparse Core Ops, SparseCore 0:
  10.9 108.5 all-gather.1
  425.0 157.2 reduce-scatter.1
